TPU v7x, 128 devices: a whole 4x4x4 slice. The times are simulated.
128 devices in a mesh: dp: 16 (over x, y_hi, core), mp: 8 (over y_lo, z).
Axes of the slice: x: 4, y: 4 (y_hi: 2, y_lo: 2; y = y_hi * 2 + y_lo), z: 4, core: 2. Of those that a mesh axis runs over, the one named last changes fastest.
Arguments:
- hidden: bfloat16 [16384, 2048], P(('dp', 'mp')), may hold values from -4 to 4
- norm_gains: float32 [3, 2048], replicated, may hold values from 0.5 to 1.5
- head_gains: float32 [3, 128], replicated, may hold values from 0.25 to 1.75
- query_weight: bfloat16 [2048, 2048], P(('dp', 'mp')), may hold values from -0.125 to 0.125
- kv_weight: bfloat16 [2048, 512], P(('dp', 'mp')), may hold values from -0.125 to 0.125
- out_weight: bfloat16 [2048, 2048], P(('dp', 'mp')), may hold values from -0.5 to 0.5
- gate_up: bfloat16 [128, 2048, 1536], P(('dp', 'mp')), may hold values from -0.125 to 0.125
- down_weight: bfloat16 [128, 768, 2048], P(('dp', 'mp')), may hold values from -0.21875 to 0.21875
- next_weight: bfloat16 [2048, 512], P(('dp', 'mp')), may hold values from -0.125 to 0.125
- expert_ids: int32 [16384, 8], P(('dp', 'mp')), may hold values from 0 to 127, all different within a row; in each aligned block of 128 rows (0 to 127, 128 to 255, ...) at most 10 rows name the same one
- route_weights: float32 [16384, 8], P(('dp', 'mp')), may hold values from 0.05 to 0.5
- token_request: int32 [16384], P('dp'), may hold values from 0 to 31, as said below
- request_leaf: int32 [32], replicated, may hold values from 0 to 15
- leaf_parent: int32 [16], replicated, may hold values from 0 to 7
- mid_parent: int32 [8], replicated, may hold values from 0 to 7
- root_length: int32 [8], replicated, may hold values from 1 to 512, as said below
- mid_length: int32 [8], replicated, may hold values from 1 to 256, as said below
- leaf_length: int32 [16], replicated, may hold values from 1 to 128, as said below
- root_slot: int32 [8], replicated, may hold values from 0 to 7, each once
- mid_slot: int32 [8], replicated, may hold values from 0 to 7, each once
- leaf_slot: int32 [16], replicated, may hold values from 0 to 15, each once
- root_cache: bfloat16 [8, 512, 512], P('mp'), may hold values from -300 to 300
- mid_cache: bfloat16 [8, 256, 512], P('mp'), may hold values from -300 to 300
- leaf_cache: bfloat16 [16, 128, 512], P('mp'), may hold values from -300 to 300
Outputs:
- layer_out: bfloat16 [16384, 2048], P(('dp', 'mp'))
- next_rows: bfloat16 [16384, 512], P(('dp', 'mp'))
Inputs may be any that keep to these rules, and one draw needn't show every extreme that they name: `expert_ids`: each row names 8 different experts; among the rows of one device no expert is named more than 10 times, a bound that some block reaches. `token_request`: Nondecreasing; tokens g * 1024 to (g + 1) * 1024 - 1 belong to requests g * 2 to (g + 1) * 2 - 1, and every request has at least one token. `root_length`: some root node has the full length. `mid_length`: some middle node has the full length. `leaf_length`: some leaf node has the full length. `root_slot`: each slot once; slot s is on index s // 1 of mp. `mid_slot`: each slot once; slot s is on index s // 1 of mp. `leaf_slot`: each slot once; slot s is on index s // 2 of mp.
All inputs are finite; a program needn't handle non-finite values.
Results may differ from a plain program's by a relative error of at most 0.024.
Values may be sent and summed in bfloat16 or wider, within the bound.
No kernel may reach another device: no remote copies, remote signals or barrier semaphores. Data moves between devices by JAX's collectives and lax.ppermute only.
A program may use at most 192 MiB of HBM per device.

v0:
```python
import jax
import jax.numpy as jnp
from jax import lax
from jax.sharding import PartitionSpec as P

REQ_GRP = 2


EPS = 1e-06
THETA = 1000000.0
MASKED = -1e30


def rms_norm(values, weight_row):
    values = values.astype(jnp.float32)
    return values * lax.rsqrt(jnp.mean(values * values, axis=-1, keepdims=True) + EPS) * weight_row


def rotate(values, positions):
    half_dim = values.shape[-1] // 2
    frequency = THETA ** (-2.0 * jnp.arange(half_dim, dtype=jnp.float32) / values.shape[-1])
    angles = positions.astype(jnp.float32)[:, None] * frequency[None, :]
    cosine = jnp.cos(angles)[:, None, :]
    sine_part = jnp.sin(angles)[:, None, :]
    front_part = values[..., :half_dim]
    back_part = values[..., half_dim:]
    return jnp.concatenate(
        [front_part * cosine - back_part * sine_part, back_part * cosine + front_part * sine_part],
        axis=-1,
    )


def look_up(lookup_table, indices):
    places = jnp.arange(lookup_table.shape[0], dtype=jnp.int32)
    return jnp.sum(jnp.where(indices[:, None] == places[None, :], lookup_table[None, :], 0), axis=1)


def tree_paths(requests, request_leaf, leaf_parent, mid_parent, lengths, slot_tables):
    leaf_node = look_up(request_leaf, requests)
    mid_node = look_up(leaf_parent, leaf_node)
    root_node = look_up(mid_parent, mid_node)
    node_sets = (root_node, mid_node, leaf_node)
    path_slots = [
        look_up(slot_table, node_ids) for slot_table, node_ids in zip(slot_tables, node_sets)
    ]
    path_lengths = [
        look_up(length_table, node_ids) for length_table, node_ids in zip(lengths, node_sets)
    ]
    return (path_slots, path_lengths)


def head_scores(queries, key_rows, allowed):
    kv_heads = queries.shape[1]
    head_dim = queries.shape[3]
    score_scale = head_dim ** (-0.5)
    outcome = []
    for head_no in range(kv_heads):
        key_part = key_rows[:, head_no * head_dim : (head_no + 1) * head_dim]
        raw_scores = (
            jnp.einsum(
                "ngd,pd->ngp", queries[:, head_no], key_part, preferred_element_type=jnp.float32
            )
            * score_scale
        )
        outcome.append(jnp.where(allowed[:, None, :], raw_scores, MASKED))
    return outcome


def head_peaks(score_list):
    return jnp.stack([jnp.max(scores, axis=2) for scores in score_list], axis=1)


def head_sums(score_list, row_shift, key_rows, allowed):
    kv_width = key_rows.shape[1] // 2
    head_dim = kv_width // len(score_list)
    numerators = []
    totals = []
    for head_no, scores in enumerate(score_list):
        weights = jnp.where(
            allowed[:, None, :], jnp.exp(scores - row_shift[:, head_no, :, None]), 0.0
        )
        value_part = key_rows[
            :, kv_width + head_no * head_dim : kv_width + (head_no + 1) * head_dim
        ]
        numerators.append(
            jnp.einsum(
                "ngp,pd->ngd",
                weights.astype(jnp.bfloat16),
                value_part,
                preferred_element_type=jnp.float32,
            )
        )
        totals.append(jnp.sum(weights, axis=2))
    return (jnp.stack(numerators, axis=1), jnp.stack(totals, axis=1))


def join_parts(pre_peak, pre_num, pre_total, self_peak, self_num, self_total):
    row_top = jnp.maximum(pre_peak, self_peak)
    pre_factor = jnp.exp(pre_peak - row_top)
    self_factor = jnp.exp(self_peak - row_top)
    combined = pre_num * pre_factor[..., None] + self_num * self_factor[..., None]
    divisor = pre_total * pre_factor + self_total * self_factor
    return combined / divisor[..., None]


def fold_rows(source, pieces):
    return tuple(
        (jnp.dot(source, piece_now, preferred_element_type=jnp.float32) for piece_now in pieces)
    )


def per_device(
    hidden,
    norm_gains,
    head_gains,
    query_weight,
    kv_weight,
    out_weight,
    gate_up,
    down_weight,
    next_weight,
    expert_ids,
    route_weights,
    token_request,
    request_leaf,
    leaf_parent,
    mid_parent,
    root_length,
    mid_length,
    leaf_length,
    root_slot,
    mid_slot,
    leaf_slot,
    root_cache,
    mid_cache,
    leaf_cache,
):
    tok_rows = hidden.shape[0]
    model_dim = hidden.shape[1]
    head_dim = head_gains.shape[1]
    kv_width = kv_weight.shape[1] // 2
    kv_heads = kv_width // head_dim
    query_width = query_weight.shape[1]
    head_count = query_width // head_dim
    head_ratio = head_count // kv_heads
    group_tok = token_request.shape[0]
    mp_size = lax.axis_size("mp")
    devices_all = lax.axis_size("dp") * mp_size
    my_first = lax.axis_index("mp") * tok_rows
    lengths = (root_length, mid_length, leaf_length)
    slot_tables = (root_slot, mid_slot, leaf_slot)
    my_request = lax.dynamic_slice_in_dim(token_request, my_first, tok_rows)
    request_first = jnp.sum(
        (token_request[None, :] < my_request[:, None]).astype(jnp.int32), axis=1
    )
    my_places = my_first + jnp.arange(tok_rows, dtype=jnp.int32)
    my_slots, my_lengths = tree_paths(
        my_request, request_leaf, leaf_parent, mid_parent, lengths, slot_tables
    )
    positions = my_lengths[0] + my_lengths[1] + my_lengths[2] + my_places - request_first
    normed = rms_norm(hidden, norm_gains[0]).astype(jnp.bfloat16)
    query_raw, kv_raw = fold_rows(
        normed,
        (
            lax.all_gather(query_weight, ("dp", "mp"), axis=0, tiled=True),
            lax.all_gather(kv_weight, ("dp", "mp"), axis=0, tiled=True),
        ),
    )
    queries = rotate(
        rms_norm(query_raw.reshape(tok_rows, head_count, head_dim), head_gains[0]), positions
    ).astype(jnp.bfloat16)
    new_keys = rotate(
        rms_norm(kv_raw[:, :kv_width].reshape(tok_rows, kv_heads, head_dim), head_gains[1]),
        positions,
    ).astype(jnp.bfloat16)
    new_rows = jnp.concatenate(
        [new_keys.reshape(tok_rows, kv_width), kv_raw[:, kv_width:].astype(jnp.bfloat16)], axis=1
    )
    group_rows = lax.all_gather(new_rows, "mp", axis=0, tiled=True)
    self_allowed = (my_request[:, None] == token_request[None, :]) & (
        jnp.arange(group_tok, dtype=jnp.int32)[None, :] <= my_places[:, None]
    )
    my_queries = queries.reshape(tok_rows, kv_heads, head_ratio, head_dim)
    self_scores = head_scores(my_queries, group_rows, self_allowed)
    self_peak = head_peaks(self_scores)
    self_num, self_total = head_sums(self_scores, self_peak, group_rows, self_allowed)
    gathered = (
        lax.all_gather(root_cache, "mp", axis=0, tiled=True),
        lax.all_gather(mid_cache, "mp", axis=0, tiled=True),
        lax.all_gather(leaf_cache, "mp", axis=0, tiled=True),
    )
    first_request = token_request[0]
    path_rows = []
    path_masks = []
    for request_no in range(REQ_GRP):
        request_id = first_request + request_no
        chosen_slots, chosen_lengths = tree_paths(
            jnp.reshape(request_id, (1,)),
            request_leaf,
            leaf_parent,
            mid_parent,
            lengths,
            slot_tables,
        )
        mine = my_request == request_id
        for level_no in range(3):
            level_part = gathered[level_no]
            path_rows.append(
                lax.dynamic_index_in_dim(level_part, chosen_slots[level_no][0], 0, keepdims=False)
            )
            within = jnp.arange(level_part.shape[1], dtype=jnp.int32)
            path_masks.append(mine[:, None] & (within[None, :] < chosen_lengths[level_no][0]))
    prefix_rows = jnp.concatenate(path_rows, axis=0)
    prefix_allowed = jnp.concatenate(path_masks, axis=1)
    pre_scores = head_scores(my_queries, prefix_rows, prefix_allowed)
    pre_peak = head_peaks(pre_scores)
    pre_num, pre_total = head_sums(pre_scores, pre_peak, prefix_rows, prefix_allowed)
    attended = (
        join_parts(pre_peak, pre_num, pre_total, self_peak, self_num, self_total)
        .reshape(tok_rows, query_width)
        .astype(jnp.bfloat16)
    )
    projected = fold_rows(
        attended, (lax.all_gather(out_weight, ("dp", "mp"), axis=0, tiled=True),)
    )[0]
    after_attention = (hidden.astype(jnp.float32) + projected).astype(jnp.bfloat16)
    moe_in = rms_norm(after_attention, norm_gains[1]).astype(jnp.bfloat16)
    top_k = expert_ids.shape[1]
    experts_all = gate_up.shape[0] * devices_all
    capacity = max(2, 5 * tok_rows * top_k // (4 * experts_all))
    flat_ids = expert_ids.reshape(-1)
    flat_count = flat_ids.shape[0]
    order_ids = jnp.arange(flat_count, dtype=jnp.int32)
    earlier = (flat_ids[:, None] == flat_ids[None, :]) & (order_ids[None, :] < order_ids[:, None])
    slot_no = jnp.sum(earlier.astype(jnp.int32), axis=1)
    target = flat_ids * capacity + slot_no
    spread_rows = jnp.broadcast_to(moe_in[:, None, :], (tok_rows, top_k, model_dim)).reshape(
        flat_count, model_dim
    )
    outbound = (
        jnp.zeros((experts_all * capacity, model_dim), jnp.bfloat16).at[target].set(spread_rows)
    )
    block_in = lax.all_to_all(
        outbound.reshape(devices_all, 1, capacity, model_dim),
        ("dp", "mp"),
        split_axis=0,
        concat_axis=1,
        tiled=True,
    )
    rows_in = block_in.reshape(-1, model_dim)
    gate_up_out = jnp.dot(rows_in, gate_up[0], preferred_element_type=jnp.float32)
    ff_width = down_weight.shape[1]
    active = (jax.nn.silu(gate_up_out[:, :ff_width]) * gate_up_out[:, ff_width:]).astype(
        jnp.bfloat16
    )
    served = (
        jnp.dot(active, down_weight[0], preferred_element_type=jnp.float32)
        .astype(jnp.bfloat16)
        .reshape(block_in.shape)
    )
    returned = lax.all_to_all(served, ("dp", "mp"), split_axis=1, concat_axis=0, tiled=True)
    expert_rows = returned.reshape(experts_all * capacity, model_dim)[target]
    mixture = jnp.sum(
        expert_rows.astype(jnp.float32).reshape(tok_rows, top_k, model_dim)
        * route_weights[:, :, None],
        axis=1,
    )
    layer_out = (after_attention.astype(jnp.float32) + mixture).astype(jnp.bfloat16)
    next_in = rms_norm(layer_out, norm_gains[2]).astype(jnp.bfloat16)
    next_raw = fold_rows(next_in, (lax.all_gather(next_weight, ("dp", "mp"), axis=0, tiled=True),))[
        0
    ]
    next_keys = rotate(
        rms_norm(next_raw[:, :kv_width].reshape(tok_rows, kv_heads, head_dim), head_gains[2]),
        positions,
    ).astype(jnp.bfloat16)
    next_rows = jnp.concatenate(
        [next_keys.reshape(tok_rows, kv_width), next_raw[:, kv_width:].astype(jnp.bfloat16)], axis=1
    )
    return (layer_out, next_rows)


def solution(mesh):
    placed = (
        P(("dp", "mp"), None),
        P(),
        P(),
        P(("dp", "mp"), None),
        P(("dp", "mp"), None),
        P(("dp", "mp"), None),
        P(("dp", "mp"), None, None),
        P(("dp", "mp"), None, None),
        P(("dp", "mp"), None),
        P(("dp", "mp"), None),
        P(("dp", "mp"), None),
        P("dp"),
        P(),
        P(),
        P(),
        P(),
        P(),
        P(),
        P(),
        P(),
        P(),
        P("mp", None, None),
        P("mp", None, None),
        P("mp", None, None),
    )
    return jax.shard_map(
        per_device,
        mesh=mesh,
        in_specs=placed,
        out_specs=(P(("dp", "mp"), None), P(("dp", "mp"), None)),
        check_vma=False,
    )
```

profile of v0, /device:TPU:0, one launch (start us, length us, event | category | flops | bytes accessed | tf_op | source)
XLA Modules:
  0.0 1666.3 jit_solution(7209893921031694401)
XLA Ops:
  20.6 1.5 fusion.100
  22.1 290.0 %all-gather.17.cloned.1.call-done = bf16[2048,512]{1,0:T(8,128)(2,1)} async-done(((bf16[16,512]{1,0:T(8,128)(2,1)}), bf16[2048,512]{1,0:T(8,128)(2,1)}) %all-gather.17.cloned.1.call-update) | async-done | bytes 2097168 | tf_op jit(solution)/shard_map/all_gather | solution.py:166
  312.1 2.2 fusion.71
  316.7 1.5 pad_maximum_fusion.1
  319.0 2.0 fusion.82
  321.0 2.7 select_reduce_fusion.13
  323.7 2.7 select_reduce_fusion.12
  326.4 2.7 fusion.79
  330.3 2.7 select_reduce_fusion.7
  336.8 2.7 select_reduce_fusion.6
  356.3 11.5 all-gather.11.cloned.1.call-done
  367.9 1.9 bitcast_dynamic-update-slice_fusion.1
  369.8 40.3 %all-gather.13.cloned.1.call-done = bf16[8,256,512]{2,1,0:T(8,128)(2,1)} async-done(((bf16[1,256,512]{2,1,0:T(8,128)(2,1)}), bf16[8,256,512]{2,1,0:T(8,128)(2,1)}) %all-gather.13.cloned.1.call-update) | async-done | bytes 2097168 | tf_op jit(solution)/shard_map/all_gather | solution.py:189
  410.1 1.7 bitcast_dynamic-update-slice_fusion.3
  411.8 40.7 %all-gather.15.cloned.1.call-done = bf16[16,128,512]{2,1,0:T(8,128)(2,1)} async-done(((bf16[2,128,512]{2,1,0:T(8,128)(2,1)}), bf16[16,128,512]{2,1,0:T(8,128)(2,1)}) %all-gather.15.cloned.1.call-update) | async-done | bytes 2097168 | tf_op jit(solution)/shard_map/all_gather | solution.py:190
  452.4 1.6 bitcast_dynamic-update-slice_fusion.5
  454.0 1.9 bitcast_dynamic-update-slice_fusion
  455.9 1.7 bitcast_dynamic-update-slice_fusion.2
  457.6 1.6 bitcast_dynamic-update-slice_fusion.4
  459.1 305.2 %all-gather.9.cloned.1.call-done = bf16[2048,2048]{1,0:T(8,128)(2,1)} async-done(((bf16[16,2048]{1,0:T(8,128)(2,1)}), bf16[2048,2048]{1,0:T(8,128)(2,1)}) %all-gather.9.cloned.1.call-update) | async-done | bytes 8388624 | tf_op jit(solution)/shard_map/all_gather | solution.py:165
  764.3 4.9 convolution_bitcast_fusion
  773.0 1.6 multiply_multiply_fusion
  774.6 1.4 subtract_convert_fusion
  777.9 28.7 %all-gather.19.cloned.1.call-done = bf16[1024,512]{1,0:T(8,128)(2,1)} async-done(((bf16[128,512]{1,0:T(8,128)(2,1)}), bf16[1024,512]{1,0:T(8,128)(2,1)}) %all-gather.19.cloned.1.call-update) | async-done | bytes 1048592 | tf_op jit(solution)/shard_map/all_gather | solution.py:179
  806.6 2.3 fusion.13
  809.0 1.6 fusion.1
  810.6 2.3 fusion.22
  814.2 3.7 fusion.5
  817.9 2.2 fusion.7
  822.7 2.1 fusion.41
  824.8 2.1 fusion.38
  827.9 289.7 %all-gather.21.cloned.1.call-done = bf16[2048,2048]{1,0:T(8,128)(2,1)} async-done(((bf16[16,2048]{1,0:T(8,128)(2,1)}), bf16[2048,2048]{1,0:T(8,128)(2,1)}) %all-gather.21.cloned.1.call-update) | async-done | bytes 8388624 | tf_op jit(solution)/shard_map/all_gather | solution.py:224
  1117.6 4.9 multiply_reduce_fusion
  1124.5 10.4 scatter_custom_fusion
  1134.9 9.5 reshape.559
  1144.4 109.3 %all_to_all.8 = bf16[128,1,10,2048]{3,2,1,0:T(8,128)(2,1)} all-to-all(bf16[128,1,10,2048]{3,2,1,0:T(8,128)(2,1)} %bitcast.122), channel_id=1, replica_groups=mesh['dp'=16,'mp'=8] {'dp','mp'}, dimensions={0} | all-to-all | bytes 10485760 | tf_op jit(solution)/shard_map/all_to_all | solution.py:243
  1253.7 9.8 reshape.560
  1263.5 12.1 fusion.3
  1275.6 6.1 convolution_convert_fusion
  1281.7 9.5 reshape.561
  1291.2 6.3 all-to-all-start.1
  1298.4 102.2 %all-to-all-done.1 = bf16[1,128,10,2048]{3,2,0,1:T(8,128)(2,1)} async-done(((bf16[1,128,10,2048]{3,2,0,1:T(8,128)(2,1)}), bf16[1,128,10,2048]{3,2,0,1:T(8,128)(2,1)}, u32[]{:S(2)}, u32[]{:S(2)}) %all-to-all-start.1) | async-done | bytes 5242912 | tf_op jit(solution)/shard_map/all_to_all | solution.py:261
  1400.6 9.8 reshape.562
  1410.5 12.0 gather_fusion
  1422.5 6.6 fusion
  1430.1 223.7 %all-gather.23.cloned.1.call-done = bf16[2048,512]{1,0:T(8,128)(2,1)} async-done(((bf16[16,512]{1,0:T(8,128)(2,1)}), bf16[2048,512]{1,0:T(8,128)(2,1)}) %all-gather.23.cloned.1.call-update) | async-done | bytes 2097168 | tf_op jit(solution)/shard_map/all_gather | solution.py:270
  1653.7 2.3 fusion.59
  1657.7 1.5 pad_maximum_fusion.2
  (132 shorter events, 42.3 us)
Async XLA Ops:
  7.2 1268.4 %copy-start = (bf16[1,768,2048]{2,1,0:T(8,128)(2,1)S(1)}, bf16[1,768,2048]{2,1,0:T(8,128)(2,1)}, u32[]{:S(2)}) copy-start(bf16[1,768,2048]{2,1,0:T(8,128)(2,1)} %param.31) | copy-start | bytes 9437188
  7.2 305.0 %all-gather.17.cloned.1.call-start = ((), (), s32[]{:S(2)}) async-start(), calls=%async_computation.6 | async-start | bytes 2113536 | tf_op jit(solution)/shard_map/all_gather | solution.py:166
  7.9 359.9 %all-gather.11.cloned.1.call-start = ((), (), s32[]{:S(2)}) async-start(), calls=%async_computation.3 | async-start | bytes 4718592 | tf_op jit(solution)/shard_map/all_gather | solution.py:188
  8.7 401.4 %all-gather.13.cloned.1.call-start = ((), (), s32[]{:S(2)}) async-start(), calls=%async_computation.4 | async-start | bytes 2359296 | tf_op jit(solution)/shard_map/all_gather | solution.py:189
  9.4 443.0 %all-gather.15.cloned.1.call-start = ((), (), s32[]{:S(2)}) async-start(), calls=%async_computation.5 | async-start | bytes 2359296 | tf_op jit(solution)/shard_map/all_gather | solution.py:190
  10.0 754.3 %all-gather.9.cloned.1.call-start = ((), (), s32[]{:S(2)}) async-start(), calls=%async_computation.2 | async-start | bytes 8454144 | tf_op jit(solution)/shard_map/all_gather | solution.py:165
  10.6 796.1 %all-gather.19.cloned.1.call-start = ((), (), s32[]{:S(2)}) async-start(), calls=%async_computation.7 | async-start | bytes 1179648 | tf_op jit(solution)/shard_map/all_gather | solution.py:179
  13.7 3.0 copy-start.18
  18.9 296.2 %copy-start.16 = (f32[128]{0:T(128)}, f32[128]{0:T(128)S(1)}, u32[]{:S(2)}) copy-start(f32[128]{0:T(128)S(1)} %add_rsqrt_fusion.5) | copy-start | bytes 1540
  20.6 332.4 %copy-start.8 = (f32[128,64]{1,0:T(8,128)}, f32[128,64]{1,0:T(8,128)S(1)}, u32[]{:S(2)}) copy-start(f32[128,64]{1,0:T(8,128)S(1)} %get-tuple-element.47) | copy-start | bytes 98308
  20.6 332.4 %copy-start.10 = (f32[128,64]{1,0:T(8,128)}, f32[128,64]{1,0:T(8,128)S(1)}, u32[]{:S(2)}) copy-start(f32[128,64]{1,0:T(8,128)S(1)} %get-tuple-element.48) | copy-start | bytes 98308
  315.1 449.2 %copy-start.17 = (f32[128]{0:T(128)S(1)}, f32[128]{0:T(128)}, u32[]{:S(2)}) copy-start(f32[128]{0:T(128)} %copy-done.16) | copy-start | bytes 1540
  318.3 799.3 %all-gather.21.cloned.1.call-start = ((), (), s32[]{:S(2)}) async-start(), calls=%async_computation.8 | async-start | bytes 8454144 | tf_op jit(solution)/shard_map/all_gather | solution.py:224
  459.1 313.9 %copy-start.21 = (f32[128]{0:T(128)S(1)}, f32[128]{0:T(128)}, u32[]{:S(2)}) copy-start(f32[128]{0:T(128)} %get-tuple-element.45) | copy-start | bytes 1540
  769.3 1.0 copy-start.3
  776.1 0.8 copy-start.4
  776.3 0.8 copy-start.6
  806.6 2.3 copy-start.5
  806.6 2.3 copy-start.7
  806.6 2.3 copy-start.12
  809.0 1.6 copy-start.13
  809.0 1.6 copy-start.14
  1117.6 5.9 copy-start.15
  1122.6 1.0 copy-start.1
  1291.2 7.1 copy-start.19
  1291.2 109.4 %all-to-all-start.1 = ((bf16[1,128,10,2048]{3,2,0,1:T(8,128)(2,1)}), bf16[1,128,10,2048]{3,2,0,1:T(8,128)(2,1)}, u32[]{:S(2)}, u32[]{:S(2)}) async-start(bf16[1,128,10,2048]{3,2,0,1:T(8,128)(2,1)} %bitcast.121), calls=%async_computation.1 | async-start | bytes 16777216 | tf_op jit(solution)/shard_map/all_to_all | solution.py:261
  1297.5 356.2 %all-gather.23.cloned.1.call-start = ((), (), s32[]{:S(2)}) async-start(), calls=%async_computation.9 | async-start | bytes 2113536 | tf_op jit(solution)/shard_map/all_gather | solution.py:270
  1422.5 6.6 copy-start.2
  1429.1 227.9 %copy-start.20 = (f32[128]{0:T(128)S(1)}, f32[128]{0:T(128)}, u32[]{:S(2)}) copy-start(f32[128]{0:T(128)} %get-tuple-element.44) | copy-start | bytes 1540
  1429.1 228.1 %copy-start.9 = (f32[128,64]{1,0:T(8,128)S(1)}, f32[128,64]{1,0:T(8,128)}, u32[]{:S(2)}) copy-start(f32[128,64]{1,0:T(8,128)} %copy-done.8) | copy-start | bytes 98308
  1429.1 228.1 %copy-start.11 = (f32[128,64]{1,0:T(8,128)S(1)}, f32[128,64]{1,0:T(8,128)}, u32[]{:S(2)}) copy-start(f32[128,64]{1,0:T(8,128)} %copy-done.10) | copy-start | bytes 98308
Sparse Core Ops, SparseCore 0:
  9.7 302.3 all-gather.16
  313.8 54.0 all-gather.10
  369.5 40.5 all-gather.12
  411.6 40.8 all-gather.14
  454.0 310.2 all-gather.8
  766.3 40.2 all-gather.18
  808.3 309.2 all-gather.20
  1300.1 353.6 all-gather.22
where the time goes:
time: 1680 us; the launch traced here: 1670 us
  waiting for transfers between devices  1340 us (80%)
  blocking collectives  109 us (6%)
  local copies, waits for them, and re-layouts  83 us (5%)
  other arithmetic  55.1 us (3%)
  matrix products  49 us (3%)
  between operations  26.7 us (2%)
    all_gather x1, waiting for transfers between devices, per_device(): lax.all_gather(query_weight, ('dp', 'mp'), axis=0, tiled=True)  305 us
    all_gather x1, waiting for transfers between devices, per_device(): lax.all_gather(kv_weight, ('dp', 'mp'), axis=0, tiled=True)  290 us
    all_gather x1, waiting for transfers between devices, per_device(): lax.all_gather(out_weight, ('dp', 'mp'), axis=0, tiled=True)  290 us
    all_gather x1, waiting for transfers between devices, per_device(): lax.all_gather(next_weight, ('dp', 'mp'), axis=0, tiled=True)  224 us
    all_to_all x1, blocking collectives, per_device(): lax.all_to_all(outbound.reshape(devices_all, 1, capacity, model_dim), ('d...  109 us
    all_to_all x1, waiting for transfers between devices, per_device(): lax.all_to_all(served, ('dp', 'mp'), split_axis=1, concat_axis=0, tiled=T...  102 us
    all_gather x1, waiting for transfers between devices, per_device(): lax.all_gather(leaf_cache, 'mp', axis=0, tiled=True)  40.7 us
    all_gather x1, waiting for transfers between devices, per_device(): lax.all_gather(mid_cache, 'mp', axis=0, tiled=True)  40.3 us
  transfers between devices with their start and end apart: 9, of which 9 were waited for; matrix products, arithmetic and copies ran while one was open for 7% of the time, Pallas kernels for 0%

commit v1 on v0

v1 whole, which is shorter than its diff:
```python
import jax
import jax.numpy as jnp
from jax import lax
from jax.experimental import pallas as pl
from jax.experimental.pallas import tpu as pltpu
from jax.sharding import PartitionSpec as P

EPS = 1e-06
THETA = 1000000.0
MASKED = -1e30
LOG2E = 1.4426950408889634
BOTH = ("dp", "mp")
MAIN = 8


def rms_norm(values, weight_row):
    values = values.astype(jnp.float32)
    return values * lax.rsqrt(jnp.mean(values * values, axis=-1, keepdims=True) + EPS) * weight_row


def look_up(lookup_table, indices):
    places = jnp.arange(lookup_table.shape[0], dtype=jnp.int32)
    return jnp.sum(jnp.where(indices[:, None] == places[None, :], lookup_table[None, :], 0), axis=1)


def pack_weights_kernel(query, kv, out_rows, next_rows, packed):
    count = packed.shape[0]
    dim = out_rows.shape[1]
    extra = next_rows.shape[1]
    wide = query.shape[1] // count
    hd = wide // 2
    heads = kv.shape[1] // 2 // hd
    base = dim + extra
    for dest in range(count):
        head = dest * heads // count
        packed[dest, :, 0:dim] = out_rows[...]
        packed[dest, :, dim:base] = next_rows[...]
        packed[dest, :, base : base + wide] = query[:, dest * wide : (dest + 1) * wide]
        for half in range(2):
            source = (half * heads + head) * hd
            target = base + wide + half * hd
            packed[dest, :, target : target + hd] = kv[:, source : source + hd]


def pack_weights(query, kv, out_rows, next_rows, count):
    rows = query.shape[0]
    width = out_rows.shape[1] + next_rows.shape[1] + 2 * (query.shape[1] // count)
    in_vmem = pl.BlockSpec(memory_space=pltpu.VMEM)
    return pl.pallas_call(
        pack_weights_kernel,
        out_shape=jax.ShapeDtypeStruct((count, rows, width), jnp.bfloat16),
        in_specs=[in_vmem] * 4,
        out_specs=in_vmem,
        name="pack_weights",
    )(query, kv, out_rows, next_rows)


def pack_paths_kernel(meta, root, mid, leaf, packed):
    me = meta[0]
    heads = packed.shape[0] // 4
    hd = packed.shape[2] // 2
    part = packed.shape[1]
    for req in range(2):
        own = [meta[8 + 3 * req + level] for level in range(3)]
        levels = []
        for level, cache in enumerate((root, mid, leaf)):
            here = cache.shape[0]
            rows = jnp.zeros(cache.shape[1:], cache.dtype)
            for local in range(here):
                rows = jnp.where(own[level] == me * here + local, cache[local], rows)
            levels.append(rows)
        top = levels[0].shape[0] - part
        middle = levels[1].shape[0]
        for head in range(heads):
            for half in range(2):
                source = slice((half * heads + head) * hd, (half * heads + head + 1) * hd)
                target = slice(half * hd, (half + 1) * hd)
                place = 4 * head + 2 * req
                packed[place, :, target] = levels[0][:part, source]
                packed[place + 1, 0:top, target] = levels[0][part:, source]
                packed[place + 1, top : top + middle, target] = levels[1][:, source]
                packed[place + 1, top + middle :, target] = levels[2][:, source]


def pack_paths(meta, root, mid, leaf, count):
    hd = root.shape[2] // 4
    part = (root.shape[1] + mid.shape[1] + leaf.shape[1]) // 2
    in_vmem = pl.BlockSpec(memory_space=pltpu.VMEM)
    return pl.pallas_call(
        pack_paths_kernel,
        out_shape=jax.ShapeDtypeStruct((count, part, 2 * hd), jnp.bfloat16),
        in_specs=[pl.BlockSpec(memory_space=pltpu.SMEM)] + [in_vmem] * 3,
        out_specs=in_vmem,
        compiler_params=pltpu.CompilerParams(vmem_limit_bytes=24 * 1024 * 1024),
        name="pack_paths",
    )(meta, root, mid, leaf)


def attention_kernel(
    meta,
    rows_all,
    weight,
    piece_0,
    piece_1,
    piece_2,
    piece_3,
    gains,
    cosine,
    sine,
    out,
    q_all,
    k_all,
    v_all,
    pk_all,
    pv_all,
):
    pieces = (piece_0, piece_1, piece_2, piece_3)
    me = meta[0]
    cut = meta[1]
    tok = 128
    count = rows_all.shape[0] // tok
    hd = gains.shape[1]
    span = pk_all.shape[0] // 2
    part = piece_0.shape[0]

    def turn(raw, gain, cos_now, sin_now):
        scaled = raw * lax.rsqrt(jnp.mean(raw * raw, axis=-1, keepdims=True) + EPS) * gain
        return (scaled * cos_now + pltpu.roll(scaled, hd // 2, 1) * sin_now).astype(jnp.bfloat16)

    for step in range(count):
        rows = slice(step * tok, (step + 1) * tok)
        raw = jnp.dot(rows_all[rows, :], weight[...], preferred_element_type=jnp.float32)
        cos_now = cosine[rows, :]
        sin_now = sine[rows, :]
        q_at = 2 * step * tok
        q_all[q_at : q_at + tok, :] = turn(raw[:, :hd], gains[0:1, :], cos_now, sin_now)
        q_all[q_at + tok : q_at + 2 * tok, :] = turn(
            raw[:, hd : 2 * hd], gains[0:1, :], cos_now, sin_now
        )
        k_all[rows, :] = turn(raw[:, 2 * hd : 3 * hd], gains[1:2, :], cos_now, sin_now)
        v_all[rows, :] = raw[:, 3 * hd :].astype(jnp.bfloat16)
    quarter = lax.rem(me, 4)
    for step, piece in enumerate(pieces):
        place = pl.multiple_of((quarter ^ step) * part, part)
        pk_all[pl.ds(place, part), :] = piece[:, :hd]
        pv_all[pl.ds(place, part), :] = piece[:, hd:]

    scale = hd ** (-0.5) * LOG2E
    col = lax.broadcasted_iota(jnp.int32, (1, span), 1)
    row = lax.broadcasted_iota(jnp.int32, (2 * tok, 1), 0)
    row = jnp.where(row >= tok, row - tok, row)

    def join(state, scores, values):
        peak, total, acc = state
        top = jnp.maximum(peak, jnp.max(scores, axis=1, keepdims=True))
        keep = jnp.exp2(peak - top)
        weights = jnp.exp2(scores - top)
        total = total * keep + jnp.sum(weights, axis=1, keepdims=True)
        acc = acc * keep + jnp.dot(
            weights.astype(jnp.bfloat16), values, preferred_element_type=jnp.float32
        )
        return top, total, acc

    for step in range(count):
        first = step * tok
        q_now = q_all[2 * first : 2 * first + 2 * tok, :]
        token = row + first
        late = token >= cut

        def prefix(req, state, q_now=q_now, late=late):
            start = pl.multiple_of(req * span, span)
            scores = scale * lax.dot_general(
                q_now,
                pk_all[pl.ds(start, span), :],
                (((1,), (1,)), ((), ())),
                preferred_element_type=jnp.float32,
            )
            base = 2 + 3 * req
            inside = jnp.where(
                col < 512,
                (col < meta[base]).astype(jnp.int32),
                jnp.where(
                    col < 768,
                    (col - 512 < meta[base + 1]).astype(jnp.int32),
                    (col - 768 < meta[base + 2]).astype(jnp.int32),
                ),
            )
            mine = (late.astype(jnp.int32) == req).astype(jnp.int32)
            scores = jnp.where(inside * mine > 0, scores, MASKED)
            return join(state, scores, pv_all[pl.ds(start, span), :])

        state = (
            jnp.full((2 * tok, 1), MASKED, jnp.float32),
            jnp.zeros((2 * tok, 1), jnp.float32),
            jnp.zeros((2 * tok, hd), jnp.float32),
        )
        low = (first >= cut).astype(jnp.int32)
        high = (first + tok > cut).astype(jnp.int32)
        state = lax.fori_loop(low, high + 1, prefix, state)
        keys = first + tok
        scores = scale * lax.dot_general(
            q_now,
            k_all[0:keys, :],
            (((1,), (1,)), ((), ())),
            preferred_element_type=jnp.float32,
        )
        other = lax.broadcasted_iota(jnp.int32, (1, keys), 1)
        bottom = jnp.where(late, cut, 0)
        scores = jnp.where(
            jnp.logical_and(other <= token, other >= bottom), scores, MASKED
        )
        peak, total, acc = join(state, scores, v_all[0:keys, :])
        done = (acc / total).astype(jnp.bfloat16)
        out[first : first + tok, 0:hd] = done[:tok]
        out[first : first + tok, hd : 2 * hd] = done[tok:]


def attend(meta, rows_all, weight, pieces, gains, cosine, sine):
    group = cosine.shape[0]
    hd = gains.shape[1]
    rows = 4 * pieces[0].shape[0]
    in_vmem = pl.BlockSpec(memory_space=pltpu.VMEM)
    return pl.pallas_call(
        attention_kernel,
        out_shape=jax.ShapeDtypeStruct((group, 2 * hd), jnp.bfloat16),
        in_specs=[pl.BlockSpec(memory_space=pltpu.SMEM)] + [in_vmem] * 9,
        out_specs=in_vmem,
        scratch_shapes=[
            pltpu.VMEM((2 * group, hd), jnp.bfloat16),
            pltpu.VMEM((group, hd), jnp.bfloat16),
            pltpu.VMEM((group, hd), jnp.bfloat16),
            pltpu.VMEM((rows, hd), jnp.bfloat16),
            pltpu.VMEM((rows, hd), jnp.bfloat16),
        ],
        compiler_params=pltpu.CompilerParams(vmem_limit_bytes=40 * 1024 * 1024),
        name="tree_attention",
    )(meta, rows_all, weight, *pieces, gains, cosine, sine)


def exchange(values):
    return lax.all_to_all(values, BOTH, split_axis=0, concat_axis=0, tiled=True)


def expert(rows, gate_up, down_weight):
    ff_width = down_weight.shape[0]
    both = jnp.dot(rows, gate_up, preferred_element_type=jnp.float32)
    active = (jax.nn.silu(both[:, :ff_width]) * both[:, ff_width:]).astype(jnp.bfloat16)
    return jnp.dot(active, down_weight, preferred_element_type=jnp.float32).astype(jnp.bfloat16)


def per_device(
    hidden,
    norm_gains,
    head_gains,
    query_weight,
    kv_weight,
    out_weight,
    gate_up,
    down_weight,
    next_weight,
    expert_ids,
    route_weights,
    token_request,
    request_leaf,
    leaf_parent,
    mid_parent,
    root_length,
    mid_length,
    leaf_length,
    root_slot,
    mid_slot,
    leaf_slot,
    root_cache,
    mid_cache,
    leaf_cache,
):
    tok, dim = hidden.shape
    hd = head_gains.shape[1]
    kv_width = kv_weight.shape[1] // 2
    kv_heads = kv_width // hd
    group = token_request.shape[0]
    mp_size = lax.axis_size("mp")
    dp_size = lax.axis_size("dp")
    devices = dp_size * mp_size
    me = lax.axis_index("mp")
    own_rows = query_weight.shape[0]

    pair = token_request[0] + jnp.arange(2, dtype=jnp.int32)
    cut = jnp.sum((token_request == pair[0]).astype(jnp.int32))
    leaf_node = look_up(request_leaf, pair)
    mid_node = look_up(leaf_parent, leaf_node)
    root_node = look_up(mid_parent, mid_node)
    slots = (
        look_up(root_slot, root_node),
        look_up(mid_slot, mid_node),
        look_up(leaf_slot, leaf_node),
    )
    lengths = (
        look_up(root_length, root_node),
        look_up(mid_length, mid_node),
        look_up(leaf_length, leaf_node),
    )
    prefix_length = lengths[0] + lengths[1] + lengths[2]
    token = jnp.arange(group, dtype=jnp.int32)
    positions = token + jnp.where(token >= cut, prefix_length[1] - cut, prefix_length[0])
    frequency = THETA ** (-2.0 * jnp.arange(hd // 2, dtype=jnp.float32) / hd)
    angles = positions.astype(jnp.float32)[:, None] * frequency[None, :]
    cos_half = jnp.cos(angles)
    sin_half = jnp.sin(angles)
    cosine = jnp.concatenate([cos_half, cos_half], axis=1)
    sine = jnp.concatenate([-sin_half, sin_half], axis=1)

    normed = rms_norm(hidden, norm_gains[0]).astype(jnp.bfloat16)
    rows_all = lax.all_gather(normed, "mp", axis=0, tiled=True)
    packed = pack_weights(query_weight, kv_weight, out_weight, next_weight, mp_size)
    packed = lax.all_to_all(packed, "mp", split_axis=0, concat_axis=0, tiled=True)
    packed = packed.reshape(mp_size * own_rows, -1)
    late_width = dim + next_weight.shape[1]
    late = lax.all_gather(packed[:, :late_width], "dp", axis=0, tiled=True)
    early = packed[:, late_width:]
    early = jnp.broadcast_to(early[None], (dp_size,) + early.shape)
    weight = lax.all_to_all(early, "dp", split_axis=0, concat_axis=0, tiled=True)
    weight = weight.reshape(dim, -1)

    meta = jnp.concatenate(
        [
            jnp.stack([me, cut]),
            jnp.stack(lengths, axis=1).reshape(-1),
            jnp.stack(slots, axis=1).reshape(-1),
        ]
    ).astype(jnp.int32)
    path = pack_paths(meta, root_cache, mid_cache, leaf_cache, mp_size)
    path = lax.all_to_all(path, "mp", split_axis=0, concat_axis=0, tiled=True)
    own_piece = jnp.sum(path.astype(jnp.float32), axis=0).astype(jnp.bfloat16)
    pieces = [own_piece] + [
        lax.ppermute(own_piece, "mp", [(j, j ^ s) for j in range(mp_size)]) for s in range(1, 4)
    ]
    attended = attend(meta, rows_all, weight, pieces, head_gains, cosine, sine)
    attended = lax.all_to_all(
        attended.reshape(mp_size, tok, 2 * hd), "mp", split_axis=0, concat_axis=0, tiled=True
    )
    out_full = late[:, :dim]
    next_full = late[:, dim:]
    projected = jnp.einsum(
        "mtk,mkd->td",
        attended,
        out_full.reshape(mp_size, 2 * hd, dim),
        preferred_element_type=jnp.float32,
    )
    after_attention = (hidden.astype(jnp.float32) + projected).astype(jnp.bfloat16)
    moe_in = rms_norm(after_attention, norm_gains[1]).astype(jnp.bfloat16)

    top_k = expert_ids.shape[1]
    capacity = max(2, 5 * tok * top_k // (4 * devices))
    names = expert_ids[:, :, None] == jnp.arange(devices, dtype=jnp.int32)[None, None, :]
    named = jnp.any(names, axis=1)
    route = jnp.sum(jnp.where(names, route_weights[:, :, None], 0.0), axis=1)
    before = jnp.tril(jnp.ones((tok, tok), jnp.bfloat16), -1)
    slot_no = jnp.dot(before, named.astype(jnp.bfloat16), preferred_element_type=jnp.float32)
    slot_no = jnp.where(named, slot_no.astype(jnp.int32), -1)

    def spread(first, last):
        count = jnp.arange(first, last, dtype=jnp.int32)
        taken = slot_no.T[:, None, :] == count[None, :, None]
        return taken.astype(jnp.bfloat16).reshape(devices * (last - first), tok)

    def gather_back(first, last):
        count = jnp.arange(first, last, dtype=jnp.int32)
        taken = slot_no[:, :, None] == count[None, None, :]
        share = jnp.where(taken, route[:, :, None], 0.0).reshape(tok, devices * (last - first))
        upper = lax.reduce_precision(share, 8, 7)
        return jnp.concatenate([upper, share - upper], axis=0).astype(jnp.bfloat16)

    def outbound(first, last, source):
        picked = jnp.dot(spread(first, last), source, preferred_element_type=jnp.float32)
        return picked.astype(jnp.bfloat16).reshape(devices, last - first, dim)

    def mixed(first, last, returned):
        returned = returned.reshape(-1, dim)
        halves = jnp.dot(gather_back(first, last), returned, preferred_element_type=jnp.float32)
        return halves[:tok] + halves[tok:]

    main_in = exchange(outbound(0, MAIN, moe_in))
    main_in, moe_again = lax.optimization_barrier((main_in, moe_in))
    rest_in = exchange(outbound(MAIN, capacity, moe_again))
    main_out = expert(main_in.reshape(-1, dim), gate_up[0], down_weight[0])
    main_out = exchange(main_out.reshape(devices, MAIN, dim))
    rest_out = expert(rest_in.reshape(-1, dim), gate_up[0], down_weight[0])
    main_out, rest_out = lax.optimization_barrier((main_out, rest_out))
    rest_out = exchange(rest_out.reshape(devices, capacity - MAIN, dim))
    mixture = mixed(0, MAIN, main_out) + mixed(MAIN, capacity, rest_out)
    layer_out = (after_attention.astype(jnp.float32) + mixture).astype(jnp.bfloat16)
    next_in = rms_norm(layer_out, norm_gains[2]).astype(jnp.bfloat16)
    next_raw = jnp.dot(next_in, next_full, preferred_element_type=jnp.float32)
    my_cos = lax.dynamic_slice_in_dim(cosine, me * tok, tok)[:, None, :]
    my_sin = lax.dynamic_slice_in_dim(sine, me * tok, tok)[:, None, :]
    next_keys = rms_norm(next_raw[:, :kv_width].reshape(tok, kv_heads, hd), head_gains[2])
    swapped = jnp.concatenate([next_keys[..., hd // 2 :], next_keys[..., : hd // 2]], axis=-1)
    next_keys = (next_keys * my_cos + swapped * my_sin).astype(jnp.bfloat16)
    next_rows = jnp.concatenate(
        [next_keys.reshape(tok, kv_width), next_raw[:, kv_width:].astype(jnp.bfloat16)], axis=1
    )
    return (layer_out, next_rows)


def solution(mesh):
    both = P(BOTH, None)
    placed = (
        both,
        P(),
        P(),
        both,
        both,
        both,
        P(BOTH, None, None),
        P(BOTH, None, None),
        both,
        both,
        both,
        P("dp"),
        P(),
        P(),
        P(),
        P(),
        P(),
        P(),
        P(),
        P(),
        P(),
        P("mp", None, None),
        P("mp", None, None),
        P("mp", None, None),
    )
    return jax.shard_map(
        per_device,
        mesh=mesh,
        in_specs=placed,
        out_specs=(both, both),
        check_vma=False,
    )
```

time: 1680 us -> 413 us (0.25)
  waiting for transfers between devices: 1340 us -> 203 us
  blocking collectives: 109 us -> 25.8 us
  local copies, waits for them, and re-layouts: 83 us -> 37.8 us
  starting transfers between devices: 7.15 us -> 45.2 us
  other arithmetic: 55.1 us -> 22.1 us
  Pallas kernels: 0 us -> 18.7 us
    all_gather x8 -> x2, waiting for transfers between devices: 1230 us -> 33.7 us  [the longest x1 33.7 us: per_device(): late = lax.all_gather(packed[:, :late_width], 'dp', axis=0, tiled=True)]
    all_to_all x1, blocking collectives: 109 us -> 25.8 us  [per_device(): lax.all_to_all(packed, 'mp', split_axis=0, concat_axis=0, tiled=True)]
    all_to_all x1 -> x7, waiting for transfers between devices: 102 us -> 165 us  [the longest x4 110 us: exchange(): return lax.all_to_all(values, BOTH, split_axis=0, concat_axis=0, tiled=True)]
    all_to_all x1 -> x7, starting transfers between devices: 6.31 us -> 40.9 us  [the longest x4 25.6 us: exchange(): return lax.all_to_all(values, BOTH, split_axis=0, concat_axis=0, tiled=True)]
    reshape x6 -> x7, local copies, waits for them, and re-layouts: 38.9 us -> 9.82 us  [the longest x1 2.54 us: outbound(): return picked.astype(jnp.bfloat16).reshape(devices, last - first, dim)]
    pallas_call x0 -> x3, Pallas kernels: none -> 18.7 us  [the longest x1 16 us: attend(): pl.pallas_call(attention_kernel, out_shape=jax.ShapeDtypeStruct((group, 2...]
    reduce_sum x10 -> x4, other arithmetic: 18.5 us -> 0.79 us  [look_up(): jnp.sum(jnp.where(indices[:, None] == places[None, :], lookup_table[None,...]
    dot_general x14 -> x11, matrix products: 49 us -> 41.9 us  [the longest x2 14.9 us: expert(): both = jnp.dot(rows, gate_up, preferred_element_type=jnp.float32)]
  transfers between devices with their start and end apart: 9 -> 12, of which waited for: 9 -> 9; matrix products, arithmetic and copies ran while one was open for 7% -> 14% of each run, Pallas kernels for 0% -> 5%
where the time goes in v1:
time: 413 us; the launch traced here: 411 us
  waiting for transfers between devices  203 us (49%)
  starting transfers between devices  45.2 us (11%)
  matrix products  41.9 us (10%)
  local copies, waits for them, and re-layouts  37.8 us (9%)
  blocking collectives  25.8 us (6%)
  other arithmetic  22.1 us (5%)
  Pallas kernels  18.7 us (5%)
  between operations  15.9 us (4%)
    all_to_all x4, waiting for transfers between devices, exchange(): return lax.all_to_all(values, BOTH, split_axis=0, concat_axis=0, tiled=True)  110 us
    all_to_all x1, waiting for transfers between devices, per_device(): path = lax.all_to_all(path, 'mp', split_axis=0, concat_axis=0, tiled=True)  38.9 us
    all_gather x1, waiting for transfers between devices, per_device(): late = lax.all_gather(packed[:, :late_width], 'dp', axis=0, tiled=True)  33.7 us
    all_to_all x1, blocking collectives, per_device(): lax.all_to_all(packed, 'mp', split_axis=0, concat_axis=0, tiled=True)  25.8 us
    all_to_all x4, starting transfers between devices, exchange(): return lax.all_to_all(values, BOTH, split_axis=0, concat_axis=0, tiled=True)  25.6 us
    all_to_all x1, waiting for transfers between devices, per_device(): lax.all_to_all(early, 'dp', split_axis=0, concat_axis=0, tiled=True)  16.3 us
    pallas_call x1, Pallas kernels, attend(): pl.pallas_call(attention_kernel, out_shape=jax.ShapeDtypeStruct((group, 2...  16 us
    dot_general x2, matrix products, expert(): both = jnp.dot(rows, gate_up, preferred_element_type=jnp.float32)  14.9 us
  transfers between devices with their start and end apart: 12, of which 9 were waited for; matrix products, arithmetic and copies ran while one was open for 14% of the time, Pallas kernels for 5%

profile of v1, /device:TPU:0, one launch (start us, length us, event | category | flops | bytes accessed | tf_op | source)
XLA Modules:
  0.0 410.5 jit_solution(12710240801305823608)
XLA Ops:
  7.2 1.4 fusion.25
  9.6 2.0 fusion.27
  11.7 1.8 pack_weights.1
  13.6 25.8 %all_to_all.40 = bf16[8,16,3072]{2,1,0:T(8,128)(2,1)S(1)} all-to-all(bf16[8,16,3072]{2,1,0:T(8,128)(2,1)} %pack_weights.1), channel_id=1, replica_groups=mesh['dp'=16,'mp'=8] {'mp'}, dimensions={0} | all-to-all | bytes 1572864 | tf_op jit(solution)/shard_map/all_to_all | solution.py:316
  45.0 1.1 copy-done.6
  47.9 1.2 copy-done.1
  49.1 4.3 %all-to-all-start.2 = ((bf16[8,448,256]{2,1,0:T(8,128)(2,1)}), bf16[8,448,256]{2,1,0:T(8,128)(2,1)}, u32[]{:S(2)}, u32[]{:S(2)}) async-start(bf16[8,448,256]{2,1,0:T(8,128)(2,1)} %copy-done.1), calls=%async_computation.2 | async-start | bytes 3670016 | tf_op jit(solution)/shard_map/all_to_all | solution.py:333
  54.4 38.9 %all-to-all-done.2 = bf16[8,448,256]{2,1,0:T(8,128)(2,1)} async-done(((bf16[8,448,256]{2,1,0:T(8,128)(2,1)}), bf16[8,448,256]{2,1,0:T(8,128)(2,1)}, u32[]{:S(2)}, u32[]{:S(2)}) %all-to-all-start.2) | async-done | bytes 1835040 | tf_op jit(solution)/shard_map/all_to_all | solution.py:333
  93.3 1.5 broadcast_in_dim.195
  94.9 6.8 %all-to-all-start.1 = ((bf16[16,128,512]{2,1,0:T(8,128)(2,1)}), bf16[16,128,512]{2,1,0:T(8,128)(2,1)}, u32[]{:S(2)}, u32[]{:S(2)}) async-start(bf16[16,128,512]{2,1,0:T(8,128)(2,1)} %broadcast_in_dim.195), calls=%async_computation.1 | async-start | bytes 4194304 | tf_op jit(solution)/shard_map/all_to_all | solution.py:322
  103.5 1.3 add_convert_fusion
  104.9 2.0 reduce_sum.158.piece_0
  107.0 4.0 collective-permute-start
  111.0 3.2 fusion.44
  114.3 2.8 pad_maximum_fusion
  117.2 3.9 collective-permute-done.2.piece_3
  121.7 16.3 %all-to-all-done.1 = bf16[16,128,512]{2,1,0:T(8,128)(2,1)} async-done(((bf16[16,128,512]{2,1,0:T(8,128)(2,1)}), bf16[16,128,512]{2,1,0:T(8,128)(2,1)}, u32[]{:S(2)}, u32[]{:S(2)}) %all-to-all-start.1) | async-done | bytes 2097184 | tf_op jit(solution)/shard_map/all_to_all | solution.py:322
  138.0 2.2 copy-done.2
  140.2 1.0 copy-done.3
  141.2 1.0 copy-done.4
  142.2 16.0 %tree_attention.1 = bf16[1024,256]{1,0:T(8,128)(2,1)S(1)} custom-call(s32[14]{0:T(128)S(1)} %pad_add_fusion.2.meta, bf16[1024,2048]{1,0:T(8,128)(2,1)S(1)} %copy-done.2, bf16[2048,512]{1,0:T(8,128)(2,1)} %bitcast.12.weight, bf16[448,256]{1,0:T(8,128)(2,1)S(1)} %reduce_sum.158.piece_0, bf16[448,256]{1,0:T(8,128)(2,1)} %collective-permute-done.piece_1, ...), custom_call_target="tpu_custom_call" | custom-call | tf_op jit(solution)/shard_map/tree_attention/pallas_call | solution.py:223
  159.1 4.2 %all-to-all-start.3 = ((bf16[8,128,256]{2,1,0:T(8,128)(2,1)}), bf16[8,128,256]{2,1,0:T(8,128)(2,1)}, u32[]{:S(2)}, u32[]{:S(2)}) async-start(bf16[8,128,256]{2,1,0:T(8,128)(2,1)} %bitcast.97), calls=%async_computation.3 | async-start | bytes 1048576 | tf_op jit(solution)/shard_map/all_to_all | solution.py:339
  163.9 33.7 %all-gather.5.cloned.1.call-done = bf16[2048,2560]{1,0:T(8,128)(2,1)} async-done(((bf16[128,2560]{1,0:T(8,128)(2,1)}), bf16[2048,2560]{1,0:T(8,128)(2,1)}) %all-gather.5.cloned.1.call-update) | async-done | bytes 10485776 | tf_op jit(solution)/shard_map/all_gather | solution.py:319
  197.6 8.4 %slice.99 = bf16[2048,2048]{1,0:T(8,128)(2,1)} slice(bf16[2048,2560]{1,0:T(8,128)(2,1)} %all-gather.5.cloned.1.call-done), slice={[0:2048], [0:2048]} | slice | bytes 16777216 | tf_op jit(solution)/shard_map/slice | solution.py:342
  206.0 5.0 %multiply_reduce_fusion = (f32[128]{0:T(128)S(1)}, f32[128,2048]{1,0:T(8,128)S(1)}) fusion(bf16[8,128,256]{2,1,0:T(8,128)(2,1)} %all-to-all-done.3, bf16[8,256,2048]{2,1,0:T(8,128)(2,1)} %bitcast.98, bf16[128,2048]{1,0:T(8,128)(2,1)} %param.24), kind=kOutput, calls=%fused_computation.41 | convolution fusion | flops 1075314560 | bytes 10486272 | tf_op jit(solution)/shard_map/mtk,mkd->td/dot_general | solution.py:344
  213.0 3.3 convert_bitcast_fusion.1
  216.3 7.1 %all-to-all-start.4 = ((bf16[128,8,2048]{2,1,0:T(8,128)(2,1)}), bf16[128,8,2048]{2,1,0:T(8,128)(2,1)}, u32[]{:S(2)}, u32[]{:S(2)}) async-start(bf16[128,8,2048]{2,1,0:T(8,128)(2,1)} %convert_bitcast_fusion.1), calls=%async_computation.4 | async-start | bytes 8388608 | tf_op jit(solution)/shard_map/all_to_all | solution.py:241
  223.5 52.5 %all-to-all-done.4 = bf16[128,8,2048]{2,1,0:T(8,128)(2,1)} async-done(((bf16[128,8,2048]{2,1,0:T(8,128)(2,1)}), bf16[128,8,2048]{2,1,0:T(8,128)(2,1)}, u32[]{:S(2)}, u32[]{:S(2)}) %all-to-all-start.4) | async-done | bytes 4194336 | tf_op jit(solution)/shard_map/all_to_all | solution.py:241
  276.1 2.5 convolution_convert_fusion
  278.6 2.5 reshape.157
  281.1 6.0 %all-to-all-start.6 = ((bf16[128,2,2048]{2,1,0:T(2,128)(2,1)}), bf16[128,2,2048]{2,1,0:T(2,128)(2,1)}, u32[]{:S(2)}, u32[]{:S(2)}) async-start(bf16[128,2,2048]{2,1,0:T(2,128)(2,1)} %reshape.157), calls=%async_computation.6 | async-start | bytes 2097152 | tf_op jit(solution)/shard_map/all_to_all | solution.py:241
  287.1 10.0 %fusion.2 = f32[1024,1536]{1,0:T(8,128)S(1)} fusion(bf16[1,2048,1536]{2,1,0:T(8,128)(2,1)} %param.30, bf16[128,8,2048]{2,1,0:T(8,128)(2,1)} %all-to-all-done.4), kind=kOutput, calls=%fused_computation.2 | convolution fusion | flops 6442450944 | bytes 16777216 | tf_op jit(solution)/shard_map/dot_general | solution.py:246
  297.1 5.0 %convert_bitcast_fusion = bf16[128,8,2048]{2,1,0:T(8,128)(2,1)} fusion(bf16[1,768,2048]{2,1,0:T(8,128)(2,1)S(1)} %copy-done, f32[1024,1536]{1,0:T(8,128)S(1)} %fusion.2), kind=kOutput, calls=%fused_computation.7 | convolution fusion | flops 3228041216 | bytes 13631488 | tf_op jit(solution)/shard_map/dot_general | solution.py:248
  302.2 3.5 all-to-all-done.6
  305.6 6.6 %all-to-all-start.5 = ((bf16[128,8,2048]{2,1,0:T(8,128)(2,1)}), bf16[128,8,2048]{2,1,0:T(8,128)(2,1)}, u32[]{:S(2)}, u32[]{:S(2)}) async-start(bf16[128,8,2048]{2,1,0:T(8,128)(2,1)} %convert_bitcast_fusion), calls=%async_computation.5 | async-start | bytes 8388608 | tf_op jit(solution)/shard_map/all_to_all | solution.py:241
  312.9 1.0 fusion.53
  313.9 2.3 reshape.158
  316.2 4.9 %fusion = f32[256,1536]{1,0:T(8,128)S(1)} fusion(bf16[256,2048]{1,0:T(8,128)(2,1)} %reshape.158, bf16[1,2048,1536]{2,1,0:T(8,128)(2,1)} %param.30), kind=kOutput, calls=%fused_computation | convolution fusion | flops 1610612736 | bytes 8912896 | tf_op jit(solution)/shard_map/dot_general | solution.py:246
  321.1 2.1 fusion.11
  323.2 41.7 %all-to-all-done.5 = bf16[128,8,2048]{2,1,0:T(8,128)(2,1)} async-done(((bf16[128,8,2048]{2,1,0:T(8,128)(2,1)}), bf16[128,8,2048]{2,1,0:T(8,128)(2,1)}, u32[]{:S(2)}, u32[]{:S(2)}) %all-to-all-start.5) | async-done | bytes 4194336 | tf_op jit(solution)/shard_map/all_to_all | solution.py:241
  364.9 2.5 reshape.160
  367.4 6.0 %all-to-all-start.7 = ((bf16[128,2,2048]{2,1,0:T(2,128)(2,1)}), bf16[128,2,2048]{2,1,0:T(2,128)(2,1)}, u32[]{:S(2)}, u32[]{:S(2)}) async-start(bf16[128,2,2048]{2,1,0:T(2,128)(2,1)} %reshape.160), calls=%async_computation.7 | async-start | bytes 2097152 | tf_op jit(solution)/shard_map/all_to_all | solution.py:241
  375.1 4.8 %fusion.4 = f32[256,2048]{1,0:T(8,128)} fusion(bf16[128,8,2048]{2,1,0:T(8,128)(2,1)} %all-to-all-done.5, bf16[128,1024]{0,1:T(8,128)(2,1)S(1)} %get-tuple-element.23, bf16[128,1024]{0,1:T(8,128)(2,1)S(1)} %get-tuple-element.22), kind=kOutput, calls=%fused_computation.4 | convolution fusion | flops 1074790400 | bytes 6815744 | tf_op jit(solution)/shard_map/dot_general | solution.py:380
  379.9 12.0 %all-to-all-done.7 = bf16[128,2,2048]{2,1,0:T(2,128)(2,1)} async-done(((bf16[128,2,2048]{2,1,0:T(2,128)(2,1)}), bf16[128,2,2048]{2,1,0:T(2,128)(2,1)}, u32[]{:S(2)}, u32[]{:S(2)}) %all-to-all-start.7) | async-done | bytes 1048608 | tf_op jit(solution)/shard_map/all_to_all | solution.py:241
  391.9 2.3 reshape.161
  394.2 1.8 fusion.48
  397.0 2.3 fusion.17
  402.2 1.5 pad_maximum_fusion.2
  (129 shorter events, 20.5 us)
Async XLA Ops:
  7.2 290.0 %copy-start = (bf16[1,768,2048]{2,1,0:T(8,128)(2,1)S(1)}, bf16[1,768,2048]{2,1,0:T(8,128)(2,1)}, u32[]{:S(2)}) copy-start(bf16[1,768,2048]{2,1,0:T(8,128)(2,1)} %param.31) | copy-start | bytes 9437188
  7.2 130.8 %all-gather.3.cloned.1.call-start = ((), (), s32[]{:S(2)}) async-start(), calls=%async_computation.8 | async-start | bytes 4718592 | tf_op jit(solution)/shard_map/all_gather | solution.py:314
  8.6 32.6 %copy-start.20 = (s32[1024]{0:T(1024)S(1)}, s32[1024]{0:T(1024)}, u32[]{:S(2)}) copy-start(s32[1024]{0:T(1024)} %param.35) | copy-start | bytes 12292
  8.6 33.7 %copy-start.32 = (s32[32]{0:T(128)S(1)}, s32[32]{0:T(128)}, u32[]{:S(2)}) copy-start(s32[32]{0:T(128)} %param.36) | copy-start | bytes 388
  8.6 33.9 %copy-start.24 = (s32[16]{0:T(128)S(1)}, s32[16]{0:T(128)}, u32[]{:S(2)}) copy-start(s32[16]{0:T(128)} %param.41) | copy-start | bytes 196
  8.6 33.9 %copy-start.25 = (s32[16]{0:T(128)S(1)}, s32[16]{0:T(128)}, u32[]{:S(2)}) copy-start(s32[16]{0:T(128)} %param.44) | copy-start | bytes 196
  8.6 33.9 %copy-start.26 = (s32[16]{0:T(128)S(1)}, s32[16]{0:T(128)}, u32[]{:S(2)}) copy-start(s32[16]{0:T(128)} %param.37) | copy-start | bytes 196
  8.7 34.1 %copy-start.27 = (s32[8]{0:T(128)S(1)}, s32[8]{0:T(128)}, u32[]{:S(2)}) copy-start(s32[8]{0:T(128)} %param.40) | copy-start | bytes 100
  8.7 34.1 %copy-start.28 = (s32[8]{0:T(128)S(1)}, s32[8]{0:T(128)}, u32[]{:S(2)}) copy-start(s32[8]{0:T(128)} %param.43) | copy-start | bytes 100
  8.7 34.1 %copy-start.29 = (s32[8]{0:T(128)S(1)}, s32[8]{0:T(128)}, u32[]{:S(2)}) copy-start(s32[8]{0:T(128)} %param.38) | copy-start | bytes 100
  8.7 34.3 %copy-start.30 = (s32[8]{0:T(128)S(1)}, s32[8]{0:T(128)}, u32[]{:S(2)}) copy-start(s32[8]{0:T(128)} %param.39) | copy-start | bytes 100
  8.7 34.3 %copy-start.31 = (s32[8]{0:T(128)S(1)}, s32[8]{0:T(128)}, u32[]{:S(2)}) copy-start(s32[8]{0:T(128)} %param.42) | copy-start | bytes 100
  8.7 36.3 %copy-start.7 = (bf16[1,256,512]{2,1,0:T(8,128)(2,1)S(1)}, bf16[1,256,512]{2,1,0:T(8,128)(2,1)}, u32[]{:S(2)}) copy-start(bf16[1,256,512]{2,1,0:T(8,128)(2,1)} %mid.1) | copy-start | bytes 786436
  11.7 186.0 %all-gather.5.cloned.1.call-start = ((), (), s32[]{:S(2)}) async-start(), calls=%async_computation.9 | async-start | bytes 11141120 | tf_op jit(solution)/shard_map/all_gather | solution.py:319
  39.3 0.9 copy-start.13
  45.0 1.1 copy-start.6
  46.0 0.9 copy-start.8
  47.9 1.2 copy-start.1
  49.1 44.2 %all-to-all-start.2 = ((bf16[8,448,256]{2,1,0:T(8,128)(2,1)}), bf16[8,448,256]{2,1,0:T(8,128)(2,1)}, u32[]{:S(2)}, u32[]{:S(2)}) async-start(bf16[8,448,256]{2,1,0:T(8,128)(2,1)} %copy-done.1), calls=%async_computation.2 | async-start | bytes 3670016 | tf_op jit(solution)/shard_map/all_to_all | solution.py:333
  94.9 19.4 %copy-start.18 = (s32[128,8]{0,1:T(8,128)S(1)}, s32[128,8]{0,1:T(8,128)}, u32[]{:S(2)}) copy-start(s32[128,8]{0,1:T(8,128)} %param.33) | copy-start | bytes 12292
  94.9 43.1 %all-to-all-start.1 = ((bf16[16,128,512]{2,1,0:T(8,128)(2,1)}), bf16[16,128,512]{2,1,0:T(8,128)(2,1)}, u32[]{:S(2)}, u32[]{:S(2)}) async-start(bf16[16,128,512]{2,1,0:T(8,128)(2,1)} %broadcast_in_dim.195), calls=%async_computation.1 | async-start | bytes 4194304 | tf_op jit(solution)/shard_map/all_to_all | solution.py:322
  104.9 33.1 %copy-start.9 = (f32[3,128]{1,0:T(4,128)S(1)}, f32[3,128]{1,0:T(4,128)}, u32[]{:S(2)}) copy-start(f32[3,128]{1,0:T(4,128)} %gains.1) | copy-start | bytes 4612
  106.9 14.2 %collective-permute-start.2 = (bf16[448,256]{1,0:T(8,128)(2,1)S(1)}, bf16[448,256]{1,0:T(8,128)(2,1)}, u32[]{:S(2)}, u32[]{:S(2)}) collective-permute-start(bf16[448,256]{1,0:T(8,128)(2,1)S(1)} %reduce_sum.158.piece_0), channel_id=1, source_target_pairs={{0,3},{1,2},{2,1},{3,0},{4,7},{5,6},{6,5},{7,4},{8,11},{9,10},{10,... | collective-permute-start | bytes 688136 | tf_op jit(solution)/shard_map/ppermute | solution.py:336
  107.0 14.1 %collective-permute-start.1 = (bf16[448,256]{1,0:T(8,128)(2,1)S(1)}, bf16[448,256]{1,0:T(8,128)(2,1)}, u32[]{:S(2)}, u32[]{:S(2)}) collective-permute-start(bf16[448,256]{1,0:T(8,128)(2,1)S(1)} %reduce_sum.158.piece_0), channel_id=1, source_target_pairs={{0,2},{1,3},{2,0},{3,1},{4,6},{5,7},{6,4},{7,5},{8,10},{9,11},{10,... | collective-permute-start | bytes 688136 | tf_op jit(solution)/shard_map/ppermute | solution.py:336
  107.0 14.6 %collective-permute-start = (bf16[448,256]{1,0:T(8,128)(2,1)S(1)}, bf16[448,256]{1,0:T(8,128)(2,1)}, u32[]{:S(2)}, u32[]{:S(2)}) collective-permute-start(bf16[448,256]{1,0:T(8,128)(2,1)S(1)} %reduce_sum.158.piece_0), channel_id=1, source_target_pairs={{0,1},{1,0},{2,3},{3,2},{4,5},{5,4},{6,7},{7,6},{8,9},{9,8},{10,11... | collective-permute-start | bytes 688136 | tf_op jit(solution)/shard_map/ppermute | solution.py:336
  138.0 2.2 copy-start.2
  140.2 1.0 copy-start.3
  141.2 1.0 copy-start.4
  158.3 0.8 copy-start.5
  159.1 47.0 %all-to-all-start.3 = ((bf16[8,128,256]{2,1,0:T(8,128)(2,1)}), bf16[8,128,256]{2,1,0:T(8,128)(2,1)}, u32[]{:S(2)}, u32[]{:S(2)}) async-start(bf16[8,128,256]{2,1,0:T(8,128)(2,1)} %bitcast.97), calls=%async_computation.3 | async-start | bytes 1048576 | tf_op jit(solution)/shard_map/all_to_all | solution.py:339
  211.1 1.0 copy-start.10
  212.2 0.8 copy-start.12
  216.3 59.7 %all-to-all-start.4 = ((bf16[128,8,2048]{2,1,0:T(8,128)(2,1)}), bf16[128,8,2048]{2,1,0:T(8,128)(2,1)}, u32[]{:S(2)}, u32[]{:S(2)}) async-start(bf16[128,8,2048]{2,1,0:T(8,128)(2,1)} %convert_bitcast_fusion.1), calls=%async_computation.4 | async-start | bytes 8388608 | tf_op jit(solution)/shard_map/all_to_all | solution.py:241
  281.1 24.5 %all-to-all-start.6 = ((bf16[128,2,2048]{2,1,0:T(2,128)(2,1)}), bf16[128,2,2048]{2,1,0:T(2,128)(2,1)}, u32[]{:S(2)}, u32[]{:S(2)}) async-start(bf16[128,2,2048]{2,1,0:T(2,128)(2,1)} %reshape.157), calls=%async_computation.6 | async-start | bytes 2097152 | tf_op jit(solution)/shard_map/all_to_all | solution.py:241
  302.2 10.1 %copy-start.19 = (f32[128,8]{0,1:T(8,128)S(1)}, f32[128,8]{0,1:T(8,128)}, u32[]{:S(2)}) copy-start(f32[128,8]{0,1:T(8,128)} %param.34) | copy-start | bytes 12292
  305.6 59.2 %all-to-all-start.5 = ((bf16[128,8,2048]{2,1,0:T(8,128)(2,1)}), bf16[128,8,2048]{2,1,0:T(8,128)(2,1)}, u32[]{:S(2)}, u32[]{:S(2)}) async-start(bf16[128,8,2048]{2,1,0:T(8,128)(2,1)} %convert_bitcast_fusion), calls=%async_computation.5 | async-start | bytes 8388608 | tf_op jit(solution)/shard_map/all_to_all | solution.py:241
  313.9 59.5 %copy-start.22 = (f32[128]{0:T(128)}, f32[128]{0:T(128)S(1)}, u32[]{:S(2)}) copy-start(f32[128]{0:T(128)S(1)} %slice_bitcast_fusion) | copy-start | bytes 1540
  367.4 24.5 %all-to-all-start.7 = ((bf16[128,2,2048]{2,1,0:T(2,128)(2,1)}), bf16[128,2,2048]{2,1,0:T(2,128)(2,1)}, u32[]{:S(2)}, u32[]{:S(2)}) async-start(bf16[128,2,2048]{2,1,0:T(2,128)(2,1)} %reshape.160), calls=%async_computation.7 | async-start | bytes 2097152 | tf_op jit(solution)/shard_map/all_to_all | solution.py:241
  375.1 19.1 %copy-start.17 = (bf16[128,256]{0,1:T(8,128)(2,1)S(1)}, bf16[128,256]{0,1:T(8,128)(2,1)}, u32[]{:S(2)}) copy-start(bf16[128,256]{0,1:T(8,128)(2,1)} %get-tuple-element.21) | copy-start | bytes 196612
  394.2 1.8 copy-start.11
  394.2 2.2 copy-start.14
  397.0 3.0 copy-start.15
  397.0 3.4 copy-start.23
  397.0 4.2 %copy-start.21 = (f32[256]{0:T(256)S(1)}, f32[256]{0:T(256)}, u32[]{:S(2)}) copy-start(f32[256]{0:T(256)} %broadcast_bitcast_fusion) | copy-start | bytes 3076
  399.3 0.7 copy-start.16
Sparse Core Ops, SparseCore 0:
  11.8 81.7 all-gather.2
  96.0 101.5 all-gather.4

commit v2 on v1

v2 whole, which is shorter than its diff:
```python
import jax
import jax.numpy as jnp
from jax import lax
from jax.experimental import pallas as pl
from jax.experimental.pallas import tpu as pltpu
from jax.sharding import PartitionSpec as P

EPS = 1e-06
THETA = 1000000.0
MASKED = -1e30
LOG2E = 1.4426950408889634
BOTH = ("dp", "mp")
MAIN = 8


def rms_norm(values, weight_row):
    values = values.astype(jnp.float32)
    return values * lax.rsqrt(jnp.mean(values * values, axis=-1, keepdims=True) + EPS) * weight_row


def look_up(lookup_table, indices):
    places = jnp.arange(lookup_table.shape[0], dtype=jnp.int32)
    return jnp.sum(jnp.where(indices[:, None] == places[None, :], lookup_table[None, :], 0), axis=1)


def pack_kernel(meta, query, kv, out_rows, next_rows, root, mid, leaf, packed):
    count, _, wide = packed.shape
    own_rows = query.shape[0]
    hd = wide // 2
    heads = kv.shape[1] // wide
    columns = [out_rows[:, at : at + wide] for at in range(0, out_rows.shape[1], wide)]
    columns += [next_rows[:, at : at + wide] for at in range(0, next_rows.shape[1], wide)]
    shared = len(columns)
    for dest in range(count):
        head = dest * heads // count
        for place, column in enumerate(columns):
            packed[dest, place * own_rows : (place + 1) * own_rows, :] = column
        at = shared * own_rows
        packed[dest, at : at + own_rows, :] = query[:, dest * wide : (dest + 1) * wide]
        at += own_rows
        for half in range(2):
            source = (half * heads + head) * hd
            packed[dest, at : at + own_rows, half * hd : (half + 1) * hd] = kv[
                :, source : source + hd
            ]
    begin = (shared + 2) * own_rows
    part = packed.shape[1] - begin
    me = meta[0]
    for req in range(2):
        levels = []
        for level, cache in enumerate((root, mid, leaf)):
            here = cache.shape[0]
            rows = jnp.zeros(cache.shape[1:], cache.dtype)
            for local in range(here):
                wanted = meta[8 + 3 * req + level] == me * here + local
                rows = jnp.where(wanted, cache[local], rows)
            levels.append(rows)
        top = levels[0].shape[0] - part
        middle = levels[1].shape[0]
        for head in range(heads):
            for half in range(2):
                source = slice((half * heads + head) * hd, (half * heads + head + 1) * hd)
                target = slice(half * hd, (half + 1) * hd)
                place = 4 * head + 2 * req
                packed[place, begin:, target] = levels[0][:part, source]
                packed[place + 1, begin : begin + top, target] = levels[0][part:, source]
                packed[place + 1, begin + top : begin + top + middle, target] = levels[1][:, source]
                packed[place + 1, begin + top + middle :, target] = levels[2][:, source]


def pack(meta, query, kv, out_rows, next_rows, root, mid, leaf, count):
    wide = query.shape[1] // count
    pieces = (out_rows.shape[1] + next_rows.shape[1]) // wide + 2
    part = (root.shape[1] + mid.shape[1] + leaf.shape[1]) // 2
    in_vmem = pl.BlockSpec(memory_space=pltpu.VMEM)
    return pl.pallas_call(
        pack_kernel,
        out_shape=jax.ShapeDtypeStruct(
            (count, pieces * query.shape[0] + part, wide), jnp.bfloat16
        ),
        in_specs=[pl.BlockSpec(memory_space=pltpu.SMEM)] + [in_vmem] * 7,
        out_specs=in_vmem,
        compiler_params=pltpu.CompilerParams(vmem_limit_bytes=24 * 1024 * 1024),
        name="pack",
    )(meta, query, kv, out_rows, next_rows, root, mid, leaf)


def attention_kernel(
    meta,
    own,
    across,
    own_left,
    own_right,
    across_left,
    across_right,
    own_far_top,
    own_far_bottom,
    across_far_top,
    across_far_bottom,
    weight,
    piece_0,
    piece_1,
    piece_2,
    piece_3,
    gains,
    cosine,
    sine,
    out,
    rows_all,
    q_all,
    k_all,
    v_all,
    pk_all,
    pv_all,
):
    pieces = (piece_0, piece_1, piece_2, piece_3)
    me = meta[0]
    cut = meta[1]
    tok, dim = own.shape
    count = rows_all.shape[0] // tok
    hd = gains.shape[1]
    span = pk_all.shape[0] // 2
    part = piece_0.shape[0]
    ring = lax.rem(me, 4)
    base = me - ring
    far_base = 4 - base

    def put(first, step, block, offset=0):
        at = (first + lax.rem(ring + step, 4)) * tok + offset
        at = pl.multiple_of(at, block.shape[0])
        rows_all[pl.ds(at, block.shape[0]), :] = block[...]

    put(base, 0, own)
    put(far_base, 0, across)
    put(base, 3, own_left)
    put(base, 1, own_right)
    put(far_base, 3, across_left)
    put(far_base, 1, across_right)
    put(base, 2, own_far_top)
    put(base, 2, own_far_bottom, tok // 2)
    put(far_base, 2, across_far_top)
    put(far_base, 2, across_far_bottom, tok // 2)
    for step, piece in enumerate(pieces):
        place = pl.multiple_of((ring ^ step) * part, part)
        pk_all[pl.ds(place, part), :] = piece[:, :hd]
        pv_all[pl.ds(place, part), :] = piece[:, hd:]
    weight_q = weight[:, 0].reshape(dim, 2 * hd)
    weight_kv = weight[:, 1].reshape(dim, 2 * hd)

    def turn(raw, gain, cos_now, sin_now):
        scaled = raw * lax.rsqrt(jnp.mean(raw * raw, axis=-1, keepdims=True) + EPS) * gain
        return (scaled * cos_now + pltpu.roll(scaled, hd // 2, 1) * sin_now).astype(jnp.bfloat16)

    @pl.loop(0, count)
    def _(step):
        at = pl.multiple_of(step * tok, tok)
        rows = rows_all[pl.ds(at, tok), :]
        cos_now = cosine[pl.ds(at, tok), :]
        sin_now = sine[pl.ds(at, tok), :]
        raw = jnp.dot(rows, weight_q, preferred_element_type=jnp.float32)
        q_at = pl.multiple_of(2 * step * tok, 2 * tok)
        q_all[pl.ds(q_at, tok), :] = turn(raw[:, :hd], gains[0:1, :], cos_now, sin_now)
        q_all[pl.ds(q_at + tok, tok), :] = turn(raw[:, hd:], gains[0:1, :], cos_now, sin_now)
        raw = jnp.dot(rows, weight_kv, preferred_element_type=jnp.float32)
        k_all[pl.ds(at, tok), :] = turn(raw[:, :hd], gains[1:2, :], cos_now, sin_now)
        v_all[pl.ds(at, tok), :] = raw[:, hd:].astype(jnp.bfloat16)

    scale = hd ** (-0.5) * LOG2E
    col = lax.broadcasted_iota(jnp.int32, (1, span), 1)
    row = lax.broadcasted_iota(jnp.int32, (2 * tok, 1), 0)
    row = jnp.where(row >= tok, row - tok, row)
    chunk = 2 * tok
    key_col = lax.broadcasted_iota(jnp.int32, (1, chunk), 1)

    def join(state, q_now, keys, values, allowed):
        peak, total, acc = state
        scores = scale * lax.dot_general(
            q_now, keys, (((1,), (1,)), ((), ())), preferred_element_type=jnp.float32
        )
        scores = jnp.where(allowed, scores, MASKED)
        top = jnp.maximum(peak, jnp.max(scores, axis=1, keepdims=True))
        keep = jnp.exp2(peak - top)
        weights = jnp.exp2(scores - top)
        total = total * keep + jnp.sum(weights, axis=1, keepdims=True)
        acc = acc * keep + jnp.dot(
            weights.astype(jnp.bfloat16), values, preferred_element_type=jnp.float32
        )
        return top, total, acc

    @pl.loop(0, count)
    def _(step):
        first = pl.multiple_of(step * tok, tok)
        q_now = q_all[pl.ds(pl.multiple_of(2 * step * tok, 2 * tok), 2 * tok), :]
        token = row + first
        late = token >= cut

        def prefix(req, state):
            start = pl.multiple_of(req * span, span)
            at = 2 + 3 * req
            inside = jnp.where(
                col < 512,
                (col < meta[at]).astype(jnp.int32),
                jnp.where(
                    col < 768,
                    (col - 512 < meta[at + 1]).astype(jnp.int32),
                    (col - 768 < meta[at + 2]).astype(jnp.int32),
                ),
            )
            mine = (late.astype(jnp.int32) == req).astype(jnp.int32)
            return join(
                state,
                q_now,
                pk_all[pl.ds(start, span), :],
                pv_all[pl.ds(start, span), :],
                inside * mine > 0,
            )

        state = (
            jnp.full((2 * tok, 1), MASKED, jnp.float32),
            jnp.zeros((2 * tok, 1), jnp.float32),
            jnp.zeros((2 * tok, hd), jnp.float32),
        )
        low = (first >= cut).astype(jnp.int32)
        high = (first + tok > cut).astype(jnp.int32)
        state = lax.fori_loop(low, high + 1, prefix, state)
        bottom = jnp.where(late, cut, 0)

        def new(number, state):
            start = pl.multiple_of(number * chunk, chunk)
            other = key_col + start
            return join(
                state,
                q_now,
                k_all[pl.ds(start, chunk), :],
                v_all[pl.ds(start, chunk), :],
                jnp.logical_and(other <= token, other >= bottom),
            )

        peak, total, acc = lax.fori_loop(0, step // 2 + 1, new, state)
        done = (acc / total).astype(jnp.bfloat16)
        out[pl.ds(first, tok), 0:hd] = done[:tok]
        out[pl.ds(first, tok), hd : 2 * hd] = done[tok:]


def attend(meta, rows, weight, pieces, gains, cosine, sine):
    group = cosine.shape[0]
    hd = gains.shape[1]
    path_rows = 4 * pieces[0].shape[0]
    in_vmem = pl.BlockSpec(memory_space=pltpu.VMEM)
    return pl.pallas_call(
        attention_kernel,
        out_shape=jax.ShapeDtypeStruct((group, 2 * hd), jnp.bfloat16),
        in_specs=[pl.BlockSpec(memory_space=pltpu.SMEM)] + [in_vmem] * 18,
        out_specs=in_vmem,
        scratch_shapes=[
            pltpu.VMEM((group, rows[0].shape[1]), jnp.bfloat16),
            pltpu.VMEM((2 * group, hd), jnp.bfloat16),
            pltpu.VMEM((group, hd), jnp.bfloat16),
            pltpu.VMEM((group, hd), jnp.bfloat16),
            pltpu.VMEM((path_rows, hd), jnp.bfloat16),
            pltpu.VMEM((path_rows, hd), jnp.bfloat16),
        ],
        compiler_params=pltpu.CompilerParams(vmem_limit_bytes=40 * 1024 * 1024),
        name="tree_attention",
    )(meta, *rows, weight, *pieces, gains, cosine, sine)


def exchange(values):
    return lax.all_to_all(values, BOTH, split_axis=0, concat_axis=0, tiled=True)


def expert(rows, gate_up, down_weight):
    ff_width = down_weight.shape[0]
    both = jnp.dot(rows, gate_up, preferred_element_type=jnp.float32)
    active = (jax.nn.silu(both[:, :ff_width]) * both[:, ff_width:]).astype(jnp.bfloat16)
    return jnp.dot(active, down_weight, preferred_element_type=jnp.float32).astype(jnp.bfloat16)


def per_device(
    hidden,
    norm_gains,
    head_gains,
    query_weight,
    kv_weight,
    out_weight,
    gate_up,
    down_weight,
    next_weight,
    expert_ids,
    route_weights,
    token_request,
    request_leaf,
    leaf_parent,
    mid_parent,
    root_length,
    mid_length,
    leaf_length,
    root_slot,
    mid_slot,
    leaf_slot,
    root_cache,
    mid_cache,
    leaf_cache,
):
    tok, dim = hidden.shape
    hd = head_gains.shape[1]
    kv_width = kv_weight.shape[1] // 2
    kv_heads = kv_width // hd
    group = token_request.shape[0]
    mp_size = lax.axis_size("mp")
    dp_size = lax.axis_size("dp")
    devices = dp_size * mp_size
    me = lax.axis_index("mp")
    own_rows = query_weight.shape[0]

    pair = token_request[0] + jnp.arange(2, dtype=jnp.int32)
    cut = jnp.sum((token_request == pair[0]).astype(jnp.int32))
    leaf_node = look_up(request_leaf, pair)
    mid_node = look_up(leaf_parent, leaf_node)
    root_node = look_up(mid_parent, mid_node)
    slots = (
        look_up(root_slot, root_node),
        look_up(mid_slot, mid_node),
        look_up(leaf_slot, leaf_node),
    )
    lengths = (
        look_up(root_length, root_node),
        look_up(mid_length, mid_node),
        look_up(leaf_length, leaf_node),
    )
    prefix_length = lengths[0] + lengths[1] + lengths[2]
    token = jnp.arange(group, dtype=jnp.int32)
    positions = token + jnp.where(token >= cut, prefix_length[1] - cut, prefix_length[0])
    frequency = THETA ** (-2.0 * jnp.arange(hd // 2, dtype=jnp.float32) / hd)
    angles = positions.astype(jnp.float32)[:, None] * frequency[None, :]
    cos_half = jnp.cos(angles)
    sin_half = jnp.sin(angles)
    cosine = jnp.concatenate([cos_half, cos_half], axis=1)
    sine = jnp.concatenate([-sin_half, sin_half], axis=1)

    normed = rms_norm(hidden, norm_gains[0]).astype(jnp.bfloat16)
    def shift(values, step):
        moves = [(j, j - j % 4 + (j % 4 + step) % 4) for j in range(mp_size)]
        return lax.ppermute(values, "mp", moves)

    across = lax.ppermute(normed, "mp", [(j, (j + 4) % mp_size) for j in range(mp_size)])
    sides = []
    far = []
    for block in (normed, across):
        left = shift(block, 1)
        right = shift(block, -1)
        sides += [left, right]
        far += [shift(left[: tok // 2], 1), shift(right[tok // 2 :], -1)]
    rows = [normed, across] + sides + far

    meta = jnp.concatenate(
        [
            jnp.stack([me, cut]),
            jnp.stack(lengths, axis=1).reshape(-1),
            jnp.stack(slots, axis=1).reshape(-1),
        ]
    ).astype(jnp.int32)
    packed = pack(
        meta,
        query_weight,
        kv_weight,
        out_weight,
        next_weight,
        root_cache,
        mid_cache,
        leaf_cache,
        mp_size,
    )
    packed = lax.all_to_all(packed, "mp", split_axis=0, concat_axis=0, tiled=True)
    wide = packed.shape[2]
    out_end = dim // wide * own_rows
    next_end = out_end + next_weight.shape[1] // wide * own_rows
    early_end = next_end + 2 * own_rows

    def whole_rows(values):
        values = values.reshape(mp_size, -1, own_rows, wide).transpose(0, 2, 1, 3)
        return lax.all_gather(
            values.reshape(mp_size * own_rows, -1), "dp", axis=0, tiled=True
        )

    out_full = whole_rows(packed[:, :out_end])
    next_full = whole_rows(packed[:, out_end:next_end])
    early = packed[:, next_end:early_end].reshape(1, mp_size, 2, own_rows, wide)
    early = jnp.broadcast_to(early, (dp_size, mp_size, 2, own_rows, wide))
    weight = lax.all_to_all(early, "dp", split_axis=0, concat_axis=0, tiled=True)
    weight = weight.reshape(devices, 2, own_rows, wide)
    own_piece = jnp.sum(packed[:, early_end:].astype(jnp.float32), axis=0).astype(jnp.bfloat16)
    pieces = [own_piece] + [
        lax.ppermute(own_piece, "mp", [(j, j ^ s) for j in range(mp_size)]) for s in range(1, 4)
    ]
    attended = attend(meta, rows, weight, pieces, head_gains, cosine, sine)
    attended = lax.all_to_all(
        attended.reshape(mp_size, tok, 2 * hd), "mp", split_axis=0, concat_axis=0, tiled=True
    )
    projected = jnp.einsum(
        "mtk,mkd->td",
        attended,
        out_full.reshape(mp_size, 2 * hd, dim),
        preferred_element_type=jnp.float32,
    )
    after_attention = (hidden.astype(jnp.float32) + projected).astype(jnp.bfloat16)
    moe_in = rms_norm(after_attention, norm_gains[1]).astype(jnp.bfloat16)

    top_k = expert_ids.shape[1]
    capacity = max(2, 5 * tok * top_k // (4 * devices))
    names = expert_ids[:, :, None] == jnp.arange(devices, dtype=jnp.int32)[None, None, :]
    named = jnp.any(names, axis=1)
    route = jnp.sum(jnp.where(names, route_weights[:, :, None], 0.0), axis=1)
    before = jnp.tril(jnp.ones((tok, tok), jnp.bfloat16), -1)
    slot_no = jnp.dot(before, named.astype(jnp.bfloat16), preferred_element_type=jnp.float32)
    slot_no = jnp.where(named, slot_no.astype(jnp.int32), -1)

    def spread(first, last):
        count = jnp.arange(first, last, dtype=jnp.int32)
        taken = slot_no.T[:, None, :] == count[None, :, None]
        return taken.astype(jnp.bfloat16).reshape(devices * (last - first), tok)

    def gather_back(first, last):
        count = jnp.arange(first, last, dtype=jnp.int32)
        taken = slot_no[:, :, None] == count[None, None, :]
        share = jnp.where(taken, route[:, :, None], 0.0).reshape(tok, devices * (last - first))
        upper = lax.reduce_precision(share, 8, 7)
        return jnp.concatenate([upper, share - upper], axis=0).astype(jnp.bfloat16)

    def outbound(first, last, source):
        picked = jnp.dot(spread(first, last), source, preferred_element_type=jnp.float32)
        return picked.astype(jnp.bfloat16).reshape(devices, last - first, dim)

    def mixed(first, last, returned):
        returned = returned.reshape(-1, dim)
        halves = jnp.dot(gather_back(first, last), returned, preferred_element_type=jnp.float32)
        return halves[:tok] + halves[tok:]

    main_in = exchange(outbound(0, MAIN, moe_in))
    main_in, rest_in = lax.optimization_barrier((main_in, outbound(MAIN, capacity, moe_in)))
    rest_in = exchange(rest_in)
    main_out = expert(main_in.reshape(-1, dim), gate_up[0], down_weight[0])
    main_out = exchange(main_out.reshape(devices, MAIN, dim))
    rest_out = expert(rest_in.reshape(-1, dim), gate_up[0], down_weight[0])
    rest_out = rest_out.reshape(devices, capacity - MAIN, dim)
    main_out, rest_out = lax.optimization_barrier((main_out, rest_out))
    rest_out = exchange(rest_out)
    mixture = mixed(0, MAIN, main_out) + mixed(MAIN, capacity, rest_out)
    layer_out = (after_attention.astype(jnp.float32) + mixture).astype(jnp.bfloat16)
    next_in = rms_norm(layer_out, norm_gains[2]).astype(jnp.bfloat16)
    next_raw = jnp.dot(next_in, next_full, preferred_element_type=jnp.float32)
    my_cos = lax.dynamic_slice_in_dim(cosine, me * tok, tok)[:, None, :]
    my_sin = lax.dynamic_slice_in_dim(sine, me * tok, tok)[:, None, :]
    next_keys = rms_norm(next_raw[:, :kv_width].reshape(tok, kv_heads, hd), head_gains[2])
    swapped = jnp.concatenate([next_keys[..., hd // 2 :], next_keys[..., : hd // 2]], axis=-1)
    next_keys = (next_keys * my_cos + swapped * my_sin).astype(jnp.bfloat16)
    next_rows = jnp.concatenate(
        [next_keys.reshape(tok, kv_width), next_raw[:, kv_width:].astype(jnp.bfloat16)], axis=1
    )
    return (layer_out, next_rows)


def solution(mesh):
    both = P(BOTH, None)
    placed = (
        both,
        P(),
        P(),
        both,
        both,
        both,
        P(BOTH, None, None),
        P(BOTH, None, None),
        both,
        both,
        both,
        P("dp"),
        P(),
        P(),
        P(),
        P(),
        P(),
        P(),
        P(),
        P(),
        P(),
        P("mp", None, None),
        P("mp", None, None),
        P("mp", None, None),
    )
    return jax.shard_map(
        per_device,
        mesh=mesh,
        in_specs=placed,
        out_specs=(both, both),
        check_vma=False,
    )
```

time: 413 us -> 401 us (0.971)
  waiting for transfers between devices: 203 us -> 151 us
  blocking collectives: 25.8 us -> 39.1 us
  starting transfers between devices: 45.2 us -> 55.3 us
  Pallas kernels: 18.7 us -> 26.1 us
  local copies, waits for them, and re-layouts: 37.8 us -> 43.1 us
    ppermute x0 -> x9, waiting for transfers between devices: none -> 39.5 us  [the longest x1 34.9 us: per_device(): lax.ppermute(normed, 'mp', [(j, (j + 4) % mp_size) for j in range(mp_size)])]
    all_to_all x1 -> x0, waiting for transfers between devices: 38.9 us -> none  [per_device(): path = lax.all_to_all(path, 'mp', split_axis=0, concat_axis=0, tiled=True)]
    all_gather x2, waiting for transfers between devices: 33.7 us -> 0.01 us  [whole_rows(): lax.all_gather(values.reshape(mp_size * own_rows, -1), 'dp', axis=0, tile...]
    all_to_all x1, waiting for transfers between devices: 16.3 us -> 0.01 us  [per_device(): lax.all_to_all(early, 'dp', split_axis=0, concat_axis=0, tiled=True)]
    all_to_all x1, blocking collectives: 25.8 us -> 39.1 us  [per_device(): lax.all_to_all(packed, 'mp', split_axis=0, concat_axis=0, tiled=True)]
    ppermute x0 -> x9, starting transfers between devices: none -> 13.1 us  [the longest x8 13.1 us: shift(): return lax.ppermute(values, 'mp', moves)]
    pallas_call x1, Pallas kernels: 16 us -> 25.2 us  [attend(): pl.pallas_call(attention_kernel, out_shape=jax.ShapeDtypeStruct((group, 2...]
    all_to_all x1, waiting for transfers between devices: 0.01 us -> 7.7 us  [per_device(): lax.all_to_all(attended.reshape(mp_size, tok, 2 * hd), 'mp', split_axis=0...]
  transfers between devices with their start and end apart: 12 -> 20, of which waited for: 9 -> 8; matrix products, arithmetic and copies ran while one was open for 14% -> 17% of each run, Pallas kernels for 5% -> 6%
where the time goes in v2:
time: 401 us; the launch traced here: 398 us
  waiting for transfers between devices  151 us (38%)
  starting transfers between devices  55.3 us (14%)
  local copies, waits for them, and re-layouts  43.1 us (11%)
  matrix products  42.2 us (11%)
  blocking collectives  39.1 us (10%)
  Pallas kernels  26.1 us (7%)
  other arithmetic  25.4 us (6%)
  between operations  15.8 us (4%)
    all_to_all x4, waiting for transfers between devices, exchange(): return lax.all_to_all(values, BOTH, split_axis=0, concat_axis=0, tiled=True)  103 us
    all_to_all x1, blocking collectives, per_device(): lax.all_to_all(packed, 'mp', split_axis=0, concat_axis=0, tiled=True)  39.1 us
    ppermute x1, waiting for transfers between devices, per_device(): lax.ppermute(normed, 'mp', [(j, (j + 4) % mp_size) for j in range(mp_size)])  34.9 us
    all_to_all x4, starting transfers between devices, exchange(): return lax.all_to_all(values, BOTH, split_axis=0, concat_axis=0, tiled=True)  26.6 us
    pallas_call x1, Pallas kernels, attend(): pl.pallas_call(attention_kernel, out_shape=jax.ShapeDtypeStruct((group, 2...  25.2 us
    unnamed x50, local copies, waits for them, and re-layouts  17.1 us
    dot_general x2, matrix products, expert(): both = jnp.dot(rows, gate_up, preferred_element_type=jnp.float32)  14.9 us
    ppermute x8, starting transfers between devices, shift(): return lax.ppermute(values, 'mp', moves)  13.1 us
  transfers between devices with their start and end apart: 20, of which 8 were waited for; matrix products, arithmetic and copies ran while one was open for 17% of the time, Pallas kernels for 6%

profile of v2, /device:TPU:0, one launch (start us, length us, event | category | flops | bytes accessed | tf_op | source)
XLA Modules:
  0.0 398.3 jit_solution(16843048798001171707)
XLA Ops:
  7.2 1.4 slice.85
  10.1 1.4 convert_reduce_fusion
  22.1 39.1 %all_to_all.35 = bf16[8,640,256]{2,1,0:T(8,128)(2,1)S(1)} all-to-all(bf16[8,640,256]{2,1,0:T(8,128)(2,1)S(1)} %pack.1), channel_id=1, replica_groups=mesh['dp'=16,'mp'=8] {'mp'}, dimensions={0} | all-to-all | bytes 5242880 | tf_op jit(solution)/shard_map/all_to_all | solution.py:374
  61.2 1.5 copy-done.18
  65.2 1.6 fusion.68
  66.9 1.6 broadcast_in_dim.197
  68.5 6.8 %all-to-all-start.1 = ((bf16[16,8,2,16,256]{4,3,2,1,0:T(8,128)(2,1)}), bf16[16,8,2,16,256]{4,3,2,1,0:T(8,128)(2,1)}, u32[]{:S(2)}, u32[]{:S(2)}) async-start(bf16[16,8,2,16,256]{4,3,2,1,0:T(8,128)(2,1)} %broadcast_in_dim.197), calls=%async_computation.1 | async-start | bytes 4194304 | tf_op jit(solution)/shard_map/all_to_all | solution.py:390
  75.3 2.0 fusion.25.own
  77.8 2.8 collective-permute-start.2
  80.6 34.9 %collective-permute-done.across = bf16[128,2048]{1,0:T(8,128)(2,1)} collective-permute-done((bf16[128,2048]{1,0:T(8,128)(2,1)}, bf16[128,2048]{1,0:T(8,128)(2,1)}, u32[]{:S(2)}, u32[]{:S(2)}) %collective-permute-start) | collective-permute-done | bytes 524320 | tf_op jit(solution)/shard_map/ppermute | solution.py:346
  116.6 2.2 collective-permute-start.4
  123.9 3.3 collective-permute-start.6
  127.2 4.6 %collective-permute-done.3.across_left = bf16[128,2048]{1,0:T(8,128)(2,1)} collective-permute-done((bf16[128,2048]{1,0:T(8,128)(2,1)}, bf16[128,2048]{1,0:T(8,128)(2,1)}, u32[]{:S(2)}, u32[]{:S(2)}) %collective-permute-start.3) | collective-permute-done | bytes 524320 | tf_op jit(solution)/shard_map/ppermute | solution.py:344
  131.8 1.7 slice.115
  133.5 1.7 slice.116
  135.2 3.2 collective-permute-start.8
  138.4 1.7 slice_reduce_fusion.piece_0
  141.0 1.4 collective-permute-start.11
  143.1 2.0 collective-permute-start.9
  145.1 3.1 fusion.43
  148.4 2.9 pad_maximum_fusion
  156.4 25.2 %tree_attention.1 = bf16[1024,256]{1,0:T(8,128)(2,1)S(1)} custom-call(s32[14]{0:T(128)S(1)} %pad_add_fusion.2.meta, bf16[128,2048]{1,0:T(8,128)(2,1)} %fusion.25.own, bf16[128,2048]{1,0:T(8,128)(2,1)} %collective-permute-done.across, bf16[128,2048]{1,0:T(8,128)(2,1)} %collective-permute-done.1.own_left, bf16[128,2048]{1,0:T(8,128)(2,1)} %collective-permute-done.2.own_right, ...), custom_call_target="tpu_custom_call" | custom-call | tf_op jit(solution)/shard_map/tree_attention/pallas_call | solution.py:250
  182.4 5.0 %all-to-all-start.2 = ((bf16[8,128,256]{2,1,0:T(8,128)(2,1)}), bf16[8,128,256]{2,1,0:T(8,128)(2,1)}, u32[]{:S(2)}, u32[]{:S(2)}) async-start(bf16[8,128,256]{2,1,0:T(8,128)(2,1)} %bitcast.106), calls=%async_computation.2 | async-start | bytes 1048576 | tf_op jit(solution)/shard_map/all_to_all | solution.py:397
  188.1 7.7 %all-to-all-done.2 = bf16[8,128,256]{2,1,0:T(8,128)(2,1)} async-done(((bf16[8,128,256]{2,1,0:T(8,128)(2,1)}), bf16[8,128,256]{2,1,0:T(8,128)(2,1)}, u32[]{:S(2)}, u32[]{:S(2)}) %all-to-all-start.2) | async-done | bytes 524320 | tf_op jit(solution)/shard_map/all_to_all | solution.py:397
  195.8 5.0 %multiply_reduce_fusion = (f32[128]{0:T(128)S(1)}, f32[128,2048]{1,0:T(8,128)S(1)}) fusion(bf16[8,128,256]{2,1,0:T(8,128)(2,1)} %all-to-all-done.2, bf16[8,256,2048]{2,1,0:T(8,128)(2,1)} %bitcast.107, bf16[128,2048]{1,0:T(8,128)(2,1)} %param.24), kind=kOutput, calls=%fused_computation.40 | convolution fusion | flops 1075314560 | bytes 10486272 | tf_op jit(solution)/shard_map/mtk,mkd->td/dot_general | solution.py:400
  201.8 3.3 convert_bitcast_fusion.1
  205.1 8.5 %all-to-all-start.3 = ((bf16[128,8,2048]{2,1,0:T(8,128)(2,1)}), bf16[128,8,2048]{2,1,0:T(8,128)(2,1)}, u32[]{:S(2)}, u32[]{:S(2)}) async-start(bf16[128,8,2048]{2,1,0:T(8,128)(2,1)} %convert_bitcast_fusion.1), calls=%async_computation.3 | async-start | bytes 8388608 | tf_op jit(solution)/shard_map/all_to_all | solution.py:269
  213.8 2.7 convolution_convert_fusion
  216.5 2.6 reshape.166
  219.1 47.2 %all-to-all-done.3 = bf16[128,8,2048]{2,1,0:T(8,128)(2,1)} async-done(((bf16[128,8,2048]{2,1,0:T(8,128)(2,1)}), bf16[128,8,2048]{2,1,0:T(8,128)(2,1)}, u32[]{:S(2)}, u32[]{:S(2)}) %all-to-all-start.3) | async-done | bytes 4194336 | tf_op jit(solution)/shard_map/all_to_all | solution.py:269
  266.2 5.8 %all-to-all-start.5 = ((bf16[128,2,2048]{2,1,0:T(2,128)(2,1)}), bf16[128,2,2048]{2,1,0:T(2,128)(2,1)}, u32[]{:S(2)}, u32[]{:S(2)}) async-start(bf16[128,2,2048]{2,1,0:T(2,128)(2,1)} %reshape.166), calls=%async_computation.5 | async-start | bytes 2097152 | tf_op jit(solution)/shard_map/all_to_all | solution.py:269
  272.0 10.0 %fusion.2 = f32[1024,1536]{1,0:T(8,128)S(1)} fusion(bf16[1,2048,1536]{2,1,0:T(8,128)(2,1)} %param.30, bf16[128,8,2048]{2,1,0:T(8,128)(2,1)} %all-to-all-done.3), kind=kOutput, calls=%fused_computation.2 | convolution fusion | flops 6442450944 | bytes 16777216 | tf_op jit(solution)/shard_map/dot_general | solution.py:274
  282.0 5.1 %convert_bitcast_fusion = bf16[128,8,2048]{2,1,0:T(8,128)(2,1)} fusion(bf16[1,768,2048]{2,1,0:T(8,128)(2,1)S(1)} %copy-done, f32[1024,1536]{1,0:T(8,128)S(1)} %fusion.2), kind=kOutput, calls=%fused_computation.7 | convolution fusion | flops 3228041216 | bytes 13631488 | tf_op jit(solution)/shard_map/dot_general | solution.py:276
  287.1 3.6 all-to-all-done.5
  290.7 6.6 %all-to-all-start.4 = ((bf16[128,8,2048]{2,1,0:T(8,128)(2,1)}), bf16[128,8,2048]{2,1,0:T(8,128)(2,1)}, u32[]{:S(2)}, u32[]{:S(2)}) async-start(bf16[128,8,2048]{2,1,0:T(8,128)(2,1)} %convert_bitcast_fusion), calls=%async_computation.4 | async-start | bytes 8388608 | tf_op jit(solution)/shard_map/all_to_all | solution.py:269
  300.0 1.7 fusion.52
  301.7 2.3 reshape.169
  303.9 4.9 %fusion = f32[256,1536]{1,0:T(8,128)S(1)} fusion(bf16[256,2048]{1,0:T(8,128)(2,1)} %reshape.169, bf16[1,2048,1536]{2,1,0:T(8,128)(2,1)} %param.30), kind=kOutput, calls=%fused_computation | convolution fusion | flops 1610612736 | bytes 8912896 | tf_op jit(solution)/shard_map/dot_general | solution.py:274
  308.8 2.1 fusion.11
  310.9 2.5 reshape.170
  313.5 38.4 %all-to-all-done.4 = bf16[128,8,2048]{2,1,0:T(8,128)(2,1)} async-done(((bf16[128,8,2048]{2,1,0:T(8,128)(2,1)}), bf16[128,8,2048]{2,1,0:T(8,128)(2,1)}, u32[]{:S(2)}, u32[]{:S(2)}) %all-to-all-start.4) | async-done | bytes 4194336 | tf_op jit(solution)/shard_map/all_to_all | solution.py:269
  351.9 5.8 %all-to-all-start.6 = ((bf16[128,2,2048]{2,1,0:T(2,128)(2,1)}), bf16[128,2,2048]{2,1,0:T(2,128)(2,1)}, u32[]{:S(2)}, u32[]{:S(2)}) async-start(bf16[128,2,2048]{2,1,0:T(2,128)(2,1)} %reshape.170), calls=%async_computation.6 | async-start | bytes 2097152 | tf_op jit(solution)/shard_map/all_to_all | solution.py:269
  358.1 4.8 %fusion.4 = f32[256,2048]{1,0:T(8,128)} fusion(bf16[128,8,2048]{2,1,0:T(8,128)(2,1)} %all-to-all-done.4, bf16[128,1024]{0,1:T(8,128)(2,1)S(1)} %get-tuple-element.25, bf16[128,1024]{0,1:T(8,128)(2,1)S(1)} %get-tuple-element.24), kind=kOutput, calls=%fused_computation.4 | convolution fusion | flops 1074790400 | bytes 6815744 | tf_op jit(solution)/shard_map/dot_general | solution.py:436
  362.9 13.8 %all-to-all-done.6 = bf16[128,2,2048]{2,1,0:T(2,128)(2,1)} async-done(((bf16[128,2,2048]{2,1,0:T(2,128)(2,1)}), bf16[128,2,2048]{2,1,0:T(2,128)(2,1)}, u32[]{:S(2)}, u32[]{:S(2)}) %all-to-all-start.6) | async-done | bytes 1048608 | tf_op jit(solution)/shard_map/all_to_all | solution.py:269
  376.7 2.3 reshape.172
  379.0 1.8 fusion.47
  382.6 2.3 fusion.31
  390.0 1.5 pad_maximum_fusion.2
  (130 shorter events, 39.2 us)
Async XLA Ops:
  7.2 274.9 %copy-start = (bf16[1,768,2048]{2,1,0:T(8,128)(2,1)S(1)}, bf16[1,768,2048]{2,1,0:T(8,128)(2,1)}, u32[]{:S(2)}) copy-start(bf16[1,768,2048]{2,1,0:T(8,128)(2,1)} %param.31) | copy-start | bytes 9437188
  7.2 188.6 %all-gather.3.cloned.1.call-start = ((), (), s32[]{:S(2)}) async-start(), calls=%async_computation.7 | async-start | bytes 8912896 | tf_op jit(solution)/shard_map/all_gather | solution.py:382
  15.2 1.0 copy-start.4
  16.2 0.9 copy-start.5
  17.1 0.9 copy-start.6
  18.1 0.8 copy-start.11
  18.9 0.8 copy-start.12
  19.8 0.7 copy-start.13
  20.5 0.7 copy-start.14
  61.2 1.5 copy-start.18
  62.8 2.4 copy-start.20
  68.5 83.9 %all-to-all-start.1 = ((bf16[16,8,2,16,256]{4,3,2,1,0:T(8,128)(2,1)}), bf16[16,8,2,16,256]{4,3,2,1,0:T(8,128)(2,1)}, u32[]{:S(2)}, u32[]{:S(2)}) async-start(bf16[16,8,2,16,256]{4,3,2,1,0:T(8,128)(2,1)} %broadcast_in_dim.197), calls=%async_computation.1 | async-start | bytes 4194304 | tf_op jit(solution)/shard_map/all_to_all | solution.py:390
  75.3 73.0 %copy-start.21 = (s32[128,8]{0,1:T(8,128)S(1)}, s32[128,8]{0,1:T(8,128)}, u32[]{:S(2)}) copy-start(s32[128,8]{0,1:T(8,128)} %param.33) | copy-start | bytes 12292
  77.3 38.2 %collective-permute-start = (bf16[128,2048]{1,0:T(8,128)(2,1)}, bf16[128,2048]{1,0:T(8,128)(2,1)}, u32[]{:S(2)}, u32[]{:S(2)}) collective-permute-start(bf16[128,2048]{1,0:T(8,128)(2,1)} %fusion.25.own), channel_id=1, source_target_pairs={{0,4},{1,5},{2,6},{3,7},{4,0},{5,1},{6,2},{7,3},{8,12},{9,13},{10,... | collective-permute-start | bytes 1572872 | tf_op jit(solution)/shard_map/ppermute | solution.py:346
  77.3 44.6 %collective-permute-start.1 = (bf16[128,2048]{1,0:T(8,128)(2,1)}, bf16[128,2048]{1,0:T(8,128)(2,1)}, u32[]{:S(2)}, u32[]{:S(2)}) collective-permute-start(bf16[128,2048]{1,0:T(8,128)(2,1)} %fusion.25.own), channel_id=1, source_target_pairs={{0,1},{1,2},{2,3},{3,0},{4,5},{5,6},{6,7},{7,4},{8,9},{9,10},{10,1... | collective-permute-start | bytes 1572872 | tf_op jit(solution)/shard_map/ppermute | solution.py:344
  77.8 45.1 %collective-permute-start.2 = (bf16[128,2048]{1,0:T(8,128)(2,1)}, bf16[128,2048]{1,0:T(8,128)(2,1)}, u32[]{:S(2)}, u32[]{:S(2)}) collective-permute-start(bf16[128,2048]{1,0:T(8,128)(2,1)} %fusion.25.own), channel_id=1, source_target_pairs={{0,3},{1,0},{2,1},{3,2},{4,7},{5,4},{6,5},{7,6},{8,11},{9,8},{10,9... | collective-permute-start | bytes 1572872 | tf_op jit(solution)/shard_map/ppermute | solution.py:344
  115.5 16.3 %collective-permute-start.3 = (bf16[128,2048]{1,0:T(8,128)(2,1)}, bf16[128,2048]{1,0:T(8,128)(2,1)}, u32[]{:S(2)}, u32[]{:S(2)}) collective-permute-start(bf16[128,2048]{1,0:T(8,128)(2,1)} %collective-permute-done.across), channel_id=1, source_target_pairs={{0,1},{1,2},{2,3},{3,0},{4,5},{5,6},{6,7},{7,4},{8,9},{9,10},{10,1... | collective-permute-start | bytes 1572872 | tf_op jit(solution)/shard_map/ppermute | solution.py:344
  116.6 16.9 %collective-permute-start.4 = (bf16[128,2048]{1,0:T(8,128)(2,1)}, bf16[128,2048]{1,0:T(8,128)(2,1)}, u32[]{:S(2)}, u32[]{:S(2)}) collective-permute-start(bf16[128,2048]{1,0:T(8,128)(2,1)} %collective-permute-done.across), channel_id=1, source_target_pairs={{0,3},{1,0},{2,1},{3,2},{4,7},{5,4},{6,5},{7,6},{8,11},{9,8},{10,9... | collective-permute-start | bytes 1572872 | tf_op jit(solution)/shard_map/ppermute | solution.py:344
  122.9 17.4 %collective-permute-start.5 = (bf16[64,2048]{1,0:T(8,128)(2,1)S(1)}, bf16[64,2048]{1,0:T(8,128)(2,1)S(1)}, u32[]{:S(2)}, u32[]{:S(2)}) collective-permute-start(bf16[64,2048]{1,0:T(8,128)(2,1)S(1)} %slice.113), channel_id=1, source_target_pairs={{0,1},{1,2},{2,3},{3,0},{4,5},{5,6},{6,7},{7,4},{8,9},{9,10},{10,1... | collective-permute-start | bytes 786440 | tf_op jit(solution)/shard_map/ppermute | solution.py:344
  123.9 18.5 %collective-permute-start.6 = (bf16[64,2048]{1,0:T(8,128)(2,1)S(1)}, bf16[64,2048]{1,0:T(8,128)(2,1)S(1)}, u32[]{:S(2)}, u32[]{:S(2)}) collective-permute-start(bf16[64,2048]{1,0:T(8,128)(2,1)S(1)} %slice.114), channel_id=1, source_target_pairs={{0,3},{1,0},{2,1},{3,2},{4,7},{5,4},{6,5},{7,6},{8,11},{9,8},{10,9... | collective-permute-start | bytes 786440 | tf_op jit(solution)/shard_map/ppermute | solution.py:344
  133.5 17.8 %collective-permute-start.7 = (bf16[64,2048]{1,0:T(8,128)(2,1)}, bf16[64,2048]{1,0:T(8,128)(2,1)}, u32[]{:S(2)}, u32[]{:S(2)}) collective-permute-start(bf16[64,2048]{1,0:T(8,128)(2,1)} %slice.115), channel_id=1, source_target_pairs={{0,1},{1,2},{2,3},{3,0},{4,5},{5,6},{6,7},{7,4},{8,9},{9,10},{10,1... | collective-permute-start | bytes 786440 | tf_op jit(solution)/shard_map/ppermute | solution.py:344
  135.2 17.2 %copy-start.15 = (f32[3,128]{1,0:T(4,128)S(1)}, f32[3,128]{1,0:T(4,128)}, u32[]{:S(2)}) copy-start(f32[3,128]{1,0:T(4,128)} %gains.1) | copy-start | bytes 4612
  135.2 16.2 %collective-permute-start.8 = (bf16[64,2048]{1,0:T(8,128)(2,1)}, bf16[64,2048]{1,0:T(8,128)(2,1)}, u32[]{:S(2)}, u32[]{:S(2)}) collective-permute-start(bf16[64,2048]{1,0:T(8,128)(2,1)} %slice.116), channel_id=1, source_target_pairs={{0,3},{1,0},{2,1},{3,2},{4,7},{5,4},{6,5},{7,6},{8,11},{9,8},{10,9... | collective-permute-start | bytes 786440 | tf_op jit(solution)/shard_map/ppermute | solution.py:344
  140.1 11.2 %collective-permute-start.10 = (bf16[448,256]{1,0:T(8,128)(2,1)S(1)}, bf16[448,256]{1,0:T(8,128)(2,1)}, u32[]{:S(2)}, u32[]{:S(2)}) collective-permute-start(bf16[448,256]{1,0:T(8,128)(2,1)S(1)} %slice_reduce_fusion.piece_0), channel_id=1, source_target_pairs={{0,2},{1,3},{2,0},{3,1},{4,6},{5,7},{6,4},{7,5},{8,10},{9,11},{10,... | collective-permute-start | bytes 688136 | tf_op jit(solution)/shard_map/ppermute | solution.py:394
  140.3 0.7 copy-start.7
  141.0 11.4 %collective-permute-start.11 = (bf16[448,256]{1,0:T(8,128)(2,1)S(1)}, bf16[448,256]{1,0:T(8,128)(2,1)}, u32[]{:S(2)}, u32[]{:S(2)}) collective-permute-start(bf16[448,256]{1,0:T(8,128)(2,1)S(1)} %slice_reduce_fusion.piece_0), channel_id=1, source_target_pairs={{0,3},{1,2},{2,1},{3,0},{4,7},{5,6},{6,5},{7,4},{8,11},{9,10},{10,... | collective-permute-start | bytes 688136 | tf_op jit(solution)/shard_map/ppermute | solution.py:394
  142.4 0.7 copy-start.9
  143.1 9.2 %collective-permute-start.9 = (bf16[448,256]{1,0:T(8,128)(2,1)S(1)}, bf16[448,256]{1,0:T(8,128)(2,1)}, u32[]{:S(2)}, u32[]{:S(2)}) collective-permute-start(bf16[448,256]{1,0:T(8,128)(2,1)S(1)} %slice_reduce_fusion.piece_0), channel_id=1, source_target_pairs={{0,1},{1,0},{2,3},{3,2},{4,5},{5,4},{6,7},{7,6},{8,9},{9,8},{10,11... | collective-permute-start | bytes 688136 | tf_op jit(solution)/shard_map/ppermute | solution.py:394
  152.3 1.0 copy-start.1
  153.4 1.1 copy-start.2
  154.5 0.9 copy-start.8
  155.5 1.0 copy-start.10
  181.6 0.8 copy-start.3
  182.4 13.4 %all-to-all-start.2 = ((bf16[8,128,256]{2,1,0:T(8,128)(2,1)}), bf16[8,128,256]{2,1,0:T(8,128)(2,1)}, u32[]{:S(2)}, u32[]{:S(2)}) async-start(bf16[8,128,256]{2,1,0:T(8,128)(2,1)} %bitcast.106), calls=%async_computation.2 | async-start | bytes 1048576 | tf_op jit(solution)/shard_map/all_to_all | solution.py:397
  200.8 1.0 copy-start.16
  205.1 61.2 %all-to-all-start.3 = ((bf16[128,8,2048]{2,1,0:T(8,128)(2,1)}), bf16[128,8,2048]{2,1,0:T(8,128)(2,1)}, u32[]{:S(2)}, u32[]{:S(2)}) async-start(bf16[128,8,2048]{2,1,0:T(8,128)(2,1)} %convert_bitcast_fusion.1), calls=%async_computation.3 | async-start | bytes 8388608 | tf_op jit(solution)/shard_map/all_to_all | solution.py:269
  266.2 24.5 %all-to-all-start.5 = ((bf16[128,2,2048]{2,1,0:T(2,128)(2,1)}), bf16[128,2,2048]{2,1,0:T(2,128)(2,1)}, u32[]{:S(2)}, u32[]{:S(2)}) async-start(bf16[128,2,2048]{2,1,0:T(2,128)(2,1)} %reshape.166), calls=%async_computation.5 | async-start | bytes 2097152 | tf_op jit(solution)/shard_map/all_to_all | solution.py:269
  287.1 12.3 %copy-start.22 = (f32[128,8]{0,1:T(8,128)S(1)}, f32[128,8]{0,1:T(8,128)}, u32[]{:S(2)}) copy-start(f32[128,8]{0,1:T(8,128)} %param.34) | copy-start | bytes 12292
  290.7 61.1 %all-to-all-start.4 = ((bf16[128,8,2048]{2,1,0:T(8,128)(2,1)}), bf16[128,8,2048]{2,1,0:T(8,128)(2,1)}, u32[]{:S(2)}, u32[]{:S(2)}) async-start(bf16[128,8,2048]{2,1,0:T(8,128)(2,1)} %convert_bitcast_fusion), calls=%async_computation.4 | async-start | bytes 8388608 | tf_op jit(solution)/shard_map/all_to_all | solution.py:269
  297.3 85.3 %all-gather.5.cloned.1.call-start = ((), (), s32[]{:S(2)}) async-start(), calls=%async_computation.8 | async-start | bytes 2228224 | tf_op jit(solution)/shard_map/all_gather | solution.py:382
  351.9 24.8 %all-to-all-start.6 = ((bf16[128,2,2048]{2,1,0:T(2,128)(2,1)}), bf16[128,2,2048]{2,1,0:T(2,128)(2,1)}, u32[]{:S(2)}, u32[]{:S(2)}) async-start(bf16[128,2,2048]{2,1,0:T(2,128)(2,1)} %reshape.170), calls=%async_computation.6 | async-start | bytes 2097152 | tf_op jit(solution)/shard_map/all_to_all | solution.py:269
  379.0 1.8 copy-start.17
  379.0 2.2 copy-start.19
Sparse Core Ops, SparseCore 0:
  64.1 92.5 all-gather.2
  301.1 65.5 all-gather.4

commit v3 on v2

--- a/solution.py
+++ b/solution.py
@@ -23,37 +23,46 @@
     return jnp.sum(jnp.where(indices[:, None] == places[None, :], lookup_table[None, :], 0), axis=1)
 
 
-def pack_kernel(meta, query, kv, out_rows, next_rows, root, mid, leaf, packed):
+def pack_kernel(
+    token_request,
+    request_leaf,
+    leaf_parent,
+    mid_parent,
+    root_slot,
+    mid_slot,
+    leaf_slot,
+    query,
+    kv,
+    root,
+    mid,
+    leaf,
+    packed,
+):
     count, _, wide = packed.shape
     own_rows = query.shape[0]
     hd = wide // 2
     heads = kv.shape[1] // wide
-    columns = [out_rows[:, at : at + wide] for at in range(0, out_rows.shape[1], wide)]
-    columns += [next_rows[:, at : at + wide] for at in range(0, next_rows.shape[1], wide)]
-    shared = len(columns)
     for dest in range(count):
         head = dest * heads // count
-        for place, column in enumerate(columns):
-            packed[dest, place * own_rows : (place + 1) * own_rows, :] = column
-        at = shared * own_rows
-        packed[dest, at : at + own_rows, :] = query[:, dest * wide : (dest + 1) * wide]
-        at += own_rows
+        packed[dest, 0:own_rows, :] = query[:, dest * wide : (dest + 1) * wide]
         for half in range(2):
             source = (half * heads + head) * hd
-            packed[dest, at : at + own_rows, half * hd : (half + 1) * hd] = kv[
+            packed[dest, own_rows : 2 * own_rows, half * hd : (half + 1) * hd] = kv[
                 :, source : source + hd
             ]
-    begin = (shared + 2) * own_rows
+    begin = 2 * own_rows
     part = packed.shape[1] - begin
-    me = meta[0]
+    me = lax.axis_index("mp")
     for req in range(2):
+        leaf_node = request_leaf[token_request[0] + req]
+        mid_node = leaf_parent[leaf_node]
+        slots = (root_slot[mid_parent[mid_node]], mid_slot[mid_node], leaf_slot[leaf_node])
         levels = []
-        for level, cache in enumerate((root, mid, leaf)):
+        for slot, cache in zip(slots, (root, mid, leaf)):
             here = cache.shape[0]
             rows = jnp.zeros(cache.shape[1:], cache.dtype)
             for local in range(here):
-                wanted = meta[8 + 3 * req + level] == me * here + local
-                rows = jnp.where(wanted, cache[local], rows)
+                rows = jnp.where(slot == me * here + local, cache[local], rows)
             levels.append(rows)
         top = levels[0].shape[0] - part
         middle = levels[1].shape[0]
@@ -68,21 +77,19 @@
                 packed[place + 1, begin + top + middle :, target] = levels[2][:, source]
 
 
-def pack(meta, query, kv, out_rows, next_rows, root, mid, leaf, count):
+def pack(tables, query, kv, root, mid, leaf, count):
     wide = query.shape[1] // count
-    pieces = (out_rows.shape[1] + next_rows.shape[1]) // wide + 2
     part = (root.shape[1] + mid.shape[1] + leaf.shape[1]) // 2
     in_vmem = pl.BlockSpec(memory_space=pltpu.VMEM)
+    in_smem = pl.BlockSpec(memory_space=pltpu.SMEM)
     return pl.pallas_call(
         pack_kernel,
-        out_shape=jax.ShapeDtypeStruct(
-            (count, pieces * query.shape[0] + part, wide), jnp.bfloat16
-        ),
-        in_specs=[pl.BlockSpec(memory_space=pltpu.SMEM)] + [in_vmem] * 7,
+        out_shape=jax.ShapeDtypeStruct((count, 2 * query.shape[0] + part, wide), jnp.bfloat16),
+        in_specs=[in_smem] * len(tables) + [in_vmem] * 5,
         out_specs=in_vmem,
         compiler_params=pltpu.CompilerParams(vmem_limit_bytes=24 * 1024 * 1024),
         name="pack",
-    )(meta, query, kv, out_rows, next_rows, root, mid, leaf)
+    )(*tables, query, kv, root, mid, leaf)
 
 
 def attention_kernel(
@@ -97,7 +104,8 @@
     own_far_bottom,
     across_far_top,
     across_far_bottom,
-    weight,
+    weight_own,
+    weight_other,
     piece_0,
     piece_1,
     piece_2,
@@ -107,11 +115,15 @@
     sine,
     out,
     rows_all,
+    weights,
     q_all,
     k_all,
     v_all,
     pk_all,
     pv_all,
+    peak_all,
+    total_all,
+    acc_all,
 ):
     pieces = (piece_0, piece_1, piece_2, piece_3)
     me = meta[0]
@@ -144,33 +156,41 @@
         place = pl.multiple_of((ring ^ step) * part, part)
         pk_all[pl.ds(place, part), :] = piece[:, :hd]
         pv_all[pl.ds(place, part), :] = piece[:, hd:]
-    weight_q = weight[:, 0].reshape(dim, 2 * hd)
-    weight_kv = weight[:, 1].reshape(dim, 2 * hd)
+    core = meta[8]
+    weights[core] = weight_own[...].reshape(dim, 2 * hd)
+    weights[1 - core] = weight_other[...].reshape(dim, 2 * hd)
+    weight_q = weights[0]
+    weight_kv = weights[1]
 
     def turn(raw, gain, cos_now, sin_now):
         scaled = raw * lax.rsqrt(jnp.mean(raw * raw, axis=-1, keepdims=True) + EPS) * gain
         return (scaled * cos_now + pltpu.roll(scaled, hd // 2, 1) * sin_now).astype(jnp.bfloat16)
 
-    @pl.loop(0, count)
+    large = 4 * tok
+
+    @pl.loop(0, count // 4)
     def _(step):
-        at = pl.multiple_of(step * tok, tok)
-        rows = rows_all[pl.ds(at, tok), :]
-        cos_now = cosine[pl.ds(at, tok), :]
-        sin_now = sine[pl.ds(at, tok), :]
+        at = pl.multiple_of(step * large, large)
+        rows = rows_all[pl.ds(at, large), :]
+        cos_now = cosine[pl.ds(at, large), :]
+        sin_now = sine[pl.ds(at, large), :]
         raw = jnp.dot(rows, weight_q, preferred_element_type=jnp.float32)
-        q_at = pl.multiple_of(2 * step * tok, 2 * tok)
-        q_all[pl.ds(q_at, tok), :] = turn(raw[:, :hd], gains[0:1, :], cos_now, sin_now)
-        q_all[pl.ds(q_at + tok, tok), :] = turn(raw[:, hd:], gains[0:1, :], cos_now, sin_now)
+        heads = [
+            turn(raw[:, half * hd : (half + 1) * hd], gains[0:1, :], cos_now, sin_now)
+            for half in range(2)
+        ]
+        for block in range(4):
+            for half in range(2):
+                q_at = pl.multiple_of(2 * at + (2 * block + half) * tok, tok)
+                q_all[pl.ds(q_at, tok), :] = heads[half][block * tok : (block + 1) * tok]
         raw = jnp.dot(rows, weight_kv, preferred_element_type=jnp.float32)
-        k_all[pl.ds(at, tok), :] = turn(raw[:, :hd], gains[1:2, :], cos_now, sin_now)
-        v_all[pl.ds(at, tok), :] = raw[:, hd:].astype(jnp.bfloat16)
+        k_all[pl.ds(at, large), :] = turn(raw[:, :hd], gains[1:2, :], cos_now, sin_now)
+        v_all[pl.ds(at, large), :] = raw[:, hd:].astype(jnp.bfloat16)
 
     scale = hd ** (-0.5) * LOG2E
     col = lax.broadcasted_iota(jnp.int32, (1, span), 1)
     row = lax.broadcasted_iota(jnp.int32, (2 * tok, 1), 0)
     row = jnp.where(row >= tok, row - tok, row)
-    chunk = 2 * tok
-    key_col = lax.broadcasted_iota(jnp.int32, (1, chunk), 1)
 
     def join(state, q_now, keys, values, allowed):
         peak, total, acc = state
@@ -215,34 +235,41 @@
                 inside * mine > 0,
             )
 
-        state = (
-            jnp.full((2 * tok, 1), MASKED, jnp.float32),
-            jnp.zeros((2 * tok, 1), jnp.float32),
-            jnp.zeros((2 * tok, hd), jnp.float32),
-        )
+        peak_all[...] = jnp.full((2 * tok, 1), MASKED, jnp.float32)
+        total_all[...] = jnp.zeros((2 * tok, 1), jnp.float32)
+        acc_all[...] = jnp.zeros((2 * tok, hd), jnp.float32)
         low = (first >= cut).astype(jnp.int32)
         high = (first + tok > cut).astype(jnp.int32)
-        state = lax.fori_loop(low, high + 1, prefix, state)
+
+        @pl.loop(low, high + 1)
+        def _(req):
+            peak, total, acc = prefix(req, (peak_all[...], total_all[...], acc_all[...]))
+            peak_all[...] = peak
+            total_all[...] = total
+            acc_all[...] = acc
+
         bottom = jnp.where(late, cut, 0)
 
-        def new(number, state):
-            start = pl.multiple_of(number * chunk, chunk)
-            other = key_col + start
-            return join(
-                state,
-                q_now,
-                k_all[pl.ds(start, chunk), :],
-                v_all[pl.ds(start, chunk), :],
-                jnp.logical_and(other <= token, other >= bottom),
-            )
-
-        peak, total, acc = lax.fori_loop(0, step // 2 + 1, new, state)
-        done = (acc / total).astype(jnp.bfloat16)
-        out[pl.ds(first, tok), 0:hd] = done[:tok]
-        out[pl.ds(first, tok), hd : 2 * hd] = done[tok:]
-
-
-def attend(meta, rows, weight, pieces, gains, cosine, sine):
+        for quarter in range(count // 2):
+
+            @pl.when(step // 2 == quarter)
+            def _(quarter=quarter):
+                keys = 2 * tok * (quarter + 1)
+                other = lax.broadcasted_iota(jnp.int32, (1, keys), 1)
+                allowed = jnp.logical_and(other <= token, other >= bottom)
+                peak, total, acc = join(
+                    (peak_all[...], total_all[...], acc_all[...]),
+                    q_now,
+                    k_all[0:keys, :],
+                    v_all[0:keys, :],
+                    allowed,
+                )
+                done = (acc / total).astype(jnp.bfloat16)
+                out[pl.ds(first, tok), 0:hd] = done[:tok]
+                out[pl.ds(first, tok), hd : 2 * hd] = done[tok:]
+
+
+def attend(meta, rows, weights, pieces, gains, cosine, sine):
     group = cosine.shape[0]
     hd = gains.shape[1]
     path_rows = 4 * pieces[0].shape[0]
@@ -250,19 +277,23 @@
     return pl.pallas_call(
         attention_kernel,
         out_shape=jax.ShapeDtypeStruct((group, 2 * hd), jnp.bfloat16),
-        in_specs=[pl.BlockSpec(memory_space=pltpu.SMEM)] + [in_vmem] * 18,
+        in_specs=[pl.BlockSpec(memory_space=pltpu.SMEM)] + [in_vmem] * 19,
         out_specs=in_vmem,
         scratch_shapes=[
             pltpu.VMEM((group, rows[0].shape[1]), jnp.bfloat16),
+            pltpu.VMEM((2, rows[0].shape[1], 2 * hd), jnp.bfloat16),
             pltpu.VMEM((2 * group, hd), jnp.bfloat16),
             pltpu.VMEM((group, hd), jnp.bfloat16),
             pltpu.VMEM((group, hd), jnp.bfloat16),
             pltpu.VMEM((path_rows, hd), jnp.bfloat16),
             pltpu.VMEM((path_rows, hd), jnp.bfloat16),
+            pltpu.VMEM((256, 1), jnp.float32),
+            pltpu.VMEM((256, 1), jnp.float32),
+            pltpu.VMEM((256, hd), jnp.float32),
         ],
         compiler_params=pltpu.CompilerParams(vmem_limit_bytes=40 * 1024 * 1024),
         name="tree_attention",
-    )(meta, *rows, weight, *pieces, gains, cosine, sine)
+    )(meta, *rows, *weights, *pieces, gains, cosine, sine)
 
 
 def exchange(values):
@@ -318,11 +349,6 @@
     leaf_node = look_up(request_leaf, pair)
     mid_node = look_up(leaf_parent, leaf_node)
     root_node = look_up(mid_parent, mid_node)
-    slots = (
-        look_up(root_slot, root_node),
-        look_up(mid_slot, mid_node),
-        look_up(leaf_slot, leaf_node),
-    )
     lengths = (
         look_up(root_length, root_node),
         look_up(mid_length, mid_node),
@@ -344,56 +370,58 @@
         return lax.ppermute(values, "mp", moves)
 
     across = lax.ppermute(normed, "mp", [(j, (j + 4) % mp_size) for j in range(mp_size)])
-    sides = []
+    left = shift(normed, 1)
+    right = shift(normed, -1)
+    late = jnp.concatenate([out_weight, next_weight], axis=1)
+    late = jnp.broadcast_to(late[None], (mp_size,) + late.shape)
+    late = lax.all_to_all(late, "mp", split_axis=0, concat_axis=0, tiled=True)
+    late = late.reshape(mp_size * own_rows, -1)
+    out_full = lax.all_gather(late[:, :dim], "dp", axis=0, tiled=True)
+    next_full = lax.all_gather(late[:, dim:], "dp", axis=0, tiled=True)
+
+    tables = (
+        token_request,
+        request_leaf,
+        leaf_parent,
+        mid_parent,
+        root_slot,
+        mid_slot,
+        leaf_slot,
+    )
+    packed = pack(
+        tables, query_weight, kv_weight, root_cache, mid_cache, leaf_cache, mp_size
+    )
+    packed, across, left, right, late = lax.optimization_barrier(
+        (packed, across, left, right, late)
+    )
+    packed = lax.all_to_all(packed, "mp", split_axis=0, concat_axis=0, tiled=True)
+    wide = packed.shape[2]
+    early_end = 2 * own_rows
+    early = packed[:, :early_end].reshape(mp_size, 2, own_rows, wide).transpose(1, 0, 2, 3)
+    early = jnp.broadcast_to(early[None], (dp_size // 2, 2, mp_size, own_rows, wide))
+    early = early.reshape(dp_size, mp_size, own_rows, wide)
+    sides = [left, right, shift(across, 1), shift(across, -1)]
+    early, *sides = lax.optimization_barrier((early, *sides))
+    early = lax.all_to_all(early, "dp", split_axis=0, concat_axis=0, tiled=True)
     far = []
-    for block in (normed, across):
-        left = shift(block, 1)
-        right = shift(block, -1)
-        sides += [left, right]
-        far += [shift(left[: tok // 2], 1), shift(right[tok // 2 :], -1)]
+    for near in range(0, 4, 2):
+        far += [shift(sides[near][: tok // 2], 1), shift(sides[near + 1][tok // 2 :], -1)]
+    own_piece = jnp.sum(packed[:, early_end:].astype(jnp.float32), axis=0).astype(jnp.bfloat16)
+    pieces = [own_piece] + [
+        lax.ppermute(own_piece, "mp", [(j, j ^ s) for j in range(mp_size)]) for s in range(1, 4)
+    ]
+    early, far, pieces = lax.optimization_barrier((early, far, pieces))
+    early = early.reshape(devices, own_rows, wide)
+    weights = (early, lax.ppermute(early, "dp", [(j, j ^ 1) for j in range(dp_size)]))
     rows = [normed, across] + sides + far
-
     meta = jnp.concatenate(
         [
             jnp.stack([me, cut]),
             jnp.stack(lengths, axis=1).reshape(-1),
-            jnp.stack(slots, axis=1).reshape(-1),
+            jnp.stack([lax.rem(lax.axis_index("dp"), 2)]),
         ]
     ).astype(jnp.int32)
-    packed = pack(
-        meta,
-        query_weight,
-        kv_weight,
-        out_weight,
-        next_weight,
-        root_cache,
-        mid_cache,
-        leaf_cache,
-        mp_size,
-    )
-    packed = lax.all_to_all(packed, "mp", split_axis=0, concat_axis=0, tiled=True)
-    wide = packed.shape[2]
-    out_end = dim // wide * own_rows
-    next_end = out_end + next_weight.shape[1] // wide * own_rows
-    early_end = next_end + 2 * own_rows
-
-    def whole_rows(values):
-        values = values.reshape(mp_size, -1, own_rows, wide).transpose(0, 2, 1, 3)
-        return lax.all_gather(
-            values.reshape(mp_size * own_rows, -1), "dp", axis=0, tiled=True
-        )
-
-    out_full = whole_rows(packed[:, :out_end])
-    next_full = whole_rows(packed[:, out_end:next_end])
-    early = packed[:, next_end:early_end].reshape(1, mp_size, 2, own_rows, wide)
-    early = jnp.broadcast_to(early, (dp_size, mp_size, 2, own_rows, wide))
-    weight = lax.all_to_all(early, "dp", split_axis=0, concat_axis=0, tiled=True)
-    weight = weight.reshape(devices, 2, own_rows, wide)
-    own_piece = jnp.sum(packed[:, early_end:].astype(jnp.float32), axis=0).astype(jnp.bfloat16)
-    pieces = [own_piece] + [
-        lax.ppermute(own_piece, "mp", [(j, j ^ s) for j in range(mp_size)]) for s in range(1, 4)
-    ]
-    attended = attend(meta, rows, weight, pieces, head_gains, cosine, sine)
+    attended = attend(meta, rows, weights, pieces, head_gains, cosine, sine)
     attended = lax.all_to_all(
         attended.reshape(mp_size, tok, 2 * hd), "mp", split_axis=0, concat_axis=0, tiled=True
     )

time: 401 us -> 372 us (0.928)
  blocking collectives: 39.1 us -> 17.7 us
  starting transfers between devices: 55.3 us -> 62.4 us
  other arithmetic: 25.4 us -> 18.8 us
  local copies, waits for them, and re-layouts: 43.1 us -> 37.7 us
  Pallas kernels: 26.1 us -> 21.9 us
    all_to_all x1 -> x2, waiting for transfers between devices: 0.01 us -> 25.9 us  [the longest x1 25.9 us: per_device(): lax.all_to_all(packed, 'mp', split_axis=0, concat_axis=0, tiled=True)]
    ppermute x1, waiting for transfers between devices: 34.9 us -> 9.16 us  [per_device(): lax.ppermute(normed, 'mp', [(j, (j + 4) % mp_size) for j in range(mp_size)])]
    all_to_all x1, blocking collectives: 39.1 us -> 17.7 us  [per_device(): late = lax.all_to_all(late, 'mp', split_axis=0, concat_axis=0, tiled=True)]
    unnamed x50 -> x78, local copies, waits for them, and re-layouts: 17.1 us -> 10.4 us
    all_to_all x1 -> x2, starting transfers between devices: 6.79 us -> 11.4 us  [the longest x1 7.07 us: per_device(): early = lax.all_to_all(early, 'dp', split_axis=0, concat_axis=0, tiled=True)]
    pallas_call x1, Pallas kernels: 25.2 us -> 20.9 us  [attend(): pl.pallas_call(attention_kernel, out_shape=jax.ShapeDtypeStruct((group, 2...]
    slice x6 -> x7, local copies, waits for them, and re-layouts: 6.95 us -> 10 us  [the longest x2 3.36 us: per_device(): sides[near][:tok // 2]]
  transfers between devices with their start and end apart: 20 -> 22, of which waited for: 8 -> 10; matrix products, arithmetic and copies ran while one was open for 17% -> 19% of each run, Pallas kernels for 6% -> 6%
where the time goes in v3:
time: 372 us; the launch traced here: 370 us
  waiting for transfers between devices  153 us (41%)
  starting transfers between devices  62.4 us (17%)
  matrix products  42.3 us (11%)
  local copies, waits for them, and re-layouts  37.7 us (10%)
  Pallas kernels  21.9 us (6%)
  other arithmetic  18.8 us (5%)
  blocking collectives  17.7 us (5%)
  between operations  16.1 us (4%)
    all_to_all x4, waiting for transfers between devices, exchange(): return lax.all_to_all(values, BOTH, split_axis=0, concat_axis=0, tiled=True)  103 us
    all_to_all x4, starting transfers between devices, exchange(): return lax.all_to_all(values, BOTH, split_axis=0, concat_axis=0, tiled=True)  27.9 us
    all_to_all x1, waiting for transfers between devices, per_device(): lax.all_to_all(packed, 'mp', split_axis=0, concat_axis=0, tiled=True)  25.9 us
    pallas_call x1, Pallas kernels, attend(): pl.pallas_call(attention_kernel, out_shape=jax.ShapeDtypeStruct((group, 2...  20.9 us
    all_to_all x1, blocking collectives, per_device(): late = lax.all_to_all(late, 'mp', split_axis=0, concat_axis=0, tiled=True)  17.7 us
    dot_general x2, matrix products, expert(): both = jnp.dot(rows, gate_up, preferred_element_type=jnp.float32)  14.9 us
    ppermute x8, starting transfers between devices, shift(): return lax.ppermute(values, 'mp', moves)  13 us
    unnamed x78, local copies, waits for them, and re-layouts  10.4 us
  transfers between devices with their start and end apart: 22, of which 10 were waited for; matrix products, arithmetic and copies ran while one was open for 19% of the time, Pallas kernels for 6%

profile of v3, /device:TPU:0, one launch (start us, length us, event | category | flops | bytes accessed | tf_op | source)
XLA Modules:
  0.0 370.3 jit_solution(14244764728309864166)
XLA Ops:
  8.4 17.7 %all_to_all.40 = bf16[8,16,2560]{2,1,0:T(8,128)(2,1)S(1)} all-to-all(bf16[8,16,2560]{2,1,0:T(8,128)(2,1)S(1)} %broadcast_in_dim.171), channel_id=1, replica_groups=mesh['dp'=16,'mp'=8] {'mp'}, dimensions={0} | all-to-all | bytes 1310720 | tf_op jit(solution)/shard_map/all_to_all | solution.py:377
  32.7 2.5 collective-permute-start.2
  39.7 9.2 %collective-permute-done.across = bf16[128,2048]{1,0:T(8,128)(2,1)S(1)} collective-permute-done((bf16[128,2048]{1,0:T(8,128)(2,1)S(1)}, bf16[128,2048]{1,0:T(8,128)(2,1)S(1)}, u32[]{:S(2)}, u32[]{:S(2)}) %collective-permute-start) | collective-permute-done | bytes 524320 | tf_op jit(solution)/shard_map/ppermute | solution.py:372
  50.5 4.4 %all-to-all-start.1 = ((bf16[8,480,256]{2,1,0:T(8,128)(2,1)}), bf16[8,480,256]{2,1,0:T(8,128)(2,1)}, u32[]{:S(2)}, u32[]{:S(2)}) async-start(bf16[8,480,256]{2,1,0:T(8,128)(2,1)} %copy-done.1), calls=%async_computation.1 | async-start | bytes 3932160 | tf_op jit(solution)/shard_map/all_to_all | solution.py:397
  54.8 1.9 collective-permute-start.3
  56.7 1.4 collective-permute-start.4
  58.7 25.9 %all-to-all-done.1 = bf16[8,480,256]{2,1,0:T(8,128)(2,1)} async-done(((bf16[8,480,256]{2,1,0:T(8,128)(2,1)}), bf16[8,480,256]{2,1,0:T(8,128)(2,1)}, u32[]{:S(2)}, u32[]{:S(2)}) %all-to-all-start.1) | async-done | bytes 1966112 | tf_op jit(solution)/shard_map/all_to_all | solution.py:397
  86.6 7.1 %all-to-all-start.2 = ((bf16[16,8,16,256]{3,2,1,0:T(8,128)(2,1)}), bf16[16,8,16,256]{3,2,1,0:T(8,128)(2,1)}, u32[]{:S(2)}, u32[]{:S(2)}) async-start(bf16[16,8,16,256]{3,2,1,0:T(8,128)(2,1)} %bitcast.100), calls=%async_computation.2 | async-start | bytes 2097152 | tf_op jit(solution)/shard_map/all_to_all | solution.py:405
  94.4 1.8 slice_reduce_fusion.piece_0
  96.1 2.7 collective-permute-start.10
  98.8 2.3 collective-permute-start.11
  101.8 1.7 slice.89
  103.5 2.0 collective-permute-start.5
  105.5 1.7 slice.90
  108.4 1.7 slice.91
  110.0 1.7 slice.92
  113.9 2.4 collective-permute-start.8
  117.3 4.5 %collective-permute-done.7.across_far_top = bf16[64,2048]{1,0:T(8,128)(2,1)} collective-permute-done((bf16[64,2048]{1,0:T(8,128)(2,1)}, bf16[64,2048]{1,0:T(8,128)(2,1)}, u32[]{:S(2)}, u32[]{:S(2)}) %collective-permute-start.7) | collective-permute-done | bytes 262176 | tf_op jit(solution)/shard_map/ppermute | solution.py:370
  126.4 1.3 add_convert_fusion
  127.7 1.9 fusion.43
  130.8 20.9 %tree_attention.1 = bf16[1024,256]{1,0:T(8,128)(2,1)S(1)} custom-call(s32[9]{0:T(128)S(1)} %pad_add_fusion.1.meta, bf16[128,2048]{1,0:T(8,128)(2,1)S(1)} %copy-done.4, bf16[128,2048]{1,0:T(8,128)(2,1)S(1)} %copy-done.9, bf16[128,2048]{1,0:T(8,128)(2,1)S(1)} %copy-done.6, bf16[128,2048]{1,0:T(8,128)(2,1)} %collective-permute-done.2.own_right, ...), custom_call_target="tpu_custom_call" | custom-call | tf_op jit(solution)/shard_map/tree_attention/pallas_call | solution.py:277
  152.5 4.1 %all-to-all-start.3 = ((bf16[8,128,256]{2,1,0:T(8,128)(2,1)}), bf16[8,128,256]{2,1,0:T(8,128)(2,1)}, u32[]{:S(2)}, u32[]{:S(2)}) async-start(bf16[8,128,256]{2,1,0:T(8,128)(2,1)} %bitcast.98), calls=%async_computation.3 | async-start | bytes 1048576 | tf_op jit(solution)/shard_map/all_to_all | solution.py:425
  157.3 9.5 %all-to-all-done.3 = bf16[8,128,256]{2,1,0:T(8,128)(2,1)} async-done(((bf16[8,128,256]{2,1,0:T(8,128)(2,1)}), bf16[8,128,256]{2,1,0:T(8,128)(2,1)}, u32[]{:S(2)}, u32[]{:S(2)}) %all-to-all-start.3) | async-done | bytes 524320 | tf_op jit(solution)/shard_map/all_to_all | solution.py:425
  166.8 5.0 %multiply_reduce_fusion = (f32[128]{0:T(128)S(1)}, f32[128,2048]{1,0:T(8,128)S(1)}) fusion(bf16[8,128,256]{2,1,0:T(8,128)(2,1)} %all-to-all-done.3, bf16[8,256,2048]{2,1,0:T(8,128)(2,1)} %bitcast.99, bf16[128,2048]{1,0:T(8,128)(2,1)} %param.24), kind=kOutput, calls=%fused_computation.40 | convolution fusion | flops 1075314560 | bytes 10486272 | tf_op jit(solution)/shard_map/mtk,mkd->td/dot_general | solution.py:428
  172.8 3.4 convert_bitcast_fusion.1
  176.1 9.5 %all-to-all-start.4 = ((bf16[128,8,2048]{2,1,0:T(8,128)(2,1)}), bf16[128,8,2048]{2,1,0:T(8,128)(2,1)}, u32[]{:S(2)}, u32[]{:S(2)}) async-start(bf16[128,8,2048]{2,1,0:T(8,128)(2,1)} %convert_bitcast_fusion.1), calls=%async_computation.4 | async-start | bytes 8388608 | tf_op jit(solution)/shard_map/all_to_all | solution.py:300
  185.9 2.7 convolution_convert_fusion
  188.6 2.5 reshape.157
  191.1 47.0 %all-to-all-done.4 = bf16[128,8,2048]{2,1,0:T(8,128)(2,1)} async-done(((bf16[128,8,2048]{2,1,0:T(8,128)(2,1)}), bf16[128,8,2048]{2,1,0:T(8,128)(2,1)}, u32[]{:S(2)}, u32[]{:S(2)}) %all-to-all-start.4) | async-done | bytes 4194336 | tf_op jit(solution)/shard_map/all_to_all | solution.py:300
  238.1 5.8 %all-to-all-start.6 = ((bf16[128,2,2048]{2,1,0:T(2,128)(2,1)}), bf16[128,2,2048]{2,1,0:T(2,128)(2,1)}, u32[]{:S(2)}, u32[]{:S(2)}) async-start(bf16[128,2,2048]{2,1,0:T(2,128)(2,1)} %reshape.157), calls=%async_computation.6 | async-start | bytes 2097152 | tf_op jit(solution)/shard_map/all_to_all | solution.py:300
  243.9 10.0 %fusion.2 = f32[1024,1536]{1,0:T(8,128)S(1)} fusion(bf16[1,2048,1536]{2,1,0:T(8,128)(2,1)} %param.30, bf16[128,8,2048]{2,1,0:T(8,128)(2,1)} %all-to-all-done.4), kind=kOutput, calls=%fused_computation.2 | convolution fusion | flops 6442450944 | bytes 16777216 | tf_op jit(solution)/shard_map/dot_general | solution.py:305
  253.9 5.1 %convert_bitcast_fusion = bf16[128,8,2048]{2,1,0:T(8,128)(2,1)} fusion(bf16[1,768,2048]{2,1,0:T(8,128)(2,1)S(1)} %copy-done, f32[1024,1536]{1,0:T(8,128)S(1)} %fusion.2), kind=kOutput, calls=%fused_computation.7 | convolution fusion | flops 3228041216 | bytes 13631488 | tf_op jit(solution)/shard_map/dot_general | solution.py:307
  259.0 3.6 all-to-all-done.6
  262.6 6.6 %all-to-all-start.5 = ((bf16[128,8,2048]{2,1,0:T(8,128)(2,1)}), bf16[128,8,2048]{2,1,0:T(8,128)(2,1)}, u32[]{:S(2)}, u32[]{:S(2)}) async-start(bf16[128,8,2048]{2,1,0:T(8,128)(2,1)} %convert_bitcast_fusion), calls=%async_computation.5 | async-start | bytes 8388608 | tf_op jit(solution)/shard_map/all_to_all | solution.py:300
  269.3 1.6 slice.124
  271.6 1.7 fusion.52
  273.3 2.2 reshape.160
  275.5 4.9 %fusion = f32[256,1536]{1,0:T(8,128)S(1)} fusion(bf16[256,2048]{1,0:T(8,128)(2,1)} %reshape.160, bf16[1,2048,1536]{2,1,0:T(8,128)(2,1)} %param.30), kind=kOutput, calls=%fused_computation | convolution fusion | flops 1610612736 | bytes 8912896 | tf_op jit(solution)/shard_map/dot_general | solution.py:305
  280.4 2.0 fusion.11
  282.4 2.6 reshape.161
  285.0 38.8 %all-to-all-done.5 = bf16[128,8,2048]{2,1,0:T(8,128)(2,1)} async-done(((bf16[128,8,2048]{2,1,0:T(8,128)(2,1)}), bf16[128,8,2048]{2,1,0:T(8,128)(2,1)}, u32[]{:S(2)}, u32[]{:S(2)}) %all-to-all-start.5) | async-done | bytes 4194336 | tf_op jit(solution)/shard_map/all_to_all | solution.py:300
  323.8 6.0 %all-to-all-start.7 = ((bf16[128,2,2048]{2,1,0:T(2,128)(2,1)}), bf16[128,2,2048]{2,1,0:T(2,128)(2,1)}, u32[]{:S(2)}, u32[]{:S(2)}) async-start(bf16[128,2,2048]{2,1,0:T(2,128)(2,1)} %reshape.161), calls=%async_computation.7 | async-start | bytes 2097152 | tf_op jit(solution)/shard_map/all_to_all | solution.py:300
  330.3 4.9 %fusion.4 = f32[256,2048]{1,0:T(8,128)} fusion(bf16[128,8,2048]{2,1,0:T(8,128)(2,1)} %all-to-all-done.5, bf16[128,1024]{0,1:T(8,128)(2,1)S(1)} %get-tuple-element.55, bf16[128,1024]{0,1:T(8,128)(2,1)S(1)} %get-tuple-element.54), kind=kOutput, calls=%fused_computation.4 | convolution fusion | flops 1074790400 | bytes 6815744 | tf_op jit(solution)/shard_map/dot_general | solution.py:464
  335.1 13.5 %all-to-all-done.7 = bf16[128,2,2048]{2,1,0:T(2,128)(2,1)} async-done(((bf16[128,2,2048]{2,1,0:T(2,128)(2,1)}), bf16[128,2,2048]{2,1,0:T(2,128)(2,1)}, u32[]{:S(2)}, u32[]{:S(2)}) %all-to-all-start.7) | async-done | bytes 1048608 | tf_op jit(solution)/shard_map/all_to_all | solution.py:300
  348.7 2.3 reshape.163
  351.0 1.8 fusion.47
  354.5 2.3 fusion.31
  361.9 1.5 pad_maximum_fusion.2
  (161 shorter events, 36.7 us)
Async XLA Ops:
  7.2 246.7 %copy-start = (bf16[1,768,2048]{2,1,0:T(8,128)(2,1)S(1)}, bf16[1,768,2048]{2,1,0:T(8,128)(2,1)}, u32[]{:S(2)}) copy-start(bf16[1,768,2048]{2,1,0:T(8,128)(2,1)} %param.31) | copy-start | bytes 9437188
  7.2 28.1 %copy-start.16 = (bf16[16,2048]{1,0:T(8,128)(2,1)S(1)}, bf16[16,2048]{1,0:T(8,128)(2,1)}, u32[]{:S(2)}) copy-start(bf16[16,2048]{1,0:T(8,128)(2,1)} %query.1) | copy-start | bytes 196612
  7.2 28.1 %copy-start.17 = (bf16[16,512]{1,0:T(8,128)(2,1)S(1)}, bf16[16,512]{1,0:T(8,128)(2,1)}, u32[]{:S(2)}) copy-start(bf16[16,512]{1,0:T(8,128)(2,1)} %kv.1) | copy-start | bytes 49156
  7.2 28.0 %copy-start.18 = (s32[1024]{0:T(1024)S(1)}, s32[1024]{0:T(1024)}, u32[]{:S(2)}) copy-start(s32[1024]{0:T(1024)} %token_request.1) | copy-start | bytes 12292
  7.2 28.0 %copy-start.25 = (s32[32]{0:T(128)S(1)}, s32[32]{0:T(128)}, u32[]{:S(2)}) copy-start(s32[32]{0:T(128)} %request_leaf.1) | copy-start | bytes 388
  7.2 28.0 %copy-start.20 = (s32[16]{0:T(128)S(1)}, s32[16]{0:T(128)}, u32[]{:S(2)}) copy-start(s32[16]{0:T(128)} %leaf_parent.1) | copy-start | bytes 196
  7.2 28.0 %copy-start.21 = (s32[8]{0:T(128)S(1)}, s32[8]{0:T(128)}, u32[]{:S(2)}) copy-start(s32[8]{0:T(128)} %mid_parent.1) | copy-start | bytes 100
  7.2 28.0 %copy-start.22 = (s32[8]{0:T(128)S(1)}, s32[8]{0:T(128)}, u32[]{:S(2)}) copy-start(s32[8]{0:T(128)} %root_slot.1) | copy-start | bytes 100
  7.3 28.0 %copy-start.23 = (s32[8]{0:T(128)S(1)}, s32[8]{0:T(128)}, u32[]{:S(2)}) copy-start(s32[8]{0:T(128)} %mid_slot.1) | copy-start | bytes 100
  7.3 28.0 %copy-start.24 = (s32[16]{0:T(128)S(1)}, s32[16]{0:T(128)}, u32[]{:S(2)}) copy-start(s32[16]{0:T(128)} %leaf_slot.1) | copy-start | bytes 196
  7.3 28.0 %copy-start.10 = (bf16[1,256,512]{2,1,0:T(8,128)(2,1)S(1)}, bf16[1,256,512]{2,1,0:T(8,128)(2,1)}, u32[]{:S(2)}) copy-start(bf16[1,256,512]{2,1,0:T(8,128)(2,1)} %mid.1) | copy-start | bytes 786436
  7.3 159.5 %all-gather.3.cloned.1.call-start = ((), (), s32[]{:S(2)}) async-start(), calls=%async_computation.8 | async-start | bytes 8912896 | tf_op jit(solution)/shard_map/all_gather | solution.py:379
  31.3 7.1 %copy-start.3 = (bf16[128,2048]{1,0:T(8,128)(2,1)}, bf16[128,2048]{1,0:T(8,128)(2,1)S(1)}, u32[]{:S(2)}) copy-start(bf16[128,2048]{1,0:T(8,128)(2,1)S(1)} %fusion.25.own) | copy-start | bytes 1572868
  31.3 17.5 %collective-permute-start = (bf16[128,2048]{1,0:T(8,128)(2,1)S(1)}, bf16[128,2048]{1,0:T(8,128)(2,1)S(1)}, u32[]{:S(2)}, u32[]{:S(2)}) collective-permute-start(bf16[128,2048]{1,0:T(8,128)(2,1)S(1)} %fusion.25.own), channel_id=1, source_target_pairs={{0,4},{1,5},{2,6},{3,7},{4,0},{5,1},{6,2},{7,3},{8,12},{9,13},{10,... | collective-permute-start | bytes 1572872 | tf_op jit(solution)/shard_map/ppermute | solution.py:372
  32.0 16.8 %collective-permute-start.1 = (bf16[128,2048]{1,0:T(8,128)(2,1)S(1)}, bf16[128,2048]{1,0:T(8,128)(2,1)S(1)}, u32[]{:S(2)}, u32[]{:S(2)}) collective-permute-start(bf16[128,2048]{1,0:T(8,128)(2,1)S(1)} %fusion.25.own), channel_id=1, source_target_pairs={{0,1},{1,2},{2,3},{3,0},{4,5},{5,6},{6,7},{7,4},{8,9},{9,10},{10,1... | collective-permute-start | bytes 1572872 | tf_op jit(solution)/shard_map/ppermute | solution.py:370
  32.7 17.7 %collective-permute-start.2 = (bf16[128,2048]{1,0:T(8,128)(2,1)S(1)}, bf16[128,2048]{1,0:T(8,128)(2,1)}, u32[]{:S(2)}, u32[]{:S(2)}) collective-permute-start(bf16[128,2048]{1,0:T(8,128)(2,1)S(1)} %fusion.25.own), channel_id=1, source_target_pairs={{0,3},{1,0},{2,1},{3,2},{4,7},{5,4},{6,5},{7,6},{8,11},{9,8},{10,9... | collective-permute-start | bytes 1572872 | tf_op jit(solution)/shard_map/ppermute | solution.py:370
  38.4 1.3 copy-start.1
  50.5 34.1 %all-to-all-start.1 = ((bf16[8,480,256]{2,1,0:T(8,128)(2,1)}), bf16[8,480,256]{2,1,0:T(8,128)(2,1)}, u32[]{:S(2)}, u32[]{:S(2)}) async-start(bf16[8,480,256]{2,1,0:T(8,128)(2,1)} %copy-done.1), calls=%async_computation.1 | async-start | bytes 3932160 | tf_op jit(solution)/shard_map/all_to_all | solution.py:397
  54.8 46.5 %copy-start.35 = (s32[16]{0:T(128)S(1)}, s32[16]{0:T(128)}, u32[]{:S(2)}) copy-start(s32[16]{0:T(128)} %param.41) | copy-start | bytes 196
  54.8 46.7 %copy-start.36 = (s32[8]{0:T(128)S(1)}, s32[8]{0:T(128)}, u32[]{:S(2)}) copy-start(s32[8]{0:T(128)} %param.40) | copy-start | bytes 100
  54.8 30.6 %collective-permute-start.3 = (bf16[128,2048]{1,0:T(8,128)(2,1)}, bf16[128,2048]{1,0:T(8,128)(2,1)}, u32[]{:S(2)}, u32[]{:S(2)}) collective-permute-start(bf16[128,2048]{1,0:T(8,128)(2,1)} %copy-done.8), channel_id=1, source_target_pairs={{0,1},{1,2},{2,3},{3,0},{4,5},{5,6},{6,7},{7,4},{8,9},{9,10},{10,1... | collective-permute-start | bytes 1572872 | tf_op jit(solution)/shard_map/ppermute | solution.py:370
  56.7 28.8 %collective-permute-start.4 = (bf16[128,2048]{1,0:T(8,128)(2,1)}, bf16[128,2048]{1,0:T(8,128)(2,1)}, u32[]{:S(2)}, u32[]{:S(2)}) collective-permute-start(bf16[128,2048]{1,0:T(8,128)(2,1)} %copy-done.8), channel_id=1, source_target_pairs={{0,3},{1,0},{2,1},{3,2},{4,7},{5,4},{6,5},{7,6},{8,11},{9,8},{10,9... | collective-permute-start | bytes 1572872 | tf_op jit(solution)/shard_map/ppermute | solution.py:370
  86.6 29.7 %copy-start.37 = (s32[8]{0:T(128)S(1)}, s32[8]{0:T(128)}, u32[]{:S(2)}) copy-start(s32[8]{0:T(128)} %param.39) | copy-start | bytes 100
  86.6 36.0 %copy-start.33 = (s32[128,8]{0,1:T(8,128)S(1)}, s32[128,8]{0,1:T(8,128)}, u32[]{:S(2)}) copy-start(s32[128,8]{0,1:T(8,128)} %param.33) | copy-start | bytes 12292
  86.6 35.8 %all-to-all-start.2 = ((bf16[16,8,16,256]{3,2,1,0:T(8,128)(2,1)}), bf16[16,8,16,256]{3,2,1,0:T(8,128)(2,1)}, u32[]{:S(2)}, u32[]{:S(2)}) async-start(bf16[16,8,16,256]{3,2,1,0:T(8,128)(2,1)} %bitcast.100), calls=%async_computation.2 | async-start | bytes 2097152 | tf_op jit(solution)/shard_map/all_to_all | solution.py:405
  96.1 15.6 %collective-permute-start.10 = (bf16[448,256]{1,0:T(8,128)(2,1)S(1)}, bf16[448,256]{1,0:T(8,128)(2,1)S(1)}, u32[]{:S(2)}, u32[]{:S(2)}) collective-permute-start(bf16[448,256]{1,0:T(8,128)(2,1)S(1)} %slice_reduce_fusion.piece_0), channel_id=1, source_target_pairs={{0,2},{1,3},{2,0},{3,1},{4,6},{5,7},{6,4},{7,5},{8,10},{9,11},{10,... | collective-permute-start | bytes 688136 | tf_op jit(solution)/shard_map/ppermute | solution.py:411
  98.8 14.4 %collective-permute-start.11 = (bf16[448,256]{1,0:T(8,128)(2,1)S(1)}, bf16[448,256]{1,0:T(8,128)(2,1)S(1)}, u32[]{:S(2)}, u32[]{:S(2)}) collective-permute-start(bf16[448,256]{1,0:T(8,128)(2,1)S(1)} %slice_reduce_fusion.piece_0), channel_id=1, source_target_pairs={{0,3},{1,2},{2,1},{3,0},{4,7},{5,6},{6,5},{7,4},{8,11},{9,10},{10,... | collective-permute-start | bytes 688136 | tf_op jit(solution)/shard_map/ppermute | solution.py:411
  101.7 29.1 %copy-start.19 = (f32[3,128]{1,0:T(4,128)S(1)}, f32[3,128]{1,0:T(4,128)}, u32[]{:S(2)}) copy-start(f32[3,128]{1,0:T(4,128)} %gains.1) | copy-start | bytes 4612
  101.7 14.8 %collective-permute-start.9 = (bf16[448,256]{1,0:T(8,128)(2,1)S(1)}, bf16[448,256]{1,0:T(8,128)(2,1)}, u32[]{:S(2)}, u32[]{:S(2)}) collective-permute-start(bf16[448,256]{1,0:T(8,128)(2,1)S(1)} %slice_reduce_fusion.piece_0), channel_id=1, source_target_pairs={{0,1},{1,0},{2,3},{3,2},{4,5},{5,4},{6,7},{7,6},{8,9},{9,8},{10,11... | collective-permute-start | bytes 688136 | tf_op jit(solution)/shard_map/ppermute | solution.py:411
  103.5 13.1 %collective-permute-start.5 = (bf16[64,2048]{1,0:T(8,128)(2,1)}, bf16[64,2048]{1,0:T(8,128)(2,1)}, u32[]{:S(2)}, u32[]{:S(2)}) collective-permute-start(bf16[64,2048]{1,0:T(8,128)(2,1)} %slice.89), channel_id=1, source_target_pairs={{0,1},{1,2},{2,3},{3,0},{4,5},{5,6},{6,7},{7,4},{8,9},{9,10},{10,1... | collective-permute-start | bytes 786440 | tf_op jit(solution)/shard_map/ppermute | solution.py:370
  107.1 10.2 %collective-permute-start.6 = (bf16[64,2048]{1,0:T(8,128)(2,1)}, bf16[64,2048]{1,0:T(8,128)(2,1)}, u32[]{:S(2)}, u32[]{:S(2)}) collective-permute-start(bf16[64,2048]{1,0:T(8,128)(2,1)} %slice.90), channel_id=1, source_target_pairs={{0,3},{1,0},{2,1},{3,2},{4,7},{5,4},{6,5},{7,6},{8,11},{9,8},{10,9... | collective-permute-start | bytes 786440 | tf_op jit(solution)/shard_map/ppermute | solution.py:370
  112.4 9.4 %collective-permute-start.7 = (bf16[64,2048]{1,0:T(8,128)(2,1)}, bf16[64,2048]{1,0:T(8,128)(2,1)}, u32[]{:S(2)}, u32[]{:S(2)}) collective-permute-start(bf16[64,2048]{1,0:T(8,128)(2,1)} %slice.91), channel_id=1, source_target_pairs={{0,1},{1,2},{2,3},{3,0},{4,5},{5,6},{6,7},{7,4},{8,9},{9,10},{10,1... | collective-permute-start | bytes 786440 | tf_op jit(solution)/shard_map/ppermute | solution.py:370
  113.9 8.5 %collective-permute-start.8 = (bf16[64,2048]{1,0:T(8,128)(2,1)}, bf16[64,2048]{1,0:T(8,128)(2,1)}, u32[]{:S(2)}, u32[]{:S(2)}) collective-permute-start(bf16[64,2048]{1,0:T(8,128)(2,1)} %slice.92), channel_id=1, source_target_pairs={{0,3},{1,0},{2,1},{3,2},{4,7},{5,4},{6,5},{7,6},{8,11},{9,8},{10,9... | collective-permute-start | bytes 786440 | tf_op jit(solution)/shard_map/ppermute | solution.py:370
  122.4 7.6 %collective-permute-start.12 = (bf16[128,16,256]{2,1,0:T(8,128)(2,1)}, bf16[128,16,256]{2,1,0:T(8,128)(2,1)}, u32[]{:S(2)}, u32[]{:S(2)}) collective-permute-start(bf16[128,16,256]{2,1,0:T(8,128)(2,1)} %bitcast.13.weight_own), channel_id=1, source_target_pairs={{0,8},{8,0},{16,24},{24,16},{32,40},{40,32},{48,56},{56,48},{64,72... | collective-permute-start | bytes 3145736 | tf_op jit(solution)/shard_map/ppermute | solution.py:415
  125.5 5.3 %copy-start.4 = (bf16[128,2048]{1,0:T(8,128)(2,1)S(1)}, bf16[128,2048]{1,0:T(8,128)(2,1)}, u32[]{:S(2)}) copy-start(bf16[128,2048]{1,0:T(8,128)(2,1)} %copy-done.3) | copy-start | bytes 1572868
  125.5 5.3 %copy-start.6 = (bf16[128,2048]{1,0:T(8,128)(2,1)S(1)}, bf16[128,2048]{1,0:T(8,128)(2,1)}, u32[]{:S(2)}) copy-start(bf16[128,2048]{1,0:T(8,128)(2,1)} %copy-done.5) | copy-start | bytes 1572868
  125.5 5.3 %copy-start.9 = (bf16[128,2048]{1,0:T(8,128)(2,1)S(1)}, bf16[128,2048]{1,0:T(8,128)(2,1)}, u32[]{:S(2)}) copy-start(bf16[128,2048]{1,0:T(8,128)(2,1)} %copy-done.8) | copy-start | bytes 1572868
  125.5 5.3 %copy-start.13 = (bf16[448,256]{1,0:T(8,128)(2,1)S(1)}, bf16[448,256]{1,0:T(8,128)(2,1)}, u32[]{:S(2)}) copy-start(bf16[448,256]{1,0:T(8,128)(2,1)} %copy-done.12) | copy-start | bytes 688132
  125.5 5.3 %copy-start.15 = (bf16[448,256]{1,0:T(8,128)(2,1)S(1)}, bf16[448,256]{1,0:T(8,128)(2,1)}, u32[]{:S(2)}) copy-start(bf16[448,256]{1,0:T(8,128)(2,1)} %copy-done.14) | copy-start | bytes 688132
  152.5 14.3 %all-to-all-start.3 = ((bf16[8,128,256]{2,1,0:T(8,128)(2,1)}), bf16[8,128,256]{2,1,0:T(8,128)(2,1)}, u32[]{:S(2)}, u32[]{:S(2)}) async-start(bf16[8,128,256]{2,1,0:T(8,128)(2,1)} %bitcast.98), calls=%async_computation.3 | async-start | bytes 1048576 | tf_op jit(solution)/shard_map/all_to_all | solution.py:425
  176.1 62.0 %all-to-all-start.4 = ((bf16[128,8,2048]{2,1,0:T(8,128)(2,1)}), bf16[128,8,2048]{2,1,0:T(8,128)(2,1)}, u32[]{:S(2)}, u32[]{:S(2)}) async-start(bf16[128,8,2048]{2,1,0:T(8,128)(2,1)} %convert_bitcast_fusion.1), calls=%async_computation.4 | async-start | bytes 8388608 | tf_op jit(solution)/shard_map/all_to_all | solution.py:300
  238.1 24.5 %all-to-all-start.6 = ((bf16[128,2,2048]{2,1,0:T(2,128)(2,1)}), bf16[128,2,2048]{2,1,0:T(2,128)(2,1)}, u32[]{:S(2)}, u32[]{:S(2)}) async-start(bf16[128,2,2048]{2,1,0:T(2,128)(2,1)} %reshape.157), calls=%async_computation.6 | async-start | bytes 2097152 | tf_op jit(solution)/shard_map/all_to_all | solution.py:300
  259.0 12.0 %copy-start.34 = (f32[128,8]{0,1:T(8,128)S(1)}, f32[128,8]{0,1:T(8,128)}, u32[]{:S(2)}) copy-start(f32[128,8]{0,1:T(8,128)} %param.34) | copy-start | bytes 12292
  262.6 61.2 %all-to-all-start.5 = ((bf16[128,8,2048]{2,1,0:T(8,128)(2,1)}), bf16[128,8,2048]{2,1,0:T(8,128)(2,1)}, u32[]{:S(2)}, u32[]{:S(2)}) async-start(bf16[128,8,2048]{2,1,0:T(8,128)(2,1)} %convert_bitcast_fusion), calls=%async_computation.5 | async-start | bytes 8388608 | tf_op jit(solution)/shard_map/all_to_all | solution.py:300
  269.3 85.3 %all-gather.5.cloned.1.call-start = ((), (), s32[]{:S(2)}) async-start(), calls=%async_computation.9 | async-start | bytes 2228224 | tf_op jit(solution)/shard_map/all_gather | solution.py:380
  323.8 24.8 %all-to-all-start.7 = ((bf16[128,2,2048]{2,1,0:T(2,128)(2,1)}), bf16[128,2,2048]{2,1,0:T(2,128)(2,1)}, u32[]{:S(2)}, u32[]{:S(2)}) async-start(bf16[128,2,2048]{2,1,0:T(2,128)(2,1)} %reshape.161), calls=%async_computation.7 | async-start | bytes 2097152 | tf_op jit(solution)/shard_map/all_to_all | solution.py:300
  351.0 1.8 copy-start.27
  351.0 2.2 copy-start.32
  (12 other events, 10.6 us)
Sparse Core Ops, SparseCore 0:
  28.0 87.2 all-gather.2
  273.1 65.5 all-gather.4

commit v4 on v3

--- a/solution.py
+++ b/solution.py
@@ -23,7 +23,39 @@
     return jnp.sum(jnp.where(indices[:, None] == places[None, :], lookup_table[None, :], 0), axis=1)
 
 
-def pack_kernel(
+def pack_weights_kernel(query, kv, out_rows, next_rows, packed):
+    count = packed.shape[0]
+    dim = out_rows.shape[1]
+    extra = next_rows.shape[1]
+    wide = query.shape[1] // count
+    hd = wide // 2
+    heads = kv.shape[1] // 2 // hd
+    base = dim + extra
+    for dest in range(count):
+        head = dest * heads // count
+        packed[dest, :, 0:dim] = out_rows[...]
+        packed[dest, :, dim:base] = next_rows[...]
+        packed[dest, :, base : base + wide] = query[:, dest * wide : (dest + 1) * wide]
+        for half in range(2):
+            source = (half * heads + head) * hd
+            target = base + wide + half * hd
+            packed[dest, :, target : target + hd] = kv[:, source : source + hd]
+
+
+def pack_weights(query, kv, out_rows, next_rows, count):
+    rows = query.shape[0]
+    width = out_rows.shape[1] + next_rows.shape[1] + 2 * (query.shape[1] // count)
+    in_vmem = pl.BlockSpec(memory_space=pltpu.VMEM)
+    return pl.pallas_call(
+        pack_weights_kernel,
+        out_shape=jax.ShapeDtypeStruct((count, rows, width), jnp.bfloat16),
+        in_specs=[in_vmem] * 4,
+        out_specs=in_vmem,
+        name="pack_weights",
+    )(query, kv, out_rows, next_rows)
+
+
+def pack_paths_kernel(
     token_request,
     request_leaf,
     leaf_parent,
@@ -31,27 +63,14 @@
     root_slot,
     mid_slot,
     leaf_slot,
-    query,
-    kv,
     root,
     mid,
     leaf,
     packed,
 ):
-    count, _, wide = packed.shape
-    own_rows = query.shape[0]
+    count, part, wide = packed.shape
     hd = wide // 2
-    heads = kv.shape[1] // wide
-    for dest in range(count):
-        head = dest * heads // count
-        packed[dest, 0:own_rows, :] = query[:, dest * wide : (dest + 1) * wide]
-        for half in range(2):
-            source = (half * heads + head) * hd
-            packed[dest, own_rows : 2 * own_rows, half * hd : (half + 1) * hd] = kv[
-                :, source : source + hd
-            ]
-    begin = 2 * own_rows
-    part = packed.shape[1] - begin
+    heads = count // 4
     me = lax.axis_index("mp")
     for req in range(2):
         leaf_node = request_leaf[token_request[0] + req]
@@ -71,25 +90,25 @@
                 source = slice((half * heads + head) * hd, (half * heads + head + 1) * hd)
                 target = slice(half * hd, (half + 1) * hd)
                 place = 4 * head + 2 * req
-                packed[place, begin:, target] = levels[0][:part, source]
-                packed[place + 1, begin : begin + top, target] = levels[0][part:, source]
-                packed[place + 1, begin + top : begin + top + middle, target] = levels[1][:, source]
-                packed[place + 1, begin + top + middle :, target] = levels[2][:, source]
-
-
-def pack(tables, query, kv, root, mid, leaf, count):
-    wide = query.shape[1] // count
+                packed[place, :, target] = levels[0][:part, source]
+                packed[place + 1, 0:top, target] = levels[0][part:, source]
+                packed[place + 1, top : top + middle, target] = levels[1][:, source]
+                packed[place + 1, top + middle :, target] = levels[2][:, source]
+
+
+def pack_paths(tables, root, mid, leaf, count):
+    wide = root.shape[2] // 2
     part = (root.shape[1] + mid.shape[1] + leaf.shape[1]) // 2
     in_vmem = pl.BlockSpec(memory_space=pltpu.VMEM)
     in_smem = pl.BlockSpec(memory_space=pltpu.SMEM)
     return pl.pallas_call(
-        pack_kernel,
-        out_shape=jax.ShapeDtypeStruct((count, 2 * query.shape[0] + part, wide), jnp.bfloat16),
-        in_specs=[in_smem] * len(tables) + [in_vmem] * 5,
+        pack_paths_kernel,
+        out_shape=jax.ShapeDtypeStruct((count, part, wide), jnp.bfloat16),
+        in_specs=[in_smem] * len(tables) + [in_vmem] * 3,
         out_specs=in_vmem,
         compiler_params=pltpu.CompilerParams(vmem_limit_bytes=24 * 1024 * 1024),
-        name="pack",
-    )(*tables, query, kv, root, mid, leaf)
+        name="pack_paths",
+    )(*tables, root, mid, leaf)
 
 
 def attention_kernel(
@@ -100,10 +119,8 @@
     own_right,
     across_left,
     across_right,
-    own_far_top,
-    own_far_bottom,
-    across_far_top,
-    across_far_bottom,
+    own_far,
+    across_far,
     weight_own,
     weight_other,
     piece_0,
@@ -137,10 +154,9 @@
     base = me - ring
     far_base = 4 - base
 
-    def put(first, step, block, offset=0):
-        at = (first + lax.rem(ring + step, 4)) * tok + offset
-        at = pl.multiple_of(at, block.shape[0])
-        rows_all[pl.ds(at, block.shape[0]), :] = block[...]
+    def put(first, step, block):
+        at = pl.multiple_of((first + lax.rem(ring + step, 4)) * tok, tok)
+        rows_all[pl.ds(at, tok), :] = block[...]
 
     put(base, 0, own)
     put(far_base, 0, across)
@@ -148,17 +164,15 @@
     put(base, 1, own_right)
     put(far_base, 3, across_left)
     put(far_base, 1, across_right)
-    put(base, 2, own_far_top)
-    put(base, 2, own_far_bottom, tok // 2)
-    put(far_base, 2, across_far_top)
-    put(far_base, 2, across_far_bottom, tok // 2)
+    put(base, 2, own_far)
+    put(far_base, 2, across_far)
     for step, piece in enumerate(pieces):
         place = pl.multiple_of((ring ^ step) * part, part)
         pk_all[pl.ds(place, part), :] = piece[:, :hd]
         pv_all[pl.ds(place, part), :] = piece[:, hd:]
     core = meta[8]
-    weights[core] = weight_own[...].reshape(dim, 2 * hd)
-    weights[1 - core] = weight_other[...].reshape(dim, 2 * hd)
+    weights[core] = weight_own[...]
+    weights[1 - core] = weight_other[...]
     weight_q = weights[0]
     weight_kv = weights[1]
 
@@ -277,7 +291,7 @@
     return pl.pallas_call(
         attention_kernel,
         out_shape=jax.ShapeDtypeStruct((group, 2 * hd), jnp.bfloat16),
-        in_specs=[pl.BlockSpec(memory_space=pltpu.SMEM)] + [in_vmem] * 19,
+        in_specs=[pl.BlockSpec(memory_space=pltpu.SMEM)] + [in_vmem] * 17,
         out_specs=in_vmem,
         scratch_shapes=[
             pltpu.VMEM((group, rows[0].shape[1]), jnp.bfloat16),
@@ -296,6 +310,60 @@
     )(meta, *rows, *weights, *pieces, gains, cosine, sine)
 
 
+def project_kernel(attended, weight, hidden, gain, out, normed, joined, layer):
+    count, _, wide = attended.shape
+    step = pl.program_id(0)
+
+    @pl.when(step == 0)
+    def _():
+        for source in range(count):
+            joined[:, source * wide : (source + 1) * wide] = attended[source]
+
+    added = jnp.dot(joined[...], weight[...], preferred_element_type=jnp.float32)
+    done = (hidden[...].astype(jnp.float32) + added).astype(jnp.bfloat16)
+    out[...] = done
+    layer[step] = done
+
+    @pl.when(step == layer.shape[0] - 1)
+    def _():
+        columns = layer.shape[2]
+        parts = [layer[at].astype(jnp.float32) for at in range(layer.shape[0])]
+        square = sum(jnp.sum(part * part, axis=1, keepdims=True) for part in parts)
+        inverse = lax.rsqrt(square / (columns * len(parts)) + EPS)
+        for at, part in enumerate(parts):
+            place = slice(at * columns, (at + 1) * columns)
+            normed[:, place] = (part * inverse * gain[:, place]).astype(jnp.bfloat16)
+
+
+def project(attended, weight, hidden, gain):
+    tok, dim = hidden.shape
+    columns = dim // 4
+    return pl.pallas_call(
+        project_kernel,
+        grid=(4,),
+        out_shape=(
+            jax.ShapeDtypeStruct(hidden.shape, hidden.dtype),
+            jax.ShapeDtypeStruct(hidden.shape, hidden.dtype),
+        ),
+        in_specs=[
+            pl.BlockSpec(attended.shape, lambda j: (0, 0, 0)),
+            pl.BlockSpec((dim, columns), lambda j: (0, j)),
+            pl.BlockSpec((tok, columns), lambda j: (0, j)),
+            pl.BlockSpec((1, dim), lambda j: (0, 0)),
+        ],
+        out_specs=(
+            pl.BlockSpec((tok, columns), lambda j: (0, j)),
+            pl.BlockSpec((tok, dim), lambda j: (0, 0)),
+        ),
+        scratch_shapes=[
+            pltpu.VMEM((tok, dim), jnp.bfloat16),
+            pltpu.VMEM((4, tok, columns), jnp.bfloat16),
+        ],
+        compiler_params=pltpu.CompilerParams(vmem_limit_bytes=24 * 1024 * 1024),
+        name="project",
+    )(attended, weight, hidden, gain)
+
+
 def exchange(values):
     return lax.all_to_all(values, BOTH, split_axis=0, concat_axis=0, tiled=True)
 
@@ -305,6 +373,148 @@
     both = jnp.dot(rows, gate_up, preferred_element_type=jnp.float32)
     active = (jax.nn.silu(both[:, :ff_width]) * both[:, ff_width:]).astype(jnp.bfloat16)
     return jnp.dot(active, down_weight, preferred_element_type=jnp.float32).astype(jnp.bfloat16)
+
+
+def rest_kernel(rows, gate_up, down_weight, main_block, out):
+    del main_block
+    ff_width = down_weight.shape[0]
+    spans = out.shape[0]
+    wide = out.shape[2]
+    chunks = down_weight.shape[1] // wide
+    per = rows.shape[0] // spans
+    both = jnp.dot(rows[...], gate_up[...], preferred_element_type=jnp.float32)
+    gate = both[:, :ff_width]
+    active = (gate / (1.0 + jnp.exp(-gate)) * both[:, ff_width:]).astype(jnp.bfloat16)
+    served = jnp.dot(active, down_weight[...], preferred_element_type=jnp.float32)
+    served = served.astype(jnp.bfloat16)
+    batch = 16
+    size = batch * per * chunks
+    to = lax.broadcasted_iota(jnp.int32, (size, size), 0)
+    source = lax.broadcasted_iota(jnp.int32, (size, size), 1)
+    device = to // (per * chunks)
+    chunk = to // per % chunks
+    wanted = chunk * (batch * per) + device * per + to % per
+    order = (source == wanted).astype(jnp.bfloat16)
+    for first in range(0, spans, batch):
+        stacked = jnp.concatenate(
+            [
+                served[first * per : (first + batch) * per, at * wide : (at + 1) * wide]
+                for at in range(chunks)
+            ],
+            axis=0,
+        )
+        sorted_rows = jnp.dot(order, stacked, preferred_element_type=jnp.float32)
+        out[first : first + batch] = sorted_rows.reshape(batch, per * chunks, wide).astype(
+            jnp.bfloat16
+        )
+
+
+def expert_rest(rows, gate_up, down_weight, main_block):
+    spans, height, wide = main_block.shape
+    extra = rows.shape[0] // spans * down_weight.shape[1] // wide
+    in_vmem = pl.BlockSpec(memory_space=pltpu.VMEM)
+    return pl.pallas_call(
+        rest_kernel,
+        grid=(1,),
+        out_shape=jax.ShapeDtypeStruct(main_block.shape, main_block.dtype),
+        in_specs=[in_vmem, in_vmem, in_vmem, pl.BlockSpec(memory_space=pl.ANY)],
+        out_specs=pl.BlockSpec((spans, extra, wide), lambda i: (0, height // extra - 1, 0)),
+        input_output_aliases={3: 0},
+        compiler_params=pltpu.CompilerParams(vmem_limit_bytes=48 * 1024 * 1024),
+        name="expert_rest",
+    )(rows, gate_up, down_weight, main_block)
+
+
+def finish_kernel(
+    main_share,
+    rest_share,
+    main_rows,
+    rest_rows,
+    stream,
+    next_weight,
+    norm_gain,
+    head_gain,
+    cosine,
+    sine,
+    out,
+    next_rows,
+    layer,
+):
+    tok = stream.shape[0]
+    count = main_share.shape[1]
+    wide = main_rows.shape[2]
+    hd = head_gain.shape[1]
+    step = pl.program_id(0)
+
+    def flat(values):
+        values = values[...].astype(jnp.float32).reshape(count, wide)
+        return values.astype(jnp.bfloat16)
+
+    total = jnp.dot(main_share[...], flat(main_rows), preferred_element_type=jnp.float32)
+    total += jnp.dot(rest_share[0], flat(rest_rows), preferred_element_type=jnp.float32)
+    done = (stream[...].astype(jnp.float32) + total[:tok] + total[tok:]).astype(jnp.bfloat16)
+    out[...] = done
+    layer[step] = done
+
+    @pl.when(step == layer.shape[0] - 1)
+    def _():
+        parts = [layer[at].astype(jnp.float32) for at in range(layer.shape[0])]
+        square = sum(jnp.sum(part * part, axis=1, keepdims=True) for part in parts)
+        inverse = lax.rsqrt(square / (wide * len(parts)) + EPS)
+        raw = jnp.zeros((tok, next_weight.shape[1]), jnp.float32)
+        for at, part in enumerate(parts):
+            columns = slice(at * wide, (at + 1) * wide)
+            normed = (part * inverse * norm_gain[:, columns]).astype(jnp.bfloat16)
+            raw += jnp.dot(normed, next_weight[columns, :], preferred_element_type=jnp.float32)
+        half = raw.shape[1] // 2
+        for head in range(half // hd):
+            columns = slice(head * hd, (head + 1) * hd)
+            values = raw[:, columns]
+            values = values * lax.rsqrt(jnp.mean(values * values, axis=-1, keepdims=True) + EPS)
+            values = values * head_gain[...]
+            values = values * cosine[...] + pltpu.roll(values, hd // 2, 1) * sine[...]
+            next_rows[:, columns] = values.astype(jnp.bfloat16)
+        next_rows[:, half:] = raw[:, half:].astype(jnp.bfloat16)
+
+
+def finish(main_share, rest_share, returned, stream, late, norm_gain, head_gain, cos, sin):
+    devices, height, wide = returned.shape
+    tok, dim = stream.shape
+    extra = late.shape[1] - dim
+    chunks = dim // wide
+    rows = height // (chunks + 1)
+    shape = main_share.shape
+
+    def fixed(values):
+        return pl.BlockSpec(values.shape, lambda j: (0, 0))
+
+    return pl.pallas_call(
+        finish_kernel,
+        grid=(chunks,),
+        out_shape=(
+            jax.ShapeDtypeStruct(stream.shape, stream.dtype),
+            jax.ShapeDtypeStruct((tok, extra), stream.dtype),
+        ),
+        in_specs=[
+            fixed(main_share),
+            pl.BlockSpec((1,) + shape, lambda j: (j, 0, 0)),
+            pl.BlockSpec((devices, rows, wide), lambda j: (0, j, 0)),
+            pl.BlockSpec((devices, rows, wide), lambda j: (0, chunks, 0)),
+            pl.BlockSpec((tok, wide), lambda j: (0, j)),
+            pl.BlockSpec((dim, extra), lambda j: (0, dim // extra)),
+            fixed(norm_gain),
+            fixed(head_gain),
+            fixed(cos),
+            fixed(sin),
+        ],
+        out_specs=(
+            pl.BlockSpec((tok, wide), lambda j: (0, j)),
+            pl.BlockSpec((tok, extra), lambda j: (0, 0)),
+        ),
+        scratch_shapes=[pltpu.VMEM((chunks, tok, wide), jnp.bfloat16)],
+        compiler_params=pltpu.CompilerParams(vmem_limit_bytes=32 * 1024 * 1024),
+        name="finish",
+    )(main_share, rest_share, returned, returned, stream, late, norm_gain, head_gain, cos, sin)
 
 
 def per_device(
@@ -335,8 +545,6 @@
 ):
     tok, dim = hidden.shape
     hd = head_gains.shape[1]
-    kv_width = kv_weight.shape[1] // 2
-    kv_heads = kv_width // hd
     group = token_request.shape[0]
     mp_size = lax.axis_size("mp")
     dp_size = lax.axis_size("dp")
@@ -372,13 +580,19 @@
     across = lax.ppermute(normed, "mp", [(j, (j + 4) % mp_size) for j in range(mp_size)])
     left = shift(normed, 1)
     right = shift(normed, -1)
-    late = jnp.concatenate([out_weight, next_weight], axis=1)
-    late = jnp.broadcast_to(late[None], (mp_size,) + late.shape)
-    late = lax.all_to_all(late, "mp", split_axis=0, concat_axis=0, tiled=True)
-    late = late.reshape(mp_size * own_rows, -1)
-    out_full = lax.all_gather(late[:, :dim], "dp", axis=0, tiled=True)
-    next_full = lax.all_gather(late[:, dim:], "dp", axis=0, tiled=True)
-
+    packed = pack_weights(query_weight, kv_weight, out_weight, next_weight, mp_size)
+    packed = lax.all_to_all(packed, "mp", split_axis=0, concat_axis=0, tiled=True)
+    packed = packed.reshape(mp_size * own_rows, -1)
+    late_width = dim + next_weight.shape[1]
+    late = lax.all_gather(packed[:, :late_width], "dp", axis=0, tiled=True)
+    early = packed[:, late_width:].reshape(packed.shape[0], 2, 2 * hd).transpose(1, 0, 2)
+    early = jnp.broadcast_to(early[None], (dp_size // 2,) + early.shape)
+    early = early.reshape(dp_size, packed.shape[0], 2 * hd)
+    early = lax.all_to_all(early, "dp", split_axis=0, concat_axis=0, tiled=True)
+    early = early.reshape(dim, 2 * hd)
+    weights = (early, lax.ppermute(early, "dp", [(j, j ^ 1) for j in range(dp_size)]))
+    sides = [left, right, shift(across, 1), shift(across, -1)]
+    far = [shift(left, 1), shift(sides[3], -1)]
     tables = (
         token_request,
         request_leaf,
@@ -388,31 +602,14 @@
         mid_slot,
         leaf_slot,
     )
-    packed = pack(
-        tables, query_weight, kv_weight, root_cache, mid_cache, leaf_cache, mp_size
-    )
-    packed, across, left, right, late = lax.optimization_barrier(
-        (packed, across, left, right, late)
-    )
-    packed = lax.all_to_all(packed, "mp", split_axis=0, concat_axis=0, tiled=True)
-    wide = packed.shape[2]
-    early_end = 2 * own_rows
-    early = packed[:, :early_end].reshape(mp_size, 2, own_rows, wide).transpose(1, 0, 2, 3)
-    early = jnp.broadcast_to(early[None], (dp_size // 2, 2, mp_size, own_rows, wide))
-    early = early.reshape(dp_size, mp_size, own_rows, wide)
-    sides = [left, right, shift(across, 1), shift(across, -1)]
-    early, *sides = lax.optimization_barrier((early, *sides))
-    early = lax.all_to_all(early, "dp", split_axis=0, concat_axis=0, tiled=True)
-    far = []
-    for near in range(0, 4, 2):
-        far += [shift(sides[near][: tok // 2], 1), shift(sides[near + 1][tok // 2 :], -1)]
-    own_piece = jnp.sum(packed[:, early_end:].astype(jnp.float32), axis=0).astype(jnp.bfloat16)
+    path = pack_paths(tables, root_cache, mid_cache, leaf_cache, mp_size)
+    path, sides = lax.optimization_barrier((path, sides))
+    path = lax.all_to_all(path, "mp", split_axis=0, concat_axis=0, tiled=True)
+    own_piece = jnp.sum(path.astype(jnp.float32), axis=0).astype(jnp.bfloat16)
+    own_piece, far = lax.optimization_barrier((own_piece, far))
     pieces = [own_piece] + [
         lax.ppermute(own_piece, "mp", [(j, j ^ s) for j in range(mp_size)]) for s in range(1, 4)
     ]
-    early, far, pieces = lax.optimization_barrier((early, far, pieces))
-    early = early.reshape(devices, own_rows, wide)
-    weights = (early, lax.ppermute(early, "dp", [(j, j ^ 1) for j in range(dp_size)]))
     rows = [normed, across] + sides + far
     meta = jnp.concatenate(
         [
@@ -425,14 +622,7 @@
     attended = lax.all_to_all(
         attended.reshape(mp_size, tok, 2 * hd), "mp", split_axis=0, concat_axis=0, tiled=True
     )
-    projected = jnp.einsum(
-        "mtk,mkd->td",
-        attended,
-        out_full.reshape(mp_size, 2 * hd, dim),
-        preferred_element_type=jnp.float32,
-    )
-    after_attention = (hidden.astype(jnp.float32) + projected).astype(jnp.bfloat16)
-    moe_in = rms_norm(after_attention, norm_gains[1]).astype(jnp.bfloat16)
+    after_attention, moe_in = project(attended, late, hidden, norm_gains[1:2])
 
     top_k = expert_ids.shape[1]
     capacity = max(2, 5 * tok * top_k // (4 * devices))
@@ -459,31 +649,33 @@
         picked = jnp.dot(spread(first, last), source, preferred_element_type=jnp.float32)
         return picked.astype(jnp.bfloat16).reshape(devices, last - first, dim)
 
-    def mixed(first, last, returned):
-        returned = returned.reshape(-1, dim)
-        halves = jnp.dot(gather_back(first, last), returned, preferred_element_type=jnp.float32)
-        return halves[:tok] + halves[tok:]
-
     main_in = exchange(outbound(0, MAIN, moe_in))
     main_in, rest_in = lax.optimization_barrier((main_in, outbound(MAIN, capacity, moe_in)))
     rest_in = exchange(rest_in)
+    chunks = MAIN // (capacity - MAIN)
+    wide = dim // chunks
     main_out = expert(main_in.reshape(-1, dim), gate_up[0], down_weight[0])
-    main_out = exchange(main_out.reshape(devices, MAIN, dim))
-    rest_out = expert(rest_in.reshape(-1, dim), gate_up[0], down_weight[0])
-    rest_out = rest_out.reshape(devices, capacity - MAIN, dim)
-    main_out, rest_out = lax.optimization_barrier((main_out, rest_out))
-    rest_out = exchange(rest_out)
-    mixture = mixed(0, MAIN, main_out) + mixed(MAIN, capacity, rest_out)
-    layer_out = (after_attention.astype(jnp.float32) + mixture).astype(jnp.bfloat16)
-    next_in = rms_norm(layer_out, norm_gains[2]).astype(jnp.bfloat16)
-    next_raw = jnp.dot(next_in, next_full, preferred_element_type=jnp.float32)
-    my_cos = lax.dynamic_slice_in_dim(cosine, me * tok, tok)[:, None, :]
-    my_sin = lax.dynamic_slice_in_dim(sine, me * tok, tok)[:, None, :]
-    next_keys = rms_norm(next_raw[:, :kv_width].reshape(tok, kv_heads, hd), head_gains[2])
-    swapped = jnp.concatenate([next_keys[..., hd // 2 :], next_keys[..., : hd // 2]], axis=-1)
-    next_keys = (next_keys * my_cos + swapped * my_sin).astype(jnp.bfloat16)
-    next_rows = jnp.concatenate(
-        [next_keys.reshape(tok, kv_width), next_raw[:, kv_width:].astype(jnp.bfloat16)], axis=1
+    main_out = main_out.reshape(devices, MAIN, chunks, wide).transpose(0, 2, 1, 3)
+    main_out = main_out.reshape(devices, MAIN * chunks, wide)
+    main_out = jnp.pad(main_out, ((0, 0), (0, MAIN), (0, 0)))
+    main_out, rest_in = lax.optimization_barrier((main_out, rest_in))
+    returned = exchange(expert_rest(rest_in.reshape(-1, dim), gate_up[0], down_weight[0], main_out))
+    main_share = gather_back(0, MAIN)
+    rest_share = gather_back(MAIN, capacity).reshape(1, 2 * tok, devices, 1, capacity - MAIN)
+    which = jnp.eye(chunks, dtype=jnp.bfloat16).reshape(chunks, 1, 1, chunks, 1)
+    rest_share = (rest_share * which).reshape(chunks, 2 * tok, devices * MAIN)
+    my_cos = lax.dynamic_slice_in_dim(cosine, me * tok, tok)
+    my_sin = lax.dynamic_slice_in_dim(sine, me * tok, tok)
+    layer_out, next_rows = finish(
+        main_share,
+        rest_share,
+        returned,
+        after_attention,
+        late,
+        norm_gains[2:3],
+        head_gains[2:3],
+        my_cos,
+        my_sin,
     )
     return (layer_out, next_rows)
 

time: 372 us -> 361 us (0.970)
  matrix products: 42.3 us -> 17.9 us
  Pallas kernels: 21.9 us -> 40.7 us
  waiting for transfers between devices: 153 us -> 169 us
  starting transfers between devices: 62.4 us -> 52.9 us
  other arithmetic: 18.8 us -> 12.4 us
  local copies, waits for them, and re-layouts: 37.7 us -> 32.3 us
    pallas_call x1 -> x5, Pallas kernels: 0.99 us -> 20.2 us  [the longest x1 6.75 us: expert_rest(): pl.pallas_call(rest_kernel, grid=(1,), out_shape=jax.ShapeDtypeStruct(mai...]
    dot_general x4 -> x0, matrix products: 13.9 us -> none  [the longest x2 6.68 us: mixed(): jnp.dot(gather_back(first, last), returned, preferred_element_type=jnp.fl...]
    slice x11 -> x4, local copies, waits for them, and re-layouts: 12.4 us -> 0.91 us  [the longest x1 0.88 us: per_device(): late = lax.all_gather(packed[:, :late_width], 'dp', axis=0, tiled=True)]
    all_to_all x4 -> x3, waiting for transfers between devices: 103 us -> 113 us  [exchange(): return lax.all_to_all(values, BOTH, split_axis=0, concat_axis=0, tiled=True)]
    unnamed x78 -> x74, local copies, waits for them, and re-layouts: 10.4 us -> 19.5 us
    ppermute x8 -> x6, waiting for transfers between devices: 5.87 us -> 14.1 us  [shift(): return lax.ppermute(values, 'mp', moves)]
    reshape x4 -> x2, local copies, waits for them, and re-layouts: 8.1 us -> 0.45 us  [the longest x1 0.42 us: per_device(): rest_in.reshape(-1, dim)]
    ppermute x1, waiting for transfers between devices: 9.16 us -> 2.02 us  [per_device(): lax.ppermute(normed, 'mp', [(j, (j + 4) % mp_size) for j in range(mp_size)])]
  transfers between devices with their start and end apart: 22 -> 18, of which waited for: 10 -> 10; matrix products, arithmetic and copies ran while one was open for 19% -> 11% of each run, Pallas kernels for 6% -> 6%
where the time goes in v4:
time: 361 us; the launch traced here: 360 us
  waiting for transfers between devices  169 us (47%)
  starting transfers between devices  52.9 us (15%)
  Pallas kernels  40.7 us (11%)
  local copies, waits for them, and re-layouts  32.3 us (9%)
  blocking collectives  19.3 us (5%)
  matrix products  17.9 us (5%)
  between operations  15.8 us (4%)
  other arithmetic  12.4 us (3%)
    all_to_all x3, waiting for transfers between devices, exchange(): return lax.all_to_all(values, BOTH, split_axis=0, concat_axis=0, tiled=True)  113 us
    all_to_all x1, waiting for transfers between devices, per_device(): path = lax.all_to_all(path, 'mp', split_axis=0, concat_axis=0, tiled=True)  28.6 us
    all_to_all x3, starting transfers between devices, exchange(): return lax.all_to_all(values, BOTH, split_axis=0, concat_axis=0, tiled=True)  22.7 us
    pallas_call x1, Pallas kernels, attend(): pl.pallas_call(attention_kernel, out_shape=jax.ShapeDtypeStruct((group, 2...  20.5 us
    unnamed x74, local copies, waits for them, and re-layouts  19.5 us
    all_to_all x1, blocking collectives, per_device(): lax.all_to_all(packed, 'mp', split_axis=0, concat_axis=0, tiled=True)  19.3 us
    ppermute x6, waiting for transfers between devices, shift(): return lax.ppermute(values, 'mp', moves)  14.1 us
    dot_general x1, matrix products, expert(): both = jnp.dot(rows, gate_up, preferred_element_type=jnp.float32)  10.1 us
  transfers between devices with their start and end apart: 18, of which 10 were waited for; matrix products, arithmetic and copies ran while one was open for 11% of the time, Pallas kernels for 6%

profile of v4, /device:TPU:0, one launch (start us, length us, event | category | flops | bytes accessed | tf_op | source)
XLA Modules:
  0.0 360.0 jit_solution(12903250230176744065)
XLA Ops:
  7.2 1.9 pack_weights.1
  9.1 19.3 %all_to_all.35 = bf16[8,16,3072]{2,1,0:T(8,128)(2,1)S(1)} all-to-all(bf16[8,16,3072]{2,1,0:T(8,128)(2,1)} %pack_weights.1), channel_id=1, replica_groups=mesh['dp'=16,'mp'=8] {'mp'}, dimensions={0} | all-to-all | bytes 1572864 | tf_op jit(solution)/shard_map/all_to_all | solution.py:584
  30.6 1.1 broadcast_in_dim.167
  31.7 6.9 %all-to-all-start.2 = ((bf16[16,128,256]{2,1,0:T(8,128)(2,1)}), bf16[16,128,256]{2,1,0:T(8,128)(2,1)S(1)}, u32[]{:S(2)}, u32[]{:S(2)}) async-start(bf16[16,128,256]{2,1,0:T(8,128)(2,1)} %bitcast.53), calls=%async_computation.2 | async-start | bytes 2097152 | tf_op jit(solution)/shard_map/all_to_all | solution.py:591
  39.5 2.5 collective-permute-start.2
  41.9 2.0 collective-permute-done.across
  44.3 1.7 collective-permute-start.3
  47.5 2.2 pack_paths.1
  49.7 4.9 %collective-permute-done.1.own_left = bf16[128,2048]{1,0:T(8,128)(2,1)S(1)} collective-permute-done((bf16[128,2048]{1,0:T(8,128)(2,1)S(1)}, bf16[128,2048]{1,0:T(8,128)(2,1)S(1)}, u32[]{:S(2)}, u32[]{:S(2)}) %collective-permute-start.1) | collective-permute-done | bytes 524320 | tf_op jit(solution)/shard_map/ppermute | solution.py:578
  55.5 9.1 %collective-permute-done.4.across_right = bf16[128,2048]{1,0:T(8,128)(2,1)S(1)} collective-permute-done((bf16[128,2048]{1,0:T(8,128)(2,1)S(1)}, bf16[128,2048]{1,0:T(8,128)(2,1)S(1)}, u32[]{:S(2)}, u32[]{:S(2)}) %collective-permute-start.4) | collective-permute-done | bytes 524320 | tf_op jit(solution)/shard_map/ppermute | solution.py:578
  66.2 5.2 %all-to-all-start = ((bf16[8,448,256]{2,1,0:T(8,128)(2,1)}), bf16[8,448,256]{2,1,0:T(8,128)(2,1)}, u32[]{:S(2)}, u32[]{:S(2)}) async-start(bf16[8,448,256]{2,1,0:T(8,128)(2,1)} %pack_paths.1), calls=%async_computation | async-start | bytes 3670016 | tf_op jit(solution)/shard_map/all_to_all | solution.py:607
  74.2 2.0 collective-permute-start.5
  76.2 1.2 collective-permute-start.6
  78.9 1.2 add_convert_fusion
  80.1 3.2 fusion.13
  83.3 28.6 %all-to-all-done = bf16[8,448,256]{2,1,0:T(8,128)(2,1)} async-done(((bf16[8,448,256]{2,1,0:T(8,128)(2,1)}), bf16[8,448,256]{2,1,0:T(8,128)(2,1)}, u32[]{:S(2)}, u32[]{:S(2)}) %all-to-all-start) | async-done | bytes 1835040 | tf_op jit(solution)/shard_map/all_to_all | solution.py:607
  111.9 1.8 reduce_sum.102.piece_0
  113.8 2.5 collective-permute-start.10
  116.6 2.0 collective-permute-start.9
  119.2 1.9 pad_maximum_fusion.1
  121.1 1.2 collective-permute-done.8.piece_1
  122.3 2.7 collective-permute-done.9.piece_2
  125.0 1.0 copy-done.6
  126.1 1.0 copy-done.8
  127.1 1.0 copy-done.10
  128.1 1.0 copy-done.12
  129.2 1.0 copy-done.14
  130.2 20.5 %tree_attention.1 = bf16[1024,256]{1,0:T(8,128)(2,1)} custom-call(s32[9]{0:T(128)S(1)} %pad_add_fusion.1.meta, bf16[128,2048]{1,0:T(8,128)(2,1)S(1)} %fusion.8.own, bf16[128,2048]{1,0:T(8,128)(2,1)S(1)} %copy-done.6, bf16[128,2048]{1,0:T(8,128)(2,1)S(1)} %copy-done.8, bf16[128,2048]{1,0:T(8,128)(2,1)S(1)} %copy-done.10, bf16[128,2048]{1,0:T(8,128)(2,1)S(1)} %copy-done.14, ...), custom_call_target="tpu_custom_call" | custom-call | tf_op jit(solution)/shard_map/tree_attention/pallas_call | solution.py:291
  150.8 3.9 %all-to-all-start.3 = ((bf16[8,128,256]{2,1,0:T(8,128)(2,1)}), bf16[8,128,256]{2,1,0:T(8,128)(2,1)S(1)}, u32[]{:S(2)}, u32[]{:S(2)}) async-start(bf16[8,128,256]{2,1,0:T(8,128)(2,1)} %bitcast.20), calls=%async_computation.3 | async-start | bytes 1048576 | tf_op jit(solution)/shard_map/all_to_all | solution.py:622
  155.4 7.6 %all-to-all-done.3.attended = bf16[8,128,256]{2,1,0:T(8,128)(2,1)S(1)} async-done(((bf16[8,128,256]{2,1,0:T(8,128)(2,1)}), bf16[8,128,256]{2,1,0:T(8,128)(2,1)S(1)}, u32[]{:S(2)}, u32[]{:S(2)}) %all-to-all-start.3) | async-done | bytes 524320 | tf_op jit(solution)/shard_map/all_to_all | solution.py:622
  163.0 4.0 %copy-done = bf16[2048,2560]{1,0:T(8,128)(2,1)S(1)} copy-done((bf16[2048,2560]{1,0:T(8,128)(2,1)S(1)}, bf16[2048,2560]{1,0:T(8,128)(2,1)}, u32[]{:S(2)}) %copy-start) | copy-done | bytes 10485784
  167.0 2.8 project.1
  169.8 3.3 convert_bitcast_fusion
  173.1 10.1 %all-to-all-start.4 = ((bf16[128,8,2048]{2,1,0:T(8,128)(2,1)}), bf16[128,8,2048]{2,1,0:T(8,128)(2,1)}, u32[]{:S(2)}, u32[]{:S(2)}) async-start(bf16[128,8,2048]{2,1,0:T(8,128)(2,1)} %convert_bitcast_fusion), calls=%async_computation.4 | async-start | bytes 8388608 | tf_op jit(solution)/shard_map/all_to_all | solution.py:368
  183.9 1.5 reshape.153
  185.4 50.4 %all-to-all-done.4 = bf16[128,8,2048]{2,1,0:T(8,128)(2,1)} async-done(((bf16[128,8,2048]{2,1,0:T(8,128)(2,1)}), bf16[128,8,2048]{2,1,0:T(8,128)(2,1)}, u32[]{:S(2)}, u32[]{:S(2)}) %all-to-all-start.4) | async-done | bytes 4194336 | tf_op jit(solution)/shard_map/all_to_all | solution.py:368
  235.8 4.8 %all-to-all-start.5 = ((bf16[128,2,2048]{2,1,0:T(2,128)(2,1)}), bf16[128,2,2048]{2,1,0:T(2,128)(2,1)S(1)}, u32[]{:S(2)}, u32[]{:S(2)}) async-start(bf16[128,2,2048]{2,1,0:T(2,128)(2,1)} %reshape.153), calls=%async_computation.5 | async-start | bytes 2097152 | tf_op jit(solution)/shard_map/all_to_all | solution.py:368
  240.7 10.1 %fusion = f32[1024,1536]{1,0:T(8,128)S(1)} fusion(bf16[128,8,2048]{2,1,0:T(8,128)(2,1)} %all-to-all-done.4, bf16[1,2048,1536]{2,1,0:T(8,128)(2,1)} %param.30), kind=kOutput, calls=%fused_computation | convolution fusion | flops 6442450944 | bytes 16777216 | tf_op jit(solution)/shard_map/dot_general | solution.py:373
  250.9 3.7 %convolution_convert_fusion = bf16[1024,2048]{1,0:T(8,128)(2,1)S(1)} fusion(f32[1024,1536]{1,0:T(8,128)S(1)} %fusion, bf16[1,768,2048]{2,1,0:T(8,128)(2,1)S(1)} %copy-done.3), kind=kOutput, calls=%fused_computation.3 | convolution fusion | flops 3228041216 | bytes 13631488 | tf_op jit(solution)/shard_map/dot_general | solution.py:375
  254.6 2.8 pad.4.main_block
  257.4 2.2 all-to-all-done.5
  260.1 1.9 copy-done.4
  262.0 6.7 %expert_rest.1 = bf16[128,40,512]{2,1,0:T(8,128)(2,1)} custom-call(bf16[256,2048]{1,0:T(8,128)(2,1)S(1)} %reshape.157.rows, bf16[2048,1536]{1,0:T(8,128)(2,1)} %bitcast.51, bf16[768,2048]{1,0:T(8,128)(2,1)S(1)} %bitcast.50, bf16[128,40,512]{2,1,0:T(8,128)(2,1)} %pad.4.main_block), custom_call_target="tpu_custom_call", output_to_operand_aliasing={{}: (3, {})} | custom-call | tf_op jit(solution)/shard_map/expert_rest/pallas_call | solution.py:416
  268.7 7.8 %all-to-all-start.6 = ((bf16[128,40,512]{2,1,0:T(8,128)(2,1)}), bf16[128,40,512]{2,1,0:T(8,128)(2,1)}, u32[]{:S(2)}, u32[]{:S(2)}) async-start(bf16[128,40,512]{2,1,0:T(8,128)(2,1)} %expert_rest.1), calls=%async_computation.6 | async-start | bytes 10485760 | tf_op jit(solution)/shard_map/all_to_all | solution.py:368
  280.4 1.2 copy.64
  282.8 59.8 %all-to-all-done.6.main_rows.rest_rows = bf16[128,40,512]{2,1,0:T(8,128)(2,1)} async-done(((bf16[128,40,512]{2,1,0:T(8,128)(2,1)}), bf16[128,40,512]{2,1,0:T(8,128)(2,1)}, u32[]{:S(2)}, u32[]{:S(2)}) %all-to-all-start.6) | async-done | bytes 5242912 | tf_op jit(solution)/shard_map/all_to_all | solution.py:368
  342.7 4.0 %copy-done.1 = bf16[2048,2560]{1,0:T(8,128)(2,1)S(1)} copy-done((bf16[2048,2560]{1,0:T(8,128)(2,1)S(1)}, bf16[2048,2560]{1,0:T(8,128)(2,1)}, u32[]{:S(2)}) %copy-start.1) | copy-done | bytes 10485784
  346.7 6.5 %finish.1 = (bf16[128,2048]{1,0:T(8,128)(2,1)}, bf16[128,512]{1,0:T(8,128)(2,1)}) custom-call(bf16[256,1024]{1,0:T(8,128)(2,1)S(1)} %pad_maximum_fusion.main_share, bf16[4,256,1024]{2,1,0:T(8,128)(2,1)S(1)} %broadcast_multiply_fusion.rest_share, bf16[128,40,512]{2,1,0:T(8,128)(2,1)} %all-to-all-done.6.main_rows.rest_rows, ...), custom_call_target="tpu_custom_call" | custom-call | tf_op jit(solution)/shard_map/finish/pallas_call | solution.py:491
  (135 shorter events, 17.9 us)
Async XLA Ops:
  7.2 22.2 %copy-start.2 = (bf16[128,2048]{1,0:T(8,128)(2,1)S(1)}, bf16[128,2048]{1,0:T(8,128)(2,1)}, u32[]{:S(2)}) copy-start(bf16[128,2048]{1,0:T(8,128)(2,1)} %hidden.1) | copy-start | bytes 1572868
  7.2 22.4 %copy-start.30 = (f32[3,2048]{1,0:T(4,128)S(1)}, f32[3,2048]{1,0:T(4,128)}, u32[]{:S(2)}) copy-start(f32[3,2048]{1,0:T(4,128)} %param.25) | copy-start | bytes 73732
  7.2 155.8 %all-gather.2.cloned.1.call-start = ((), (), s32[]{:S(2)}) async-start(), calls=%async_computation.7 | async-start | bytes 11141120 | tf_op jit(solution)/shard_map/all_gather | solution.py:587
  28.4 17.5 %copy-start.18 = (s32[1024]{0:T(1024)S(1)}, s32[1024]{0:T(1024)}, u32[]{:S(2)}) copy-start(s32[1024]{0:T(1024)} %token_request.1) | copy-start | bytes 12292
  28.4 18.1 %copy-start.15 = (bf16[1,512,512]{2,1,0:T(8,128)(2,1)S(1)}, bf16[1,512,512]{2,1,0:T(8,128)(2,1)}, u32[]{:S(2)}) copy-start(bf16[1,512,512]{2,1,0:T(8,128)(2,1)} %root.1) | copy-start | bytes 1572868
  28.4 18.1 %copy-start.16 = (bf16[1,256,512]{2,1,0:T(8,128)(2,1)S(1)}, bf16[1,256,512]{2,1,0:T(8,128)(2,1)}, u32[]{:S(2)}) copy-start(bf16[1,256,512]{2,1,0:T(8,128)(2,1)} %mid.1) | copy-start | bytes 786436
  28.4 18.1 %copy-start.20 = (s32[16]{0:T(128)S(1)}, s32[16]{0:T(128)}, u32[]{:S(2)}) copy-start(s32[16]{0:T(128)} %leaf_parent.1) | copy-start | bytes 196
  28.4 18.1 %copy-start.21 = (s32[8]{0:T(128)S(1)}, s32[8]{0:T(128)}, u32[]{:S(2)}) copy-start(s32[8]{0:T(128)} %mid_parent.1) | copy-start | bytes 100
  28.5 18.0 %copy-start.22 = (s32[8]{0:T(128)S(1)}, s32[8]{0:T(128)}, u32[]{:S(2)}) copy-start(s32[8]{0:T(128)} %root_slot.1) | copy-start | bytes 100
  28.5 18.0 %copy-start.23 = (s32[8]{0:T(128)S(1)}, s32[8]{0:T(128)}, u32[]{:S(2)}) copy-start(s32[8]{0:T(128)} %mid_slot.1) | copy-start | bytes 100
  28.5 18.0 %copy-start.24 = (s32[16]{0:T(128)S(1)}, s32[16]{0:T(128)}, u32[]{:S(2)}) copy-start(s32[16]{0:T(128)} %leaf_slot.1) | copy-start | bytes 196
  28.5 18.0 %copy-start.25 = (s32[32]{0:T(128)S(1)}, s32[32]{0:T(128)}, u32[]{:S(2)}) copy-start(s32[32]{0:T(128)} %request_leaf.1) | copy-start | bytes 388
  29.8 14.1 %collective-permute-start = (bf16[128,2048]{1,0:T(8,128)(2,1)S(1)}, bf16[128,2048]{1,0:T(8,128)(2,1)S(1)}, u32[]{:S(2)}, u32[]{:S(2)}) collective-permute-start(bf16[128,2048]{1,0:T(8,128)(2,1)S(1)} %fusion.8.own), channel_id=1, source_target_pairs={{0,4},{1,5},{2,6},{3,7},{4,0},{5,1},{6,2},{7,3},{8,12},{9,13},{10,... | collective-permute-start | bytes 1572872 | tf_op jit(solution)/shard_map/ppermute | solution.py:580
  31.7 40.5 %copy-start.33 = (s32[16]{0:T(128)S(1)}, s32[16]{0:T(128)}, u32[]{:S(2)}) copy-start(s32[16]{0:T(128)} %param.41) | copy-start | bytes 196
  31.7 40.7 %copy-start.34 = (s32[8]{0:T(128)S(1)}, s32[8]{0:T(128)}, u32[]{:S(2)}) copy-start(s32[8]{0:T(128)} %param.40) | copy-start | bytes 100
  31.7 40.9 %copy-start.35 = (s32[8]{0:T(128)S(1)}, s32[8]{0:T(128)}, u32[]{:S(2)}) copy-start(s32[8]{0:T(128)} %param.39) | copy-start | bytes 100
  31.7 45.9 %copy-start.31 = (s32[128,8]{0,1:T(8,128)S(1)}, s32[128,8]{0,1:T(8,128)}, u32[]{:S(2)}) copy-start(s32[128,8]{0,1:T(8,128)} %param.33) | copy-start | bytes 12292
  31.7 34.5 %all-to-all-start.2 = ((bf16[16,128,256]{2,1,0:T(8,128)(2,1)}), bf16[16,128,256]{2,1,0:T(8,128)(2,1)S(1)}, u32[]{:S(2)}, u32[]{:S(2)}) async-start(bf16[16,128,256]{2,1,0:T(8,128)(2,1)} %bitcast.53), calls=%async_computation.2 | async-start | bytes 2097152 | tf_op jit(solution)/shard_map/all_to_all | solution.py:591
  38.6 16.0 %collective-permute-start.1 = (bf16[128,2048]{1,0:T(8,128)(2,1)S(1)}, bf16[128,2048]{1,0:T(8,128)(2,1)S(1)}, u32[]{:S(2)}, u32[]{:S(2)}) collective-permute-start(bf16[128,2048]{1,0:T(8,128)(2,1)S(1)} %fusion.8.own), channel_id=1, source_target_pairs={{0,1},{1,2},{2,3},{3,0},{4,5},{5,6},{6,7},{7,4},{8,9},{9,10},{10,1... | collective-permute-start | bytes 1572872 | tf_op jit(solution)/shard_map/ppermute | solution.py:578
  39.5 15.2 %collective-permute-start.2 = (bf16[128,2048]{1,0:T(8,128)(2,1)S(1)}, bf16[128,2048]{1,0:T(8,128)(2,1)S(1)}, u32[]{:S(2)}, u32[]{:S(2)}) collective-permute-start(bf16[128,2048]{1,0:T(8,128)(2,1)S(1)} %fusion.8.own), channel_id=1, source_target_pairs={{0,3},{1,0},{2,1},{3,2},{4,7},{5,4},{6,5},{7,6},{8,11},{9,8},{10,9... | collective-permute-start | bytes 1572872 | tf_op jit(solution)/shard_map/ppermute | solution.py:578
  43.9 28.8 %copy-start.5 = (bf16[128,2048]{1,0:T(8,128)(2,1)}, bf16[128,2048]{1,0:T(8,128)(2,1)S(1)}, u32[]{:S(2)}) copy-start(bf16[128,2048]{1,0:T(8,128)(2,1)S(1)} %collective-permute-done.across) | copy-start | bytes 1572868
  43.9 20.6 %collective-permute-start.4 = (bf16[128,2048]{1,0:T(8,128)(2,1)S(1)}, bf16[128,2048]{1,0:T(8,128)(2,1)S(1)}, u32[]{:S(2)}, u32[]{:S(2)}) collective-permute-start(bf16[128,2048]{1,0:T(8,128)(2,1)S(1)} %collective-permute-done.across), channel_id=1, source_target_pairs={{0,3},{1,0},{2,1},{3,2},{4,7},{5,4},{6,5},{7,6},{8,11},{9,8},{10,9... | collective-permute-start | bytes 1572872 | tf_op jit(solution)/shard_map/ppermute | solution.py:578
  44.3 21.1 %collective-permute-start.3 = (bf16[128,2048]{1,0:T(8,128)(2,1)S(1)}, bf16[128,2048]{1,0:T(8,128)(2,1)S(1)}, u32[]{:S(2)}, u32[]{:S(2)}) collective-permute-start(bf16[128,2048]{1,0:T(8,128)(2,1)S(1)} %collective-permute-done.across), channel_id=1, source_target_pairs={{0,1},{1,2},{2,3},{3,0},{4,5},{5,6},{6,7},{7,4},{8,9},{9,10},{10,1... | collective-permute-start | bytes 1572872 | tf_op jit(solution)/shard_map/ppermute | solution.py:578
  49.7 75.3 %copy-start.19 = (f32[3,128]{1,0:T(4,128)S(1)}, f32[3,128]{1,0:T(4,128)}, u32[]{:S(2)}) copy-start(f32[3,128]{1,0:T(4,128)} %gains.1) | copy-start | bytes 4612
  54.6 10.0 %copy-start.7 = (bf16[128,2048]{1,0:T(8,128)(2,1)}, bf16[128,2048]{1,0:T(8,128)(2,1)S(1)}, u32[]{:S(2)}) copy-start(bf16[128,2048]{1,0:T(8,128)(2,1)S(1)} %collective-permute-done.1.own_left) | copy-start | bytes 1572868
  66.2 45.7 %all-to-all-start = ((bf16[8,448,256]{2,1,0:T(8,128)(2,1)}), bf16[8,448,256]{2,1,0:T(8,128)(2,1)}, u32[]{:S(2)}, u32[]{:S(2)}) async-start(bf16[8,448,256]{2,1,0:T(8,128)(2,1)} %pack_paths.1), calls=%async_computation | async-start | bytes 3670016 | tf_op jit(solution)/shard_map/all_to_all | solution.py:607
  72.8 48.3 %collective-permute-start.7 = (bf16[2048,256]{1,0:T(8,128)(2,1)S(1)}, bf16[2048,256]{1,0:T(8,128)(2,1)S(1)}, u32[]{:S(2)}, u32[]{:S(2)}) collective-permute-start(bf16[2048,256]{1,0:T(8,128)(2,1)S(1)} %bitcast.48), channel_id=1, source_target_pairs={{0,8},{8,0},{16,24},{24,16},{32,40},{40,32},{48,56},{56,48},{64,72... | collective-permute-start | bytes 3145736 | tf_op jit(solution)/shard_map/ppermute | solution.py:593
  74.2 39.6 %collective-permute-start.5 = (bf16[128,2048]{1,0:T(8,128)(2,1)}, bf16[128,2048]{1,0:T(8,128)(2,1)}, u32[]{:S(2)}, u32[]{:S(2)}) collective-permute-start(bf16[128,2048]{1,0:T(8,128)(2,1)} %copy-done.7), channel_id=1, source_target_pairs={{0,1},{1,2},{2,3},{3,0},{4,5},{5,6},{6,7},{7,4},{8,9},{9,10},{10,1... | collective-permute-start | bytes 1572872 | tf_op jit(solution)/shard_map/ppermute | solution.py:578
  76.2 37.6 %collective-permute-start.6 = (bf16[128,2048]{1,0:T(8,128)(2,1)}, bf16[128,2048]{1,0:T(8,128)(2,1)}, u32[]{:S(2)}, u32[]{:S(2)}) collective-permute-start(bf16[128,2048]{1,0:T(8,128)(2,1)} %copy-done.11), channel_id=1, source_target_pairs={{0,3},{1,0},{2,1},{3,2},{4,7},{5,4},{6,5},{7,6},{8,11},{9,8},{10,9... | collective-permute-start | bytes 1572872 | tf_op jit(solution)/shard_map/ppermute | solution.py:578
  113.8 7.3 %collective-permute-start.10 = (bf16[448,256]{1,0:T(8,128)(2,1)S(1)}, bf16[448,256]{1,0:T(8,128)(2,1)S(1)}, u32[]{:S(2)}, u32[]{:S(2)}) collective-permute-start(bf16[448,256]{1,0:T(8,128)(2,1)S(1)} %reduce_sum.102.piece_0), channel_id=1, source_target_pairs={{0,3},{1,2},{2,1},{3,0},{4,7},{5,6},{6,5},{7,4},{8,11},{9,10},{10,... | collective-permute-start | bytes 688136 | tf_op jit(solution)/shard_map/ppermute | solution.py:611
  116.3 6.0 %collective-permute-start.8 = (bf16[448,256]{1,0:T(8,128)(2,1)S(1)}, bf16[448,256]{1,0:T(8,128)(2,1)S(1)}, u32[]{:S(2)}, u32[]{:S(2)}) collective-permute-start(bf16[448,256]{1,0:T(8,128)(2,1)S(1)} %reduce_sum.102.piece_0), channel_id=1, source_target_pairs={{0,1},{1,0},{2,3},{3,2},{4,5},{5,4},{6,7},{7,6},{8,9},{9,8},{10,11... | collective-permute-start | bytes 688136 | tf_op jit(solution)/shard_map/ppermute | solution.py:611
  116.6 8.4 %collective-permute-start.9 = (bf16[448,256]{1,0:T(8,128)(2,1)S(1)}, bf16[448,256]{1,0:T(8,128)(2,1)S(1)}, u32[]{:S(2)}, u32[]{:S(2)}) collective-permute-start(bf16[448,256]{1,0:T(8,128)(2,1)S(1)} %reduce_sum.102.piece_0), channel_id=1, source_target_pairs={{0,2},{1,3},{2,0},{3,1},{4,6},{5,7},{6,4},{7,5},{8,10},{9,11},{10,... | collective-permute-start | bytes 688136 | tf_op jit(solution)/shard_map/ppermute | solution.py:611
  125.0 1.0 copy-start.6
  126.1 1.0 copy-start.8
  127.1 1.0 copy-start.10
  150.8 12.2 %all-to-all-start.3 = ((bf16[8,128,256]{2,1,0:T(8,128)(2,1)}), bf16[8,128,256]{2,1,0:T(8,128)(2,1)S(1)}, u32[]{:S(2)}, u32[]{:S(2)}) async-start(bf16[8,128,256]{2,1,0:T(8,128)(2,1)} %bitcast.20), calls=%async_computation.3 | async-start | bytes 1048576 | tf_op jit(solution)/shard_map/all_to_all | solution.py:622
  163.0 4.0 %copy-start = (bf16[2048,2560]{1,0:T(8,128)(2,1)S(1)}, bf16[2048,2560]{1,0:T(8,128)(2,1)}, u32[]{:S(2)}) copy-start(bf16[2048,2560]{1,0:T(8,128)(2,1)} %all-gather.2.cloned.1.call-done.weight.next_weight) | copy-start | bytes 31457284
  173.1 62.7 %all-to-all-start.4 = ((bf16[128,8,2048]{2,1,0:T(8,128)(2,1)}), bf16[128,8,2048]{2,1,0:T(8,128)(2,1)}, u32[]{:S(2)}, u32[]{:S(2)}) async-start(bf16[128,8,2048]{2,1,0:T(8,128)(2,1)} %convert_bitcast_fusion), calls=%async_computation.4 | async-start | bytes 8388608 | tf_op jit(solution)/shard_map/all_to_all | solution.py:368
  235.8 23.8 %all-to-all-start.5 = ((bf16[128,2,2048]{2,1,0:T(2,128)(2,1)}), bf16[128,2,2048]{2,1,0:T(2,128)(2,1)S(1)}, u32[]{:S(2)}, u32[]{:S(2)}) async-start(bf16[128,2,2048]{2,1,0:T(2,128)(2,1)} %reshape.153), calls=%async_computation.5 | async-start | bytes 2097152 | tf_op jit(solution)/shard_map/all_to_all | solution.py:368
  240.7 10.2 %copy-start.3 = (bf16[1,768,2048]{2,1,0:T(8,128)(2,1)S(1)}, bf16[1,768,2048]{2,1,0:T(8,128)(2,1)}, u32[]{:S(2)}) copy-start(bf16[1,768,2048]{2,1,0:T(8,128)(2,1)} %param.31) | copy-start | bytes 9437188
  260.1 1.9 copy-start.4
  268.7 7.9 %copy-start.32 = (f32[128,8]{0,1:T(8,128)S(1)}, f32[128,8]{0,1:T(8,128)}, u32[]{:S(2)}) copy-start(f32[128,8]{0,1:T(8,128)} %param.34) | copy-start | bytes 12292
  268.7 74.0 %all-to-all-start.6 = ((bf16[128,40,512]{2,1,0:T(8,128)(2,1)}), bf16[128,40,512]{2,1,0:T(8,128)(2,1)}, u32[]{:S(2)}, u32[]{:S(2)}) async-start(bf16[128,40,512]{2,1,0:T(8,128)(2,1)} %expert_rest.1), calls=%async_computation.6 | async-start | bytes 10485760 | tf_op jit(solution)/shard_map/all_to_all | solution.py:368
  276.5 5.1 %copy-start.26 = (f32[1024,64]{1,0:T(8,128)S(1)}, f32[1024,64]{1,0:T(8,128)}, u32[]{:S(2)}) copy-start(f32[1024,64]{1,0:T(8,128)} %get-tuple-element.41) | copy-start | bytes 786436
  276.5 5.1 %copy-start.27 = (f32[1024,64]{1,0:T(8,128)S(1)}, f32[1024,64]{1,0:T(8,128)}, u32[]{:S(2)}) copy-start(f32[1024,64]{1,0:T(8,128)} %get-tuple-element.42) | copy-start | bytes 786436
  276.5 5.1 %copy-start.28 = (f32[1024,64]{1,0:T(8,128)S(1)}, f32[1024,64]{1,0:T(8,128)}, u32[]{:S(2)}) copy-start(f32[1024,64]{1,0:T(8,128)} %get-tuple-element.43) | copy-start | bytes 786436
  281.6 1.0 copy-start.29
  342.7 4.0 %copy-start.1 = (bf16[2048,2560]{1,0:T(8,128)(2,1)S(1)}, bf16[2048,2560]{1,0:T(8,128)(2,1)}, u32[]{:S(2)}) copy-start(bf16[2048,2560]{1,0:T(8,128)(2,1)} %all-gather.2.cloned.1.call-done.weight.next_weight) | copy-start | bytes 31457284
  (6 other events, 5.5 us)
Sparse Core Ops, SparseCore 0:
  29.5 107.7 all-gather.1

commit v5 on v4

--- a/solution.py
+++ b/solution.py
@@ -33,8 +33,14 @@
     base = dim + extra
     for dest in range(count):
         head = dest * heads // count
-        packed[dest, :, 0:dim] = out_rows[...]
-        packed[dest, :, dim:base] = next_rows[...]
+        for half in range(2):
+            at = half * base // 2
+            packed[dest, :, at : at + dim // 2] = out_rows[
+                :, half * dim // 2 : (half + 1) * dim // 2
+            ]
+            packed[dest, :, at + dim // 2 : at + base // 2] = next_rows[
+                :, half * extra // 2 : (half + 1) * extra // 2
+            ]
         packed[dest, :, base : base + wide] = query[:, dest * wide : (dest + 1) * wide]
         for half in range(2):
             source = (half * heads + head) * hd
@@ -305,24 +311,49 @@
             pltpu.VMEM((256, 1), jnp.float32),
             pltpu.VMEM((256, hd), jnp.float32),
         ],
-        compiler_params=pltpu.CompilerParams(vmem_limit_bytes=40 * 1024 * 1024),
+        compiler_params=pltpu.CompilerParams(vmem_limit_bytes=60 * 1024 * 1024),
+        cost_estimate=pl.CostEstimate(
+            flops=16 * group * group * hd, bytes_accessed=16 * group * 512, transcendentals=3 * group * group
+        ),
         name="tree_attention",
     )(meta, *rows, *weights, *pieces, gains, cosine, sine)
 
 
-def project_kernel(attended, weight, hidden, gain, out, normed, joined, layer):
-    count, _, wide = attended.shape
+def column_block(step, core):
+    half = jnp.where(step < 2, core, 1 - core)
+    return 2 * half + lax.rem(step, 2)
+
+
+def project_kernel(
+    place, attended, own, other, hidden, gain, out, normed, joined_own, joined_other, layer
+):
+    wide = attended.shape[2]
     step = pl.program_id(0)
+    x, y, core = place[0], place[1], place[2]
 
     @pl.when(step == 0)
     def _():
-        for source in range(count):
-            joined[:, source * wide : (source + 1) * wide] = attended[source]
-
-    added = jnp.dot(joined[...], weight[...], preferred_element_type=jnp.float32)
-    done = (hidden[...].astype(jnp.float32) + added).astype(jnp.bfloat16)
-    out[...] = done
-    layer[step] = done
+        for at, shift in enumerate((0, 3, 1, 2)):
+            for turn in range(2):
+                block = attended[lax.rem(x + shift, 4) * 2 + lax.rem(y + turn, 2)]
+                swapped = jnp.concatenate([block[:, wide // 2 :], block[:, : wide // 2]], axis=1)
+                columns = slice((2 * at + turn) * wide, (2 * at + turn + 1) * wide)
+                joined_own[:, columns] = jnp.where(core == 0, block, swapped)
+                joined_other[:, columns] = jnp.where(core == 0, swapped, block)
+
+    def add(joined, weight):
+        added = jnp.dot(joined[...], weight[...], preferred_element_type=jnp.float32)
+        done = (hidden[...].astype(jnp.float32) + added).astype(jnp.bfloat16)
+        out[...] = done
+        layer[column_block(step, core)] = done
+
+    @pl.when(step < 2)
+    def _():
+        add(joined_own, own)
+
+    @pl.when(step >= 2)
+    def _():
+        add(joined_other, other)
 
     @pl.when(step == layer.shape[0] - 1)
     def _():
@@ -331,37 +362,42 @@
         square = sum(jnp.sum(part * part, axis=1, keepdims=True) for part in parts)
         inverse = lax.rsqrt(square / (columns * len(parts)) + EPS)
         for at, part in enumerate(parts):
-            place = slice(at * columns, (at + 1) * columns)
-            normed[:, place] = (part * inverse * gain[:, place]).astype(jnp.bfloat16)
-
-
-def project(attended, weight, hidden, gain):
+            where = slice(at * columns, (at + 1) * columns)
+            normed[:, where] = (part * inverse * gain[:, where]).astype(jnp.bfloat16)
+
+
+def project(place, attended, halves, hidden, gain):
     tok, dim = hidden.shape
     columns = dim // 4
     return pl.pallas_call(
         project_kernel,
-        grid=(4,),
+        grid_spec=pltpu.PrefetchScalarGridSpec(
+            num_scalar_prefetch=1,
+            grid=(4,),
+            in_specs=[
+                pl.BlockSpec(attended.shape, lambda j, at: (0, 0, 0)),
+                pl.BlockSpec((dim, columns), lambda j, at: (0, jnp.minimum(j, 1))),
+                pl.BlockSpec((dim, columns), lambda j, at: (0, jnp.maximum(j - 2, 0))),
+                pl.BlockSpec((tok, columns), lambda j, at: (0, column_block(j, at[2]))),
+                pl.BlockSpec((1, dim), lambda j, at: (0, 0)),
+            ],
+            out_specs=(
+                pl.BlockSpec((tok, columns), lambda j, at: (0, column_block(j, at[2]))),
+                pl.BlockSpec((tok, dim), lambda j, at: (0, 0)),
+            ),
+            scratch_shapes=[
+                pltpu.VMEM((tok, dim), jnp.bfloat16),
+                pltpu.VMEM((tok, dim), jnp.bfloat16),
+                pltpu.VMEM((4, tok, columns), jnp.bfloat16),
+            ],
+        ),
         out_shape=(
             jax.ShapeDtypeStruct(hidden.shape, hidden.dtype),
             jax.ShapeDtypeStruct(hidden.shape, hidden.dtype),
         ),
-        in_specs=[
-            pl.BlockSpec(attended.shape, lambda j: (0, 0, 0)),
-            pl.BlockSpec((dim, columns), lambda j: (0, j)),
-            pl.BlockSpec((tok, columns), lambda j: (0, j)),
-            pl.BlockSpec((1, dim), lambda j: (0, 0)),
-        ],
-        out_specs=(
-            pl.BlockSpec((tok, columns), lambda j: (0, j)),
-            pl.BlockSpec((tok, dim), lambda j: (0, 0)),
-        ),
-        scratch_shapes=[
-            pltpu.VMEM((tok, dim), jnp.bfloat16),
-            pltpu.VMEM((4, tok, columns), jnp.bfloat16),
-        ],
-        compiler_params=pltpu.CompilerParams(vmem_limit_bytes=24 * 1024 * 1024),
+        compiler_params=pltpu.CompilerParams(vmem_limit_bytes=60 * 1024 * 1024),
         name="project",
-    )(attended, weight, hidden, gain)
+    )(place, attended, *halves, hidden, gain)
 
 
 def exchange(values):
@@ -420,18 +456,34 @@
         in_specs=[in_vmem, in_vmem, in_vmem, pl.BlockSpec(memory_space=pl.ANY)],
         out_specs=pl.BlockSpec((spans, extra, wide), lambda i: (0, height // extra - 1, 0)),
         input_output_aliases={3: 0},
-        compiler_params=pltpu.CompilerParams(vmem_limit_bytes=48 * 1024 * 1024),
+        compiler_params=pltpu.CompilerParams(vmem_limit_bytes=60 * 1024 * 1024),
         name="expert_rest",
     )(rows, gate_up, down_weight, main_block)
 
 
+def reorder(place, joined):
+    x, y, core = place[0], place[1], place[2]
+    wide = joined.shape[1] // 8
+    mine, theirs = [], []
+    for shift in (0, 3, 1, 2):
+        for turn in range(2):
+            block_no = lax.rem(x + shift, 4) * 2 + lax.rem(y + turn, 2)
+            block = joined[:, pl.ds(pl.multiple_of(block_no * wide, wide), wide)]
+            swapped = jnp.concatenate([block[:, wide // 2 :], block[:, : wide // 2]], axis=1)
+            mine.append(jnp.where(core == 0, block, swapped))
+            theirs.append(jnp.where(core == 0, swapped, block))
+    return jnp.concatenate(mine, axis=1), jnp.concatenate(theirs, axis=1)
+
+
 def finish_kernel(
+    place,
     main_share,
     rest_share,
     main_rows,
     rest_rows,
     stream,
-    next_weight,
+    next_own,
+    next_other,
     norm_gain,
     head_gain,
     cosine,
@@ -439,6 +491,7 @@
     out,
     next_rows,
     layer,
+    joined,
 ):
     tok = stream.shape[0]
     count = main_share.shape[1]
@@ -461,60 +514,83 @@
         parts = [layer[at].astype(jnp.float32) for at in range(layer.shape[0])]
         square = sum(jnp.sum(part * part, axis=1, keepdims=True) for part in parts)
         inverse = lax.rsqrt(square / (wide * len(parts)) + EPS)
-        raw = jnp.zeros((tok, next_weight.shape[1]), jnp.float32)
         for at, part in enumerate(parts):
             columns = slice(at * wide, (at + 1) * wide)
             normed = (part * inverse * norm_gain[:, columns]).astype(jnp.bfloat16)
-            raw += jnp.dot(normed, next_weight[columns, :], preferred_element_type=jnp.float32)
-        half = raw.shape[1] // 2
+            joined[:, columns] = normed
+        mine, theirs = reorder(place, joined)
+        raw_own = jnp.dot(mine, next_own[...], preferred_element_type=jnp.float32)
+        raw_other = jnp.dot(theirs, next_other[...], preferred_element_type=jnp.float32)
+        keys = jnp.where(place[2] == 0, raw_own, raw_other)
+        values = jnp.where(place[2] == 0, raw_other, raw_own)
+        half = keys.shape[1]
         for head in range(half // hd):
             columns = slice(head * hd, (head + 1) * hd)
-            values = raw[:, columns]
-            values = values * lax.rsqrt(jnp.mean(values * values, axis=-1, keepdims=True) + EPS)
-            values = values * head_gain[...]
-            values = values * cosine[...] + pltpu.roll(values, hd // 2, 1) * sine[...]
-            next_rows[:, columns] = values.astype(jnp.bfloat16)
-        next_rows[:, half:] = raw[:, half:].astype(jnp.bfloat16)
-
-
-def finish(main_share, rest_share, returned, stream, late, norm_gain, head_gain, cos, sin):
+            key = keys[:, columns]
+            key = key * lax.rsqrt(jnp.mean(key * key, axis=-1, keepdims=True) + EPS)
+            key = key * head_gain[...]
+            key = key * cosine[...] + pltpu.roll(key, hd // 2, 1) * sine[...]
+            next_rows[:, columns] = key.astype(jnp.bfloat16)
+        next_rows[:, half:] = values.astype(jnp.bfloat16)
+
+
+def finish(place, main_share, rest_share, returned, stream, halves, norm_gain, head_gain, turns):
     devices, height, wide = returned.shape
     tok, dim = stream.shape
-    extra = late.shape[1] - dim
+    extra = halves[0].shape[1] - dim // 2
     chunks = dim // wide
     rows = height // (chunks + 1)
     shape = main_share.shape
 
     def fixed(values):
-        return pl.BlockSpec(values.shape, lambda j: (0, 0))
-
+        return pl.BlockSpec(values.shape, lambda j, at: (0, 0))
+
+    next_spec = pl.BlockSpec((dim, extra), lambda j, at: (0, dim // 2 // extra))
     return pl.pallas_call(
         finish_kernel,
-        grid=(chunks,),
+        grid_spec=pltpu.PrefetchScalarGridSpec(
+            num_scalar_prefetch=1,
+            grid=(chunks,),
+            in_specs=[
+                fixed(main_share),
+                pl.BlockSpec((1,) + shape, lambda j, at: (j, 0, 0)),
+                pl.BlockSpec((devices, rows, wide), lambda j, at: (0, j, 0)),
+                pl.BlockSpec((devices, rows, wide), lambda j, at: (0, chunks, 0)),
+                pl.BlockSpec((tok, wide), lambda j, at: (0, j)),
+                next_spec,
+                next_spec,
+                fixed(norm_gain),
+                fixed(head_gain),
+                fixed(turns[0]),
+                fixed(turns[1]),
+            ],
+            out_specs=(
+                pl.BlockSpec((tok, wide), lambda j, at: (0, j)),
+                pl.BlockSpec((tok, 2 * extra), lambda j, at: (0, 0)),
+            ),
+            scratch_shapes=[
+                pltpu.VMEM((chunks, tok, wide), jnp.bfloat16),
+                pltpu.VMEM((tok, dim), jnp.bfloat16),
+            ],
+        ),
         out_shape=(
             jax.ShapeDtypeStruct(stream.shape, stream.dtype),
-            jax.ShapeDtypeStruct((tok, extra), stream.dtype),
+            jax.ShapeDtypeStruct((tok, 2 * extra), stream.dtype),
         ),
-        in_specs=[
-            fixed(main_share),
-            pl.BlockSpec((1,) + shape, lambda j: (j, 0, 0)),
-            pl.BlockSpec((devices, rows, wide), lambda j: (0, j, 0)),
-            pl.BlockSpec((devices, rows, wide), lambda j: (0, chunks, 0)),
-            pl.BlockSpec((tok, wide), lambda j: (0, j)),
-            pl.BlockSpec((dim, extra), lambda j: (0, dim // extra)),
-            fixed(norm_gain),
-            fixed(head_gain),
-            fixed(cos),
-            fixed(sin),
-        ],
-        out_specs=(
-            pl.BlockSpec((tok, wide), lambda j: (0, j)),
-            pl.BlockSpec((tok, extra), lambda j: (0, 0)),
-        ),
-        scratch_shapes=[pltpu.VMEM((chunks, tok, wide), jnp.bfloat16)],
-        compiler_params=pltpu.CompilerParams(vmem_limit_bytes=32 * 1024 * 1024),
+        compiler_params=pltpu.CompilerParams(vmem_limit_bytes=60 * 1024 * 1024),
         name="finish",
-    )(main_share, rest_share, returned, returned, stream, late, norm_gain, head_gain, cos, sin)
+    )(
+        place,
+        main_share,
+        rest_share,
+        returned,
+        returned,
+        stream,
+        *halves,
+        norm_gain,
+        head_gain,
+        *turns,
+    )
 
 
 def per_device(
@@ -584,13 +660,26 @@
     packed = lax.all_to_all(packed, "mp", split_axis=0, concat_axis=0, tiled=True)
     packed = packed.reshape(mp_size * own_rows, -1)
     late_width = dim + next_weight.shape[1]
-    late = lax.all_gather(packed[:, :late_width], "dp", axis=0, tiled=True)
+    dp_at = lax.axis_index("dp")
+    core = lax.rem(dp_at, 2)
+    place = jnp.stack([dp_at // 4, lax.rem(dp_at // 2, 2), core]).astype(jnp.int32)
+
+    def swap(values, bit):
+        return lax.ppermute(values, "dp", [(j, j ^ bit) for j in range(dp_size)])
+
+    def shift_x(values, step):
+        moves = [(j, (j + 4 * step) % dp_size) for j in range(dp_size)]
+        return lax.ppermute(values, "dp", moves)
+
+    low, high = packed[:, : late_width // 2], packed[:, late_width // 2 : late_width]
+    kept = jnp.where(core == 0, low, high)
+    late = jnp.concatenate([kept, swap(jnp.where(core == 0, high, low), 1)], axis=0)
+    late = jnp.concatenate([late, swap(late, 2)], axis=0)
     early = packed[:, late_width:].reshape(packed.shape[0], 2, 2 * hd).transpose(1, 0, 2)
     early = jnp.broadcast_to(early[None], (dp_size // 2,) + early.shape)
     early = early.reshape(dp_size, packed.shape[0], 2 * hd)
     early = lax.all_to_all(early, "dp", split_axis=0, concat_axis=0, tiled=True)
     early = early.reshape(dim, 2 * hd)
-    weights = (early, lax.ppermute(early, "dp", [(j, j ^ 1) for j in range(dp_size)]))
     sides = [left, right, shift(across, 1), shift(across, -1)]
     far = [shift(left, 1), shift(sides[3], -1)]
     tables = (
@@ -603,10 +692,15 @@
         leaf_slot,
     )
     path = pack_paths(tables, root_cache, mid_cache, leaf_cache, mp_size)
-    path, sides = lax.optimization_barrier((path, sides))
+    path, sides, late, early = lax.optimization_barrier((path, sides, late, early))
+    weights = (early, swap(early, 1))
+    x_left = shift_x(late, 1)
+    x_right = shift_x(late, -1)
     path = lax.all_to_all(path, "mp", split_axis=0, concat_axis=0, tiled=True)
     own_piece = jnp.sum(path.astype(jnp.float32), axis=0).astype(jnp.bfloat16)
-    own_piece, far = lax.optimization_barrier((own_piece, far))
+    own_piece, far, x_left, x_right = lax.optimization_barrier((own_piece, far, x_left, x_right))
+    middle = x_left.shape[0] // 2
+    x_far = [shift_x(x_left[:middle], 1), shift_x(x_right[middle:], -1)]
     pieces = [own_piece] + [
         lax.ppermute(own_piece, "mp", [(j, j ^ s) for j in range(mp_size)]) for s in range(1, 4)
     ]
@@ -619,10 +713,13 @@
         ]
     ).astype(jnp.int32)
     attended = attend(meta, rows, weights, pieces, head_gains, cosine, sine)
+    attended, x_far = lax.optimization_barrier((attended, x_far))
+    own_half = jnp.concatenate([late, x_left, x_right] + x_far, axis=0)
+    halves = (own_half, swap(own_half, 1))
     attended = lax.all_to_all(
         attended.reshape(mp_size, tok, 2 * hd), "mp", split_axis=0, concat_axis=0, tiled=True
     )
-    after_attention, moe_in = project(attended, late, hidden, norm_gains[1:2])
+    after_attention, moe_in = project(place, attended, halves, hidden, norm_gains[1:2])
 
     top_k = expert_ids.shape[1]
     capacity = max(2, 5 * tok * top_k // (4 * devices))
@@ -667,15 +764,15 @@
     my_cos = lax.dynamic_slice_in_dim(cosine, me * tok, tok)
     my_sin = lax.dynamic_slice_in_dim(sine, me * tok, tok)
     layer_out, next_rows = finish(
+        place,
         main_share,
         rest_share,
         returned,
         after_attention,
-        late,
+        halves,
         norm_gains[2:3],
         head_gains[2:3],
-        my_cos,
-        my_sin,
+        (my_cos, my_sin),
     )
     return (layer_out, next_rows)
 

time: 361 us -> 351 us (0.972)
  blocking collectives: 19.3 us -> 0 us
  between operations: 15.8 us -> 2.71 us
  starting transfers between devices: 52.9 us -> 63.6 us
  Pallas kernels: 40.7 us -> 51.4 us
  local copies, waits for them, and re-layouts: 32.3 us -> 26.8 us
  other arithmetic: 12.4 us -> 16.8 us
    all_to_all x1, waiting for transfers between devices: 28.6 us -> 7.43 us  [per_device(): path = lax.all_to_all(path, 'mp', split_axis=0, concat_axis=0, tiled=True)]
    ppermute x1 -> x8, waiting for transfers between devices: 0.01 us -> 19.6 us  [the longest x4 19.6 us: swap(): return lax.ppermute(values, 'dp', [(j, j ^ bit) for j in range(dp_size)])]
    all_to_all x1 -> x0, blocking collectives: 19.3 us -> none  [per_device(): lax.all_to_all(packed, 'mp', split_axis=0, concat_axis=0, tiled=True)]
    unnamed x74 -> x66, local copies, waits for them, and re-layouts: 19.5 us -> 8.85 us
    ppermute x1 -> x8, starting transfers between devices: 0.09 us -> 9.74 us  [the longest x4 6.19 us: shift_x(): return lax.ppermute(values, 'dp', moves)]
    all_to_all x0 -> x1, waiting for transfers between devices: none -> 9.25 us  [per_device(): lax.all_to_all(packed, 'mp', split_axis=0, concat_axis=0, tiled=True)]
    pallas_call x2, Pallas kernels: 9.34 us -> 16.5 us  [the longest x1 8.95 us: finish(): pl.pallas_call(finish_kernel, grid_spec=pltpu.PrefetchScalarGridSpec(num_...]
    all_to_all x0 -> x1, starting transfers between devices: none -> 6.41 us  [per_device(): lax.all_to_all(packed, 'mp', split_axis=0, concat_axis=0, tiled=True)]
  transfers between devices with their start and end apart: 18 -> 25, of which waited for: 10 -> 9; matrix products, arithmetic and copies ran while one was open for 11% -> 15% of each run, Pallas kernels for 6% -> 7%
where the time goes in v5:
time: 351 us; the launch traced here: 350 us
  waiting for transfers between devices  170 us (48%)
  starting transfers between devices  63.6 us (18%)
  Pallas kernels  51.4 us (15%)
  local copies, waits for them, and re-layouts  26.8 us (8%)
  matrix products  18.8 us (5%)
  other arithmetic  16.8 us (5%)
    all_to_all x3, waiting for transfers between devices, exchange(): return lax.all_to_all(values, BOTH, split_axis=0, concat_axis=0, tiled=True)  110 us
    pallas_call x1, Pallas kernels, attend(): pl.pallas_call(attention_kernel, out_shape=jax.ShapeDtypeStruct((group, 2...  22.7 us
    ppermute x4, waiting for transfers between devices, swap(): return lax.ppermute(values, 'dp', [(j, j ^ bit) for j in range(dp_size)])  19.6 us
    all_to_all x3, starting transfers between devices, exchange(): return lax.all_to_all(values, BOTH, split_axis=0, concat_axis=0, tiled=True)  18.6 us
    ppermute x6, waiting for transfers between devices, shift(): return lax.ppermute(values, 'mp', moves)  10.6 us
    dot_general x1, matrix products, expert(): both = jnp.dot(rows, gate_up, preferred_element_type=jnp.float32)  10.1 us
    all_to_all x1, waiting for transfers between devices, per_device(): lax.all_to_all(packed, 'mp', split_axis=0, concat_axis=0, tiled=True)  9.25 us
    pallas_call x1, Pallas kernels, finish(): pl.pallas_call(finish_kernel, grid_spec=pltpu.PrefetchScalarGridSpec(num_...  8.95 us
  transfers between devices with their start and end apart: 25, of which 9 were waited for; matrix products, arithmetic and copies ran while one was open for 15% of the time, Pallas kernels for 7%

profile of v5, /device:TPU:0, one launch (start us, length us, event | category | flops | bytes accessed | tf_op | source)
XLA Modules:
  0.0 349.9 jit_solution(11067470111863716502)
XLA Ops:
  0.6 1.9 pack_weights.1
  2.5 6.4 %all-to-all-start = ((bf16[8,16,3072]{2,1,0:T(8,128)(2,1)}), bf16[8,16,3072]{2,1,0:T(8,128)(2,1)S(1)}, u32[]{:S(2)}, u32[]{:S(2)}) async-start(bf16[8,16,3072]{2,1,0:T(8,128)(2,1)} %pack_weights.1), calls=%async_computation | async-start | bytes 1572864 | tf_op jit(solution)/shard_map/all_to_all | solution.py:660
  9.0 1.2 fusion.6
  10.2 1.5 fusion.32
  11.7 9.3 %all-to-all-done = bf16[8,16,3072]{2,1,0:T(8,128)(2,1)S(1)} async-done(((bf16[8,16,3072]{2,1,0:T(8,128)(2,1)}), bf16[8,16,3072]{2,1,0:T(8,128)(2,1)S(1)}, u32[]{:S(2)}, u32[]{:S(2)}) %all-to-all-start) | async-done | bytes 786464 | tf_op jit(solution)/shard_map/all_to_all | solution.py:660
  22.8 1.5 collective-permute-start
  25.4 6.9 %all-to-all-start.1 = ((bf16[16,128,256]{2,1,0:T(8,128)(2,1)}), bf16[16,128,256]{2,1,0:T(8,128)(2,1)}, u32[]{:S(2)}, u32[]{:S(2)}) async-start(bf16[16,128,256]{2,1,0:T(8,128)(2,1)} %bitcast.18), calls=%async_computation.1 | async-start | bytes 2097152 | tf_op jit(solution)/shard_map/all_to_all | solution.py:681
  32.4 3.5 collective-permute-start.6
  36.8 2.4 collective-permute-start.2
  40.9 1.6 collective-permute-start.3
  42.7 2.2 pack_paths.1
  45.3 19.6 %collective-permute-done.6 = bf16[256,1280]{1,0:T(8,128)(2,1)S(1)} collective-permute-done((bf16[256,1280]{1,0:T(8,128)(2,1)S(1)}, bf16[256,1280]{1,0:T(8,128)(2,1)S(1)}, u32[]{:S(2)}, u32[]{:S(2)}) %collective-permute-start.6) | collective-permute-done | bytes 655392 | tf_op jit(solution)/shard_map/ppermute | solution.py:668
  66.1 3.6 %all-to-all-start.2 = ((bf16[8,448,256]{2,1,0:T(8,128)(2,1)}), bf16[8,448,256]{2,1,0:T(8,128)(2,1)S(1)}, u32[]{:S(2)}, u32[]{:S(2)}) async-start(bf16[8,448,256]{2,1,0:T(8,128)(2,1)} %pack_paths.1), calls=%async_computation.2 | async-start | bytes 3670016 | tf_op jit(solution)/shard_map/all_to_all | solution.py:699
  69.9 2.8 collective-permute-start.10
  75.6 1.3 add_convert_fusion
  77.0 1.9 fusion.13
  78.9 2.0 collective-permute-start.7
  80.9 1.3 collective-permute-start.8
  82.2 1.2 pad_add_fusion.2.meta
  83.5 1.3 pad_maximum_fusion.3
  86.0 7.4 %all-to-all-done.2 = bf16[8,448,256]{2,1,0:T(8,128)(2,1)S(1)} async-done(((bf16[8,448,256]{2,1,0:T(8,128)(2,1)}), bf16[8,448,256]{2,1,0:T(8,128)(2,1)S(1)}, u32[]{:S(2)}, u32[]{:S(2)}) %all-to-all-start.2) | async-done | bytes 1835040 | tf_op jit(solution)/shard_map/all_to_all | solution.py:699
  93.7 10.6 %collective-permute-done.7.own_far = bf16[128,2048]{1,0:T(8,128)(2,1)} collective-permute-done((bf16[128,2048]{1,0:T(8,128)(2,1)}, bf16[128,2048]{1,0:T(8,128)(2,1)}, u32[]{:S(2)}, u32[]{:S(2)}) %collective-permute-start.7) | collective-permute-done | bytes 524320 | tf_op jit(solution)/shard_map/ppermute | solution.py:654
  104.3 1.4 collective-permute-start.12
  105.8 2.7 collective-permute-start.13
  110.8 3.3 collective-permute-start.16
  114.1 2.5 constant_dynamic-update-slice_fusion.3
  117.3 2.5 constant_dynamic-update-slice_fusion.2
  119.8 4.1 %collective-permute-done.14.piece_3 = bf16[448,256]{1,0:T(8,128)(2,1)S(1)} collective-permute-done((bf16[448,256]{1,0:T(8,128)(2,1)S(1)}, bf16[448,256]{1,0:T(8,128)(2,1)S(1)}, u32[]{:S(2)}, u32[]{:S(2)}) %collective-permute-start.14) | collective-permute-done | bytes 229408 | tf_op jit(solution)/shard_map/ppermute | solution.py:705
  124.6 22.7 %tree_attention.1 = bf16[1024,256]{1,0:T(8,128)(2,1)} custom-call(s32[9]{0:T(128)} %pad_add_fusion.2.meta, bf16[128,2048]{1,0:T(8,128)(2,1)} %fusion.8.own, bf16[128,2048]{1,0:T(8,128)(2,1)} %collective-permute-done.across, bf16[128,2048]{1,0:T(8,128)(2,1)} %collective-permute-done.1.own_left, bf16[128,2048]{1,0:T(8,128)(2,1)} %collective-permute-done.2.own_right, ...), custom_call_target="tpu_custom_call" | custom-call | flops 2147483648 | bytes 8388608 | tf_op jit(solution)/shard_map/tree_attention/pallas_call | solution.py:297
  149.2 3.5 all-to-all-start.3
  154.0 8.7 %all-to-all-done.3.attended = bf16[8,128,256]{2,1,0:T(8,128)(2,1)S(1)} async-done(((bf16[8,128,256]{2,1,0:T(8,128)(2,1)}), bf16[8,128,256]{2,1,0:T(8,128)(2,1)S(1)}, u32[]{:S(2)}, u32[]{:S(2)}) %all-to-all-start.3) | async-done | bytes 524320 | tf_op jit(solution)/shard_map/all_to_all | solution.py:719
  163.5 7.6 %project.1 = (bf16[128,2048]{1,0:T(8,128)(2,1)}, bf16[128,2048]{1,0:T(8,128)(2,1)}) custom-call(s32[3]{0:T(128)} %pad_add_fusion.1.place, bf16[8,128,256]{2,1,0:T(8,128)(2,1)} %copy-done.18, bf16[2048,1280]{1,0:T(8,128)(2,1)} %constant_dynamic-update-slice_fusion.own.next_own, bf16[2048,1280]{1,0:T(8,128)(2,1)} %collective-permute-done.17.other.next_other, ...), custom_call_target="tpu_custom_call" | custom-call | tf_op jit(solution)/shard_map/project/pallas_call | solution.py:372
  171.1 4.3 %convert_bitcast_fusion = bf16[128,8,2048]{2,1,0:T(8,128)(2,1)} fusion(bf16[128,2048]{1,0:T(8,128)(2,1)} %get-tuple-element.38, s32[1024]{0:T(1024)S(1)} %eq.180, s32[128,128]{1,0:T(8,128)S(1)} %copy.68), kind=kOutput, calls=%fused_computation.2 | convolution fusion | flops 539099136 | bytes 4788224 | tf_op jit(solution)/shard_map/dot_general | solution.py:746
  175.4 6.0 %all-to-all-start.4 = ((bf16[128,8,2048]{2,1,0:T(8,128)(2,1)}), bf16[128,8,2048]{2,1,0:T(8,128)(2,1)}, u32[]{:S(2)}, u32[]{:S(2)}) async-start(bf16[128,8,2048]{2,1,0:T(8,128)(2,1)} %convert_bitcast_fusion), calls=%async_computation.4 | async-start | bytes 8388608 | tf_op jit(solution)/shard_map/all_to_all | solution.py:404
  182.0 1.5 reshape.153
  183.6 50.4 %all-to-all-done.4 = bf16[128,8,2048]{2,1,0:T(8,128)(2,1)} async-done(((bf16[128,8,2048]{2,1,0:T(8,128)(2,1)}), bf16[128,8,2048]{2,1,0:T(8,128)(2,1)}, u32[]{:S(2)}, u32[]{:S(2)}) %all-to-all-start.4) | async-done | bytes 4194336 | tf_op jit(solution)/shard_map/all_to_all | solution.py:404
  234.0 4.8 %all-to-all-start.5 = ((bf16[128,2,2048]{2,1,0:T(2,128)(2,1)}), bf16[128,2,2048]{2,1,0:T(2,128)(2,1)S(1)}, u32[]{:S(2)}, u32[]{:S(2)}) async-start(bf16[128,2,2048]{2,1,0:T(2,128)(2,1)} %reshape.153), calls=%async_computation.5 | async-start | bytes 2097152 | tf_op jit(solution)/shard_map/all_to_all | solution.py:404
  238.9 10.1 %fusion = f32[1024,1536]{1,0:T(8,128)S(1)} fusion(bf16[128,8,2048]{2,1,0:T(8,128)(2,1)} %all-to-all-done.4, bf16[1,2048,1536]{2,1,0:T(8,128)(2,1)} %param.30), kind=kOutput, calls=%fused_computation | convolution fusion | flops 6442450944 | bytes 16777216 | tf_op jit(solution)/shard_map/dot_general | solution.py:409
  249.0 3.7 %convolution_convert_fusion = bf16[1024,2048]{1,0:T(8,128)(2,1)S(1)} fusion(f32[1024,1536]{1,0:T(8,128)S(1)} %fusion, bf16[1,768,2048]{2,1,0:T(8,128)(2,1)S(1)} %copy-done.17), kind=kOutput, calls=%fused_computation.3 | convolution fusion | flops 3228041216 | bytes 13631488 | tf_op jit(solution)/shard_map/dot_general | solution.py:411
  252.8 2.8 pad.4.main_block
  255.6 2.2 all-to-all-done.5
  259.0 8.0 %expert_rest.1 = bf16[128,40,512]{2,1,0:T(8,128)(2,1)} custom-call(bf16[256,2048]{1,0:T(8,128)(2,1)} %reshape.157.rows, bf16[2048,1536]{1,0:T(8,128)(2,1)} %bitcast.50, bf16[768,2048]{1,0:T(8,128)(2,1)} %bitcast.52, bf16[128,40,512]{2,1,0:T(8,128)(2,1)} %pad.4.main_block), custom_call_target="tpu_custom_call", output_to_operand_aliasing={{}: (3, {})} | custom-call | tf_op jit(solution)/shard_map/expert_rest/pallas_call | solution.py:452
  267.1 7.8 %all-to-all-start.6 = ((bf16[128,40,512]{2,1,0:T(8,128)(2,1)}), bf16[128,40,512]{2,1,0:T(8,128)(2,1)}, u32[]{:S(2)}, u32[]{:S(2)}) async-start(bf16[128,40,512]{2,1,0:T(8,128)(2,1)} %expert_rest.1), calls=%async_computation.6 | async-start | bytes 10485760 | tf_op jit(solution)/shard_map/all_to_all | solution.py:404
  274.9 1.3 slice.59.head_gain
  279.1 1.2 copy.64
  282.1 1.6 broadcast_multiply_fusion.rest_share
  283.7 57.3 %all-to-all-done.6.main_rows.rest_rows = bf16[128,40,512]{2,1,0:T(8,128)(2,1)} async-done(((bf16[128,40,512]{2,1,0:T(8,128)(2,1)}), bf16[128,40,512]{2,1,0:T(8,128)(2,1)}, u32[]{:S(2)}, u32[]{:S(2)}) %all-to-all-start.6) | async-done | bytes 5242912 | tf_op jit(solution)/shard_map/all_to_all | solution.py:404
  341.0 8.9 %finish.1 = (bf16[128,2048]{1,0:T(8,128)(2,1)}, bf16[128,512]{1,0:T(8,128)(2,1)}) custom-call(s32[3]{0:T(128)} %pad_add_fusion.1.place, bf16[256,1024]{1,0:T(8,128)(2,1)} %pad_maximum_fusion.2.main_share, bf16[4,256,1024]{2,1,0:T(8,128)(2,1)} %broadcast_multiply_fusion.rest_share, bf16[128,40,512]{2,1,0:T(8,128)(2,1)} %all-to-all-done.6.main_rows.rest_rows, ...), custom_call_target="tpu_custom_call" | custom-call | tf_op jit(solution)/shard_map/finish/pallas_call | solution.py:549
  (145 shorter events, 24.7 us)
Async XLA Ops:
  0.6 21.1 %copy-start.10 = (bf16[128,2048]{1,0:T(8,128)(2,1)S(1)}, bf16[128,2048]{1,0:T(8,128)(2,1)}, u32[]{:S(2)}) copy-start(bf16[128,2048]{1,0:T(8,128)(2,1)} %hidden.1) | copy-start | bytes 1572868
  2.5 18.4 %all-to-all-start = ((bf16[8,16,3072]{2,1,0:T(8,128)(2,1)}), bf16[8,16,3072]{2,1,0:T(8,128)(2,1)S(1)}, u32[]{:S(2)}, u32[]{:S(2)}) async-start(bf16[8,16,3072]{2,1,0:T(8,128)(2,1)} %pack_weights.1), calls=%async_computation | async-start | bytes 1572864 | tf_op jit(solution)/shard_map/all_to_all | solution.py:660
  21.7 10.7 %collective-permute-start.5 = (bf16[128,1280]{1,0:T(8,128)(2,1)}, bf16[128,1280]{1,0:T(8,128)(2,1)S(1)}, u32[]{:S(2)}, u32[]{:S(2)}) collective-permute-start(bf16[128,1280]{1,0:T(8,128)(2,1)} %get-tuple-element.51), channel_id=1, source_target_pairs={{0,8},{8,0},{16,24},{24,16},{32,40},{40,32},{48,56},{56,48},{64,72... | collective-permute-start | bytes 983048 | tf_op jit(solution)/shard_map/ppermute | solution.py:668
  21.7 17.4 %copy-start.3 = (s32[1024]{0:T(1024)S(1)}, s32[1024]{0:T(1024)}, u32[]{:S(2)}) copy-start(s32[1024]{0:T(1024)} %token_request.1) | copy-start | bytes 12292
  21.7 20.8 %copy-start.6 = (s32[32]{0:T(128)S(1)}, s32[32]{0:T(128)}, u32[]{:S(2)}) copy-start(s32[32]{0:T(128)} %request_leaf.1) | copy-start | bytes 388
  21.7 20.9 %copy-start = (bf16[1,512,512]{2,1,0:T(8,128)(2,1)S(1)}, bf16[1,512,512]{2,1,0:T(8,128)(2,1)}, u32[]{:S(2)}) copy-start(bf16[1,512,512]{2,1,0:T(8,128)(2,1)} %root.1) | copy-start | bytes 1572868
  21.7 20.9 %copy-start.1 = (bf16[1,256,512]{2,1,0:T(8,128)(2,1)S(1)}, bf16[1,256,512]{2,1,0:T(8,128)(2,1)}, u32[]{:S(2)}) copy-start(bf16[1,256,512]{2,1,0:T(8,128)(2,1)} %mid.1) | copy-start | bytes 786436
  21.7 20.9 %copy-start.2 = (bf16[2,128,512]{2,1,0:T(8,128)(2,1)S(1)}, bf16[2,128,512]{2,1,0:T(8,128)(2,1)}, u32[]{:S(2)}) copy-start(bf16[2,128,512]{2,1,0:T(8,128)(2,1)} %leaf.1) | copy-start | bytes 786436
  21.8 20.9 %copy-start.4 = (s32[16]{0:T(128)S(1)}, s32[16]{0:T(128)}, u32[]{:S(2)}) copy-start(s32[16]{0:T(128)} %leaf_parent.1) | copy-start | bytes 196
  21.8 20.9 %copy-start.5 = (s32[8]{0:T(128)S(1)}, s32[8]{0:T(128)}, u32[]{:S(2)}) copy-start(s32[8]{0:T(128)} %mid_parent.1) | copy-start | bytes 100
  21.8 20.9 %copy-start.7 = (s32[8]{0:T(128)S(1)}, s32[8]{0:T(128)}, u32[]{:S(2)}) copy-start(s32[8]{0:T(128)} %root_slot.1) | copy-start | bytes 100
  21.8 20.9 %copy-start.8 = (s32[8]{0:T(128)S(1)}, s32[8]{0:T(128)}, u32[]{:S(2)}) copy-start(s32[8]{0:T(128)} %mid_slot.1) | copy-start | bytes 100
  21.8 20.9 %copy-start.9 = (s32[16]{0:T(128)S(1)}, s32[16]{0:T(128)}, u32[]{:S(2)}) copy-start(s32[16]{0:T(128)} %leaf_slot.1) | copy-start | bytes 196
  22.8 17.6 %collective-permute-start = (bf16[128,2048]{1,0:T(8,128)(2,1)}, bf16[128,2048]{1,0:T(8,128)(2,1)}, u32[]{:S(2)}, u32[]{:S(2)}) collective-permute-start(bf16[128,2048]{1,0:T(8,128)(2,1)} %fusion.8.own), channel_id=1, source_target_pairs={{0,4},{1,5},{2,6},{3,7},{4,0},{5,1},{6,2},{7,3},{8,12},{9,13},{10,... | collective-permute-start | bytes 1572872 | tf_op jit(solution)/shard_map/ppermute | solution.py:656
  25.4 19.5 %copy-start.27 = (s32[16]{0:T(128)S(1)}, s32[16]{0:T(128)}, u32[]{:S(2)}) copy-start(s32[16]{0:T(128)} %param.41) | copy-start | bytes 196
  25.4 19.7 %copy-start.28 = (s32[8]{0:T(128)S(1)}, s32[8]{0:T(128)}, u32[]{:S(2)}) copy-start(s32[8]{0:T(128)} %param.40) | copy-start | bytes 100
  25.4 40.6 %all-to-all-start.1 = ((bf16[16,128,256]{2,1,0:T(8,128)(2,1)}), bf16[16,128,256]{2,1,0:T(8,128)(2,1)}, u32[]{:S(2)}, u32[]{:S(2)}) async-start(bf16[16,128,256]{2,1,0:T(8,128)(2,1)} %bitcast.18), calls=%async_computation.1 | async-start | bytes 2097152 | tf_op jit(solution)/shard_map/all_to_all | solution.py:681
  32.4 12.9 %copy-start.20 = (bf16[128,1280]{1,0:T(8,128)(2,1)}, bf16[128,1280]{1,0:T(8,128)(2,1)S(1)}, u32[]{:S(2)}) copy-start(bf16[128,1280]{1,0:T(8,128)(2,1)S(1)} %collective-permute-done.5) | copy-start | bytes 983044
  32.4 32.5 %collective-permute-start.6 = (bf16[256,1280]{1,0:T(8,128)(2,1)S(1)}, bf16[256,1280]{1,0:T(8,128)(2,1)S(1)}, u32[]{:S(2)}, u32[]{:S(2)}) collective-permute-start(bf16[256,1280]{1,0:T(8,128)(2,1)S(1)} %pad_maximum_fusion.1), channel_id=1, source_target_pairs={{0,16},{8,24},{16,0},{24,8},{32,48},{40,56},{48,32},{56,40},{64,80... | collective-permute-start | bytes 1966088 | tf_op jit(solution)/shard_map/ppermute | solution.py:668
  35.9 30.1 %collective-permute-start.1 = (bf16[128,2048]{1,0:T(8,128)(2,1)}, bf16[128,2048]{1,0:T(8,128)(2,1)}, u32[]{:S(2)}, u32[]{:S(2)}) collective-permute-start(bf16[128,2048]{1,0:T(8,128)(2,1)} %fusion.8.own), channel_id=1, source_target_pairs={{0,1},{1,2},{2,3},{3,0},{4,5},{5,6},{6,7},{7,4},{8,9},{9,10},{10,1... | collective-permute-start | bytes 1572872 | tf_op jit(solution)/shard_map/ppermute | solution.py:654
  36.8 29.3 %collective-permute-start.2 = (bf16[128,2048]{1,0:T(8,128)(2,1)}, bf16[128,2048]{1,0:T(8,128)(2,1)}, u32[]{:S(2)}, u32[]{:S(2)}) collective-permute-start(bf16[128,2048]{1,0:T(8,128)(2,1)} %fusion.8.own), channel_id=1, source_target_pairs={{0,3},{1,0},{2,1},{3,2},{4,7},{5,4},{6,5},{7,6},{8,11},{9,8},{10,9... | collective-permute-start | bytes 1572872 | tf_op jit(solution)/shard_map/ppermute | solution.py:654
  40.4 25.7 %collective-permute-start.4 = (bf16[128,2048]{1,0:T(8,128)(2,1)}, bf16[128,2048]{1,0:T(8,128)(2,1)}, u32[]{:S(2)}, u32[]{:S(2)}) collective-permute-start(bf16[128,2048]{1,0:T(8,128)(2,1)} %collective-permute-done.across), channel_id=1, source_target_pairs={{0,3},{1,0},{2,1},{3,2},{4,7},{5,4},{6,5},{7,6},{8,11},{9,8},{10,9... | collective-permute-start | bytes 1572872 | tf_op jit(solution)/shard_map/ppermute | solution.py:654
  40.9 25.2 %collective-permute-start.3 = (bf16[128,2048]{1,0:T(8,128)(2,1)}, bf16[128,2048]{1,0:T(8,128)(2,1)}, u32[]{:S(2)}, u32[]{:S(2)}) collective-permute-start(bf16[128,2048]{1,0:T(8,128)(2,1)} %collective-permute-done.across), channel_id=1, source_target_pairs={{0,1},{1,2},{2,3},{3,0},{4,5},{5,6},{6,7},{7,4},{8,9},{9,10},{10,1... | collective-permute-start | bytes 1572872 | tf_op jit(solution)/shard_map/ppermute | solution.py:654
  45.3 24.4 %copy-start.29 = (s32[8]{0:T(128)S(1)}, s32[8]{0:T(128)}, u32[]{:S(2)}) copy-start(s32[8]{0:T(128)} %param.39) | copy-start | bytes 100
  66.1 27.3 %all-to-all-start.2 = ((bf16[8,448,256]{2,1,0:T(8,128)(2,1)}), bf16[8,448,256]{2,1,0:T(8,128)(2,1)S(1)}, u32[]{:S(2)}, u32[]{:S(2)}) async-start(bf16[8,448,256]{2,1,0:T(8,128)(2,1)} %pack_paths.1), calls=%async_computation.2 | async-start | bytes 3670016 | tf_op jit(solution)/shard_map/all_to_all | solution.py:699
  69.9 34.4 %collective-permute-start.10 = (bf16[512,1280]{1,0:T(8,128)(2,1)S(1)}, bf16[512,1280]{1,0:T(8,128)(2,1)}, u32[]{:S(2)}, u32[]{:S(2)}) collective-permute-start(bf16[512,1280]{1,0:T(8,128)(2,1)S(1)} %pad_maximum_fusion), channel_id=1, source_target_pairs={{0,96},{8,104},{16,112},{24,120},{32,0},{40,8},{48,16},{56,24},{64... | collective-permute-start | bytes 3932168 | tf_op jit(solution)/shard_map/ppermute | solution.py:672
  72.7 31.6 %collective-permute-start.9 = (bf16[512,1280]{1,0:T(8,128)(2,1)S(1)}, bf16[512,1280]{1,0:T(8,128)(2,1)}, u32[]{:S(2)}, u32[]{:S(2)}) collective-permute-start(bf16[512,1280]{1,0:T(8,128)(2,1)S(1)} %pad_maximum_fusion), channel_id=1, source_target_pairs={{0,32},{8,40},{16,48},{24,56},{32,64},{40,72},{48,80},{56,88},{64,... | collective-permute-start | bytes 3932168 | tf_op jit(solution)/shard_map/ppermute | solution.py:672
  76.9 39.7 %collective-permute-start.11 = (bf16[2048,256]{1,0:T(8,128)(2,1)}, bf16[2048,256]{1,0:T(8,128)(2,1)}, u32[]{:S(2)}, u32[]{:S(2)}) collective-permute-start(bf16[2048,256]{1,0:T(8,128)(2,1)} %bitcast.19.weight_own), channel_id=1, source_target_pairs={{0,8},{8,0},{16,24},{24,16},{32,40},{40,32},{48,56},{56,48},{64,72... | collective-permute-start | bytes 3145736 | tf_op jit(solution)/shard_map/ppermute | solution.py:668
  78.9 4.6 %copy-start.11 = (f32[1024,64]{1,0:T(8,128)}, f32[1024,64]{1,0:T(8,128)S(1)}, u32[]{:S(2)}) copy-start(f32[1024,64]{1,0:T(8,128)S(1)} %get-tuple-element.57) | copy-start | bytes 786436
  78.9 4.6 %copy-start.13 = (f32[1024,64]{1,0:T(8,128)}, f32[1024,64]{1,0:T(8,128)S(1)}, u32[]{:S(2)}) copy-start(f32[1024,64]{1,0:T(8,128)S(1)} %get-tuple-element.58) | copy-start | bytes 786436
  78.9 4.6 %copy-start.15 = (f32[1024,64]{1,0:T(8,128)}, f32[1024,64]{1,0:T(8,128)S(1)}, u32[]{:S(2)}) copy-start(f32[1024,64]{1,0:T(8,128)S(1)} %get-tuple-element.59) | copy-start | bytes 786436
  78.9 25.4 %collective-permute-start.7 = (bf16[128,2048]{1,0:T(8,128)(2,1)}, bf16[128,2048]{1,0:T(8,128)(2,1)}, u32[]{:S(2)}, u32[]{:S(2)}) collective-permute-start(bf16[128,2048]{1,0:T(8,128)(2,1)} %collective-permute-done.1.own_left), channel_id=1, source_target_pairs={{0,1},{1,2},{2,3},{3,0},{4,5},{5,6},{6,7},{7,4},{8,9},{9,10},{10,1... | collective-permute-start | bytes 1572872 | tf_op jit(solution)/shard_map/ppermute | solution.py:654
  80.9 23.4 %collective-permute-start.8 = (bf16[128,2048]{1,0:T(8,128)(2,1)}, bf16[128,2048]{1,0:T(8,128)(2,1)}, u32[]{:S(2)}, u32[]{:S(2)}) collective-permute-start(bf16[128,2048]{1,0:T(8,128)(2,1)} %collective-permute-done.4.across_right), channel_id=1, source_target_pairs={{0,3},{1,0},{2,1},{3,2},{4,7},{5,4},{6,5},{7,6},{8,11},{9,8},{10,9... | collective-permute-start | bytes 1572872 | tf_op jit(solution)/shard_map/ppermute | solution.py:654
  93.7 26.0 %copy-start.21 = (bf16[448,256]{1,0:T(8,128)(2,1)}, bf16[448,256]{1,0:T(8,128)(2,1)S(1)}, u32[]{:S(2)}) copy-start(bf16[448,256]{1,0:T(8,128)(2,1)S(1)} %reduce_sum.102.piece_0) | copy-start | bytes 688132
  104.3 15.4 %collective-permute-start.12 = (bf16[448,256]{1,0:T(8,128)(2,1)S(1)}, bf16[448,256]{1,0:T(8,128)(2,1)S(1)}, u32[]{:S(2)}, u32[]{:S(2)}) collective-permute-start(bf16[448,256]{1,0:T(8,128)(2,1)S(1)} %reduce_sum.102.piece_0), channel_id=1, source_target_pairs={{0,1},{1,0},{2,3},{3,2},{4,5},{5,4},{6,7},{7,6},{8,9},{9,8},{10,11... | collective-permute-start | bytes 688136 | tf_op jit(solution)/shard_map/ppermute | solution.py:705
  105.8 14.0 %collective-permute-start.13 = (bf16[448,256]{1,0:T(8,128)(2,1)S(1)}, bf16[448,256]{1,0:T(8,128)(2,1)S(1)}, u32[]{:S(2)}, u32[]{:S(2)}) collective-permute-start(bf16[448,256]{1,0:T(8,128)(2,1)S(1)} %reduce_sum.102.piece_0), channel_id=1, source_target_pairs={{0,2},{1,3},{2,0},{3,1},{4,6},{5,7},{6,4},{7,5},{8,10},{9,11},{10,... | collective-permute-start | bytes 688136 | tf_op jit(solution)/shard_map/ppermute | solution.py:705
  109.6 37.7 %collective-permute-start.15 = (bf16[256,1280]{1,0:T(8,128)(2,1)S(1)}, bf16[256,1280]{1,0:T(8,128)(2,1)S(1)}, u32[]{:S(2)}, u32[]{:S(2)}) collective-permute-start(bf16[256,1280]{1,0:T(8,128)(2,1)S(1)} %slice.53), channel_id=1, source_target_pairs={{0,32},{8,40},{16,48},{24,56},{32,64},{40,72},{48,80},{56,88},{64,... | collective-permute-start | bytes 1966088 | tf_op jit(solution)/shard_map/ppermute | solution.py:672
  110.8 36.5 %collective-permute-start.16 = (bf16[256,1280]{1,0:T(8,128)(2,1)S(1)}, bf16[256,1280]{1,0:T(8,128)(2,1)S(1)}, u32[]{:S(2)}, u32[]{:S(2)}) collective-permute-start(bf16[256,1280]{1,0:T(8,128)(2,1)S(1)} %slice.54), channel_id=1, source_target_pairs={{0,96},{8,104},{16,112},{24,120},{32,0},{40,8},{48,16},{56,24},{64... | collective-permute-start | bytes 1966088 | tf_op jit(solution)/shard_map/ppermute | solution.py:672
  116.6 7.2 %collective-permute-start.14 = (bf16[448,256]{1,0:T(8,128)(2,1)S(1)}, bf16[448,256]{1,0:T(8,128)(2,1)S(1)}, u32[]{:S(2)}, u32[]{:S(2)}) collective-permute-start(bf16[448,256]{1,0:T(8,128)(2,1)S(1)} %reduce_sum.102.piece_0), channel_id=1, source_target_pairs={{0,3},{1,2},{2,1},{3,0},{4,7},{5,6},{6,5},{7,4},{8,11},{9,10},{10,... | collective-permute-start | bytes 688136 | tf_op jit(solution)/shard_map/ppermute | solution.py:705
  124.6 24.5 %copy-start.25 = (s32[128,8]{0,1:T(8,128)S(1)}, s32[128,8]{0,1:T(8,128)}, u32[]{:S(2)}) copy-start(s32[128,8]{0,1:T(8,128)} %param.33) | copy-start | bytes 12292
  149.1 13.7 %collective-permute-start.17 = (bf16[2048,1280]{1,0:T(8,128)(2,1)}, bf16[2048,1280]{1,0:T(8,128)(2,1)}, u32[]{:S(2)}, u32[]{:S(2)}) collective-permute-start(bf16[2048,1280]{1,0:T(8,128)(2,1)} %constant_dynamic-update-slice_fusion.own.next_own), channel_id=1, source_target_pairs={{0,8},{8,0},{16,24},{24,16},{32,40},{40,32},{48,56},{56,48},{64,72... | collective-permute-start | bytes 15728648 | tf_op jit(solution)/shard_map/ppermute | solution.py:668
  149.2 13.6 %all-to-all-start.3 = ((bf16[8,128,256]{2,1,0:T(8,128)(2,1)}), bf16[8,128,256]{2,1,0:T(8,128)(2,1)S(1)}, u32[]{:S(2)}, u32[]{:S(2)}) async-start(bf16[8,128,256]{2,1,0:T(8,128)(2,1)} %bitcast.55), calls=%async_computation.3 | async-start | bytes 1048576 | tf_op jit(solution)/shard_map/all_to_all | solution.py:719
  175.4 6.2 %copy-start.19 = (bf16[128,2048]{1,0:T(8,128)(2,1)S(1)}, bf16[128,2048]{1,0:T(8,128)(2,1)}, u32[]{:S(2)}) copy-start(bf16[128,2048]{1,0:T(8,128)(2,1)} %get-tuple-element.38) | copy-start | bytes 1572868
  175.4 58.6 %all-to-all-start.4 = ((bf16[128,8,2048]{2,1,0:T(8,128)(2,1)}), bf16[128,8,2048]{2,1,0:T(8,128)(2,1)}, u32[]{:S(2)}, u32[]{:S(2)}) async-start(bf16[128,8,2048]{2,1,0:T(8,128)(2,1)} %convert_bitcast_fusion), calls=%async_computation.4 | async-start | bytes 8388608 | tf_op jit(solution)/shard_map/all_to_all | solution.py:404
  234.0 23.8 %all-to-all-start.5 = ((bf16[128,2,2048]{2,1,0:T(2,128)(2,1)}), bf16[128,2,2048]{2,1,0:T(2,128)(2,1)S(1)}, u32[]{:S(2)}, u32[]{:S(2)}) async-start(bf16[128,2,2048]{2,1,0:T(2,128)(2,1)} %reshape.153), calls=%async_computation.5 | async-start | bytes 2097152 | tf_op jit(solution)/shard_map/all_to_all | solution.py:404
  238.9 10.2 %copy-start.17 = (bf16[1,768,2048]{2,1,0:T(8,128)(2,1)S(1)}, bf16[1,768,2048]{2,1,0:T(8,128)(2,1)}, u32[]{:S(2)}) copy-start(bf16[1,768,2048]{2,1,0:T(8,128)(2,1)} %param.31) | copy-start | bytes 9437188
  267.1 9.1 %copy-start.26 = (f32[128,8]{0,1:T(8,128)S(1)}, f32[128,8]{0,1:T(8,128)}, u32[]{:S(2)}) copy-start(f32[128,8]{0,1:T(8,128)} %param.34) | copy-start | bytes 12292
  267.1 73.9 %all-to-all-start.6 = ((bf16[128,40,512]{2,1,0:T(8,128)(2,1)}), bf16[128,40,512]{2,1,0:T(8,128)(2,1)}, u32[]{:S(2)}, u32[]{:S(2)}) async-start(bf16[128,40,512]{2,1,0:T(8,128)(2,1)} %expert_rest.1), calls=%async_computation.6 | async-start | bytes 10485760 | tf_op jit(solution)/shard_map/all_to_all | solution.py:404
  (7 other events, 19.7 us)

commit v6 on v5

--- a/solution.py
+++ b/solution.py
@@ -212,12 +212,13 @@
     row = lax.broadcasted_iota(jnp.int32, (2 * tok, 1), 0)
     row = jnp.where(row >= tok, row - tok, row)
 
-    def join(state, q_now, keys, values, allowed):
-        peak, total, acc = state
-        scores = scale * lax.dot_general(
+    def score(q_now, keys):
+        return lax.dot_general(
             q_now, keys, (((1,), (1,)), ((), ())), preferred_element_type=jnp.float32
         )
-        scores = jnp.where(allowed, scores, MASKED)
+
+    def join(state, scores, values):
+        peak, total, acc = state
         top = jnp.maximum(peak, jnp.max(scores, axis=1, keepdims=True))
         keep = jnp.exp2(peak - top)
         weights = jnp.exp2(scores - top)
@@ -246,14 +247,10 @@
                     (col - 768 < meta[at + 2]).astype(jnp.int32),
                 ),
             )
-            mine = (late.astype(jnp.int32) == req).astype(jnp.int32)
-            return join(
-                state,
-                q_now,
-                pk_all[pl.ds(start, span), :],
-                pv_all[pl.ds(start, span), :],
-                inside * mine > 0,
-            )
+            outside = jnp.where(inside > 0, 0.0, MASKED)
+            foreign = jnp.where(late.astype(jnp.int32) == req, 0.0, MASKED)
+            scores = scale * score(q_now, pk_all[pl.ds(start, span), :]) + outside + foreign
+            return join(state, scores, pv_all[pl.ds(start, span), :])
 
         peak_all[...] = jnp.full((2 * tok, 1), MASKED, jnp.float32)
         total_all[...] = jnp.zeros((2 * tok, 1), jnp.float32)
@@ -277,12 +274,11 @@
                 keys = 2 * tok * (quarter + 1)
                 other = lax.broadcasted_iota(jnp.int32, (1, keys), 1)
                 allowed = jnp.logical_and(other <= token, other >= bottom)
+                scores = scale * score(q_now, k_all[0:keys, :])
                 peak, total, acc = join(
                     (peak_all[...], total_all[...], acc_all[...]),
-                    q_now,
-                    k_all[0:keys, :],
+                    jnp.where(allowed, scores, MASKED),
                     v_all[0:keys, :],
-                    allowed,
                 )
                 done = (acc / total).astype(jnp.bfloat16)
                 out[pl.ds(first, tok), 0:hd] = done[:tok]
@@ -658,6 +654,7 @@
     right = shift(normed, -1)
     packed = pack_weights(query_weight, kv_weight, out_weight, next_weight, mp_size)
     packed = lax.all_to_all(packed, "mp", split_axis=0, concat_axis=0, tiled=True)
+    packed, across, left, right = lax.optimization_barrier((packed, across, left, right))
     packed = packed.reshape(mp_size * own_rows, -1)
     late_width = dim + next_weight.shape[1]
     dp_at = lax.axis_index("dp")
@@ -681,7 +678,7 @@
     early = lax.all_to_all(early, "dp", split_axis=0, concat_axis=0, tiled=True)
     early = early.reshape(dim, 2 * hd)
     sides = [left, right, shift(across, 1), shift(across, -1)]
-    far = [shift(left, 1), shift(sides[3], -1)]
+    own_far = shift(left, 1)
     tables = (
         token_request,
         request_leaf,
@@ -692,18 +689,22 @@
         leaf_slot,
     )
     path = pack_paths(tables, root_cache, mid_cache, leaf_cache, mp_size)
-    path, sides, late, early = lax.optimization_barrier((path, sides, late, early))
+    path, sides, own_far, late, early = lax.optimization_barrier(
+        (path, sides, own_far, late, early)
+    )
+    far = [own_far, shift(sides[3], -1)]
     weights = (early, swap(early, 1))
     x_left = shift_x(late, 1)
     x_right = shift_x(late, -1)
     path = lax.all_to_all(path, "mp", split_axis=0, concat_axis=0, tiled=True)
     own_piece = jnp.sum(path.astype(jnp.float32), axis=0).astype(jnp.bfloat16)
-    own_piece, far, x_left, x_right = lax.optimization_barrier((own_piece, far, x_left, x_right))
-    middle = x_left.shape[0] // 2
-    x_far = [shift_x(x_left[:middle], 1), shift_x(x_right[middle:], -1)]
+    own_piece, far = lax.optimization_barrier((own_piece, far))
     pieces = [own_piece] + [
         lax.ppermute(own_piece, "mp", [(j, j ^ s) for j in range(mp_size)]) for s in range(1, 4)
     ]
+    pieces, x_left, x_right = lax.optimization_barrier((pieces, x_left, x_right))
+    middle = x_left.shape[0] // 2
+    x_far = [shift_x(x_left[:middle], 1), shift_x(x_right[middle:], -1)]
     rows = [normed, across] + sides + far
     meta = jnp.concatenate(
         [
@@ -713,7 +714,9 @@
         ]
     ).astype(jnp.int32)
     attended = attend(meta, rows, weights, pieces, head_gains, cosine, sine)
-    attended, x_far = lax.optimization_barrier((attended, x_far))
+    attended, late, x_left, x_right, x_far = lax.optimization_barrier(
+        (attended, late, x_left, x_right, x_far)
+    )
     own_half = jnp.concatenate([late, x_left, x_right] + x_far, axis=0)
     halves = (own_half, swap(own_half, 1))
     attended = lax.all_to_all(

time: 351 us -> 372 us (1.060)
  waiting for transfers between devices: 170 us -> 185 us
  starting transfers between devices: 63.6 us -> 67.5 us
    ppermute x1, waiting for transfers between devices: 0.01 us -> 13.8 us  [per_device(): lax.ppermute(normed, 'mp', [(j, (j + 4) % mp_size) for j in range(mp_size)])]
    all_to_all x1, waiting for transfers between devices: 9.25 us -> 0.01 us  [per_device(): lax.all_to_all(packed, 'mp', split_axis=0, concat_axis=0, tiled=True)]
    all_to_all x1, waiting for transfers between devices: 7.43 us -> 13.2 us  [per_device(): path = lax.all_to_all(path, 'mp', split_axis=0, concat_axis=0, tiled=True)]
    unnamed x66 -> x62, local copies, waits for them, and re-layouts: 8.85 us -> 9.28 us
  transfers between devices with their start and end apart: 25 -> 25, of which waited for: 9 -> 12; matrix products, arithmetic and copies ran while one was open for 15% -> 13% of each run, Pallas kernels for 7% -> 7%
where the time goes in v6:
time: 372 us; the launch traced here: 371 us
  waiting for transfers between devices  185 us (50%)
  starting transfers between devices  67.5 us (18%)
  Pallas kernels  50.8 us (14%)
  local copies, waits for them, and re-layouts  30 us (8%)
  matrix products  19 us (5%)
  other arithmetic  16.1 us (4%)
    all_to_all x3, waiting for transfers between devices, exchange(): return lax.all_to_all(values, BOTH, split_axis=0, concat_axis=0, tiled=True)  110 us
    pallas_call x1, Pallas kernels, attend(): pl.pallas_call(attention_kernel, out_shape=jax.ShapeDtypeStruct((group, 2...  22.2 us
    ppermute x4, waiting for transfers between devices, swap(): return lax.ppermute(values, 'dp', [(j, j ^ bit) for j in range(dp_size)])  20.8 us
    all_to_all x3, starting transfers between devices, exchange(): return lax.all_to_all(values, BOTH, split_axis=0, concat_axis=0, tiled=True)  18.9 us
    ppermute x1, waiting for transfers between devices, per_device(): lax.ppermute(normed, 'mp', [(j, (j + 4) % mp_size) for j in range(mp_size)])  13.8 us
    all_to_all x1, waiting for transfers between devices, per_device(): path = lax.all_to_all(path, 'mp', split_axis=0, concat_axis=0, tiled=True)  13.2 us
    ppermute x6, waiting for transfers between devices, shift(): return lax.ppermute(values, 'mp', moves)  11 us
    dot_general x1, matrix products, expert(): both = jnp.dot(rows, gate_up, preferred_element_type=jnp.float32)  10.1 us
  transfers between devices with their start and end apart: 25, of which 12 were waited for; matrix products, arithmetic and copies ran while one was open for 13% of the time, Pallas kernels for 7%

profile of v6, /device:TPU:0, one launch (start us, length us, event | category | flops | bytes accessed | tf_op | source)
XLA Modules:
  0.0 371.0 jit_solution(12310959950525386764)
XLA Ops:
  0.6 1.9 pack_weights.1
  2.5 6.4 %all-to-all-start = ((bf16[8,16,3072]{2,1,0:T(8,128)(2,1)}), bf16[8,16,3072]{2,1,0:T(8,128)(2,1)S(1)}, u32[]{:S(2)}, u32[]{:S(2)}) async-start(bf16[8,16,3072]{2,1,0:T(8,128)(2,1)} %pack_weights.1), calls=%async_computation | async-start | bytes 1572864 | tf_op jit(solution)/shard_map/all_to_all | solution.py:656
  8.9 1.5 fusion.32
  11.9 2.1 collective-permute-start
  15.5 1.8 collective-permute-start.2
  17.2 13.8 %collective-permute-done.across = bf16[128,2048]{1,0:T(8,128)(2,1)S(1)} collective-permute-done((bf16[128,2048]{1,0:T(8,128)(2,1)S(1)}, bf16[128,2048]{1,0:T(8,128)(2,1)S(1)}, u32[]{:S(2)}, u32[]{:S(2)}) %collective-permute-start) | collective-permute-done | bytes 524320 | tf_op jit(solution)/shard_map/ppermute | solution.py:652
  34.3 6.9 %all-to-all-start.1 = ((bf16[16,128,256]{2,1,0:T(8,128)(2,1)}), bf16[16,128,256]{2,1,0:T(8,128)(2,1)}, u32[]{:S(2)}, u32[]{:S(2)}) async-start(bf16[16,128,256]{2,1,0:T(8,128)(2,1)} %bitcast.18), calls=%async_computation.1 | async-start | bytes 2097152 | tf_op jit(solution)/shard_map/all_to_all | solution.py:678
  41.3 3.5 collective-permute-start.7
  45.8 2.2 collective-permute-start.4
  48.1 2.2 pack_paths.1
  50.3 20.8 %collective-permute-done.7 = bf16[256,1280]{1,0:T(8,128)(2,1)S(1)} collective-permute-done((bf16[256,1280]{1,0:T(8,128)(2,1)S(1)}, bf16[256,1280]{1,0:T(8,128)(2,1)S(1)}, u32[]{:S(2)}, u32[]{:S(2)}) %collective-permute-start.7) | collective-permute-done | bytes 655392 | tf_op jit(solution)/shard_map/ppermute | solution.py:665
  72.2 3.9 %all-to-all-start.2 = ((bf16[8,448,256]{2,1,0:T(8,128)(2,1)}), bf16[8,448,256]{2,1,0:T(8,128)(2,1)S(1)}, u32[]{:S(2)}, u32[]{:S(2)}) async-start(bf16[8,448,256]{2,1,0:T(8,128)(2,1)} %pack_paths.1), calls=%async_computation.2 | async-start | bytes 3670016 | tf_op jit(solution)/shard_map/all_to_all | solution.py:699
  76.0 1.5 collective-permute-start.13
  78.0 1.8 collective-permute-start.14
  81.0 3.3 collective-permute-start.8
  85.8 13.2 %all-to-all-done.2 = bf16[8,448,256]{2,1,0:T(8,128)(2,1)S(1)} async-done(((bf16[8,448,256]{2,1,0:T(8,128)(2,1)}), bf16[8,448,256]{2,1,0:T(8,128)(2,1)S(1)}, u32[]{:S(2)}, u32[]{:S(2)}) %all-to-all-start.2) | async-done | bytes 1835040 | tf_op jit(solution)/shard_map/all_to_all | solution.py:699
  99.4 9.8 %collective-permute-done.8.across_far = bf16[128,2048]{1,0:T(8,128)(2,1)} collective-permute-done((bf16[128,2048]{1,0:T(8,128)(2,1)}, bf16[128,2048]{1,0:T(8,128)(2,1)}, u32[]{:S(2)}, u32[]{:S(2)}) %collective-permute-start.8) | collective-permute-done | bytes 524320 | tf_op jit(solution)/shard_map/ppermute | solution.py:650
  110.6 1.5 collective-permute-start.11
  112.1 1.8 collective-permute-start.12
  117.8 4.0 %collective-permute-done.11.piece_2 = bf16[448,256]{1,0:T(8,128)(2,1)S(1)} collective-permute-done((bf16[448,256]{1,0:T(8,128)(2,1)S(1)}, bf16[448,256]{1,0:T(8,128)(2,1)S(1)}, u32[]{:S(2)}, u32[]{:S(2)}) %collective-permute-start.11) | collective-permute-done | bytes 229408 | tf_op jit(solution)/shard_map/ppermute | solution.py:703
  121.7 2.6 collective-permute-done.12.piece_3
  124.3 2.0 slice.53
  126.3 1.5 collective-permute-start.15
  127.8 2.0 slice.54
  129.8 1.8 collective-permute-start.16
  132.9 1.9 fusion.13
  136.2 22.2 %tree_attention.1 = bf16[1024,256]{1,0:T(8,128)(2,1)} custom-call(s32[9]{0:T(128)} %pad_add_fusion.2.meta, bf16[128,2048]{1,0:T(8,128)(2,1)} %copy-done.13, bf16[128,2048]{1,0:T(8,128)(2,1)} %copy-done.17, bf16[128,2048]{1,0:T(8,128)(2,1)} %copy-done.18, bf16[128,2048]{1,0:T(8,128)(2,1)} %copy-done.19, bf16[128,2048]{1,0:T(8,128)(2,1)} %collective-permute-done.3.across_left, ...), custom_call_target="tpu_custom_call" | custom-call | flops 2147483648 | bytes 8388608 | tf_op jit(solution)/shard_map/tree_attention/pallas_call | solution.py:293
  159.6 2.5 constant_dynamic-update-slice_fusion.3
  162.1 2.5 constant_dynamic-update-slice_fusion.2
  164.6 2.0 constant_dynamic-update-slice_fusion.1
  166.6 2.0 constant_dynamic-update-slice_fusion.own.next_own
  168.6 4.9 %all-to-all-start.3 = ((bf16[8,128,256]{2,1,0:T(8,128)(2,1)}), bf16[8,128,256]{2,1,0:T(8,128)(2,1)S(1)}, u32[]{:S(2)}, u32[]{:S(2)}) async-start(bf16[8,128,256]{2,1,0:T(8,128)(2,1)} %bitcast.22), calls=%async_computation.3 | async-start | bytes 1048576 | tf_op jit(solution)/shard_map/all_to_all | solution.py:722
  174.8 8.8 %all-to-all-done.3.attended = bf16[8,128,256]{2,1,0:T(8,128)(2,1)S(1)} async-done(((bf16[8,128,256]{2,1,0:T(8,128)(2,1)}), bf16[8,128,256]{2,1,0:T(8,128)(2,1)S(1)}, u32[]{:S(2)}, u32[]{:S(2)}) %all-to-all-start.3) | async-done | bytes 524320 | tf_op jit(solution)/shard_map/all_to_all | solution.py:722
  184.4 7.5 %project.1 = (bf16[128,2048]{1,0:T(8,128)(2,1)}, bf16[128,2048]{1,0:T(8,128)(2,1)}) custom-call(s32[3]{0:T(128)} %pad_add_fusion.1.place, bf16[8,128,256]{2,1,0:T(8,128)(2,1)} %copy-done.12, bf16[2048,1280]{1,0:T(8,128)(2,1)} %constant_dynamic-update-slice_fusion.own.next_own, bf16[2048,1280]{1,0:T(8,128)(2,1)} %collective-permute-done.17.other.next_other, ...), custom_call_target="tpu_custom_call" | custom-call | tf_op jit(solution)/shard_map/project/pallas_call | solution.py:368
  192.0 4.4 %convert_bitcast_fusion = bf16[128,8,2048]{2,1,0:T(8,128)(2,1)} fusion(bf16[128,2048]{1,0:T(8,128)(2,1)} %get-tuple-element.62, s32[1024]{0:T(1024)S(1)} %eq.180, s32[128,128]{1,0:T(8,128)S(1)} %copy.68), kind=kOutput, calls=%fused_computation.2 | convolution fusion | flops 539099136 | bytes 4788224 | tf_op jit(solution)/shard_map/dot_general | solution.py:749
  196.4 6.2 %all-to-all-start.4 = ((bf16[128,8,2048]{2,1,0:T(8,128)(2,1)}), bf16[128,8,2048]{2,1,0:T(8,128)(2,1)}, u32[]{:S(2)}, u32[]{:S(2)}) async-start(bf16[128,8,2048]{2,1,0:T(8,128)(2,1)} %convert_bitcast_fusion), calls=%async_computation.4 | async-start | bytes 8388608 | tf_op jit(solution)/shard_map/all_to_all | solution.py:400
  203.3 1.5 reshape.153
  204.8 50.2 %all-to-all-done.4 = bf16[128,8,2048]{2,1,0:T(8,128)(2,1)} async-done(((bf16[128,8,2048]{2,1,0:T(8,128)(2,1)}), bf16[128,8,2048]{2,1,0:T(8,128)(2,1)}, u32[]{:S(2)}, u32[]{:S(2)}) %all-to-all-start.4) | async-done | bytes 4194336 | tf_op jit(solution)/shard_map/all_to_all | solution.py:400
  255.0 4.6 %all-to-all-start.5 = ((bf16[128,2,2048]{2,1,0:T(2,128)(2,1)}), bf16[128,2,2048]{2,1,0:T(2,128)(2,1)S(1)}, u32[]{:S(2)}, u32[]{:S(2)}) async-start(bf16[128,2,2048]{2,1,0:T(2,128)(2,1)} %reshape.153), calls=%async_computation.5 | async-start | bytes 2097152 | tf_op jit(solution)/shard_map/all_to_all | solution.py:400
  259.7 10.1 %fusion = f32[1024,1536]{1,0:T(8,128)S(1)} fusion(bf16[128,8,2048]{2,1,0:T(8,128)(2,1)} %all-to-all-done.4, bf16[1,2048,1536]{2,1,0:T(8,128)(2,1)} %param.30), kind=kOutput, calls=%fused_computation | convolution fusion | flops 6442450944 | bytes 16777216 | tf_op jit(solution)/shard_map/dot_general | solution.py:405
  269.8 3.7 %convolution_convert_fusion = bf16[1024,2048]{1,0:T(8,128)(2,1)S(1)} fusion(f32[1024,1536]{1,0:T(8,128)S(1)} %fusion, bf16[1,768,2048]{2,1,0:T(8,128)(2,1)S(1)} %copy-done.11), kind=kOutput, calls=%fused_computation.3 | convolution fusion | flops 3228041216 | bytes 13631488 | tf_op jit(solution)/shard_map/dot_general | solution.py:407
  273.6 2.8 pad.4.main_block
  276.4 2.5 all-to-all-done.5
  280.1 8.0 %expert_rest.1 = bf16[128,40,512]{2,1,0:T(8,128)(2,1)} custom-call(bf16[256,2048]{1,0:T(8,128)(2,1)} %reshape.157.rows, bf16[2048,1536]{1,0:T(8,128)(2,1)} %bitcast.50, bf16[768,2048]{1,0:T(8,128)(2,1)} %bitcast.52, bf16[128,40,512]{2,1,0:T(8,128)(2,1)} %pad.4.main_block), custom_call_target="tpu_custom_call", output_to_operand_aliasing={{}: (3, {})} | custom-call | tf_op jit(solution)/shard_map/expert_rest/pallas_call | solution.py:448
  288.0 8.0 %all-to-all-start.6 = ((bf16[128,40,512]{2,1,0:T(8,128)(2,1)}), bf16[128,40,512]{2,1,0:T(8,128)(2,1)}, u32[]{:S(2)}, u32[]{:S(2)}) async-start(bf16[128,40,512]{2,1,0:T(8,128)(2,1)} %expert_rest.1), calls=%async_computation.6 | async-start | bytes 10485760 | tf_op jit(solution)/shard_map/all_to_all | solution.py:400
  303.3 1.5 broadcast_multiply_fusion.rest_share
  304.8 57.2 %all-to-all-done.6.main_rows.rest_rows = bf16[128,40,512]{2,1,0:T(8,128)(2,1)} async-done(((bf16[128,40,512]{2,1,0:T(8,128)(2,1)}), bf16[128,40,512]{2,1,0:T(8,128)(2,1)}, u32[]{:S(2)}, u32[]{:S(2)}) %all-to-all-start.6) | async-done | bytes 5242912 | tf_op jit(solution)/shard_map/all_to_all | solution.py:400
  362.0 8.9 %finish.1 = (bf16[128,2048]{1,0:T(8,128)(2,1)}, bf16[128,512]{1,0:T(8,128)(2,1)}) custom-call(s32[3]{0:T(128)} %pad_add_fusion.1.place, bf16[256,1024]{1,0:T(8,128)(2,1)} %pad_maximum_fusion.2.main_share, bf16[4,256,1024]{2,1,0:T(8,128)(2,1)} %broadcast_multiply_fusion.rest_share, bf16[128,40,512]{2,1,0:T(8,128)(2,1)} %all-to-all-done.6.main_rows.rest_rows, ...), custom_call_target="tpu_custom_call" | custom-call | tf_op jit(solution)/shard_map/finish/pallas_call | solution.py:545
  (141 shorter events, 30.8 us)
Async XLA Ops:
  0.6 11.0 %copy-start.10 = (bf16[128,2048]{1,0:T(8,128)(2,1)S(1)}, bf16[128,2048]{1,0:T(8,128)(2,1)}, u32[]{:S(2)}) copy-start(bf16[128,2048]{1,0:T(8,128)(2,1)} %hidden.1) | copy-start | bytes 1572868
  2.5 29.6 %all-to-all-start = ((bf16[8,16,3072]{2,1,0:T(8,128)(2,1)}), bf16[8,16,3072]{2,1,0:T(8,128)(2,1)S(1)}, u32[]{:S(2)}, u32[]{:S(2)}) async-start(bf16[8,16,3072]{2,1,0:T(8,128)(2,1)} %pack_weights.1), calls=%async_computation | async-start | bytes 1572864 | tf_op jit(solution)/shard_map/all_to_all | solution.py:656
  11.9 20.3 %copy-start.13 = (bf16[128,2048]{1,0:T(8,128)(2,1)}, bf16[128,2048]{1,0:T(8,128)(2,1)S(1)}, u32[]{:S(2)}) copy-start(bf16[128,2048]{1,0:T(8,128)(2,1)S(1)} %fusion.8.own) | copy-start | bytes 1572868
  11.9 19.1 %collective-permute-start = (bf16[128,2048]{1,0:T(8,128)(2,1)S(1)}, bf16[128,2048]{1,0:T(8,128)(2,1)S(1)}, u32[]{:S(2)}, u32[]{:S(2)}) collective-permute-start(bf16[128,2048]{1,0:T(8,128)(2,1)S(1)} %fusion.8.own), channel_id=1, source_target_pairs={{0,4},{1,5},{2,6},{3,7},{4,0},{5,1},{6,2},{7,3},{8,12},{9,13},{10,... | collective-permute-start | bytes 1572872 | tf_op jit(solution)/shard_map/ppermute | solution.py:652
  14.0 18.2 %collective-permute-start.1 = (bf16[128,2048]{1,0:T(8,128)(2,1)S(1)}, bf16[128,2048]{1,0:T(8,128)(2,1)S(1)}, u32[]{:S(2)}, u32[]{:S(2)}) collective-permute-start(bf16[128,2048]{1,0:T(8,128)(2,1)S(1)} %fusion.8.own), channel_id=1, source_target_pairs={{0,1},{1,2},{2,3},{3,0},{4,5},{5,6},{6,7},{7,4},{8,9},{9,10},{10,1... | collective-permute-start | bytes 1572872 | tf_op jit(solution)/shard_map/ppermute | solution.py:650
  15.5 16.7 %collective-permute-start.2 = (bf16[128,2048]{1,0:T(8,128)(2,1)S(1)}, bf16[128,2048]{1,0:T(8,128)(2,1)S(1)}, u32[]{:S(2)}, u32[]{:S(2)}) collective-permute-start(bf16[128,2048]{1,0:T(8,128)(2,1)S(1)} %fusion.8.own), channel_id=1, source_target_pairs={{0,3},{1,0},{2,1},{3,2},{4,7},{5,4},{6,5},{7,6},{8,11},{9,8},{10,9... | collective-permute-start | bytes 1572872 | tf_op jit(solution)/shard_map/ppermute | solution.py:650
  32.2 9.0 %copy-start.19 = (bf16[128,2048]{1,0:T(8,128)(2,1)}, bf16[128,2048]{1,0:T(8,128)(2,1)S(1)}, u32[]{:S(2)}) copy-start(bf16[128,2048]{1,0:T(8,128)(2,1)S(1)} %collective-permute-done.2.own_right) | copy-start | bytes 1572868
  32.2 15.8 %copy-start = (bf16[1,512,512]{2,1,0:T(8,128)(2,1)S(1)}, bf16[1,512,512]{2,1,0:T(8,128)(2,1)}, u32[]{:S(2)}) copy-start(bf16[1,512,512]{2,1,0:T(8,128)(2,1)} %root.1) | copy-start | bytes 1572868
  32.2 15.8 %copy-start.1 = (bf16[1,256,512]{2,1,0:T(8,128)(2,1)S(1)}, bf16[1,256,512]{2,1,0:T(8,128)(2,1)}, u32[]{:S(2)}) copy-start(bf16[1,256,512]{2,1,0:T(8,128)(2,1)} %mid.1) | copy-start | bytes 786436
  32.2 15.8 %copy-start.2 = (bf16[2,128,512]{2,1,0:T(8,128)(2,1)S(1)}, bf16[2,128,512]{2,1,0:T(8,128)(2,1)}, u32[]{:S(2)}) copy-start(bf16[2,128,512]{2,1,0:T(8,128)(2,1)} %leaf.1) | copy-start | bytes 786436
  32.2 15.7 %copy-start.3 = (s32[1024]{0:T(1024)S(1)}, s32[1024]{0:T(1024)}, u32[]{:S(2)}) copy-start(s32[1024]{0:T(1024)} %token_request.1) | copy-start | bytes 12292
  32.3 15.7 %copy-start.4 = (s32[16]{0:T(128)S(1)}, s32[16]{0:T(128)}, u32[]{:S(2)}) copy-start(s32[16]{0:T(128)} %leaf_parent.1) | copy-start | bytes 196
  32.3 15.7 %copy-start.5 = (s32[8]{0:T(128)S(1)}, s32[8]{0:T(128)}, u32[]{:S(2)}) copy-start(s32[8]{0:T(128)} %mid_parent.1) | copy-start | bytes 100
  32.3 15.7 %copy-start.6 = (s32[8]{0:T(128)S(1)}, s32[8]{0:T(128)}, u32[]{:S(2)}) copy-start(s32[8]{0:T(128)} %root_slot.1) | copy-start | bytes 100
  32.3 15.7 %copy-start.7 = (s32[8]{0:T(128)S(1)}, s32[8]{0:T(128)}, u32[]{:S(2)}) copy-start(s32[8]{0:T(128)} %mid_slot.1) | copy-start | bytes 100
  32.3 15.7 %copy-start.8 = (s32[16]{0:T(128)S(1)}, s32[16]{0:T(128)}, u32[]{:S(2)}) copy-start(s32[16]{0:T(128)} %leaf_slot.1) | copy-start | bytes 196
  32.3 15.7 %copy-start.9 = (s32[32]{0:T(128)S(1)}, s32[32]{0:T(128)}, u32[]{:S(2)}) copy-start(s32[32]{0:T(128)} %request_leaf.1) | copy-start | bytes 388
  33.1 8.1 %collective-permute-start.6 = (bf16[128,1280]{1,0:T(8,128)(2,1)}, bf16[128,1280]{1,0:T(8,128)(2,1)S(1)}, u32[]{:S(2)}, u32[]{:S(2)}) collective-permute-start(bf16[128,1280]{1,0:T(8,128)(2,1)} %get-tuple-element.75), channel_id=1, source_target_pairs={{0,8},{8,0},{16,24},{24,16},{32,40},{40,32},{48,56},{56,48},{64,72... | collective-permute-start | bytes 983048 | tf_op jit(solution)/shard_map/ppermute | solution.py:665
  34.3 37.9 %all-to-all-start.1 = ((bf16[16,128,256]{2,1,0:T(8,128)(2,1)}), bf16[16,128,256]{2,1,0:T(8,128)(2,1)}, u32[]{:S(2)}, u32[]{:S(2)}) async-start(bf16[16,128,256]{2,1,0:T(8,128)(2,1)} %bitcast.18), calls=%async_computation.1 | async-start | bytes 2097152 | tf_op jit(solution)/shard_map/all_to_all | solution.py:678
  41.2 9.1 %copy-start.15 = (bf16[128,1280]{1,0:T(8,128)(2,1)}, bf16[128,1280]{1,0:T(8,128)(2,1)S(1)}, u32[]{:S(2)}) copy-start(bf16[128,1280]{1,0:T(8,128)(2,1)S(1)} %collective-permute-done.6) | copy-start | bytes 983044
  41.3 29.8 %collective-permute-start.7 = (bf16[256,1280]{1,0:T(8,128)(2,1)S(1)}, bf16[256,1280]{1,0:T(8,128)(2,1)S(1)}, u32[]{:S(2)}, u32[]{:S(2)}) collective-permute-start(bf16[256,1280]{1,0:T(8,128)(2,1)S(1)} %pad_maximum_fusion.1), channel_id=1, source_target_pairs={{0,16},{8,24},{16,0},{24,8},{32,48},{40,56},{48,32},{56,40},{64,80... | collective-permute-start | bytes 1966088 | tf_op jit(solution)/shard_map/ppermute | solution.py:665
  44.7 27.4 %collective-permute-start.3 = (bf16[128,2048]{1,0:T(8,128)(2,1)}, bf16[128,2048]{1,0:T(8,128)(2,1)}, u32[]{:S(2)}, u32[]{:S(2)}) collective-permute-start(bf16[128,2048]{1,0:T(8,128)(2,1)} %copy-done.17), channel_id=1, source_target_pairs={{0,1},{1,2},{2,3},{3,0},{4,5},{5,6},{6,7},{7,4},{8,9},{9,10},{10,1... | collective-permute-start | bytes 1572872 | tf_op jit(solution)/shard_map/ppermute | solution.py:650
  45.8 26.3 %collective-permute-start.4 = (bf16[128,2048]{1,0:T(8,128)(2,1)}, bf16[128,2048]{1,0:T(8,128)(2,1)}, u32[]{:S(2)}, u32[]{:S(2)}) collective-permute-start(bf16[128,2048]{1,0:T(8,128)(2,1)} %copy-done.17), channel_id=1, source_target_pairs={{0,3},{1,0},{2,1},{3,2},{4,7},{5,4},{6,5},{7,6},{8,11},{9,8},{10,9... | collective-permute-start | bytes 1572872 | tf_op jit(solution)/shard_map/ppermute | solution.py:650
  48.0 24.2 %collective-permute-start.5 = (bf16[128,2048]{1,0:T(8,128)(2,1)}, bf16[128,2048]{1,0:T(8,128)(2,1)}, u32[]{:S(2)}, u32[]{:S(2)}) collective-permute-start(bf16[128,2048]{1,0:T(8,128)(2,1)} %copy-done.18), channel_id=1, source_target_pairs={{0,1},{1,2},{2,3},{3,0},{4,5},{5,6},{6,7},{7,4},{8,9},{9,10},{10,1... | collective-permute-start | bytes 1572872 | tf_op jit(solution)/shard_map/ppermute | solution.py:650
  50.3 30.4 %copy-start.25 = (s32[16]{0:T(128)S(1)}, s32[16]{0:T(128)}, u32[]{:S(2)}) copy-start(s32[16]{0:T(128)} %param.41) | copy-start | bytes 196
  50.3 30.5 %copy-start.26 = (s32[8]{0:T(128)S(1)}, s32[8]{0:T(128)}, u32[]{:S(2)}) copy-start(s32[8]{0:T(128)} %param.40) | copy-start | bytes 100
  50.3 34.0 %copy-start.27 = (s32[8]{0:T(128)S(1)}, s32[8]{0:T(128)}, u32[]{:S(2)}) copy-start(s32[8]{0:T(128)} %param.39) | copy-start | bytes 100
  72.2 26.9 %all-to-all-start.2 = ((bf16[8,448,256]{2,1,0:T(8,128)(2,1)}), bf16[8,448,256]{2,1,0:T(8,128)(2,1)S(1)}, u32[]{:S(2)}, u32[]{:S(2)}) async-start(bf16[8,448,256]{2,1,0:T(8,128)(2,1)} %pack_paths.1), calls=%async_computation.2 | async-start | bytes 3670016 | tf_op jit(solution)/shard_map/all_to_all | solution.py:699
  76.0 36.1 %collective-permute-start.13 = (bf16[512,1280]{1,0:T(8,128)(2,1)S(1)}, bf16[512,1280]{1,0:T(8,128)(2,1)}, u32[]{:S(2)}, u32[]{:S(2)}) collective-permute-start(bf16[512,1280]{1,0:T(8,128)(2,1)S(1)} %pad_maximum_fusion), channel_id=1, source_target_pairs={{0,32},{8,40},{16,48},{24,56},{32,64},{40,72},{48,80},{56,88},{64,... | collective-permute-start | bytes 3932168 | tf_op jit(solution)/shard_map/ppermute | solution.py:669
  78.0 38.6 %collective-permute-start.14 = (bf16[512,1280]{1,0:T(8,128)(2,1)S(1)}, bf16[512,1280]{1,0:T(8,128)(2,1)}, u32[]{:S(2)}, u32[]{:S(2)}) collective-permute-start(bf16[512,1280]{1,0:T(8,128)(2,1)S(1)} %pad_maximum_fusion), channel_id=1, source_target_pairs={{0,96},{8,104},{16,112},{24,120},{32,0},{40,8},{48,16},{56,24},{64... | collective-permute-start | bytes 3932168 | tf_op jit(solution)/shard_map/ppermute | solution.py:669
  81.0 28.2 %collective-permute-start.8 = (bf16[128,2048]{1,0:T(8,128)(2,1)}, bf16[128,2048]{1,0:T(8,128)(2,1)}, u32[]{:S(2)}, u32[]{:S(2)}) collective-permute-start(bf16[128,2048]{1,0:T(8,128)(2,1)} %collective-permute-done.4.across_right), channel_id=1, source_target_pairs={{0,3},{1,0},{2,1},{3,2},{4,7},{5,4},{6,5},{7,6},{8,11},{9,8},{10,9... | collective-permute-start | bytes 1572872 | tf_op jit(solution)/shard_map/ppermute | solution.py:650
  84.5 51.7 %collective-permute-start.9 = (bf16[2048,256]{1,0:T(8,128)(2,1)}, bf16[2048,256]{1,0:T(8,128)(2,1)}, u32[]{:S(2)}, u32[]{:S(2)}) collective-permute-start(bf16[2048,256]{1,0:T(8,128)(2,1)} %bitcast.19.weight_own), channel_id=1, source_target_pairs={{0,8},{8,0},{16,24},{24,16},{32,40},{40,32},{48,56},{56,48},{64,72... | collective-permute-start | bytes 3145736 | tf_op jit(solution)/shard_map/ppermute | solution.py:665
  99.4 36.8 %copy-start.16 = (bf16[448,256]{1,0:T(8,128)(2,1)}, bf16[448,256]{1,0:T(8,128)(2,1)S(1)}, u32[]{:S(2)}) copy-start(bf16[448,256]{1,0:T(8,128)(2,1)S(1)} %reduce_sum.102.piece_0) | copy-start | bytes 688132
  109.2 8.5 %collective-permute-start.10 = (bf16[448,256]{1,0:T(8,128)(2,1)S(1)}, bf16[448,256]{1,0:T(8,128)(2,1)S(1)}, u32[]{:S(2)}, u32[]{:S(2)}) collective-permute-start(bf16[448,256]{1,0:T(8,128)(2,1)S(1)} %reduce_sum.102.piece_0), channel_id=1, source_target_pairs={{0,1},{1,0},{2,3},{3,2},{4,5},{5,4},{6,7},{7,6},{8,9},{9,8},{10,11... | collective-permute-start | bytes 688136 | tf_op jit(solution)/shard_map/ppermute | solution.py:703
  110.6 11.1 %collective-permute-start.11 = (bf16[448,256]{1,0:T(8,128)(2,1)S(1)}, bf16[448,256]{1,0:T(8,128)(2,1)S(1)}, u32[]{:S(2)}, u32[]{:S(2)}) collective-permute-start(bf16[448,256]{1,0:T(8,128)(2,1)S(1)} %reduce_sum.102.piece_0), channel_id=1, source_target_pairs={{0,2},{1,3},{2,0},{3,1},{4,6},{5,7},{6,4},{7,5},{8,10},{9,11},{10,... | collective-permute-start | bytes 688136 | tf_op jit(solution)/shard_map/ppermute | solution.py:703
  112.1 12.2 %collective-permute-start.12 = (bf16[448,256]{1,0:T(8,128)(2,1)S(1)}, bf16[448,256]{1,0:T(8,128)(2,1)S(1)}, u32[]{:S(2)}, u32[]{:S(2)}) collective-permute-start(bf16[448,256]{1,0:T(8,128)(2,1)S(1)} %reduce_sum.102.piece_0), channel_id=1, source_target_pairs={{0,3},{1,2},{2,1},{3,0},{4,7},{5,6},{6,5},{7,4},{8,11},{9,10},{10,... | collective-permute-start | bytes 688136 | tf_op jit(solution)/shard_map/ppermute | solution.py:703
  117.8 18.4 %copy-start.20 = (bf16[448,256]{1,0:T(8,128)(2,1)}, bf16[448,256]{1,0:T(8,128)(2,1)S(1)}, u32[]{:S(2)}) copy-start(bf16[448,256]{1,0:T(8,128)(2,1)S(1)} %collective-permute-done.10.piece_1) | copy-start | bytes 688132
  121.7 9.9 %copy-start.21 = (bf16[448,256]{1,0:T(8,128)(2,1)}, bf16[448,256]{1,0:T(8,128)(2,1)S(1)}, u32[]{:S(2)}) copy-start(bf16[448,256]{1,0:T(8,128)(2,1)S(1)} %collective-permute-done.11.piece_2) | copy-start | bytes 688132
  124.3 7.3 %copy-start.22 = (bf16[448,256]{1,0:T(8,128)(2,1)}, bf16[448,256]{1,0:T(8,128)(2,1)S(1)}, u32[]{:S(2)}) copy-start(bf16[448,256]{1,0:T(8,128)(2,1)S(1)} %collective-permute-done.12.piece_3) | copy-start | bytes 688132
  126.3 32.0 %collective-permute-start.15 = (bf16[256,1280]{1,0:T(8,128)(2,1)}, bf16[256,1280]{1,0:T(8,128)(2,1)}, u32[]{:S(2)}, u32[]{:S(2)}) collective-permute-start(bf16[256,1280]{1,0:T(8,128)(2,1)} %slice.53), channel_id=1, source_target_pairs={{0,32},{8,40},{16,48},{24,56},{32,64},{40,72},{48,80},{56,88},{64,... | collective-permute-start | bytes 1966088 | tf_op jit(solution)/shard_map/ppermute | solution.py:669
  129.8 28.6 %collective-permute-start.16 = (bf16[256,1280]{1,0:T(8,128)(2,1)}, bf16[256,1280]{1,0:T(8,128)(2,1)}, u32[]{:S(2)}, u32[]{:S(2)}) collective-permute-start(bf16[256,1280]{1,0:T(8,128)(2,1)} %slice.54), channel_id=1, source_target_pairs={{0,96},{8,104},{16,112},{24,120},{32,0},{40,8},{48,16},{56,24},{64... | collective-permute-start | bytes 1966088 | tf_op jit(solution)/shard_map/ppermute | solution.py:669
  168.5 15.1 %collective-permute-start.17 = (bf16[2048,1280]{1,0:T(8,128)(2,1)}, bf16[2048,1280]{1,0:T(8,128)(2,1)}, u32[]{:S(2)}, u32[]{:S(2)}) collective-permute-start(bf16[2048,1280]{1,0:T(8,128)(2,1)} %constant_dynamic-update-slice_fusion.own.next_own), channel_id=1, source_target_pairs={{0,8},{8,0},{16,24},{24,16},{32,40},{40,32},{48,56},{56,48},{64,72... | collective-permute-start | bytes 15728648 | tf_op jit(solution)/shard_map/ppermute | solution.py:665
  168.6 15.0 %all-to-all-start.3 = ((bf16[8,128,256]{2,1,0:T(8,128)(2,1)}), bf16[8,128,256]{2,1,0:T(8,128)(2,1)S(1)}, u32[]{:S(2)}, u32[]{:S(2)}) async-start(bf16[8,128,256]{2,1,0:T(8,128)(2,1)} %bitcast.22), calls=%async_computation.3 | async-start | bytes 1048576 | tf_op jit(solution)/shard_map/all_to_all | solution.py:722
  196.4 58.7 %all-to-all-start.4 = ((bf16[128,8,2048]{2,1,0:T(8,128)(2,1)}), bf16[128,8,2048]{2,1,0:T(8,128)(2,1)}, u32[]{:S(2)}, u32[]{:S(2)}) async-start(bf16[128,8,2048]{2,1,0:T(8,128)(2,1)} %convert_bitcast_fusion), calls=%async_computation.4 | async-start | bytes 8388608 | tf_op jit(solution)/shard_map/all_to_all | solution.py:400
  255.0 23.8 %all-to-all-start.5 = ((bf16[128,2,2048]{2,1,0:T(2,128)(2,1)}), bf16[128,2,2048]{2,1,0:T(2,128)(2,1)S(1)}, u32[]{:S(2)}, u32[]{:S(2)}) async-start(bf16[128,2,2048]{2,1,0:T(2,128)(2,1)} %reshape.153), calls=%async_computation.5 | async-start | bytes 2097152 | tf_op jit(solution)/shard_map/all_to_all | solution.py:400
  259.7 10.2 %copy-start.11 = (bf16[1,768,2048]{2,1,0:T(8,128)(2,1)S(1)}, bf16[1,768,2048]{2,1,0:T(8,128)(2,1)}, u32[]{:S(2)}) copy-start(bf16[1,768,2048]{2,1,0:T(8,128)(2,1)} %param.31) | copy-start | bytes 9437188
  288.0 9.4 %copy-start.24 = (f32[128,8]{0,1:T(8,128)S(1)}, f32[128,8]{0,1:T(8,128)}, u32[]{:S(2)}) copy-start(f32[128,8]{0,1:T(8,128)} %param.34) | copy-start | bytes 12292
  288.0 74.0 %all-to-all-start.6 = ((bf16[128,40,512]{2,1,0:T(8,128)(2,1)}), bf16[128,40,512]{2,1,0:T(8,128)(2,1)}, u32[]{:S(2)}, u32[]{:S(2)}) async-start(bf16[128,40,512]{2,1,0:T(8,128)(2,1)} %expert_rest.1), calls=%async_computation.6 | async-start | bytes 10485760 | tf_op jit(solution)/shard_map/all_to_all | solution.py:400
  (5 other events, 15.8 us)

commit v7 on v6

--- a/solution.py
+++ b/solution.py
@@ -320,9 +320,19 @@
     return 2 * half + lax.rem(step, 2)
 
 
-def project_kernel(
-    place, attended, own, other, hidden, gain, out, normed, joined_own, joined_other, layer
-):
+def multiply(values, pieces):
+    rows = pieces[0].shape[0]
+    return sum(
+        jnp.dot(
+            values[:, at * rows : (at + 1) * rows], piece[...], preferred_element_type=jnp.float32
+        )
+        for at, piece in enumerate(pieces)
+    )
+
+
+def project_kernel(place, attended, *refs):
+    own, other = refs[:4], refs[4:8]
+    hidden, gain, out, normed, joined_own, joined_other, layer = refs[8:]
     wide = attended.shape[2]
     step = pl.program_id(0)
     x, y, core = place[0], place[1], place[2]
@@ -338,7 +348,7 @@
                 joined_other[:, columns] = jnp.where(core == 0, swapped, block)
 
     def add(joined, weight):
-        added = jnp.dot(joined[...], weight[...], preferred_element_type=jnp.float32)
+        added = multiply(joined[...], weight)
         done = (hidden[...].astype(jnp.float32) + added).astype(jnp.bfloat16)
         out[...] = done
         layer[column_block(step, core)] = done
@@ -372,8 +382,10 @@
             grid=(4,),
             in_specs=[
                 pl.BlockSpec(attended.shape, lambda j, at: (0, 0, 0)),
-                pl.BlockSpec((dim, columns), lambda j, at: (0, jnp.minimum(j, 1))),
-                pl.BlockSpec((dim, columns), lambda j, at: (0, jnp.maximum(j - 2, 0))),
+            ]
+            + [pl.BlockSpec((dim // 4, columns), lambda j, at: (0, jnp.minimum(j, 1)))] * 4
+            + [pl.BlockSpec((dim // 4, columns), lambda j, at: (0, jnp.maximum(j - 2, 0)))] * 4
+            + [
                 pl.BlockSpec((tok, columns), lambda j, at: (0, column_block(j, at[2]))),
                 pl.BlockSpec((1, dim), lambda j, at: (0, 0)),
             ],
@@ -471,24 +483,9 @@
     return jnp.concatenate(mine, axis=1), jnp.concatenate(theirs, axis=1)
 
 
-def finish_kernel(
-    place,
-    main_share,
-    rest_share,
-    main_rows,
-    rest_rows,
-    stream,
-    next_own,
-    next_other,
-    norm_gain,
-    head_gain,
-    cosine,
-    sine,
-    out,
-    next_rows,
-    layer,
-    joined,
-):
+def finish_kernel(place, main_share, rest_share, main_rows, rest_rows, stream, *refs):
+    next_own, next_other = refs[:4], refs[4:8]
+    norm_gain, head_gain, cosine, sine, out, next_rows, layer, joined = refs[8:]
     tok = stream.shape[0]
     count = main_share.shape[1]
     wide = main_rows.shape[2]
@@ -515,8 +512,8 @@
             normed = (part * inverse * norm_gain[:, columns]).astype(jnp.bfloat16)
             joined[:, columns] = normed
         mine, theirs = reorder(place, joined)
-        raw_own = jnp.dot(mine, next_own[...], preferred_element_type=jnp.float32)
-        raw_other = jnp.dot(theirs, next_other[...], preferred_element_type=jnp.float32)
+        raw_own = multiply(mine, next_own)
+        raw_other = multiply(theirs, next_other)
         keys = jnp.where(place[2] == 0, raw_own, raw_other)
         values = jnp.where(place[2] == 0, raw_other, raw_own)
         half = keys.shape[1]
@@ -541,7 +538,7 @@
     def fixed(values):
         return pl.BlockSpec(values.shape, lambda j, at: (0, 0))
 
-    next_spec = pl.BlockSpec((dim, extra), lambda j, at: (0, dim // 2 // extra))
+    next_spec = pl.BlockSpec((dim // 4, extra), lambda j, at: (0, dim // 2 // extra))
     return pl.pallas_call(
         finish_kernel,
         grid_spec=pltpu.PrefetchScalarGridSpec(
@@ -553,8 +550,9 @@
                 pl.BlockSpec((devices, rows, wide), lambda j, at: (0, j, 0)),
                 pl.BlockSpec((devices, rows, wide), lambda j, at: (0, chunks, 0)),
                 pl.BlockSpec((tok, wide), lambda j, at: (0, j)),
-                next_spec,
-                next_spec,
+            ]
+            + [next_spec] * 8
+            + [
                 fixed(norm_gain),
                 fixed(head_gain),
                 fixed(turns[0]),
@@ -678,7 +676,7 @@
     early = lax.all_to_all(early, "dp", split_axis=0, concat_axis=0, tiled=True)
     early = early.reshape(dim, 2 * hd)
     sides = [left, right, shift(across, 1), shift(across, -1)]
-    own_far = shift(left, 1)
+    far = [shift(normed, 2), shift(across, 2)]
     tables = (
         token_request,
         request_leaf,
@@ -689,23 +687,6 @@
         leaf_slot,
     )
     path = pack_paths(tables, root_cache, mid_cache, leaf_cache, mp_size)
-    path, sides, own_far, late, early = lax.optimization_barrier(
-        (path, sides, own_far, late, early)
-    )
-    far = [own_far, shift(sides[3], -1)]
-    weights = (early, swap(early, 1))
-    x_left = shift_x(late, 1)
-    x_right = shift_x(late, -1)
-    path = lax.all_to_all(path, "mp", split_axis=0, concat_axis=0, tiled=True)
-    own_piece = jnp.sum(path.astype(jnp.float32), axis=0).astype(jnp.bfloat16)
-    own_piece, far = lax.optimization_barrier((own_piece, far))
-    pieces = [own_piece] + [
-        lax.ppermute(own_piece, "mp", [(j, j ^ s) for j in range(mp_size)]) for s in range(1, 4)
-    ]
-    pieces, x_left, x_right = lax.optimization_barrier((pieces, x_left, x_right))
-    middle = x_left.shape[0] // 2
-    x_far = [shift_x(x_left[:middle], 1), shift_x(x_right[middle:], -1)]
-    rows = [normed, across] + sides + far
     meta = jnp.concatenate(
         [
             jnp.stack([me, cut]),
@@ -713,12 +694,25 @@
             jnp.stack([lax.rem(lax.axis_index("dp"), 2)]),
         ]
     ).astype(jnp.int32)
+    path, sides, far, early, cosine, sine, meta = lax.optimization_barrier(
+        (path, sides, far, early, cosine, sine, meta)
+    )
+    weights = (early, swap(early, 1))
+    x_left = shift_x(late, 1)
+    x_right = shift_x(late, -1)
+    path = lax.all_to_all(path, "mp", split_axis=0, concat_axis=0, tiled=True)
+    own_piece = jnp.sum(path.astype(jnp.float32), axis=0).astype(jnp.bfloat16)
+    own_piece, weights, handed = lax.optimization_barrier((own_piece, weights, swap(late, 1)))
+    pieces = [own_piece] + [
+        lax.ppermute(own_piece, "mp", [(j, j ^ s) for j in range(mp_size)]) for s in range(1, 4)
+    ]
+    pieces, x_left, x_right = lax.optimization_barrier((pieces, x_left, x_right))
+    x_far = shift_x(x_left, 1)
+    rows = [normed, across] + sides + far
     attended = attend(meta, rows, weights, pieces, head_gains, cosine, sine)
-    attended, late, x_left, x_right, x_far = lax.optimization_barrier(
-        (attended, late, x_left, x_right, x_far)
-    )
-    own_half = jnp.concatenate([late, x_left, x_right] + x_far, axis=0)
-    halves = (own_half, swap(own_half, 1))
+    attended, x_far = lax.optimization_barrier((attended, x_far))
+    halves = (late, x_left, x_right, x_far, handed)
+    halves += tuple(swap(piece, 1) for piece in (x_left, x_right, x_far))
     attended = lax.all_to_all(
         attended.reshape(mp_size, tok, 2 * hd), "mp", split_axis=0, concat_axis=0, tiled=True
     )

time: 372 us -> 361 us (0.970)
  local copies, waits for them, and re-layouts: 30 us -> 17.3 us
  starting transfers between devices: 67.5 us -> 62.8 us
  waiting for transfers between devices: 185 us -> 189 us
    ppermute x6, waiting for transfers between devices: 11 us -> 33 us  [shift(): return lax.ppermute(values, 'mp', moves)]
    ppermute x4 -> x7, waiting for transfers between devices: 20.8 us -> 0.02 us  [swap(): return lax.ppermute(values, 'dp', [(j, j ^ bit) for j in range(dp_size)])]
    ppermute x1, waiting for transfers between devices: 13.8 us -> 0.01 us  [per_device(): lax.ppermute(normed, 'mp', [(j, (j + 4) % mp_size) for j in range(mp_size)])]
    ppermute x4 -> x3, waiting for transfers between devices: 0.01 us -> 12.7 us  [shift_x(): return lax.ppermute(values, 'dp', moves)]
    unnamed x62 -> x64, local copies, waits for them, and re-layouts: 9.28 us -> 1.56 us
    all_to_all x1, waiting for transfers between devices: 13.2 us -> 17.9 us  [per_device(): path = lax.all_to_all(path, 'mp', split_axis=0, concat_axis=0, tiled=True)]
    slice x2 -> x0, local copies, waits for them, and re-layouts: 4.06 us -> none  [per_device(): x_far = [shift_x(x_left[:middle], 1), shift_x(x_right[middle:], -1)]]
  transfers between devices with their start and end apart: 25 -> 27, of which waited for: 12 -> 15; matrix products, arithmetic and copies ran while one was open for 13% -> 12% of each run, Pallas kernels for 7% -> 7%
where the time goes in v7:
time: 361 us; the launch traced here: 359 us
  waiting for transfers between devices  189 us (52%)
  starting transfers between devices  62.8 us (17%)
  Pallas kernels  50.9 us (14%)
  matrix products  18.9 us (5%)
  other arithmetic  17.6 us (5%)
  local copies, waits for them, and re-layouts  17.3 us (5%)
    all_to_all x3, waiting for transfers between devices, exchange(): return lax.all_to_all(values, BOTH, split_axis=0, concat_axis=0, tiled=True)  110 us
    ppermute x6, waiting for transfers between devices, shift(): return lax.ppermute(values, 'mp', moves)  33 us
    pallas_call x1, Pallas kernels, attend(): pl.pallas_call(attention_kernel, out_shape=jax.ShapeDtypeStruct((group, 2...  22.2 us
    all_to_all x3, starting transfers between devices, exchange(): return lax.all_to_all(values, BOTH, split_axis=0, concat_axis=0, tiled=True)  18.7 us
    all_to_all x1, waiting for transfers between devices, per_device(): path = lax.all_to_all(path, 'mp', split_axis=0, concat_axis=0, tiled=True)  17.9 us
    ppermute x3, waiting for transfers between devices, shift_x(): return lax.ppermute(values, 'dp', moves)  12.7 us
    dot_general x1, matrix products, expert(): both = jnp.dot(rows, gate_up, preferred_element_type=jnp.float32)  10.2 us
    ppermute x6, starting transfers between devices, shift(): return lax.ppermute(values, 'mp', moves)  10.1 us
  transfers between devices with their start and end apart: 27, of which 15 were waited for; matrix products, arithmetic and copies ran while one was open for 12% of the time, Pallas kernels for 7%

profile of v7, /device:TPU:0, one launch (start us, length us, event | category | flops | bytes accessed | tf_op | source)
XLA Modules:
  0.0 359.5 jit_solution(6951090918024511077)
XLA Ops:
  0.7 1.5 fusion.30
  4.7 1.7 collective-permute-start
  6.4 1.9 collective-permute-start.1
  8.3 2.1 collective-permute-start.2
  10.5 1.9 collective-permute-start.5
  12.3 1.9 pack_weights.1
  14.2 3.5 all-to-all-start
  19.6 6.3 %collective-permute-done.1.own_left = bf16[128,2048]{1,0:T(8,128)(2,1)S(1)} collective-permute-done((bf16[128,2048]{1,0:T(8,128)(2,1)S(1)}, bf16[128,2048]{1,0:T(8,128)(2,1)S(1)}, u32[]{:S(2)}, u32[]{:S(2)}) %collective-permute-start.1) | collective-permute-done | bytes 524320 | tf_op jit(solution)/shard_map/ppermute | solution.py:648
  25.9 13.1 %collective-permute-done.2.own_right = bf16[128,2048]{1,0:T(8,128)(2,1)S(1)} collective-permute-done((bf16[128,2048]{1,0:T(8,128)(2,1)S(1)}, bf16[128,2048]{1,0:T(8,128)(2,1)S(1)}, u32[]{:S(2)}, u32[]{:S(2)}) %collective-permute-start.2) | collective-permute-done | bytes 524320 | tf_op jit(solution)/shard_map/ppermute | solution.py:648
  39.0 3.1 all-to-all-done
  45.4 6.9 %all-to-all-start.1 = ((bf16[16,128,256]{2,1,0:T(8,128)(2,1)}), bf16[16,128,256]{2,1,0:T(8,128)(2,1)}, u32[]{:S(2)}, u32[]{:S(2)}) async-start(bf16[16,128,256]{2,1,0:T(8,128)(2,1)} %bitcast.11), calls=%async_computation.1 | async-start | bytes 2097152 | tf_op jit(solution)/shard_map/all_to_all | solution.py:676
  53.3 3.4 collective-permute-start.9
  56.9 2.0 collective-permute-start.3
  63.6 2.2 pack_paths.1
  67.2 1.9 fusion.13
  70.4 1.7 collective-permute-done.3.across_left
  72.1 1.8 collective-permute-done.4.across_right
  73.8 10.2 %collective-permute-done.6.across_far = bf16[128,2048]{1,0:T(8,128)(2,1)} collective-permute-done((bf16[128,2048]{1,0:T(8,128)(2,1)S(1)}, bf16[128,2048]{1,0:T(8,128)(2,1)}, u32[]{:S(2)}, u32[]{:S(2)}) %collective-permute-start.6) | collective-permute-done | bytes 524320 | tf_op jit(solution)/shard_map/ppermute | solution.py:648
  84.0 3.6 %all-to-all-start.2 = ((bf16[8,448,256]{2,1,0:T(8,128)(2,1)}), bf16[8,448,256]{2,1,0:T(8,128)(2,1)S(1)}, u32[]{:S(2)}, u32[]{:S(2)}) async-start(bf16[8,448,256]{2,1,0:T(8,128)(2,1)} %pack_paths.1), calls=%async_computation.2 | async-start | bytes 3670016 | tf_op jit(solution)/shard_map/all_to_all | solution.py:703
  89.0 1.5 collective-permute-start.14
  90.5 1.8 collective-permute-start.15
  92.3 17.9 %all-to-all-done.2 = bf16[8,448,256]{2,1,0:T(8,128)(2,1)S(1)} async-done(((bf16[8,448,256]{2,1,0:T(8,128)(2,1)}), bf16[8,448,256]{2,1,0:T(8,128)(2,1)S(1)}, u32[]{:S(2)}, u32[]{:S(2)}) %all-to-all-start.2) | async-done | bytes 1835040 | tf_op jit(solution)/shard_map/all_to_all | solution.py:703
  111.5 2.2 collective-permute-start.12
  113.7 1.7 collective-permute-start.13
  115.3 6.1 %collective-permute-done.14.refs_1_ = bf16[512,1280]{1,0:T(8,128)(2,1)} collective-permute-done((bf16[512,1280]{1,0:T(8,128)(2,1)S(1)}, bf16[512,1280]{1,0:T(8,128)(2,1)}, u32[]{:S(2)}, u32[]{:S(2)}) %collective-permute-start.14) | collective-permute-done | bytes 1310752 | tf_op jit(solution)/shard_map/ppermute | solution.py:667
  121.5 1.6 collective-permute-done.12.piece_2
  123.1 2.6 collective-permute-done.13.piece_3
  125.7 1.5 collective-permute-start.16
  127.6 22.2 %tree_attention.1 = bf16[1024,256]{1,0:T(8,128)(2,1)} custom-call(s32[9]{0:T(128)} %pad_add_fusion.2.meta, bf16[128,2048]{1,0:T(8,128)(2,1)} %copy-done.15, bf16[128,2048]{1,0:T(8,128)(2,1)} %copy-done.19, bf16[128,2048]{1,0:T(8,128)(2,1)} %copy-done.21, bf16[128,2048]{1,0:T(8,128)(2,1)} %copy-done.22, bf16[128,2048]{1,0:T(8,128)(2,1)} %collective-permute-done.3.across_left, ...), custom_call_target="tpu_custom_call" | custom-call | flops 2147483648 | bytes 8388608 | tf_op jit(solution)/shard_map/tree_attention/pallas_call | solution.py:293
  149.9 6.6 %collective-permute-done.16.refs_3_ = bf16[512,1280]{1,0:T(8,128)(2,1)S(1)} collective-permute-done((bf16[512,1280]{1,0:T(8,128)(2,1)}, bf16[512,1280]{1,0:T(8,128)(2,1)S(1)}, u32[]{:S(2)}, u32[]{:S(2)}) %collective-permute-start.16) | collective-permute-done | bytes 1310752 | tf_op jit(solution)/shard_map/ppermute | solution.py:667
  156.6 4.7 %all-to-all-start.3 = ((bf16[8,128,256]{2,1,0:T(8,128)(2,1)}), bf16[8,128,256]{2,1,0:T(8,128)(2,1)S(1)}, u32[]{:S(2)}, u32[]{:S(2)}) async-start(bf16[8,128,256]{2,1,0:T(8,128)(2,1)} %bitcast.55), calls=%async_computation.3 | async-start | bytes 1048576 | tf_op jit(solution)/shard_map/all_to_all | solution.py:716
  162.6 8.8 %all-to-all-done.3.attended = bf16[8,128,256]{2,1,0:T(8,128)(2,1)S(1)} async-done(((bf16[8,128,256]{2,1,0:T(8,128)(2,1)}), bf16[8,128,256]{2,1,0:T(8,128)(2,1)S(1)}, u32[]{:S(2)}, u32[]{:S(2)}) %all-to-all-start.3) | async-done | bytes 524320 | tf_op jit(solution)/shard_map/all_to_all | solution.py:716
  172.6 7.6 %project.1 = (bf16[128,2048]{1,0:T(8,128)(2,1)}, bf16[128,2048]{1,0:T(8,128)(2,1)}) custom-call(s32[3]{0:T(128)} %pad_add_fusion.1.place, bf16[8,128,256]{2,1,0:T(8,128)(2,1)} %copy-done.14, bf16[512,1280]{1,0:T(8,128)(2,1)} %copy-done.10, bf16[512,1280]{1,0:T(8,128)(2,1)} %collective-permute-done.14.refs_1_, ...), custom_call_target="tpu_custom_call" | custom-call | tf_op jit(solution)/shard_map/project/pallas_call | solution.py:378
  180.2 4.4 %convert_bitcast_fusion = bf16[128,8,2048]{2,1,0:T(8,128)(2,1)} fusion(bf16[128,2048]{1,0:T(8,128)(2,1)} %get-tuple-element.62, s32[1024]{0:T(1024)S(1)} %eq.180, s32[128,128]{1,0:T(8,128)S(1)} %copy.68), kind=kOutput, calls=%fused_computation.2 | convolution fusion | flops 539099136 | bytes 4788224 | tf_op jit(solution)/shard_map/dot_general | solution.py:743
  184.6 6.0 %all-to-all-start.4 = ((bf16[128,8,2048]{2,1,0:T(8,128)(2,1)}), bf16[128,8,2048]{2,1,0:T(8,128)(2,1)}, u32[]{:S(2)}, u32[]{:S(2)}) async-start(bf16[128,8,2048]{2,1,0:T(8,128)(2,1)} %convert_bitcast_fusion), calls=%async_computation.4 | async-start | bytes 8388608 | tf_op jit(solution)/shard_map/all_to_all | solution.py:412
  191.3 1.5 reshape.153
  192.8 50.5 %all-to-all-done.4 = bf16[128,8,2048]{2,1,0:T(8,128)(2,1)} async-done(((bf16[128,8,2048]{2,1,0:T(8,128)(2,1)}), bf16[128,8,2048]{2,1,0:T(8,128)(2,1)}, u32[]{:S(2)}, u32[]{:S(2)}) %all-to-all-start.4) | async-done | bytes 4194336 | tf_op jit(solution)/shard_map/all_to_all | solution.py:412
  243.2 4.8 %all-to-all-start.5 = ((bf16[128,2,2048]{2,1,0:T(2,128)(2,1)}), bf16[128,2,2048]{2,1,0:T(2,128)(2,1)S(1)}, u32[]{:S(2)}, u32[]{:S(2)}) async-start(bf16[128,2,2048]{2,1,0:T(2,128)(2,1)} %reshape.153), calls=%async_computation.5 | async-start | bytes 2097152 | tf_op jit(solution)/shard_map/all_to_all | solution.py:412
  248.1 10.2 %fusion = f32[1024,1536]{1,0:T(8,128)S(1)} fusion(bf16[128,8,2048]{2,1,0:T(8,128)(2,1)} %all-to-all-done.4, bf16[1,2048,1536]{2,1,0:T(8,128)(2,1)} %param.30), kind=kOutput, calls=%fused_computation | convolution fusion | flops 6442450944 | bytes 16777216 | tf_op jit(solution)/shard_map/dot_general | solution.py:417
  258.3 3.7 %convolution_convert_fusion = bf16[1024,2048]{1,0:T(8,128)(2,1)S(1)} fusion(f32[1024,1536]{1,0:T(8,128)S(1)} %fusion, bf16[1,768,2048]{2,1,0:T(8,128)(2,1)S(1)} %copy-done.13), kind=kOutput, calls=%fused_computation.3 | convolution fusion | flops 3228041216 | bytes 13631488 | tf_op jit(solution)/shard_map/dot_general | solution.py:419
  262.0 2.9 pad.4.main_block
  264.9 2.1 all-to-all-done.5
  268.2 8.1 %expert_rest.1 = bf16[128,40,512]{2,1,0:T(8,128)(2,1)} custom-call(bf16[256,2048]{1,0:T(8,128)(2,1)} %reshape.157.rows, bf16[2048,1536]{1,0:T(8,128)(2,1)} %bitcast.50, bf16[768,2048]{1,0:T(8,128)(2,1)} %bitcast.52, bf16[128,40,512]{2,1,0:T(8,128)(2,1)} %pad.4.main_block), custom_call_target="tpu_custom_call", output_to_operand_aliasing={{}: (3, {})} | custom-call | tf_op jit(solution)/shard_map/expert_rest/pallas_call | solution.py:460
  276.4 7.9 %all-to-all-start.6 = ((bf16[128,40,512]{2,1,0:T(8,128)(2,1)}), bf16[128,40,512]{2,1,0:T(8,128)(2,1)}, u32[]{:S(2)}, u32[]{:S(2)}) async-start(bf16[128,40,512]{2,1,0:T(8,128)(2,1)} %expert_rest.1), calls=%async_computation.6 | async-start | bytes 10485760 | tf_op jit(solution)/shard_map/all_to_all | solution.py:412
  288.8 1.6 broadcast_multiply_fusion.rest_share
  290.4 1.5 constant_dynamic-slice_fusion.refs_11_
  293.3 57.1 %all-to-all-done.6.main_rows.rest_rows = bf16[128,40,512]{2,1,0:T(8,128)(2,1)} async-done(((bf16[128,40,512]{2,1,0:T(8,128)(2,1)}), bf16[128,40,512]{2,1,0:T(8,128)(2,1)}, u32[]{:S(2)}, u32[]{:S(2)}) %all-to-all-start.6) | async-done | bytes 5242912 | tf_op jit(solution)/shard_map/all_to_all | solution.py:412
  350.4 8.9 %finish.1 = (bf16[128,2048]{1,0:T(8,128)(2,1)}, bf16[128,512]{1,0:T(8,128)(2,1)}) custom-call(s32[3]{0:T(128)} %pad_add_fusion.1.place, bf16[256,1024]{1,0:T(8,128)(2,1)} %pad_maximum_fusion.2.main_share, bf16[4,256,1024]{2,1,0:T(8,128)(2,1)} %broadcast_multiply_fusion.rest_share, bf16[128,40,512]{2,1,0:T(8,128)(2,1)} %all-to-all-done.6.main_rows.rest_rows, ...), custom_call_target="tpu_custom_call" | custom-call | tf_op jit(solution)/shard_map/finish/pallas_call | solution.py:542
  (145 shorter events, 28.4 us)
Async XLA Ops:
  0.6 17.1 %copy-start.3 = (s32[1024]{0:T(1024)S(1)}, s32[1024]{0:T(1024)}, u32[]{:S(2)}) copy-start(s32[1024]{0:T(1024)} %token_request.1) | copy-start | bytes 12292
  0.6 18.2 %copy-start.6 = (s32[32]{0:T(128)S(1)}, s32[32]{0:T(128)}, u32[]{:S(2)}) copy-start(s32[32]{0:T(128)} %request_leaf.1) | copy-start | bytes 388
  0.7 18.3 %copy-start.4 = (s32[16]{0:T(128)S(1)}, s32[16]{0:T(128)}, u32[]{:S(2)}) copy-start(s32[16]{0:T(128)} %leaf_parent.1) | copy-start | bytes 196
  0.7 18.3 %copy-start.28 = (s32[16]{0:T(128)S(1)}, s32[16]{0:T(128)}, u32[]{:S(2)}) copy-start(s32[16]{0:T(128)} %param.41) | copy-start | bytes 196
  0.7 18.5 %copy-start.5 = (s32[8]{0:T(128)S(1)}, s32[8]{0:T(128)}, u32[]{:S(2)}) copy-start(s32[8]{0:T(128)} %mid_parent.1) | copy-start | bytes 100
  0.7 18.5 %copy-start.29 = (s32[8]{0:T(128)S(1)}, s32[8]{0:T(128)}, u32[]{:S(2)}) copy-start(s32[8]{0:T(128)} %param.40) | copy-start | bytes 100
  0.7 18.7 %copy-start.30 = (s32[8]{0:T(128)S(1)}, s32[8]{0:T(128)}, u32[]{:S(2)}) copy-start(s32[8]{0:T(128)} %param.39) | copy-start | bytes 100
  4.7 40.7 %copy-start.15 = (bf16[128,2048]{1,0:T(8,128)(2,1)}, bf16[128,2048]{1,0:T(8,128)(2,1)S(1)}, u32[]{:S(2)}) copy-start(bf16[128,2048]{1,0:T(8,128)(2,1)S(1)} %fusion.8.own) | copy-start | bytes 1572868
  4.7 14.9 %collective-permute-start = (bf16[128,2048]{1,0:T(8,128)(2,1)S(1)}, bf16[128,2048]{1,0:T(8,128)(2,1)S(1)}, u32[]{:S(2)}, u32[]{:S(2)}) collective-permute-start(bf16[128,2048]{1,0:T(8,128)(2,1)S(1)} %fusion.8.own), channel_id=1, source_target_pairs={{0,4},{1,5},{2,6},{3,7},{4,0},{5,1},{6,2},{7,3},{8,12},{9,13},{10,... | collective-permute-start | bytes 1572872 | tf_op jit(solution)/shard_map/ppermute | solution.py:650
  6.4 19.4 %collective-permute-start.1 = (bf16[128,2048]{1,0:T(8,128)(2,1)S(1)}, bf16[128,2048]{1,0:T(8,128)(2,1)S(1)}, u32[]{:S(2)}, u32[]{:S(2)}) collective-permute-start(bf16[128,2048]{1,0:T(8,128)(2,1)S(1)} %fusion.8.own), channel_id=1, source_target_pairs={{0,1},{1,2},{2,3},{3,0},{4,5},{5,6},{6,7},{7,4},{8,9},{9,10},{10,1... | collective-permute-start | bytes 1572872 | tf_op jit(solution)/shard_map/ppermute | solution.py:648
  8.3 30.6 %collective-permute-start.2 = (bf16[128,2048]{1,0:T(8,128)(2,1)S(1)}, bf16[128,2048]{1,0:T(8,128)(2,1)S(1)}, u32[]{:S(2)}, u32[]{:S(2)}) collective-permute-start(bf16[128,2048]{1,0:T(8,128)(2,1)S(1)} %fusion.8.own), channel_id=1, source_target_pairs={{0,3},{1,0},{2,1},{3,2},{4,7},{5,4},{6,5},{7,6},{8,11},{9,8},{10,9... | collective-permute-start | bytes 1572872 | tf_op jit(solution)/shard_map/ppermute | solution.py:648
  10.5 59.9 %collective-permute-start.5 = (bf16[128,2048]{1,0:T(8,128)(2,1)S(1)}, bf16[128,2048]{1,0:T(8,128)(2,1)}, u32[]{:S(2)}, u32[]{:S(2)}) collective-permute-start(bf16[128,2048]{1,0:T(8,128)(2,1)S(1)} %fusion.8.own), channel_id=1, source_target_pairs={{0,2},{1,3},{2,0},{3,1},{4,6},{5,7},{6,4},{7,5},{8,10},{9,11},{10,... | collective-permute-start | bytes 1572872 | tf_op jit(solution)/shard_map/ppermute | solution.py:648
  14.2 27.9 %all-to-all-start = ((bf16[8,16,3072]{2,1,0:T(8,128)(2,1)}), bf16[8,16,3072]{2,1,0:T(8,128)(2,1)S(1)}, u32[]{:S(2)}, u32[]{:S(2)}) async-start(bf16[8,16,3072]{2,1,0:T(8,128)(2,1)} %pack_weights.1), calls=%async_computation | async-start | bytes 1572864 | tf_op jit(solution)/shard_map/all_to_all | solution.py:654
  19.6 22.5 %copy-start.19 = (bf16[128,2048]{1,0:T(8,128)(2,1)}, bf16[128,2048]{1,0:T(8,128)(2,1)S(1)}, u32[]{:S(2)}) copy-start(bf16[128,2048]{1,0:T(8,128)(2,1)S(1)} %collective-permute-done.across) | copy-start | bytes 1572868
  25.9 16.2 %copy-start.21 = (bf16[128,2048]{1,0:T(8,128)(2,1)}, bf16[128,2048]{1,0:T(8,128)(2,1)S(1)}, u32[]{:S(2)}) copy-start(bf16[128,2048]{1,0:T(8,128)(2,1)S(1)} %collective-permute-done.1.own_left) | copy-start | bytes 1572868
  42.0 21.5 %copy-start = (bf16[1,512,512]{2,1,0:T(8,128)(2,1)S(1)}, bf16[1,512,512]{2,1,0:T(8,128)(2,1)}, u32[]{:S(2)}) copy-start(bf16[1,512,512]{2,1,0:T(8,128)(2,1)} %root.1) | copy-start | bytes 1572868
  42.0 21.5 %copy-start.1 = (bf16[1,256,512]{2,1,0:T(8,128)(2,1)S(1)}, bf16[1,256,512]{2,1,0:T(8,128)(2,1)}, u32[]{:S(2)}) copy-start(bf16[1,256,512]{2,1,0:T(8,128)(2,1)} %mid.1) | copy-start | bytes 786436
  42.1 21.5 %copy-start.2 = (bf16[2,128,512]{2,1,0:T(8,128)(2,1)S(1)}, bf16[2,128,512]{2,1,0:T(8,128)(2,1)}, u32[]{:S(2)}) copy-start(bf16[2,128,512]{2,1,0:T(8,128)(2,1)} %leaf.1) | copy-start | bytes 786436
  42.1 21.5 %copy-start.7 = (s32[8]{0:T(128)S(1)}, s32[8]{0:T(128)}, u32[]{:S(2)}) copy-start(s32[8]{0:T(128)} %root_slot.1) | copy-start | bytes 100
  42.1 21.5 %copy-start.8 = (s32[8]{0:T(128)S(1)}, s32[8]{0:T(128)}, u32[]{:S(2)}) copy-start(s32[8]{0:T(128)} %mid_slot.1) | copy-start | bytes 100
  42.1 21.5 %copy-start.9 = (s32[16]{0:T(128)S(1)}, s32[16]{0:T(128)}, u32[]{:S(2)}) copy-start(s32[16]{0:T(128)} %leaf_slot.1) | copy-start | bytes 196
  42.9 9.4 %collective-permute-start.8 = (bf16[128,1280]{1,0:T(8,128)(2,1)}, bf16[128,1280]{1,0:T(8,128)(2,1)S(1)}, u32[]{:S(2)}, u32[]{:S(2)}) collective-permute-start(bf16[128,1280]{1,0:T(8,128)(2,1)} %get-tuple-element.75), channel_id=1, source_target_pairs={{0,8},{8,0},{16,24},{24,16},{32,40},{40,32},{48,56},{56,48},{64,72... | collective-permute-start | bytes 983048 | tf_op jit(solution)/shard_map/ppermute | solution.py:663
  45.4 38.6 %all-to-all-start.1 = ((bf16[16,128,256]{2,1,0:T(8,128)(2,1)}), bf16[16,128,256]{2,1,0:T(8,128)(2,1)}, u32[]{:S(2)}, u32[]{:S(2)}) async-start(bf16[16,128,256]{2,1,0:T(8,128)(2,1)} %bitcast.11), calls=%async_computation.1 | async-start | bytes 2097152 | tf_op jit(solution)/shard_map/all_to_all | solution.py:676
  52.3 18.1 %copy-start.17 = (bf16[128,1280]{1,0:T(8,128)(2,1)}, bf16[128,1280]{1,0:T(8,128)(2,1)S(1)}, u32[]{:S(2)}) copy-start(bf16[128,1280]{1,0:T(8,128)(2,1)S(1)} %collective-permute-done.8) | copy-start | bytes 983044
  53.3 34.3 %collective-permute-start.9 = (bf16[256,1280]{1,0:T(8,128)(2,1)}, bf16[256,1280]{1,0:T(8,128)(2,1)}, u32[]{:S(2)}, u32[]{:S(2)}) collective-permute-start(bf16[256,1280]{1,0:T(8,128)(2,1)} %pad_maximum_fusion.1), channel_id=1, source_target_pairs={{0,16},{8,24},{16,0},{24,8},{32,48},{40,56},{48,32},{56,40},{64,80... | collective-permute-start | bytes 1966088 | tf_op jit(solution)/shard_map/ppermute | solution.py:663
  56.9 15.2 %collective-permute-start.3 = (bf16[128,2048]{1,0:T(8,128)(2,1)S(1)}, bf16[128,2048]{1,0:T(8,128)(2,1)}, u32[]{:S(2)}, u32[]{:S(2)}) collective-permute-start(bf16[128,2048]{1,0:T(8,128)(2,1)S(1)} %copy-done.20), channel_id=1, source_target_pairs={{0,1},{1,2},{2,3},{3,0},{4,5},{5,6},{6,7},{7,4},{8,9},{9,10},{10,1... | collective-permute-start | bytes 1572872 | tf_op jit(solution)/shard_map/ppermute | solution.py:648
  58.9 14.9 %collective-permute-start.4 = (bf16[128,2048]{1,0:T(8,128)(2,1)S(1)}, bf16[128,2048]{1,0:T(8,128)(2,1)}, u32[]{:S(2)}, u32[]{:S(2)}) collective-permute-start(bf16[128,2048]{1,0:T(8,128)(2,1)S(1)} %copy-done.20), channel_id=1, source_target_pairs={{0,3},{1,0},{2,1},{3,2},{4,7},{5,4},{6,5},{7,6},{8,11},{9,8},{10,9... | collective-permute-start | bytes 1572872 | tf_op jit(solution)/shard_map/ppermute | solution.py:648
  60.1 23.9 %collective-permute-start.6 = (bf16[128,2048]{1,0:T(8,128)(2,1)S(1)}, bf16[128,2048]{1,0:T(8,128)(2,1)}, u32[]{:S(2)}, u32[]{:S(2)}) collective-permute-start(bf16[128,2048]{1,0:T(8,128)(2,1)S(1)} %copy-done.20), channel_id=1, source_target_pairs={{0,2},{1,3},{2,0},{3,1},{4,6},{5,7},{6,4},{7,5},{8,10},{9,11},{10,... | collective-permute-start | bytes 1572872 | tf_op jit(solution)/shard_map/ppermute | solution.py:648
  84.0 26.2 %all-to-all-start.2 = ((bf16[8,448,256]{2,1,0:T(8,128)(2,1)}), bf16[8,448,256]{2,1,0:T(8,128)(2,1)S(1)}, u32[]{:S(2)}, u32[]{:S(2)}) async-start(bf16[8,448,256]{2,1,0:T(8,128)(2,1)} %pack_paths.1), calls=%async_computation.2 | async-start | bytes 3670016 | tf_op jit(solution)/shard_map/all_to_all | solution.py:703
  88.9 61.0 %copy-start.10 = (bf16[512,1280]{1,0:T(8,128)(2,1)}, bf16[512,1280]{1,0:T(8,128)(2,1)S(1)}, u32[]{:S(2)}) copy-start(bf16[512,1280]{1,0:T(8,128)(2,1)S(1)} %pad_maximum_fusion.refs_0_) | copy-start | bytes 3932164
  88.9 21.7 %collective-permute-start.10 = (bf16[512,1280]{1,0:T(8,128)(2,1)S(1)}, bf16[512,1280]{1,0:T(8,128)(2,1)}, u32[]{:S(2)}, u32[]{:S(2)}) collective-permute-start(bf16[512,1280]{1,0:T(8,128)(2,1)S(1)} %pad_maximum_fusion.refs_0_), channel_id=1, source_target_pairs={{0,8},{8,0},{16,24},{24,16},{32,40},{40,32},{48,56},{56,48},{64,72... | collective-permute-start | bytes 3932168 | tf_op jit(solution)/shard_map/ppermute | solution.py:663
  89.0 32.5 %collective-permute-start.14 = (bf16[512,1280]{1,0:T(8,128)(2,1)S(1)}, bf16[512,1280]{1,0:T(8,128)(2,1)}, u32[]{:S(2)}, u32[]{:S(2)}) collective-permute-start(bf16[512,1280]{1,0:T(8,128)(2,1)S(1)} %pad_maximum_fusion.refs_0_), channel_id=1, source_target_pairs={{0,32},{8,40},{16,48},{24,56},{32,64},{40,72},{48,80},{56,88},{64,... | collective-permute-start | bytes 3932168 | tf_op jit(solution)/shard_map/ppermute | solution.py:667
  90.5 31.0 %collective-permute-start.15 = (bf16[512,1280]{1,0:T(8,128)(2,1)S(1)}, bf16[512,1280]{1,0:T(8,128)(2,1)}, u32[]{:S(2)}, u32[]{:S(2)}) collective-permute-start(bf16[512,1280]{1,0:T(8,128)(2,1)S(1)} %pad_maximum_fusion.refs_0_), channel_id=1, source_target_pairs={{0,96},{8,104},{16,112},{24,120},{32,0},{40,8},{48,16},{56,24},{64... | collective-permute-start | bytes 3932168 | tf_op jit(solution)/shard_map/ppermute | solution.py:667
  92.3 18.3 %collective-permute-start.7 = (bf16[2048,256]{1,0:T(8,128)(2,1)}, bf16[2048,256]{1,0:T(8,128)(2,1)}, u32[]{:S(2)}, u32[]{:S(2)}) collective-permute-start(bf16[2048,256]{1,0:T(8,128)(2,1)} %bitcast.12.weight_own), channel_id=1, source_target_pairs={{0,8},{8,0},{16,24},{24,16},{32,40},{40,32},{48,56},{56,48},{64,72... | collective-permute-start | bytes 3145736 | tf_op jit(solution)/shard_map/ppermute | solution.py:663
  110.5 17.1 %copy-start.18 = (bf16[448,256]{1,0:T(8,128)(2,1)}, bf16[448,256]{1,0:T(8,128)(2,1)S(1)}, u32[]{:S(2)}) copy-start(bf16[448,256]{1,0:T(8,128)(2,1)S(1)} %reduce_sum.102.piece_0) | copy-start | bytes 688132
  110.5 45.9 %copy-start.26 = (s32[128,8]{0,1:T(8,128)S(1)}, s32[128,8]{0,1:T(8,128)}, u32[]{:S(2)}) copy-start(s32[128,8]{0,1:T(8,128)} %param.33) | copy-start | bytes 12292
  110.6 10.9 %collective-permute-start.11 = (bf16[448,256]{1,0:T(8,128)(2,1)S(1)}, bf16[448,256]{1,0:T(8,128)(2,1)S(1)}, u32[]{:S(2)}, u32[]{:S(2)}) collective-permute-start(bf16[448,256]{1,0:T(8,128)(2,1)S(1)} %reduce_sum.102.piece_0), channel_id=1, source_target_pairs={{0,1},{1,0},{2,3},{3,2},{4,5},{5,4},{6,7},{7,6},{8,9},{9,8},{10,11... | collective-permute-start | bytes 688136 | tf_op jit(solution)/shard_map/ppermute | solution.py:707
  111.5 11.6 %collective-permute-start.12 = (bf16[448,256]{1,0:T(8,128)(2,1)S(1)}, bf16[448,256]{1,0:T(8,128)(2,1)S(1)}, u32[]{:S(2)}, u32[]{:S(2)}) collective-permute-start(bf16[448,256]{1,0:T(8,128)(2,1)S(1)} %reduce_sum.102.piece_0), channel_id=1, source_target_pairs={{0,2},{1,3},{2,0},{3,1},{4,6},{5,7},{6,4},{7,5},{8,10},{9,11},{10,... | collective-permute-start | bytes 688136 | tf_op jit(solution)/shard_map/ppermute | solution.py:707
  113.7 12.0 %collective-permute-start.13 = (bf16[448,256]{1,0:T(8,128)(2,1)S(1)}, bf16[448,256]{1,0:T(8,128)(2,1)S(1)}, u32[]{:S(2)}, u32[]{:S(2)}) collective-permute-start(bf16[448,256]{1,0:T(8,128)(2,1)S(1)} %reduce_sum.102.piece_0), channel_id=1, source_target_pairs={{0,3},{1,2},{2,1},{3,0},{4,7},{5,6},{6,5},{7,4},{8,11},{9,10},{10,... | collective-permute-start | bytes 688136 | tf_op jit(solution)/shard_map/ppermute | solution.py:707
  125.7 30.8 %collective-permute-start.16 = (bf16[512,1280]{1,0:T(8,128)(2,1)}, bf16[512,1280]{1,0:T(8,128)(2,1)S(1)}, u32[]{:S(2)}, u32[]{:S(2)}) collective-permute-start(bf16[512,1280]{1,0:T(8,128)(2,1)} %collective-permute-done.14.refs_1_), channel_id=1, source_target_pairs={{0,32},{8,40},{16,48},{24,56},{32,64},{40,72},{48,80},{56,88},{64,... | collective-permute-start | bytes 3932168 | tf_op jit(solution)/shard_map/ppermute | solution.py:667
  127.1 35.5 %collective-permute-start.17 = (bf16[512,1280]{1,0:T(8,128)(2,1)}, bf16[512,1280]{1,0:T(8,128)(2,1)}, u32[]{:S(2)}, u32[]{:S(2)}) collective-permute-start(bf16[512,1280]{1,0:T(8,128)(2,1)} %collective-permute-done.14.refs_1_), channel_id=1, source_target_pairs={{0,8},{8,0},{16,24},{24,16},{32,40},{40,32},{48,56},{56,48},{64,72... | collective-permute-start | bytes 3932168 | tf_op jit(solution)/shard_map/ppermute | solution.py:663
  127.1 35.5 %collective-permute-start.18 = (bf16[512,1280]{1,0:T(8,128)(2,1)}, bf16[512,1280]{1,0:T(8,128)(2,1)}, u32[]{:S(2)}, u32[]{:S(2)}) collective-permute-start(bf16[512,1280]{1,0:T(8,128)(2,1)} %collective-permute-done.15.refs_2_), channel_id=1, source_target_pairs={{0,8},{8,0},{16,24},{24,16},{32,40},{40,32},{48,56},{56,48},{64,72... | collective-permute-start | bytes 3932168 | tf_op jit(solution)/shard_map/ppermute | solution.py:663
  156.4 14.9 %copy-start.11 = (bf16[512,1280]{1,0:T(8,128)(2,1)}, bf16[512,1280]{1,0:T(8,128)(2,1)S(1)}, u32[]{:S(2)}) copy-start(bf16[512,1280]{1,0:T(8,128)(2,1)S(1)} %collective-permute-done.16.refs_3_) | copy-start | bytes 3932164
  156.4 14.9 %collective-permute-start.19 = (bf16[512,1280]{1,0:T(8,128)(2,1)S(1)}, bf16[512,1280]{1,0:T(8,128)(2,1)S(1)}, u32[]{:S(2)}, u32[]{:S(2)}) collective-permute-start(bf16[512,1280]{1,0:T(8,128)(2,1)S(1)} %collective-permute-done.16.refs_3_), channel_id=1, source_target_pairs={{0,8},{8,0},{16,24},{24,16},{32,40},{40,32},{48,56},{56,48},{64,72... | collective-permute-start | bytes 3932168 | tf_op jit(solution)/shard_map/ppermute | solution.py:663
  156.6 14.8 %all-to-all-start.3 = ((bf16[8,128,256]{2,1,0:T(8,128)(2,1)}), bf16[8,128,256]{2,1,0:T(8,128)(2,1)S(1)}, u32[]{:S(2)}, u32[]{:S(2)}) async-start(bf16[8,128,256]{2,1,0:T(8,128)(2,1)} %bitcast.55), calls=%async_computation.3 | async-start | bytes 1048576 | tf_op jit(solution)/shard_map/all_to_all | solution.py:716
  184.6 58.6 %all-to-all-start.4 = ((bf16[128,8,2048]{2,1,0:T(8,128)(2,1)}), bf16[128,8,2048]{2,1,0:T(8,128)(2,1)}, u32[]{:S(2)}, u32[]{:S(2)}) async-start(bf16[128,8,2048]{2,1,0:T(8,128)(2,1)} %convert_bitcast_fusion), calls=%async_computation.4 | async-start | bytes 8388608 | tf_op jit(solution)/shard_map/all_to_all | solution.py:412
  243.2 23.8 %all-to-all-start.5 = ((bf16[128,2,2048]{2,1,0:T(2,128)(2,1)}), bf16[128,2,2048]{2,1,0:T(2,128)(2,1)S(1)}, u32[]{:S(2)}, u32[]{:S(2)}) async-start(bf16[128,2,2048]{2,1,0:T(2,128)(2,1)} %reshape.153), calls=%async_computation.5 | async-start | bytes 2097152 | tf_op jit(solution)/shard_map/all_to_all | solution.py:412
  276.4 74.0 %all-to-all-start.6 = ((bf16[128,40,512]{2,1,0:T(8,128)(2,1)}), bf16[128,40,512]{2,1,0:T(8,128)(2,1)}, u32[]{:S(2)}, u32[]{:S(2)}) async-start(bf16[128,40,512]{2,1,0:T(8,128)(2,1)} %expert_rest.1), calls=%async_computation.6 | async-start | bytes 10485760 | tf_op jit(solution)/shard_map/all_to_all | solution.py:412
  (10 other events, 56.8 us)

commit v8 on v7

--- a/solution.py
+++ b/solution.py
@@ -642,7 +642,10 @@
     cosine = jnp.concatenate([cos_half, cos_half], axis=1)
     sine = jnp.concatenate([-sin_half, sin_half], axis=1)
 
-    normed = rms_norm(hidden, norm_gains[0]).astype(jnp.bfloat16)
+    packed = pack_weights(query_weight, kv_weight, out_weight, next_weight, mp_size)
+    packed = lax.all_to_all(packed, "mp", split_axis=0, concat_axis=0, tiled=True)
+    packed, stream = lax.optimization_barrier((packed, hidden))
+    normed = rms_norm(stream, norm_gains[0]).astype(jnp.bfloat16)
     def shift(values, step):
         moves = [(j, j - j % 4 + (j % 4 + step) % 4) for j in range(mp_size)]
         return lax.ppermute(values, "mp", moves)
@@ -650,9 +653,6 @@
     across = lax.ppermute(normed, "mp", [(j, (j + 4) % mp_size) for j in range(mp_size)])
     left = shift(normed, 1)
     right = shift(normed, -1)
-    packed = pack_weights(query_weight, kv_weight, out_weight, next_weight, mp_size)
-    packed = lax.all_to_all(packed, "mp", split_axis=0, concat_axis=0, tiled=True)
-    packed, across, left, right = lax.optimization_barrier((packed, across, left, right))
     packed = packed.reshape(mp_size * own_rows, -1)
     late_width = dim + next_weight.shape[1]
     dp_at = lax.axis_index("dp")
@@ -676,7 +676,6 @@
     early = lax.all_to_all(early, "dp", split_axis=0, concat_axis=0, tiled=True)
     early = early.reshape(dim, 2 * hd)
     sides = [left, right, shift(across, 1), shift(across, -1)]
-    far = [shift(normed, 2), shift(across, 2)]
     tables = (
         token_request,
         request_leaf,
@@ -694,9 +693,10 @@
             jnp.stack([lax.rem(lax.axis_index("dp"), 2)]),
         ]
     ).astype(jnp.int32)
-    path, sides, far, early, cosine, sine, meta = lax.optimization_barrier(
-        (path, sides, far, early, cosine, sine, meta)
+    path, sides, early, cosine, sine, meta = lax.optimization_barrier(
+        (path, sides, early, cosine, sine, meta)
     )
+    far = [shift(sides[0], 1), shift(sides[3], -1)]
     weights = (early, swap(early, 1))
     x_left = shift_x(late, 1)
     x_right = shift_x(late, -1)
@@ -706,7 +706,7 @@
     pieces = [own_piece] + [
         lax.ppermute(own_piece, "mp", [(j, j ^ s) for j in range(mp_size)]) for s in range(1, 4)
     ]
-    pieces, x_left, x_right = lax.optimization_barrier((pieces, x_left, x_right))
+    pieces, far, x_left, x_right = lax.optimization_barrier((pieces, far, x_left, x_right))
     x_far = shift_x(x_left, 1)
     rows = [normed, across] + sides + far
     attended = attend(meta, rows, weights, pieces, head_gains, cosine, sine)

time: 361 us -> 347 us (0.961)
  waiting for transfers between devices: 189 us -> 170 us
    ppermute x6, waiting for transfers between devices: 33 us -> 21.1 us  [shift(): return lax.ppermute(values, 'mp', moves)]
    ppermute x3, waiting for transfers between devices: 12.7 us -> 6.16 us  [shift_x(): return lax.ppermute(values, 'dp', moves)]
    all_to_all x1, waiting for transfers between devices: 17.9 us -> 13.2 us  [per_device(): path = lax.all_to_all(path, 'mp', split_axis=0, concat_axis=0, tiled=True)]
  transfers between devices with their start and end apart: 27 -> 27, of which waited for: 15 -> 12; matrix products, arithmetic and copies ran while one was open for 12% -> 14% of each run, Pallas kernels for 7% -> 7%
where the time goes in v8:
time: 347 us; the launch traced here: 346 us
  waiting for transfers between devices  170 us (49%)
  starting transfers between devices  64.3 us (19%)
  Pallas kernels  50.8 us (15%)
  other arithmetic  20 us (6%)
  local copies, waits for them, and re-layouts  19.1 us (6%)
  matrix products  18.9 us (5%)
    all_to_all x3, waiting for transfers between devices, exchange(): return lax.all_to_all(values, BOTH, split_axis=0, concat_axis=0, tiled=True)  110 us
    pallas_call x1, Pallas kernels, attend(): pl.pallas_call(attention_kernel, out_shape=jax.ShapeDtypeStruct((group, 2...  22.2 us
    ppermute x6, waiting for transfers between devices, shift(): return lax.ppermute(values, 'mp', moves)  21.1 us
    all_to_all x3, starting transfers between devices, exchange(): return lax.all_to_all(values, BOTH, split_axis=0, concat_axis=0, tiled=True)  18.7 us
    all_to_all x1, waiting for transfers between devices, per_device(): path = lax.all_to_all(path, 'mp', split_axis=0, concat_axis=0, tiled=True)  13.2 us
    dot_general x1, matrix products, expert(): both = jnp.dot(rows, gate_up, preferred_element_type=jnp.float32)  10.2 us
    ppermute x6, starting transfers between devices, shift(): return lax.ppermute(values, 'mp', moves)  9.71 us
    pallas_call x1, Pallas kernels, finish(): pl.pallas_call(finish_kernel, grid_spec=pltpu.PrefetchScalarGridSpec(num_...  8.92 us
  transfers between devices with their start and end apart: 27, of which 12 were waited for; matrix products, arithmetic and copies ran while one was open for 14% of the time, Pallas kernels for 7%

profile of v8, /device:TPU:0, one launch (start us, length us, event | category | flops | bytes accessed | tf_op | source)
XLA Modules:
  0.0 346.0 jit_solution(5947687423146027418)
XLA Ops:
  0.7 1.9 pack_weights.1
  2.6 6.4 %all-to-all-start = ((bf16[8,16,3072]{2,1,0:T(8,128)(2,1)}), bf16[8,16,3072]{2,1,0:T(8,128)(2,1)S(1)}, u32[]{:S(2)}, u32[]{:S(2)}) async-start(bf16[8,16,3072]{2,1,0:T(8,128)(2,1)} %pack_weights.1), calls=%async_computation | async-start | bytes 1572864 | tf_op jit(solution)/shard_map/all_to_all | solution.py:646
  14.9 1.5 fusion.30
  16.4 4.5 %all-to-all-done = bf16[8,16,3072]{2,1,0:T(8,128)(2,1)S(1)} async-done(((bf16[8,16,3072]{2,1,0:T(8,128)(2,1)}), bf16[8,16,3072]{2,1,0:T(8,128)(2,1)S(1)}, u32[]{:S(2)}, u32[]{:S(2)}) %all-to-all-start) | async-done | bytes 786464 | tf_op jit(solution)/shard_map/all_to_all | solution.py:646
  23.3 1.5 collective-permute-start.2
  26.7 6.8 %all-to-all-start.1 = ((bf16[16,128,256]{2,1,0:T(8,128)(2,1)}), bf16[16,128,256]{2,1,0:T(8,128)(2,1)}, u32[]{:S(2)}, u32[]{:S(2)}) async-start(bf16[16,128,256]{2,1,0:T(8,128)(2,1)} %bitcast.11), calls=%async_computation.1 | async-start | bytes 2097152 | tf_op jit(solution)/shard_map/all_to_all | solution.py:676
  33.5 1.9 pad_maximum_fusion.1
  35.4 3.4 collective-permute-start.7
  39.8 2.4 collective-permute-start.1
  42.2 3.2 collective-permute-start.4
  45.4 1.3 pad_add_fusion.2.meta
  48.1 2.2 pack_paths.1
  51.5 1.9 fusion.13
  53.4 1.3 pad_maximum_fusion.3
  55.0 10.2 %collective-permute-done.3.across_left = bf16[128,2048]{1,0:T(8,128)(2,1)} collective-permute-done((bf16[128,2048]{1,0:T(8,128)(2,1)S(1)}, bf16[128,2048]{1,0:T(8,128)(2,1)}, u32[]{:S(2)}, u32[]{:S(2)}) %collective-permute-start.3) | collective-permute-done | bytes 524320 | tf_op jit(solution)/shard_map/ppermute | solution.py:651
  65.2 4.2 %all-to-all-start.2 = ((bf16[8,448,256]{2,1,0:T(8,128)(2,1)}), bf16[8,448,256]{2,1,0:T(8,128)(2,1)S(1)}, u32[]{:S(2)}, u32[]{:S(2)}) async-start(bf16[8,448,256]{2,1,0:T(8,128)(2,1)} %pack_paths.1), calls=%async_computation.2 | async-start | bytes 3670016 | tf_op jit(solution)/shard_map/all_to_all | solution.py:703
  69.5 1.3 pad_maximum_fusion.refs_0_
  71.3 1.5 collective-permute-start.14
  72.8 1.8 collective-permute-start.15
  74.5 2.0 collective-permute-start.12
  78.7 13.2 %all-to-all-done.2 = bf16[8,448,256]{2,1,0:T(8,128)(2,1)S(1)} async-done(((bf16[8,448,256]{2,1,0:T(8,128)(2,1)}), bf16[8,448,256]{2,1,0:T(8,128)(2,1)S(1)}, u32[]{:S(2)}, u32[]{:S(2)}) %all-to-all-start.2) | async-done | bytes 1835040 | tf_op jit(solution)/shard_map/all_to_all | solution.py:703
  92.3 2.2 collective-permute-start.10
  94.5 10.6 %collective-permute-done.12.own_far = bf16[128,2048]{1,0:T(8,128)(2,1)} collective-permute-done((bf16[128,2048]{1,0:T(8,128)(2,1)}, bf16[128,2048]{1,0:T(8,128)(2,1)}, u32[]{:S(2)}, u32[]{:S(2)}) %collective-permute-start.12) | collective-permute-done | bytes 524320 | tf_op jit(solution)/shard_map/ppermute | solution.py:651
  106.2 1.8 collective-permute-done.10.piece_2
  108.0 5.0 %collective-permute-done.11.piece_3 = bf16[448,256]{1,0:T(8,128)(2,1)S(1)} collective-permute-done((bf16[448,256]{1,0:T(8,128)(2,1)S(1)}, bf16[448,256]{1,0:T(8,128)(2,1)S(1)}, u32[]{:S(2)}, u32[]{:S(2)}) %collective-permute-start.11) | collective-permute-done | bytes 229408 | tf_op jit(solution)/shard_map/ppermute | solution.py:707
  113.0 1.5 collective-permute-start.16
  115.1 22.2 %tree_attention.1 = bf16[1024,256]{1,0:T(8,128)(2,1)} custom-call(s32[9]{0:T(128)} %pad_add_fusion.2.meta, bf16[128,2048]{1,0:T(8,128)(2,1)} %copy-done.16, bf16[128,2048]{1,0:T(8,128)(2,1)} %copy-done.20, bf16[128,2048]{1,0:T(8,128)(2,1)} %copy-done.21, bf16[128,2048]{1,0:T(8,128)(2,1)} %collective-permute-done.1.own_right, ...), custom_call_target="tpu_custom_call" | custom-call | flops 2147483648 | bytes 8388608 | tf_op jit(solution)/shard_map/tree_attention/pallas_call | solution.py:293
  137.3 6.2 %collective-permute-done.16.refs_3_ = bf16[512,1280]{1,0:T(8,128)(2,1)S(1)} collective-permute-done((bf16[512,1280]{1,0:T(8,128)(2,1)}, bf16[512,1280]{1,0:T(8,128)(2,1)S(1)}, u32[]{:S(2)}, u32[]{:S(2)}) %collective-permute-start.16) | collective-permute-done | bytes 1310752 | tf_op jit(solution)/shard_map/ppermute | solution.py:667
  143.6 4.4 %all-to-all-start.3 = ((bf16[8,128,256]{2,1,0:T(8,128)(2,1)}), bf16[8,128,256]{2,1,0:T(8,128)(2,1)S(1)}, u32[]{:S(2)}, u32[]{:S(2)}) async-start(bf16[8,128,256]{2,1,0:T(8,128)(2,1)} %bitcast.55), calls=%async_computation.3 | async-start | bytes 1048576 | tf_op jit(solution)/shard_map/all_to_all | solution.py:716
  149.3 8.8 %all-to-all-done.3.attended = bf16[8,128,256]{2,1,0:T(8,128)(2,1)S(1)} async-done(((bf16[8,128,256]{2,1,0:T(8,128)(2,1)}), bf16[8,128,256]{2,1,0:T(8,128)(2,1)S(1)}, u32[]{:S(2)}, u32[]{:S(2)}) %all-to-all-start.3) | async-done | bytes 524320 | tf_op jit(solution)/shard_map/all_to_all | solution.py:716
  159.3 7.6 %project.1 = (bf16[128,2048]{1,0:T(8,128)(2,1)}, bf16[128,2048]{1,0:T(8,128)(2,1)}) custom-call(s32[3]{0:T(128)} %pad_add_fusion.1.place, bf16[8,128,256]{2,1,0:T(8,128)(2,1)} %copy-done.15, bf16[512,1280]{1,0:T(8,128)(2,1)} %copy-done.10, bf16[512,1280]{1,0:T(8,128)(2,1)} %collective-permute-done.14.refs_1_, ...), custom_call_target="tpu_custom_call" | custom-call | tf_op jit(solution)/shard_map/project/pallas_call | solution.py:378
  166.9 4.4 %convert_bitcast_fusion = bf16[128,8,2048]{2,1,0:T(8,128)(2,1)} fusion(bf16[128,2048]{1,0:T(8,128)(2,1)} %get-tuple-element.58, s32[1024]{0:T(1024)S(1)} %eq.180, s32[128,128]{1,0:T(8,128)S(1)} %copy.68), kind=kOutput, calls=%fused_computation.2 | convolution fusion | flops 539099136 | bytes 4788224 | tf_op jit(solution)/shard_map/dot_general | solution.py:743
  171.3 6.0 %all-to-all-start.4 = ((bf16[128,8,2048]{2,1,0:T(8,128)(2,1)}), bf16[128,8,2048]{2,1,0:T(8,128)(2,1)}, u32[]{:S(2)}, u32[]{:S(2)}) async-start(bf16[128,8,2048]{2,1,0:T(8,128)(2,1)} %convert_bitcast_fusion), calls=%async_computation.4 | async-start | bytes 8388608 | tf_op jit(solution)/shard_map/all_to_all | solution.py:412
  177.9 1.5 reshape.153
  179.4 50.5 %all-to-all-done.4 = bf16[128,8,2048]{2,1,0:T(8,128)(2,1)} async-done(((bf16[128,8,2048]{2,1,0:T(8,128)(2,1)}), bf16[128,8,2048]{2,1,0:T(8,128)(2,1)}, u32[]{:S(2)}, u32[]{:S(2)}) %all-to-all-start.4) | async-done | bytes 4194336 | tf_op jit(solution)/shard_map/all_to_all | solution.py:412
  229.9 4.8 %all-to-all-start.5 = ((bf16[128,2,2048]{2,1,0:T(2,128)(2,1)}), bf16[128,2,2048]{2,1,0:T(2,128)(2,1)S(1)}, u32[]{:S(2)}, u32[]{:S(2)}) async-start(bf16[128,2,2048]{2,1,0:T(2,128)(2,1)} %reshape.153), calls=%async_computation.5 | async-start | bytes 2097152 | tf_op jit(solution)/shard_map/all_to_all | solution.py:412
  234.8 10.2 %fusion = f32[1024,1536]{1,0:T(8,128)S(1)} fusion(bf16[128,8,2048]{2,1,0:T(8,128)(2,1)} %all-to-all-done.4, bf16[1,2048,1536]{2,1,0:T(8,128)(2,1)} %param.30), kind=kOutput, calls=%fused_computation | convolution fusion | flops 6442450944 | bytes 16777216 | tf_op jit(solution)/shard_map/dot_general | solution.py:417
  244.9 3.7 %convolution_convert_fusion = bf16[1024,2048]{1,0:T(8,128)(2,1)S(1)} fusion(f32[1024,1536]{1,0:T(8,128)S(1)} %fusion, bf16[1,768,2048]{2,1,0:T(8,128)(2,1)S(1)} %copy-done.14), kind=kOutput, calls=%fused_computation.3 | convolution fusion | flops 3228041216 | bytes 13631488 | tf_op jit(solution)/shard_map/dot_general | solution.py:419
  248.7 2.9 pad.4.main_block
  251.6 2.1 all-to-all-done.5
  254.9 8.0 %expert_rest.1 = bf16[128,40,512]{2,1,0:T(8,128)(2,1)} custom-call(bf16[256,2048]{1,0:T(8,128)(2,1)} %reshape.157.rows, bf16[2048,1536]{1,0:T(8,128)(2,1)} %bitcast.50, bf16[768,2048]{1,0:T(8,128)(2,1)} %bitcast.52, bf16[128,40,512]{2,1,0:T(8,128)(2,1)} %pad.4.main_block), custom_call_target="tpu_custom_call", output_to_operand_aliasing={{}: (3, {})} | custom-call | tf_op jit(solution)/shard_map/expert_rest/pallas_call | solution.py:460
  262.9 7.9 %all-to-all-start.6 = ((bf16[128,40,512]{2,1,0:T(8,128)(2,1)}), bf16[128,40,512]{2,1,0:T(8,128)(2,1)}, u32[]{:S(2)}, u32[]{:S(2)}) async-start(bf16[128,40,512]{2,1,0:T(8,128)(2,1)} %expert_rest.1), calls=%async_computation.6 | async-start | bytes 10485760 | tf_op jit(solution)/shard_map/all_to_all | solution.py:412
  270.9 1.3 slice.51.refs_9_
  275.5 1.5 broadcast_multiply_fusion.rest_share
  277.0 1.5 constant_dynamic-slice_fusion.refs_11_
  278.5 1.5 constant_dynamic-slice_fusion.1.refs_10_
  279.9 57.0 %all-to-all-done.6.main_rows.rest_rows = bf16[128,40,512]{2,1,0:T(8,128)(2,1)} async-done(((bf16[128,40,512]{2,1,0:T(8,128)(2,1)}), bf16[128,40,512]{2,1,0:T(8,128)(2,1)}, u32[]{:S(2)}, u32[]{:S(2)}) %all-to-all-start.6) | async-done | bytes 5242912 | tf_op jit(solution)/shard_map/all_to_all | solution.py:412
  336.9 8.9 %finish.1 = (bf16[128,2048]{1,0:T(8,128)(2,1)}, bf16[128,512]{1,0:T(8,128)(2,1)}) custom-call(s32[3]{0:T(128)} %pad_add_fusion.1.place, bf16[256,1024]{1,0:T(8,128)(2,1)} %pad_maximum_fusion.2.main_share, bf16[4,256,1024]{2,1,0:T(8,128)(2,1)} %broadcast_multiply_fusion.rest_share, bf16[128,40,512]{2,1,0:T(8,128)(2,1)} %all-to-all-done.6.main_rows.rest_rows, ...), custom_call_target="tpu_custom_call" | custom-call | tf_op jit(solution)/shard_map/finish/pallas_call | solution.py:542
  (137 shorter events, 25.2 us)
Async XLA Ops:
  0.6 24.2 %copy-start.3 = (s32[1024]{0:T(1024)S(1)}, s32[1024]{0:T(1024)}, u32[]{:S(2)}) copy-start(s32[1024]{0:T(1024)} %token_request.1) | copy-start | bytes 12292
  0.6 22.3 %copy-start.13 = (bf16[128,2048]{1,0:T(8,128)(2,1)S(1)}, bf16[128,2048]{1,0:T(8,128)(2,1)}, u32[]{:S(2)}) copy-start(bf16[128,2048]{1,0:T(8,128)(2,1)} %refs_8_.1) | copy-start | bytes 1572868
  2.6 18.4 %all-to-all-start = ((bf16[8,16,3072]{2,1,0:T(8,128)(2,1)}), bf16[8,16,3072]{2,1,0:T(8,128)(2,1)S(1)}, u32[]{:S(2)}, u32[]{:S(2)}) async-start(bf16[8,16,3072]{2,1,0:T(8,128)(2,1)} %pack_weights.1), calls=%async_computation | async-start | bytes 1572864 | tf_op jit(solution)/shard_map/all_to_all | solution.py:646
  23.0 10.5 %collective-permute-start.6 = (bf16[128,1280]{1,0:T(8,128)(2,1)}, bf16[128,1280]{1,0:T(8,128)(2,1)}, u32[]{:S(2)}, u32[]{:S(2)}) collective-permute-start(bf16[128,1280]{1,0:T(8,128)(2,1)} %get-tuple-element.71), channel_id=1, source_target_pairs={{0,8},{8,0},{16,24},{24,16},{32,40},{40,32},{48,56},{56,48},{64,72... | collective-permute-start | bytes 983048 | tf_op jit(solution)/shard_map/ppermute | solution.py:663
  23.0 25.0 %copy-start = (bf16[1,512,512]{2,1,0:T(8,128)(2,1)S(1)}, bf16[1,512,512]{2,1,0:T(8,128)(2,1)}, u32[]{:S(2)}) copy-start(bf16[1,512,512]{2,1,0:T(8,128)(2,1)} %root.1) | copy-start | bytes 1572868
  23.0 25.0 %copy-start.1 = (bf16[1,256,512]{2,1,0:T(8,128)(2,1)S(1)}, bf16[1,256,512]{2,1,0:T(8,128)(2,1)}, u32[]{:S(2)}) copy-start(bf16[1,256,512]{2,1,0:T(8,128)(2,1)} %mid.1) | copy-start | bytes 786436
  23.0 25.0 %copy-start.2 = (bf16[2,128,512]{2,1,0:T(8,128)(2,1)S(1)}, bf16[2,128,512]{2,1,0:T(8,128)(2,1)}, u32[]{:S(2)}) copy-start(bf16[2,128,512]{2,1,0:T(8,128)(2,1)} %leaf.1) | copy-start | bytes 786436
  23.0 25.0 %copy-start.4 = (s32[16]{0:T(128)S(1)}, s32[16]{0:T(128)}, u32[]{:S(2)}) copy-start(s32[16]{0:T(128)} %leaf_parent.1) | copy-start | bytes 196
  23.0 25.0 %copy-start.5 = (s32[8]{0:T(128)S(1)}, s32[8]{0:T(128)}, u32[]{:S(2)}) copy-start(s32[8]{0:T(128)} %mid_parent.1) | copy-start | bytes 100
  23.0 25.0 %copy-start.6 = (s32[32]{0:T(128)S(1)}, s32[32]{0:T(128)}, u32[]{:S(2)}) copy-start(s32[32]{0:T(128)} %request_leaf.1) | copy-start | bytes 388
  23.0 25.0 %copy-start.7 = (s32[8]{0:T(128)S(1)}, s32[8]{0:T(128)}, u32[]{:S(2)}) copy-start(s32[8]{0:T(128)} %root_slot.1) | copy-start | bytes 100
  23.1 25.0 %copy-start.8 = (s32[8]{0:T(128)S(1)}, s32[8]{0:T(128)}, u32[]{:S(2)}) copy-start(s32[8]{0:T(128)} %mid_slot.1) | copy-start | bytes 100
  23.1 25.0 %copy-start.9 = (s32[16]{0:T(128)S(1)}, s32[16]{0:T(128)}, u32[]{:S(2)}) copy-start(s32[16]{0:T(128)} %leaf_slot.1) | copy-start | bytes 196
  23.3 27.0 %copy-start.16 = (bf16[128,2048]{1,0:T(8,128)(2,1)}, bf16[128,2048]{1,0:T(8,128)(2,1)S(1)}, u32[]{:S(2)}) copy-start(bf16[128,2048]{1,0:T(8,128)(2,1)S(1)} %fusion.8.own) | copy-start | bytes 1572868
  23.3 18.9 %collective-permute-start.2 = (bf16[128,2048]{1,0:T(8,128)(2,1)S(1)}, bf16[128,2048]{1,0:T(8,128)(2,1)S(1)}, u32[]{:S(2)}, u32[]{:S(2)}) collective-permute-start(bf16[128,2048]{1,0:T(8,128)(2,1)S(1)} %fusion.8.own), channel_id=1, source_target_pairs={{0,4},{1,5},{2,6},{3,7},{4,0},{5,1},{6,2},{7,3},{8,12},{9,13},{10,... | collective-permute-start | bytes 1572872 | tf_op jit(solution)/shard_map/ppermute | solution.py:653
  26.7 28.3 %all-to-all-start.1 = ((bf16[16,128,256]{2,1,0:T(8,128)(2,1)}), bf16[16,128,256]{2,1,0:T(8,128)(2,1)}, u32[]{:S(2)}, u32[]{:S(2)}) async-start(bf16[16,128,256]{2,1,0:T(8,128)(2,1)} %bitcast.11), calls=%async_computation.1 | async-start | bytes 2097152 | tf_op jit(solution)/shard_map/all_to_all | solution.py:676
  35.4 34.1 %collective-permute-start.7 = (bf16[256,1280]{1,0:T(8,128)(2,1)}, bf16[256,1280]{1,0:T(8,128)(2,1)}, u32[]{:S(2)}, u32[]{:S(2)}) collective-permute-start(bf16[256,1280]{1,0:T(8,128)(2,1)} %pad_maximum_fusion.1), channel_id=1, source_target_pairs={{0,16},{8,24},{16,0},{24,8},{32,48},{40,56},{48,32},{56,40},{64,80... | collective-permute-start | bytes 1966088 | tf_op jit(solution)/shard_map/ppermute | solution.py:663
  38.9 16.0 %collective-permute-start = (bf16[128,2048]{1,0:T(8,128)(2,1)S(1)}, bf16[128,2048]{1,0:T(8,128)(2,1)S(1)}, u32[]{:S(2)}, u32[]{:S(2)}) collective-permute-start(bf16[128,2048]{1,0:T(8,128)(2,1)S(1)} %fusion.8.own), channel_id=1, source_target_pairs={{0,1},{1,2},{2,3},{3,0},{4,5},{5,6},{6,7},{7,4},{8,9},{9,10},{10,1... | collective-permute-start | bytes 1572872 | tf_op jit(solution)/shard_map/ppermute | solution.py:651
  39.8 15.2 %collective-permute-start.1 = (bf16[128,2048]{1,0:T(8,128)(2,1)S(1)}, bf16[128,2048]{1,0:T(8,128)(2,1)}, u32[]{:S(2)}, u32[]{:S(2)}) collective-permute-start(bf16[128,2048]{1,0:T(8,128)(2,1)S(1)} %fusion.8.own), channel_id=1, source_target_pairs={{0,3},{1,0},{2,1},{3,2},{4,7},{5,4},{6,5},{7,6},{8,11},{9,8},{10,9... | collective-permute-start | bytes 1572872 | tf_op jit(solution)/shard_map/ppermute | solution.py:651
  42.2 12.5 %copy-start.20 = (bf16[128,2048]{1,0:T(8,128)(2,1)}, bf16[128,2048]{1,0:T(8,128)(2,1)S(1)}, u32[]{:S(2)}) copy-start(bf16[128,2048]{1,0:T(8,128)(2,1)S(1)} %collective-permute-done.2.across) | copy-start | bytes 1572868
  42.2 23.0 %collective-permute-start.3 = (bf16[128,2048]{1,0:T(8,128)(2,1)S(1)}, bf16[128,2048]{1,0:T(8,128)(2,1)}, u32[]{:S(2)}, u32[]{:S(2)}) collective-permute-start(bf16[128,2048]{1,0:T(8,128)(2,1)S(1)} %collective-permute-done.2.across), channel_id=1, source_target_pairs={{0,1},{1,2},{2,3},{3,0},{4,5},{5,6},{6,7},{7,4},{8,9},{9,10},{10,1... | collective-permute-start | bytes 1572872 | tf_op jit(solution)/shard_map/ppermute | solution.py:651
  42.2 23.0 %collective-permute-start.4 = (bf16[128,2048]{1,0:T(8,128)(2,1)S(1)}, bf16[128,2048]{1,0:T(8,128)(2,1)}, u32[]{:S(2)}, u32[]{:S(2)}) collective-permute-start(bf16[128,2048]{1,0:T(8,128)(2,1)S(1)} %collective-permute-done.2.across), channel_id=1, source_target_pairs={{0,3},{1,0},{2,1},{3,2},{4,7},{5,4},{6,5},{7,6},{8,11},{9,8},{10,9... | collective-permute-start | bytes 1572872 | tf_op jit(solution)/shard_map/ppermute | solution.py:651
  55.0 10.2 %copy-start.21 = (bf16[128,2048]{1,0:T(8,128)(2,1)}, bf16[128,2048]{1,0:T(8,128)(2,1)S(1)}, u32[]{:S(2)}) copy-start(bf16[128,2048]{1,0:T(8,128)(2,1)S(1)} %collective-permute-done.own_left) | copy-start | bytes 1572868
  65.2 26.8 %all-to-all-start.2 = ((bf16[8,448,256]{2,1,0:T(8,128)(2,1)}), bf16[8,448,256]{2,1,0:T(8,128)(2,1)S(1)}, u32[]{:S(2)}, u32[]{:S(2)}) async-start(bf16[8,448,256]{2,1,0:T(8,128)(2,1)} %pack_paths.1), calls=%async_computation.2 | async-start | bytes 3670016 | tf_op jit(solution)/shard_map/all_to_all | solution.py:703
  69.4 7.1 %collective-permute-start.5 = (bf16[2048,256]{1,0:T(8,128)(2,1)}, bf16[2048,256]{1,0:T(8,128)(2,1)S(1)}, u32[]{:S(2)}, u32[]{:S(2)}) collective-permute-start(bf16[2048,256]{1,0:T(8,128)(2,1)} %bitcast.12.weight_own), channel_id=1, source_target_pairs={{0,8},{8,0},{16,24},{24,16},{32,40},{40,32},{48,56},{56,48},{64,72... | collective-permute-start | bytes 3145736 | tf_op jit(solution)/shard_map/ppermute | solution.py:663
  70.7 66.6 %copy-start.10 = (bf16[512,1280]{1,0:T(8,128)(2,1)}, bf16[512,1280]{1,0:T(8,128)(2,1)S(1)}, u32[]{:S(2)}) copy-start(bf16[512,1280]{1,0:T(8,128)(2,1)S(1)} %pad_maximum_fusion.refs_0_) | copy-start | bytes 3932164
  70.7 21.6 %collective-permute-start.8 = (bf16[512,1280]{1,0:T(8,128)(2,1)S(1)}, bf16[512,1280]{1,0:T(8,128)(2,1)}, u32[]{:S(2)}, u32[]{:S(2)}) collective-permute-start(bf16[512,1280]{1,0:T(8,128)(2,1)S(1)} %pad_maximum_fusion.refs_0_), channel_id=1, source_target_pairs={{0,8},{8,0},{16,24},{24,16},{32,40},{40,32},{48,56},{56,48},{64,72... | collective-permute-start | bytes 3932168 | tf_op jit(solution)/shard_map/ppermute | solution.py:663
  71.3 34.9 %collective-permute-start.14 = (bf16[512,1280]{1,0:T(8,128)(2,1)S(1)}, bf16[512,1280]{1,0:T(8,128)(2,1)}, u32[]{:S(2)}, u32[]{:S(2)}) collective-permute-start(bf16[512,1280]{1,0:T(8,128)(2,1)S(1)} %pad_maximum_fusion.refs_0_), channel_id=1, source_target_pairs={{0,32},{8,40},{16,48},{24,56},{32,64},{40,72},{48,80},{56,88},{64,... | collective-permute-start | bytes 3932168 | tf_op jit(solution)/shard_map/ppermute | solution.py:667
  72.8 33.5 %collective-permute-start.15 = (bf16[512,1280]{1,0:T(8,128)(2,1)S(1)}, bf16[512,1280]{1,0:T(8,128)(2,1)}, u32[]{:S(2)}, u32[]{:S(2)}) collective-permute-start(bf16[512,1280]{1,0:T(8,128)(2,1)S(1)} %pad_maximum_fusion.refs_0_), channel_id=1, source_target_pairs={{0,96},{8,104},{16,112},{24,120},{32,0},{40,8},{48,16},{56,24},{64... | collective-permute-start | bytes 3932168 | tf_op jit(solution)/shard_map/ppermute | solution.py:667
  74.5 30.6 %collective-permute-start.12 = (bf16[128,2048]{1,0:T(8,128)(2,1)}, bf16[128,2048]{1,0:T(8,128)(2,1)}, u32[]{:S(2)}, u32[]{:S(2)}) collective-permute-start(bf16[128,2048]{1,0:T(8,128)(2,1)} %copy-done.21), channel_id=1, source_target_pairs={{0,1},{1,2},{2,3},{3,0},{4,5},{5,6},{6,7},{7,4},{8,9},{9,10},{10,1... | collective-permute-start | bytes 1572872 | tf_op jit(solution)/shard_map/ppermute | solution.py:651
  77.5 28.7 %collective-permute-start.13 = (bf16[128,2048]{1,0:T(8,128)(2,1)}, bf16[128,2048]{1,0:T(8,128)(2,1)}, u32[]{:S(2)}, u32[]{:S(2)}) collective-permute-start(bf16[128,2048]{1,0:T(8,128)(2,1)} %collective-permute-done.4.across_right), channel_id=1, source_target_pairs={{0,3},{1,0},{2,1},{3,2},{4,7},{5,4},{6,5},{7,6},{8,11},{9,8},{10,9... | collective-permute-start | bytes 1572872 | tf_op jit(solution)/shard_map/ppermute | solution.py:651
  92.3 22.8 %copy-start.19 = (bf16[448,256]{1,0:T(8,128)(2,1)}, bf16[448,256]{1,0:T(8,128)(2,1)S(1)}, u32[]{:S(2)}) copy-start(bf16[448,256]{1,0:T(8,128)(2,1)S(1)} %reduce_sum.102.piece_0) | copy-start | bytes 688132
  92.3 51.2 %copy-start.25 = (s32[128,8]{0,1:T(8,128)S(1)}, s32[128,8]{0,1:T(8,128)}, u32[]{:S(2)}) copy-start(s32[128,8]{0,1:T(8,128)} %param.33) | copy-start | bytes 12292
  92.3 15.7 %collective-permute-start.10 = (bf16[448,256]{1,0:T(8,128)(2,1)S(1)}, bf16[448,256]{1,0:T(8,128)(2,1)S(1)}, u32[]{:S(2)}, u32[]{:S(2)}) collective-permute-start(bf16[448,256]{1,0:T(8,128)(2,1)S(1)} %reduce_sum.102.piece_0), channel_id=1, source_target_pairs={{0,2},{1,3},{2,0},{3,1},{4,6},{5,7},{6,4},{7,5},{8,10},{9,11},{10,... | collective-permute-start | bytes 688136 | tf_op jit(solution)/shard_map/ppermute | solution.py:707
  105.1 7.9 %collective-permute-start.11 = (bf16[448,256]{1,0:T(8,128)(2,1)S(1)}, bf16[448,256]{1,0:T(8,128)(2,1)S(1)}, u32[]{:S(2)}, u32[]{:S(2)}) collective-permute-start(bf16[448,256]{1,0:T(8,128)(2,1)S(1)} %reduce_sum.102.piece_0), channel_id=1, source_target_pairs={{0,3},{1,2},{2,1},{3,0},{4,7},{5,6},{6,5},{7,4},{8,11},{9,10},{10,... | collective-permute-start | bytes 688136 | tf_op jit(solution)/shard_map/ppermute | solution.py:707
  106.2 6.8 %collective-permute-start.9 = (bf16[448,256]{1,0:T(8,128)(2,1)S(1)}, bf16[448,256]{1,0:T(8,128)(2,1)S(1)}, u32[]{:S(2)}, u32[]{:S(2)}) collective-permute-start(bf16[448,256]{1,0:T(8,128)(2,1)S(1)} %reduce_sum.102.piece_0), channel_id=1, source_target_pairs={{0,1},{1,0},{2,3},{3,2},{4,5},{5,4},{6,7},{7,6},{8,9},{9,8},{10,11... | collective-permute-start | bytes 688136 | tf_op jit(solution)/shard_map/ppermute | solution.py:707
  108.0 7.1 %copy-start.22 = (bf16[448,256]{1,0:T(8,128)(2,1)}, bf16[448,256]{1,0:T(8,128)(2,1)S(1)}, u32[]{:S(2)}) copy-start(bf16[448,256]{1,0:T(8,128)(2,1)S(1)} %collective-permute-done.10.piece_2) | copy-start | bytes 688132
  113.0 30.4 %collective-permute-start.16 = (bf16[512,1280]{1,0:T(8,128)(2,1)}, bf16[512,1280]{1,0:T(8,128)(2,1)S(1)}, u32[]{:S(2)}, u32[]{:S(2)}) collective-permute-start(bf16[512,1280]{1,0:T(8,128)(2,1)} %collective-permute-done.14.refs_1_), channel_id=1, source_target_pairs={{0,32},{8,40},{16,48},{24,56},{32,64},{40,72},{48,80},{56,88},{64,... | collective-permute-start | bytes 3932168 | tf_op jit(solution)/shard_map/ppermute | solution.py:667
  114.5 34.8 %collective-permute-start.17 = (bf16[512,1280]{1,0:T(8,128)(2,1)}, bf16[512,1280]{1,0:T(8,128)(2,1)}, u32[]{:S(2)}, u32[]{:S(2)}) collective-permute-start(bf16[512,1280]{1,0:T(8,128)(2,1)} %collective-permute-done.14.refs_1_), channel_id=1, source_target_pairs={{0,8},{8,0},{16,24},{24,16},{32,40},{40,32},{48,56},{56,48},{64,72... | collective-permute-start | bytes 3932168 | tf_op jit(solution)/shard_map/ppermute | solution.py:663
  114.5 34.8 %collective-permute-start.18 = (bf16[512,1280]{1,0:T(8,128)(2,1)}, bf16[512,1280]{1,0:T(8,128)(2,1)}, u32[]{:S(2)}, u32[]{:S(2)}) collective-permute-start(bf16[512,1280]{1,0:T(8,128)(2,1)} %collective-permute-done.15.refs_2_), channel_id=1, source_target_pairs={{0,8},{8,0},{16,24},{24,16},{32,40},{40,32},{48,56},{56,48},{64,72... | collective-permute-start | bytes 3932168 | tf_op jit(solution)/shard_map/ppermute | solution.py:663
  143.5 14.6 %copy-start.11 = (bf16[512,1280]{1,0:T(8,128)(2,1)}, bf16[512,1280]{1,0:T(8,128)(2,1)S(1)}, u32[]{:S(2)}) copy-start(bf16[512,1280]{1,0:T(8,128)(2,1)S(1)} %collective-permute-done.16.refs_3_) | copy-start | bytes 3932164
  143.5 14.6 %collective-permute-start.19 = (bf16[512,1280]{1,0:T(8,128)(2,1)S(1)}, bf16[512,1280]{1,0:T(8,128)(2,1)S(1)}, u32[]{:S(2)}, u32[]{:S(2)}) collective-permute-start(bf16[512,1280]{1,0:T(8,128)(2,1)S(1)} %collective-permute-done.16.refs_3_), channel_id=1, source_target_pairs={{0,8},{8,0},{16,24},{24,16},{32,40},{40,32},{48,56},{56,48},{64,72... | collective-permute-start | bytes 3932168 | tf_op jit(solution)/shard_map/ppermute | solution.py:663
  143.6 14.5 %all-to-all-start.3 = ((bf16[8,128,256]{2,1,0:T(8,128)(2,1)}), bf16[8,128,256]{2,1,0:T(8,128)(2,1)S(1)}, u32[]{:S(2)}, u32[]{:S(2)}) async-start(bf16[8,128,256]{2,1,0:T(8,128)(2,1)} %bitcast.55), calls=%async_computation.3 | async-start | bytes 1048576 | tf_op jit(solution)/shard_map/all_to_all | solution.py:716
  171.3 58.6 %all-to-all-start.4 = ((bf16[128,8,2048]{2,1,0:T(8,128)(2,1)}), bf16[128,8,2048]{2,1,0:T(8,128)(2,1)}, u32[]{:S(2)}, u32[]{:S(2)}) async-start(bf16[128,8,2048]{2,1,0:T(8,128)(2,1)} %convert_bitcast_fusion), calls=%async_computation.4 | async-start | bytes 8388608 | tf_op jit(solution)/shard_map/all_to_all | solution.py:412
  229.9 23.8 %all-to-all-start.5 = ((bf16[128,2,2048]{2,1,0:T(2,128)(2,1)}), bf16[128,2,2048]{2,1,0:T(2,128)(2,1)S(1)}, u32[]{:S(2)}, u32[]{:S(2)}) async-start(bf16[128,2,2048]{2,1,0:T(2,128)(2,1)} %reshape.153), calls=%async_computation.5 | async-start | bytes 2097152 | tf_op jit(solution)/shard_map/all_to_all | solution.py:412
  234.7 10.2 %copy-start.14 = (bf16[1,768,2048]{2,1,0:T(8,128)(2,1)S(1)}, bf16[1,768,2048]{2,1,0:T(8,128)(2,1)}, u32[]{:S(2)}) copy-start(bf16[1,768,2048]{2,1,0:T(8,128)(2,1)} %param.31) | copy-start | bytes 9437188
  262.9 9.3 %copy-start.26 = (f32[128,8]{0,1:T(8,128)S(1)}, f32[128,8]{0,1:T(8,128)}, u32[]{:S(2)}) copy-start(f32[128,8]{0,1:T(8,128)} %param.34) | copy-start | bytes 12292
  262.9 74.0 %all-to-all-start.6 = ((bf16[128,40,512]{2,1,0:T(8,128)(2,1)}), bf16[128,40,512]{2,1,0:T(8,128)(2,1)}, u32[]{:S(2)}, u32[]{:S(2)}) async-start(bf16[128,40,512]{2,1,0:T(8,128)(2,1)} %expert_rest.1), calls=%async_computation.6 | async-start | bytes 10485760 | tf_op jit(solution)/shard_map/all_to_all | solution.py:412
  (6 other events, 13.3 us)

commit v9 on v8

--- a/solution.py
+++ b/solution.py
@@ -144,9 +144,6 @@
     v_all,
     pk_all,
     pv_all,
-    peak_all,
-    total_all,
-    acc_all,
 ):
     pieces = (piece_0, piece_1, piece_2, piece_3)
     me = meta[0]
@@ -252,19 +249,18 @@
             scores = scale * score(q_now, pk_all[pl.ds(start, span), :]) + outside + foreign
             return join(state, scores, pv_all[pl.ds(start, span), :])
 
-        peak_all[...] = jnp.full((2 * tok, 1), MASKED, jnp.float32)
-        total_all[...] = jnp.zeros((2 * tok, 1), jnp.float32)
-        acc_all[...] = jnp.zeros((2 * tok, hd), jnp.float32)
         low = (first >= cut).astype(jnp.int32)
         high = (first + tok > cut).astype(jnp.int32)
-
-        @pl.loop(low, high + 1)
-        def _(req):
-            peak, total, acc = prefix(req, (peak_all[...], total_all[...], acc_all[...]))
-            peak_all[...] = peak
-            total_all[...] = total
-            acc_all[...] = acc
-
+        before = lax.fori_loop(
+            low,
+            high + 1,
+            prefix,
+            (
+                jnp.full((2 * tok, 1), MASKED, jnp.float32),
+                jnp.zeros((2 * tok, 1), jnp.float32),
+                jnp.zeros((2 * tok, hd), jnp.float32),
+            ),
+        )
         bottom = jnp.where(late, cut, 0)
 
         for quarter in range(count // 2):
@@ -276,7 +272,7 @@
                 allowed = jnp.logical_and(other <= token, other >= bottom)
                 scores = scale * score(q_now, k_all[0:keys, :])
                 peak, total, acc = join(
-                    (peak_all[...], total_all[...], acc_all[...]),
+                    before,
                     jnp.where(allowed, scores, MASKED),
                     v_all[0:keys, :],
                 )
@@ -303,9 +299,6 @@
             pltpu.VMEM((group, hd), jnp.bfloat16),
             pltpu.VMEM((path_rows, hd), jnp.bfloat16),
             pltpu.VMEM((path_rows, hd), jnp.bfloat16),
-            pltpu.VMEM((256, 1), jnp.float32),
-            pltpu.VMEM((256, 1), jnp.float32),
-            pltpu.VMEM((256, hd), jnp.float32),
         ],
         compiler_params=pltpu.CompilerParams(vmem_limit_bytes=60 * 1024 * 1024),
         cost_estimate=pl.CostEstimate(
@@ -403,7 +396,7 @@
             jax.ShapeDtypeStruct(hidden.shape, hidden.dtype),
             jax.ShapeDtypeStruct(hidden.shape, hidden.dtype),
         ),
-        compiler_params=pltpu.CompilerParams(vmem_limit_bytes=60 * 1024 * 1024),
+        compiler_params=pltpu.CompilerParams(vmem_limit_bytes=18 * 1024 * 1024),
         name="project",
     )(place, attended, *halves, hidden, gain)
 

time: 347 us -> 346 us (level)
  no operation moved by 1% of the time
where the time goes in v9:
time: 346 us; the launch traced here: 345 us
  waiting for transfers between devices  173 us (50%)
  starting transfers between devices  63.8 us (18%)
  Pallas kernels  48.1 us (14%)
  other arithmetic  20 us (6%)
  local copies, waits for them, and re-layouts  19.2 us (6%)
  matrix products  17.9 us (5%)
    all_to_all x3, waiting for transfers between devices, exchange(): return lax.all_to_all(values, BOTH, split_axis=0, concat_axis=0, tiled=True)  110 us
    pallas_call x1, Pallas kernels, attend(): pl.pallas_call(attention_kernel, out_shape=jax.ShapeDtypeStruct((group, 2...  20.9 us
    ppermute x6, waiting for transfers between devices, shift(): return lax.ppermute(values, 'mp', moves)  19.7 us
    all_to_all x3, starting transfers between devices, exchange(): return lax.all_to_all(values, BOTH, split_axis=0, concat_axis=0, tiled=True)  18.8 us
    all_to_all x1, waiting for transfers between devices, per_device(): path = lax.all_to_all(path, 'mp', split_axis=0, concat_axis=0, tiled=True)  14.7 us
    dot_general x1, matrix products, expert(): both = jnp.dot(rows, gate_up, preferred_element_type=jnp.float32)  10.2 us
    ppermute x6, starting transfers between devices, shift(): return lax.ppermute(values, 'mp', moves)  9.71 us
    all_to_all x1, waiting for transfers between devices, per_device(): lax.all_to_all(attended.reshape(mp_size, tok, 2 * hd), 'mp', split_axis=0...  9.32 us
  transfers between devices with their start and end apart: 27, of which 12 were waited for; matrix products, arithmetic and copies ran while one was open for 14% of the time, Pallas kernels for 7%

profile of v9, /device:TPU:0, one launch (start us, length us, event | category | flops | bytes accessed | tf_op | source)
XLA Modules:
  0.0 344.8 jit_solution(16170311437636103446)
XLA Ops:
  0.7 1.9 pack_weights.1
  2.6 6.4 %all-to-all-start = ((bf16[8,16,3072]{2,1,0:T(8,128)(2,1)}), bf16[8,16,3072]{2,1,0:T(8,128)(2,1)S(1)}, u32[]{:S(2)}, u32[]{:S(2)}) async-start(bf16[8,16,3072]{2,1,0:T(8,128)(2,1)} %pack_weights.1), calls=%async_computation | async-start | bytes 1572864 | tf_op jit(solution)/shard_map/all_to_all | solution.py:639
  15.0 1.5 fusion.30
  16.4 4.5 %all-to-all-done = bf16[8,16,3072]{2,1,0:T(8,128)(2,1)S(1)} async-done(((bf16[8,16,3072]{2,1,0:T(8,128)(2,1)}), bf16[8,16,3072]{2,1,0:T(8,128)(2,1)S(1)}, u32[]{:S(2)}, u32[]{:S(2)}) %all-to-all-start) | async-done | bytes 786464 | tf_op jit(solution)/shard_map/all_to_all | solution.py:639
  23.3 1.5 collective-permute-start.2
  26.7 6.8 %all-to-all-start.1 = ((bf16[16,128,256]{2,1,0:T(8,128)(2,1)}), bf16[16,128,256]{2,1,0:T(8,128)(2,1)}, u32[]{:S(2)}, u32[]{:S(2)}) async-start(bf16[16,128,256]{2,1,0:T(8,128)(2,1)} %bitcast.11), calls=%async_computation.1 | async-start | bytes 2097152 | tf_op jit(solution)/shard_map/all_to_all | solution.py:669
  34.5 3.5 %collective-permute-start.7 = (bf16[256,1280]{1,0:T(8,128)(2,1)S(1)}, bf16[256,1280]{1,0:T(8,128)(2,1)}, u32[]{:S(2)}, u32[]{:S(2)}) collective-permute-start(bf16[256,1280]{1,0:T(8,128)(2,1)S(1)} %pad_maximum_fusion.1), channel_id=1, source_target_pairs={{0,16},{8,24},{16,0},{24,8},{32,48},{40,56},{48,32},{56,40},{64,80... | collective-permute-start | bytes 1966088 | tf_op jit(solution)/shard_map/ppermute | solution.py:656
  39.0 2.4 collective-permute-start.1
  41.4 3.2 collective-permute-start.4
  47.2 2.2 pack_paths.1
  50.6 1.9 fusion.13
  52.5 1.3 pad_maximum_fusion.3
  54.3 10.1 %collective-permute-done.3.across_left = bf16[128,2048]{1,0:T(8,128)(2,1)} collective-permute-done((bf16[128,2048]{1,0:T(8,128)(2,1)}, bf16[128,2048]{1,0:T(8,128)(2,1)}, u32[]{:S(2)}, u32[]{:S(2)}) %collective-permute-start.3) | collective-permute-done | bytes 524320 | tf_op jit(solution)/shard_map/ppermute | solution.py:644
  64.4 4.3 %all-to-all-start.2 = ((bf16[8,448,256]{2,1,0:T(8,128)(2,1)}), bf16[8,448,256]{2,1,0:T(8,128)(2,1)}, u32[]{:S(2)}, u32[]{:S(2)}) async-start(bf16[8,448,256]{2,1,0:T(8,128)(2,1)} %pack_paths.1), calls=%async_computation.2 | async-start | bytes 3670016 | tf_op jit(solution)/shard_map/all_to_all | solution.py:696
  68.8 1.3 pad_maximum_fusion.refs_0_
  70.7 1.5 collective-permute-start.14
  72.1 1.8 collective-permute-start.15
  73.9 1.8 collective-permute-start.12
  75.8 1.4 collective-permute-start.13
  77.1 14.7 %all-to-all-done.2 = bf16[8,448,256]{2,1,0:T(8,128)(2,1)} async-done(((bf16[8,448,256]{2,1,0:T(8,128)(2,1)}), bf16[8,448,256]{2,1,0:T(8,128)(2,1)}, u32[]{:S(2)}, u32[]{:S(2)}) %all-to-all-start.2) | async-done | bytes 1835040 | tf_op jit(solution)/shard_map/all_to_all | solution.py:696
  91.8 1.8 reduce_sum.102.piece_0
  93.7 1.5 collective-permute-start.10
  95.2 9.1 %collective-permute-done.12.own_far = bf16[128,2048]{1,0:T(8,128)(2,1)} collective-permute-done((bf16[128,2048]{1,0:T(8,128)(2,1)}, bf16[128,2048]{1,0:T(8,128)(2,1)}, u32[]{:S(2)}, u32[]{:S(2)}) %collective-permute-start.12) | collective-permute-done | bytes 524320 | tf_op jit(solution)/shard_map/ppermute | solution.py:644
  105.6 2.3 collective-permute-done.10.piece_2
  107.8 4.9 %collective-permute-done.11.piece_3 = bf16[448,256]{1,0:T(8,128)(2,1)S(1)} collective-permute-done((bf16[448,256]{1,0:T(8,128)(2,1)S(1)}, bf16[448,256]{1,0:T(8,128)(2,1)S(1)}, u32[]{:S(2)}, u32[]{:S(2)}) %collective-permute-start.11) | collective-permute-done | bytes 229408 | tf_op jit(solution)/shard_map/ppermute | solution.py:700
  113.4 1.5 collective-permute-start.16
  115.4 20.9 %tree_attention.1 = bf16[1024,256]{1,0:T(8,128)(2,1)} custom-call(s32[9]{0:T(128)} %pad_add_fusion.2.meta, bf16[128,2048]{1,0:T(8,128)(2,1)} %copy-done.18, bf16[128,2048]{1,0:T(8,128)(2,1)} %collective-permute-done.2.across, bf16[128,2048]{1,0:T(8,128)(2,1)} %collective-permute-done.own_left, bf16[128,2048]{1,0:T(8,128)(2,1)} %collective-permute-done.1.own_right, ...), custom_call_target="tpu_custom_call" | custom-call | flops 2147483648 | bytes 8388608 | tf_op jit(solution)/shard_map/tree_attention/pallas_call | solution.py:289
  136.3 8.0 %collective-permute-done.16.refs_3_ = bf16[512,1280]{1,0:T(8,128)(2,1)} collective-permute-done((bf16[512,1280]{1,0:T(8,128)(2,1)}, bf16[512,1280]{1,0:T(8,128)(2,1)}, u32[]{:S(2)}, u32[]{:S(2)}) %collective-permute-start.16) | collective-permute-done | bytes 1310752 | tf_op jit(solution)/shard_map/ppermute | solution.py:660
  144.5 4.2 %all-to-all-start.3 = ((bf16[8,128,256]{2,1,0:T(8,128)(2,1)}), bf16[8,128,256]{2,1,0:T(8,128)(2,1)}, u32[]{:S(2)}, u32[]{:S(2)}) async-start(bf16[8,128,256]{2,1,0:T(8,128)(2,1)} %bitcast.55), calls=%async_computation.3 | async-start | bytes 1048576 | tf_op jit(solution)/shard_map/all_to_all | solution.py:709
  149.4 9.3 %all-to-all-done.3.attended = bf16[8,128,256]{2,1,0:T(8,128)(2,1)} async-done(((bf16[8,128,256]{2,1,0:T(8,128)(2,1)}), bf16[8,128,256]{2,1,0:T(8,128)(2,1)}, u32[]{:S(2)}, u32[]{:S(2)}) %all-to-all-start.3) | async-done | bytes 524320 | tf_op jit(solution)/shard_map/all_to_all | solution.py:709
  158.8 6.1 %project.1 = (bf16[128,2048]{1,0:T(8,128)(2,1)S(1)}, bf16[128,2048]{1,0:T(8,128)(2,1)S(1)}) custom-call(s32[3]{0:T(128)S(1)} %pad_add_fusion.1.place, bf16[8,128,256]{2,1,0:T(8,128)(2,1)} %all-to-all-done.3.attended, bf16[512,1280]{1,0:T(8,128)(2,1)S(1)} %pad_maximum_fusion.refs_0_, bf16[512,1280]{1,0:T(8,128)(2,1)} %collective-permute-done.14.refs_1_, ...), custom_call_target="tpu_custom_call" | custom-call | tf_op jit(solution)/shard_map/project/pallas_call | solution.py:371
  166.5 3.3 convert_bitcast_fusion
  169.9 6.1 %all-to-all-start.4 = ((bf16[128,8,2048]{2,1,0:T(8,128)(2,1)}), bf16[128,8,2048]{2,1,0:T(8,128)(2,1)}, u32[]{:S(2)}, u32[]{:S(2)}) async-start(bf16[128,8,2048]{2,1,0:T(8,128)(2,1)} %convert_bitcast_fusion), calls=%async_computation.4 | async-start | bytes 8388608 | tf_op jit(solution)/shard_map/all_to_all | solution.py:405
  176.7 1.5 reshape.153
  178.2 50.5 %all-to-all-done.4 = bf16[128,8,2048]{2,1,0:T(8,128)(2,1)} async-done(((bf16[128,8,2048]{2,1,0:T(8,128)(2,1)}), bf16[128,8,2048]{2,1,0:T(8,128)(2,1)}, u32[]{:S(2)}, u32[]{:S(2)}) %all-to-all-start.4) | async-done | bytes 4194336 | tf_op jit(solution)/shard_map/all_to_all | solution.py:405
  228.7 4.8 %all-to-all-start.5 = ((bf16[128,2,2048]{2,1,0:T(2,128)(2,1)}), bf16[128,2,2048]{2,1,0:T(2,128)(2,1)S(1)}, u32[]{:S(2)}, u32[]{:S(2)}) async-start(bf16[128,2,2048]{2,1,0:T(2,128)(2,1)} %reshape.153), calls=%async_computation.5 | async-start | bytes 2097152 | tf_op jit(solution)/shard_map/all_to_all | solution.py:405
  233.5 10.2 %fusion = f32[1024,1536]{1,0:T(8,128)S(1)} fusion(bf16[128,8,2048]{2,1,0:T(8,128)(2,1)} %all-to-all-done.4, bf16[1,2048,1536]{2,1,0:T(8,128)(2,1)} %param.30), kind=kOutput, calls=%fused_computation | convolution fusion | flops 6442450944 | bytes 16777216 | tf_op jit(solution)/shard_map/dot_general | solution.py:410
  243.7 3.7 %convolution_convert_fusion = bf16[1024,2048]{1,0:T(8,128)(2,1)S(1)} fusion(f32[1024,1536]{1,0:T(8,128)S(1)} %fusion, bf16[1,768,2048]{2,1,0:T(8,128)(2,1)S(1)} %copy-done.17), kind=kOutput, calls=%fused_computation.3 | convolution fusion | flops 3228041216 | bytes 13631488 | tf_op jit(solution)/shard_map/dot_general | solution.py:412
  247.4 2.9 pad.4.main_block
  250.3 2.2 all-to-all-done.5
  253.7 8.0 %expert_rest.1 = bf16[128,40,512]{2,1,0:T(8,128)(2,1)} custom-call(bf16[256,2048]{1,0:T(8,128)(2,1)} %reshape.157.rows, bf16[2048,1536]{1,0:T(8,128)(2,1)} %bitcast.50, bf16[768,2048]{1,0:T(8,128)(2,1)} %bitcast.52, bf16[128,40,512]{2,1,0:T(8,128)(2,1)} %pad.4.main_block), custom_call_target="tpu_custom_call", output_to_operand_aliasing={{}: (3, {})} | custom-call | tf_op jit(solution)/shard_map/expert_rest/pallas_call | solution.py:453
  261.7 7.8 %all-to-all-start.6 = ((bf16[128,40,512]{2,1,0:T(8,128)(2,1)}), bf16[128,40,512]{2,1,0:T(8,128)(2,1)}, u32[]{:S(2)}, u32[]{:S(2)}) async-start(bf16[128,40,512]{2,1,0:T(8,128)(2,1)} %expert_rest.1), calls=%async_computation.6 | async-start | bytes 10485760 | tf_op jit(solution)/shard_map/all_to_all | solution.py:405
  269.6 1.3 slice.51.refs_9_
  274.3 1.5 broadcast_multiply_fusion.rest_share
  275.8 1.5 constant_dynamic-slice_fusion.refs_11_
  277.3 1.5 constant_dynamic-slice_fusion.1.refs_10_
  278.7 57.0 %all-to-all-done.6.main_rows.rest_rows = bf16[128,40,512]{2,1,0:T(8,128)(2,1)} async-done(((bf16[128,40,512]{2,1,0:T(8,128)(2,1)}), bf16[128,40,512]{2,1,0:T(8,128)(2,1)}, u32[]{:S(2)}, u32[]{:S(2)}) %all-to-all-start.6) | async-done | bytes 5242912 | tf_op jit(solution)/shard_map/all_to_all | solution.py:405
  335.7 8.9 %finish.1 = (bf16[128,2048]{1,0:T(8,128)(2,1)}, bf16[128,512]{1,0:T(8,128)(2,1)}) custom-call(s32[3]{0:T(128)} %copy-done.10, bf16[256,1024]{1,0:T(8,128)(2,1)} %pad_maximum_fusion.2.main_share, bf16[4,256,1024]{2,1,0:T(8,128)(2,1)} %broadcast_multiply_fusion.rest_share, bf16[128,40,512]{2,1,0:T(8,128)(2,1)} %all-to-all-done.6.main_rows.rest_rows, ...), custom_call_target="tpu_custom_call" | custom-call | tf_op jit(solution)/shard_map/finish/pallas_call | solution.py:535
  (133 shorter events, 25.8 us)
Async XLA Ops:
  0.6 24.2 %copy-start.9 = (s32[1024]{0:T(1024)S(1)}, s32[1024]{0:T(1024)}, u32[]{:S(2)}) copy-start(s32[1024]{0:T(1024)} %token_request.1) | copy-start | bytes 12292
  0.6 22.3 %copy-start.2 = (bf16[128,2048]{1,0:T(8,128)(2,1)S(1)}, bf16[128,2048]{1,0:T(8,128)(2,1)}, u32[]{:S(2)}) copy-start(bf16[128,2048]{1,0:T(8,128)(2,1)} %refs_8_.1) | copy-start | bytes 1572868
  2.6 18.4 %all-to-all-start = ((bf16[8,16,3072]{2,1,0:T(8,128)(2,1)}), bf16[8,16,3072]{2,1,0:T(8,128)(2,1)S(1)}, u32[]{:S(2)}, u32[]{:S(2)}) async-start(bf16[8,16,3072]{2,1,0:T(8,128)(2,1)} %pack_weights.1), calls=%async_computation | async-start | bytes 1572864 | tf_op jit(solution)/shard_map/all_to_all | solution.py:639
  23.0 10.5 %collective-permute-start.6 = (bf16[128,1280]{1,0:T(8,128)(2,1)}, bf16[128,1280]{1,0:T(8,128)(2,1)}, u32[]{:S(2)}, u32[]{:S(2)}) collective-permute-start(bf16[128,1280]{1,0:T(8,128)(2,1)} %get-tuple-element.71), channel_id=1, source_target_pairs={{0,8},{8,0},{16,24},{24,16},{32,40},{40,32},{48,56},{56,48},{64,72... | collective-permute-start | bytes 983048 | tf_op jit(solution)/shard_map/ppermute | solution.py:656
  23.0 24.1 %copy-start.6 = (bf16[1,512,512]{2,1,0:T(8,128)(2,1)S(1)}, bf16[1,512,512]{2,1,0:T(8,128)(2,1)}, u32[]{:S(2)}) copy-start(bf16[1,512,512]{2,1,0:T(8,128)(2,1)} %root.1) | copy-start | bytes 1572868
  23.0 24.1 %copy-start.7 = (bf16[1,256,512]{2,1,0:T(8,128)(2,1)S(1)}, bf16[1,256,512]{2,1,0:T(8,128)(2,1)}, u32[]{:S(2)}) copy-start(bf16[1,256,512]{2,1,0:T(8,128)(2,1)} %mid.1) | copy-start | bytes 786436
  23.0 24.1 %copy-start.8 = (bf16[2,128,512]{2,1,0:T(8,128)(2,1)S(1)}, bf16[2,128,512]{2,1,0:T(8,128)(2,1)}, u32[]{:S(2)}) copy-start(bf16[2,128,512]{2,1,0:T(8,128)(2,1)} %leaf.1) | copy-start | bytes 786436
  23.0 24.1 %copy-start.11 = (s32[16]{0:T(128)S(1)}, s32[16]{0:T(128)}, u32[]{:S(2)}) copy-start(s32[16]{0:T(128)} %leaf_parent.1) | copy-start | bytes 196
  23.0 24.1 %copy-start.12 = (s32[8]{0:T(128)S(1)}, s32[8]{0:T(128)}, u32[]{:S(2)}) copy-start(s32[8]{0:T(128)} %mid_parent.1) | copy-start | bytes 100
  23.0 24.1 %copy-start.13 = (s32[32]{0:T(128)S(1)}, s32[32]{0:T(128)}, u32[]{:S(2)}) copy-start(s32[32]{0:T(128)} %request_leaf.1) | copy-start | bytes 388
  23.0 24.1 %copy-start.14 = (s32[8]{0:T(128)S(1)}, s32[8]{0:T(128)}, u32[]{:S(2)}) copy-start(s32[8]{0:T(128)} %root_slot.1) | copy-start | bytes 100
  23.1 24.1 %copy-start.15 = (s32[8]{0:T(128)S(1)}, s32[8]{0:T(128)}, u32[]{:S(2)}) copy-start(s32[8]{0:T(128)} %mid_slot.1) | copy-start | bytes 100
  23.1 24.1 %copy-start.16 = (s32[16]{0:T(128)S(1)}, s32[16]{0:T(128)}, u32[]{:S(2)}) copy-start(s32[16]{0:T(128)} %leaf_slot.1) | copy-start | bytes 196
  23.3 26.1 %copy-start.18 = (bf16[128,2048]{1,0:T(8,128)(2,1)}, bf16[128,2048]{1,0:T(8,128)(2,1)S(1)}, u32[]{:S(2)}) copy-start(bf16[128,2048]{1,0:T(8,128)(2,1)S(1)} %fusion.8.own) | copy-start | bytes 1572868
  23.3 18.1 %collective-permute-start.2 = (bf16[128,2048]{1,0:T(8,128)(2,1)S(1)}, bf16[128,2048]{1,0:T(8,128)(2,1)}, u32[]{:S(2)}, u32[]{:S(2)}) collective-permute-start(bf16[128,2048]{1,0:T(8,128)(2,1)S(1)} %fusion.8.own), channel_id=1, source_target_pairs={{0,4},{1,5},{2,6},{3,7},{4,0},{5,1},{6,2},{7,3},{8,12},{9,13},{10,... | collective-permute-start | bytes 1572872 | tf_op jit(solution)/shard_map/ppermute | solution.py:646
  26.7 27.6 %all-to-all-start.1 = ((bf16[16,128,256]{2,1,0:T(8,128)(2,1)}), bf16[16,128,256]{2,1,0:T(8,128)(2,1)}, u32[]{:S(2)}, u32[]{:S(2)}) async-start(bf16[16,128,256]{2,1,0:T(8,128)(2,1)} %bitcast.11), calls=%async_computation.1 | async-start | bytes 2097152 | tf_op jit(solution)/shard_map/all_to_all | solution.py:669
  34.5 34.3 %collective-permute-start.7 = (bf16[256,1280]{1,0:T(8,128)(2,1)S(1)}, bf16[256,1280]{1,0:T(8,128)(2,1)}, u32[]{:S(2)}, u32[]{:S(2)}) collective-permute-start(bf16[256,1280]{1,0:T(8,128)(2,1)S(1)} %pad_maximum_fusion.1), channel_id=1, source_target_pairs={{0,16},{8,24},{16,0},{24,8},{32,48},{40,56},{48,32},{56,40},{64,80... | collective-permute-start | bytes 1966088 | tf_op jit(solution)/shard_map/ppermute | solution.py:656
  38.1 16.1 %collective-permute-start = (bf16[128,2048]{1,0:T(8,128)(2,1)S(1)}, bf16[128,2048]{1,0:T(8,128)(2,1)}, u32[]{:S(2)}, u32[]{:S(2)}) collective-permute-start(bf16[128,2048]{1,0:T(8,128)(2,1)S(1)} %fusion.8.own), channel_id=1, source_target_pairs={{0,1},{1,2},{2,3},{3,0},{4,5},{5,6},{6,7},{7,4},{8,9},{9,10},{10,1... | collective-permute-start | bytes 1572872 | tf_op jit(solution)/shard_map/ppermute | solution.py:644
  39.0 15.3 %collective-permute-start.1 = (bf16[128,2048]{1,0:T(8,128)(2,1)S(1)}, bf16[128,2048]{1,0:T(8,128)(2,1)}, u32[]{:S(2)}, u32[]{:S(2)}) collective-permute-start(bf16[128,2048]{1,0:T(8,128)(2,1)S(1)} %fusion.8.own), channel_id=1, source_target_pairs={{0,3},{1,0},{2,1},{3,2},{4,7},{5,4},{6,5},{7,6},{8,11},{9,8},{10,9... | collective-permute-start | bytes 1572872 | tf_op jit(solution)/shard_map/ppermute | solution.py:644
  41.4 23.0 %collective-permute-start.3 = (bf16[128,2048]{1,0:T(8,128)(2,1)}, bf16[128,2048]{1,0:T(8,128)(2,1)}, u32[]{:S(2)}, u32[]{:S(2)}) collective-permute-start(bf16[128,2048]{1,0:T(8,128)(2,1)} %collective-permute-done.2.across), channel_id=1, source_target_pairs={{0,1},{1,2},{2,3},{3,0},{4,5},{5,6},{6,7},{7,4},{8,9},{9,10},{10,1... | collective-permute-start | bytes 1572872 | tf_op jit(solution)/shard_map/ppermute | solution.py:644
  41.4 23.0 %collective-permute-start.4 = (bf16[128,2048]{1,0:T(8,128)(2,1)}, bf16[128,2048]{1,0:T(8,128)(2,1)}, u32[]{:S(2)}, u32[]{:S(2)}) collective-permute-start(bf16[128,2048]{1,0:T(8,128)(2,1)} %collective-permute-done.2.across), channel_id=1, source_target_pairs={{0,3},{1,0},{2,1},{3,2},{4,7},{5,4},{6,5},{7,6},{8,11},{9,8},{10,9... | collective-permute-start | bytes 1572872 | tf_op jit(solution)/shard_map/ppermute | solution.py:644
  64.4 27.4 %all-to-all-start.2 = ((bf16[8,448,256]{2,1,0:T(8,128)(2,1)}), bf16[8,448,256]{2,1,0:T(8,128)(2,1)}, u32[]{:S(2)}, u32[]{:S(2)}) async-start(bf16[8,448,256]{2,1,0:T(8,128)(2,1)} %pack_paths.1), calls=%async_computation.2 | async-start | bytes 3670016 | tf_op jit(solution)/shard_map/all_to_all | solution.py:696
  68.7 7.0 %collective-permute-start.5 = (bf16[2048,256]{1,0:T(8,128)(2,1)}, bf16[2048,256]{1,0:T(8,128)(2,1)}, u32[]{:S(2)}, u32[]{:S(2)}) collective-permute-start(bf16[2048,256]{1,0:T(8,128)(2,1)} %bitcast.12.weight_own), channel_id=1, source_target_pairs={{0,8},{8,0},{16,24},{24,16},{32,40},{40,32},{48,56},{56,48},{64,72... | collective-permute-start | bytes 3145736 | tf_op jit(solution)/shard_map/ppermute | solution.py:656
  70.1 88.7 %copy-start = (bf16[512,1280]{1,0:T(8,128)(2,1)}, bf16[512,1280]{1,0:T(8,128)(2,1)S(1)}, u32[]{:S(2)}) copy-start(bf16[512,1280]{1,0:T(8,128)(2,1)S(1)} %pad_maximum_fusion.refs_0_) | copy-start | bytes 3932164
  70.1 23.6 %collective-permute-start.8 = (bf16[512,1280]{1,0:T(8,128)(2,1)S(1)}, bf16[512,1280]{1,0:T(8,128)(2,1)S(1)}, u32[]{:S(2)}, u32[]{:S(2)}) collective-permute-start(bf16[512,1280]{1,0:T(8,128)(2,1)S(1)} %pad_maximum_fusion.refs_0_), channel_id=1, source_target_pairs={{0,8},{8,0},{16,24},{24,16},{32,40},{40,32},{48,56},{56,48},{64,72... | collective-permute-start | bytes 3932168 | tf_op jit(solution)/shard_map/ppermute | solution.py:656
  70.7 34.9 %collective-permute-start.14 = (bf16[512,1280]{1,0:T(8,128)(2,1)S(1)}, bf16[512,1280]{1,0:T(8,128)(2,1)}, u32[]{:S(2)}, u32[]{:S(2)}) collective-permute-start(bf16[512,1280]{1,0:T(8,128)(2,1)S(1)} %pad_maximum_fusion.refs_0_), channel_id=1, source_target_pairs={{0,32},{8,40},{16,48},{24,56},{32,64},{40,72},{48,80},{56,88},{64,... | collective-permute-start | bytes 3932168 | tf_op jit(solution)/shard_map/ppermute | solution.py:660
  72.1 33.4 %collective-permute-start.15 = (bf16[512,1280]{1,0:T(8,128)(2,1)S(1)}, bf16[512,1280]{1,0:T(8,128)(2,1)}, u32[]{:S(2)}, u32[]{:S(2)}) collective-permute-start(bf16[512,1280]{1,0:T(8,128)(2,1)S(1)} %pad_maximum_fusion.refs_0_), channel_id=1, source_target_pairs={{0,96},{8,104},{16,112},{24,120},{32,0},{40,8},{48,16},{56,24},{64... | collective-permute-start | bytes 3932168 | tf_op jit(solution)/shard_map/ppermute | solution.py:660
  73.9 30.4 %collective-permute-start.12 = (bf16[128,2048]{1,0:T(8,128)(2,1)}, bf16[128,2048]{1,0:T(8,128)(2,1)}, u32[]{:S(2)}, u32[]{:S(2)}) collective-permute-start(bf16[128,2048]{1,0:T(8,128)(2,1)} %collective-permute-done.own_left), channel_id=1, source_target_pairs={{0,1},{1,2},{2,3},{3,0},{4,5},{5,6},{6,7},{7,4},{8,9},{9,10},{10,1... | collective-permute-start | bytes 1572872 | tf_op jit(solution)/shard_map/ppermute | solution.py:644
  75.8 29.8 %collective-permute-start.13 = (bf16[128,2048]{1,0:T(8,128)(2,1)}, bf16[128,2048]{1,0:T(8,128)(2,1)}, u32[]{:S(2)}, u32[]{:S(2)}) collective-permute-start(bf16[128,2048]{1,0:T(8,128)(2,1)} %collective-permute-done.4.across_right), channel_id=1, source_target_pairs={{0,3},{1,0},{2,1},{3,2},{4,7},{5,4},{6,5},{7,6},{8,11},{9,8},{10,9... | collective-permute-start | bytes 1572872 | tf_op jit(solution)/shard_map/ppermute | solution.py:644
  93.7 21.7 %copy-start.19 = (bf16[448,256]{1,0:T(8,128)(2,1)}, bf16[448,256]{1,0:T(8,128)(2,1)S(1)}, u32[]{:S(2)}) copy-start(bf16[448,256]{1,0:T(8,128)(2,1)S(1)} %reduce_sum.102.piece_0) | copy-start | bytes 688132
  93.7 50.7 %copy-start.23 = (s32[128,8]{0,1:T(8,128)S(1)}, s32[128,8]{0,1:T(8,128)}, u32[]{:S(2)}) copy-start(s32[128,8]{0,1:T(8,128)} %param.33) | copy-start | bytes 12292
  93.7 65.1 %copy-start.1 = (bf16[512,1280]{1,0:T(8,128)(2,1)}, bf16[512,1280]{1,0:T(8,128)(2,1)S(1)}, u32[]{:S(2)}) copy-start(bf16[512,1280]{1,0:T(8,128)(2,1)S(1)} %collective-permute-done.8.refs_4_) | copy-start | bytes 3932164
  93.7 14.1 %collective-permute-start.10 = (bf16[448,256]{1,0:T(8,128)(2,1)S(1)}, bf16[448,256]{1,0:T(8,128)(2,1)S(1)}, u32[]{:S(2)}, u32[]{:S(2)}) collective-permute-start(bf16[448,256]{1,0:T(8,128)(2,1)S(1)} %reduce_sum.102.piece_0), channel_id=1, source_target_pairs={{0,2},{1,3},{2,0},{3,1},{4,6},{5,7},{6,4},{7,5},{8,10},{9,11},{10,... | collective-permute-start | bytes 688136 | tf_op jit(solution)/shard_map/ppermute | solution.py:700
  104.3 8.4 %collective-permute-start.11 = (bf16[448,256]{1,0:T(8,128)(2,1)S(1)}, bf16[448,256]{1,0:T(8,128)(2,1)S(1)}, u32[]{:S(2)}, u32[]{:S(2)}) collective-permute-start(bf16[448,256]{1,0:T(8,128)(2,1)S(1)} %reduce_sum.102.piece_0), channel_id=1, source_target_pairs={{0,3},{1,2},{2,1},{3,0},{4,7},{5,6},{6,5},{7,4},{8,11},{9,10},{10,... | collective-permute-start | bytes 688136 | tf_op jit(solution)/shard_map/ppermute | solution.py:700
  105.5 7.2 %collective-permute-start.9 = (bf16[448,256]{1,0:T(8,128)(2,1)S(1)}, bf16[448,256]{1,0:T(8,128)(2,1)S(1)}, u32[]{:S(2)}, u32[]{:S(2)}) collective-permute-start(bf16[448,256]{1,0:T(8,128)(2,1)S(1)} %reduce_sum.102.piece_0), channel_id=1, source_target_pairs={{0,1},{1,0},{2,3},{3,2},{4,5},{5,4},{6,7},{7,6},{8,9},{9,8},{10,11... | collective-permute-start | bytes 688136 | tf_op jit(solution)/shard_map/ppermute | solution.py:700
  107.8 7.6 %copy-start.20 = (bf16[448,256]{1,0:T(8,128)(2,1)}, bf16[448,256]{1,0:T(8,128)(2,1)S(1)}, u32[]{:S(2)}) copy-start(bf16[448,256]{1,0:T(8,128)(2,1)S(1)} %collective-permute-done.10.piece_2) | copy-start | bytes 688132
  113.4 30.9 %collective-permute-start.16 = (bf16[512,1280]{1,0:T(8,128)(2,1)}, bf16[512,1280]{1,0:T(8,128)(2,1)}, u32[]{:S(2)}, u32[]{:S(2)}) collective-permute-start(bf16[512,1280]{1,0:T(8,128)(2,1)} %collective-permute-done.14.refs_1_), channel_id=1, source_target_pairs={{0,32},{8,40},{16,48},{24,56},{32,64},{40,72},{48,80},{56,88},{64,... | collective-permute-start | bytes 3932168 | tf_op jit(solution)/shard_map/ppermute | solution.py:660
  114.9 34.5 %collective-permute-start.17 = (bf16[512,1280]{1,0:T(8,128)(2,1)}, bf16[512,1280]{1,0:T(8,128)(2,1)}, u32[]{:S(2)}, u32[]{:S(2)}) collective-permute-start(bf16[512,1280]{1,0:T(8,128)(2,1)} %collective-permute-done.14.refs_1_), channel_id=1, source_target_pairs={{0,8},{8,0},{16,24},{24,16},{32,40},{40,32},{48,56},{56,48},{64,72... | collective-permute-start | bytes 3932168 | tf_op jit(solution)/shard_map/ppermute | solution.py:656
  114.9 34.5 %collective-permute-start.18 = (bf16[512,1280]{1,0:T(8,128)(2,1)}, bf16[512,1280]{1,0:T(8,128)(2,1)}, u32[]{:S(2)}, u32[]{:S(2)}) collective-permute-start(bf16[512,1280]{1,0:T(8,128)(2,1)} %collective-permute-done.15.refs_2_), channel_id=1, source_target_pairs={{0,8},{8,0},{16,24},{24,16},{32,40},{40,32},{48,56},{56,48},{64,72... | collective-permute-start | bytes 3932168 | tf_op jit(solution)/shard_map/ppermute | solution.py:656
  144.4 14.4 %collective-permute-start.19 = (bf16[512,1280]{1,0:T(8,128)(2,1)}, bf16[512,1280]{1,0:T(8,128)(2,1)}, u32[]{:S(2)}, u32[]{:S(2)}) collective-permute-start(bf16[512,1280]{1,0:T(8,128)(2,1)} %collective-permute-done.16.refs_3_), channel_id=1, source_target_pairs={{0,8},{8,0},{16,24},{24,16},{32,40},{40,32},{48,56},{56,48},{64,72... | collective-permute-start | bytes 3932168 | tf_op jit(solution)/shard_map/ppermute | solution.py:656
  144.5 14.3 %all-to-all-start.3 = ((bf16[8,128,256]{2,1,0:T(8,128)(2,1)}), bf16[8,128,256]{2,1,0:T(8,128)(2,1)}, u32[]{:S(2)}, u32[]{:S(2)}) async-start(bf16[8,128,256]{2,1,0:T(8,128)(2,1)} %bitcast.55), calls=%async_computation.3 | async-start | bytes 1048576 | tf_op jit(solution)/shard_map/all_to_all | solution.py:709
  149.4 15.5 %copy-start.10 = (s32[3]{0:T(128)}, s32[3]{0:T(128)S(1)}, u32[]{:S(2)}) copy-start(s32[3]{0:T(128)S(1)} %pad_add_fusion.1.place) | copy-start | bytes 40
  169.9 6.3 %copy-start.4 = (bf16[128,2048]{1,0:T(8,128)(2,1)S(1)}, bf16[128,2048]{1,0:T(8,128)(2,1)}, u32[]{:S(2)}) copy-start(bf16[128,2048]{1,0:T(8,128)(2,1)} %copy-done.3) | copy-start | bytes 1572868
  169.9 58.8 %all-to-all-start.4 = ((bf16[128,8,2048]{2,1,0:T(8,128)(2,1)}), bf16[128,8,2048]{2,1,0:T(8,128)(2,1)}, u32[]{:S(2)}, u32[]{:S(2)}) async-start(bf16[128,8,2048]{2,1,0:T(8,128)(2,1)} %convert_bitcast_fusion), calls=%async_computation.4 | async-start | bytes 8388608 | tf_op jit(solution)/shard_map/all_to_all | solution.py:405
  228.7 23.8 %all-to-all-start.5 = ((bf16[128,2,2048]{2,1,0:T(2,128)(2,1)}), bf16[128,2,2048]{2,1,0:T(2,128)(2,1)S(1)}, u32[]{:S(2)}, u32[]{:S(2)}) async-start(bf16[128,2,2048]{2,1,0:T(2,128)(2,1)} %reshape.153), calls=%async_computation.5 | async-start | bytes 2097152 | tf_op jit(solution)/shard_map/all_to_all | solution.py:405
  233.5 10.2 %copy-start.17 = (bf16[1,768,2048]{2,1,0:T(8,128)(2,1)S(1)}, bf16[1,768,2048]{2,1,0:T(8,128)(2,1)}, u32[]{:S(2)}) copy-start(bf16[1,768,2048]{2,1,0:T(8,128)(2,1)} %param.31) | copy-start | bytes 9437188
  261.7 9.2 %copy-start.24 = (f32[128,8]{0,1:T(8,128)S(1)}, f32[128,8]{0,1:T(8,128)}, u32[]{:S(2)}) copy-start(f32[128,8]{0,1:T(8,128)} %param.34) | copy-start | bytes 12292
  261.7 74.0 %all-to-all-start.6 = ((bf16[128,40,512]{2,1,0:T(8,128)(2,1)}), bf16[128,40,512]{2,1,0:T(8,128)(2,1)}, u32[]{:S(2)}, u32[]{:S(2)}) async-start(bf16[128,40,512]{2,1,0:T(8,128)(2,1)} %expert_rest.1), calls=%async_computation.6 | async-start | bytes 10485760 | tf_op jit(solution)/shard_map/all_to_all | solution.py:405
  (4 other events, 5.0 us)
